TPU v7x, 32 devices: a whole 2x2x4 slice. The times are simulated.
32 devices in a mesh: seq: 4 (over x, core), fsdp: 8 (over z, y).
Axes of the slice: x: 2, y: 2, z: 4, core: 2. Of those that a mesh axis runs over, the one named last changes fastest.
Arguments:
- tokens: bfloat16 [8, 4096, 768], P('fsdp', 'seq'), may hold values from -6 to 6
- block_ids: int32 [8, 2048], P('fsdp'), may hold values from 0 to 15, never falling along the last dimension, each value on 1 to 256 neighbouring positions
- ln1_scale: bfloat16 [768], P('fsdp'), may hold values from 0.5 to 1.5
- ln1_bias: bfloat16 [768], P('fsdp'), may hold values from -1 to 1
- qkv_weight: bfloat16 [768, 2304], P('fsdp'), may hold values from -0.21875 to 0.21875
- qkv_bias: bfloat16 [2304], P('fsdp'), may hold values from -1 to 1
- out_weight: bfloat16 [768, 768], P('fsdp'), may hold values from -3.5 to 3.5
- out_bias: bfloat16 [768], P('fsdp'), may hold values from -1 to 1
- ln2_scale: bfloat16 [768], P('fsdp'), may hold values from 0.5 to 1.5
- ln2_bias: bfloat16 [768], P('fsdp'), may hold values from -1 to 1
- up_weight: bfloat16 [768, 3072], P('fsdp'), may hold values from -0.21875 to 0.21875
- up_bias: bfloat16 [3072], P('fsdp'), may hold values from -1 to 1
- down_weight: bfloat16 [3072, 768], P('fsdp'), may hold values from -0.109375 to 0.109375
- down_bias: bfloat16 [768], P('fsdp'), may hold values from -1 to 1
- cotangent: bfloat16 [8, 4096, 768], P('fsdp', 'seq'), may hold values from -6 to 6
Outputs:
- output: bfloat16 [8, 4096, 768], P('fsdp', 'seq')
- input_grad: float32 [8, 4096, 768], P('fsdp', 'seq')
- ln1_scale_grad: float32 [768], P('fsdp')
- ln1_bias_grad: float32 [768], P('fsdp')
- qkv_weight_grad: float32 [768, 2304], P('fsdp')
- qkv_bias_grad: float32 [2304], P('fsdp')
- out_weight_grad: float32 [768, 768], P('fsdp')
- out_bias_grad: float32 [768], P('fsdp')
- ln2_scale_grad: float32 [768], P('fsdp')
- ln2_bias_grad: float32 [768], P('fsdp')
- up_weight_grad: float32 [768, 3072], P('fsdp')
- up_bias_grad: float32 [3072], P('fsdp')
- down_weight_grad: float32 [3072, 768], P('fsdp')
- down_bias_grad: float32 [768], P('fsdp')
Inputs may be any that keep to these rules, and one draw needn't show every extreme that they name: `block_ids`: along each sequence the block id never falls; every id from 0 to 15 occurs, each block holds 1 to 256 positions, and some block holds exactly 256.
All inputs are finite; a program needn't handle non-finite values.
Results may differ from a plain program's by a relative error of at most 0.0095.
Values may be sent and summed in bfloat16 or wider, within the bound.
A program may use at most 192 MiB of HBM per device.

v0:
```python
import jax
import jax.numpy as jnp
from jax import lax
from jax.sharding import PartitionSpec as P

H = 12
HD = 64


EPSILON = 1e-05


def normalize_parts(values):
    mean_value = jnp.mean(values, -1, keepdims=True)
    centred = values - mean_value
    variance = jnp.mean(centred * centred, -1, keepdims=True)
    inverse = lax.rsqrt(variance + EPSILON)
    return (centred * inverse, inverse)


def norm_backward(grad_out, normed, inverse, scale):
    grad_norm = grad_out * scale
    return inverse * (
        grad_norm
        - jnp.mean(grad_norm, -1, keepdims=True)
        - normed * jnp.mean(grad_norm * normed, -1, keepdims=True)
    )


def tables(positions, half_dim):
    frequency = jnp.exp(-jnp.log(10000.0) * jnp.arange(half_dim, dtype=jnp.float32) / half_dim)
    angles = positions.astype(jnp.float32)[:, None] * frequency
    return (jnp.cos(angles), jnp.sin(angles))


def rotate(values, cos_table, sin_table):
    half_dim = values.shape[-1] // 2
    first_half = values[..., :half_dim]
    second_half = values[..., half_dim:]
    return jnp.concatenate(
        [
            first_half * cos_table - second_half * sin_table,
            first_half * sin_table + second_half * cos_table,
        ],
        -1,
    )


def unrotate(values, cos_table, sin_table):
    half_dim = values.shape[-1] // 2
    first_half = values[..., :half_dim]
    second_half = values[..., half_dim:]
    return jnp.concatenate(
        [
            first_half * cos_table + second_half * sin_table,
            second_half * cos_table - first_half * sin_table,
        ],
        -1,
    )


def allowed(query_blocks, query_clean, key_blocks, key_clean):
    noisy_allowed = jnp.where(
        key_clean[None, :],
        key_blocks[None, :] < query_blocks[:, None],
        key_blocks[None, :] == query_blocks[:, None],
    )
    clean_allowed = key_clean[None, :] & (key_blocks[None, :] <= query_blocks[:, None])
    return jnp.where(query_clean[:, None], clean_allowed, noisy_allowed)


def rows_contract(left, right):
    return lax.dot_general(
        left, right, (((0,), (0,)), ((), ())), preferred_element_type=jnp.float32
    )


def right_transposed(left, right):
    return lax.dot_general(
        left, right, (((1,), (1,)), ((), ())), preferred_element_type=jnp.float32
    )


def block_scores(query_block, key_rows, offset, query_rows, row_blocks, clean_rows):
    scores = right_transposed(query_block, key_rows) * 0.125
    allowed_mask = allowed(
        lax.dynamic_slice_in_dim(row_blocks, offset, query_rows, 0),
        lax.dynamic_slice_in_dim(clean_rows, offset, query_rows, 0),
        row_blocks,
        clean_rows,
    )
    return jnp.where(allowed_mask, scores, -1e30)


def attend_heads(packed, row_blocks, clean_rows):
    total_rows = packed.shape[0]
    head_dim = packed.shape[2] // 3
    query_rows = min(512, total_rows)
    starts = jnp.arange(total_rows // query_rows, dtype=jnp.int32) * query_rows

    def one_head(stacked):
        queries = stacked[:, :head_dim]
        key_rows = stacked[:, head_dim : 2 * head_dim]
        values = stacked[:, 2 * head_dim :]

        def one_block(offset):
            query_block = lax.dynamic_slice_in_dim(queries, offset, query_rows, 0)
            scores = block_scores(query_block, key_rows, offset, query_rows, row_blocks, clean_rows)
            maximum = jnp.max(scores, -1, keepdims=True)
            weights = jnp.exp(scores - maximum)
            denominator = jnp.sum(weights, -1, keepdims=True)
            probability = (weights / denominator).astype(jnp.bfloat16)
            attended = jnp.dot(probability, values, preferred_element_type=jnp.float32).astype(
                jnp.bfloat16
            )
            return (attended, (maximum + jnp.log(denominator))[:, 0])

        attended, log_sums = lax.map(one_block, starts)
        return (attended.reshape(total_rows, head_dim), log_sums.reshape(total_rows))

    attended, log_sums = lax.map(one_head, jnp.moveaxis(packed, 1, 0))
    return (jnp.moveaxis(attended, 0, 1), jnp.moveaxis(log_sums, 0, 1))


def attend_back(packed, log_sums, grad_heads, row_blocks, clean_rows, cos_table, sin_table):
    total_rows = packed.shape[0]
    head_dim = packed.shape[2] // 3
    query_rows = min(512, total_rows)
    starts = jnp.arange(total_rows // query_rows, dtype=jnp.int32) * query_rows

    def one_head(head_item):
        stacked, lse_column, grad_column = head_item
        queries = stacked[:, :head_dim]
        key_rows = stacked[:, head_dim : 2 * head_dim]
        values = stacked[:, 2 * head_dim :]

        def one_block(accumulators, offset):
            key_acc, value_acc = accumulators
            query_block = lax.dynamic_slice_in_dim(queries, offset, query_rows, 0)
            grad_block = lax.dynamic_slice_in_dim(grad_column, offset, query_rows, 0)
            lse_block = lax.dynamic_slice_in_dim(lse_column, offset, query_rows, 0)
            scores = block_scores(query_block, key_rows, offset, query_rows, row_blocks, clean_rows)
            probability = jnp.exp(scores - lse_block[:, None])
            value_acc = value_acc + rows_contract(probability.astype(jnp.bfloat16), grad_block)
            grad_probs = right_transposed(grad_block, values)
            delta_rows = jnp.sum(probability * grad_probs, -1, keepdims=True)
            grad_scores = (probability * (grad_probs - delta_rows)).astype(jnp.bfloat16)
            grad_query = jnp.dot(grad_scores, key_rows, preferred_element_type=jnp.float32) * 0.125
            key_acc = key_acc + rows_contract(grad_scores, query_block) * 0.125
            return ((key_acc, value_acc), grad_query)

        zero_rows = jnp.zeros((total_rows, head_dim), jnp.float32)
        (key_acc, value_acc), grad_query = lax.scan(one_block, (zero_rows, zero_rows), starts)
        grad_query = grad_query.reshape(total_rows, head_dim)
        return jnp.concatenate(
            [
                unrotate(grad_query, cos_table, sin_table),
                unrotate(key_acc, cos_table, sin_table),
                value_acc,
            ],
            -1,
        ).astype(jnp.bfloat16)

    result = lax.map(
        one_head,
        (jnp.moveaxis(packed, 1, 0), jnp.moveaxis(log_sums, 1, 0), jnp.moveaxis(grad_heads, 1, 0)),
    )
    return jnp.moveaxis(result, 0, 1)


def on_device(
    tokens,
    block_ids,
    ln1_scale,
    ln1_bias,
    qkv_weight,
    qkv_bias,
    out_weight,
    out_bias,
    ln2_scale,
    ln2_bias,
    up_weight,
    up_bias,
    down_weight,
    down_bias,
    cotangent,
):
    rows_in = tokens[0].astype(jnp.float32)
    local_rows, width = rows_in.shape
    id_table = block_ids[0]
    length = id_table.shape[0]
    total_rows = 2 * length
    row_blocks = jnp.concatenate([id_table, id_table])
    clean_rows = jnp.arange(total_rows, dtype=jnp.int32) >= length
    local_pos = (
        lax.axis_index("seq") * local_rows + jnp.arange(local_rows, dtype=jnp.int32)
    ) % length
    all_pos = jnp.arange(total_rows, dtype=jnp.int32) % length
    scale_one, shift_one, qkv_full, qkv_shift, out_full, out_shift = (
        lax.all_gather(ln1_scale, "fsdp", axis=0, tiled=True),
        lax.all_gather(ln1_bias, "fsdp", axis=0, tiled=True),
        lax.all_gather(qkv_weight, "fsdp", axis=0, tiled=True),
        lax.all_gather(qkv_bias, "fsdp", axis=0, tiled=True),
        lax.all_gather(out_weight, "fsdp", axis=0, tiled=True),
        lax.all_gather(out_bias, "fsdp", axis=0, tiled=True),
    )
    normed_one, inverse_one = normalize_parts(rows_in)
    first_in = (normed_one * scale_one.astype(jnp.float32) + shift_one.astype(jnp.float32)).astype(
        jnp.bfloat16
    )
    linear = (
        jnp.dot(first_in, qkv_full, preferred_element_type=jnp.float32)
        + qkv_shift.astype(jnp.float32)
    ).reshape(local_rows, H, 3, HD)
    cos_local, sin_local = tables(local_pos, HD // 2)
    packed = jnp.concatenate(
        [
            rotate(linear[:, :, 0], cos_local[:, None], sin_local[:, None]),
            rotate(linear[:, :, 1], cos_local[:, None], sin_local[:, None]),
            linear[:, :, 2],
        ],
        -1,
    ).astype(jnp.bfloat16)
    head_side = lax.all_to_all(packed, "seq", split_axis=1, concat_axis=0, tiled=True)
    head_out, log_sums = attend_heads(head_side, row_blocks, clean_rows)
    attended = lax.all_to_all(
        head_out.reshape(total_rows, -1), "seq", split_axis=0, concat_axis=1, tiled=True
    )
    hidden = (
        rows_in
        + jnp.dot(attended, out_full, preferred_element_type=jnp.float32)
        + out_shift.astype(jnp.float32)
    )
    scale_two, shift_two, up_full, up_shift, down_full, down_shift = (
        lax.all_gather(ln2_scale, "fsdp", axis=0, tiled=True),
        lax.all_gather(ln2_bias, "fsdp", axis=0, tiled=True),
        lax.all_gather(up_weight, "fsdp", axis=0, tiled=True),
        lax.all_gather(up_bias, "fsdp", axis=0, tiled=True),
        lax.all_gather(down_weight, "fsdp", axis=0, tiled=True),
        lax.all_gather(down_bias, "fsdp", axis=0, tiled=True),
    )
    normed_two, inverse_two = normalize_parts(hidden)
    second_in = (normed_two * scale_two.astype(jnp.float32) + shift_two.astype(jnp.float32)).astype(
        jnp.bfloat16
    )
    pre_act = jnp.dot(second_in, up_full, preferred_element_type=jnp.float32) + up_shift.astype(
        jnp.float32
    )
    activated, gelu_pull = jax.vjp(
        lambda pre_value: jax.nn.gelu(pre_value, approximate=True), pre_act
    )
    act_low = activated.astype(jnp.bfloat16)
    result = (
        hidden
        + jnp.dot(act_low, down_full, preferred_element_type=jnp.float32)
        + down_shift.astype(jnp.float32)
    )
    scale_two_back, up_back, down_back = (
        lax.all_gather(ln2_scale, "fsdp", axis=0, tiled=True),
        lax.all_gather(up_weight, "fsdp", axis=0, tiled=True),
        lax.all_gather(down_weight, "fsdp", axis=0, tiled=True),
    )
    grad_top = cotangent[0].astype(jnp.float32)
    grad_branch = grad_top.astype(jnp.bfloat16)
    grad_down_w = rows_contract(act_low, grad_branch)
    grad_down_b = jnp.sum(grad_branch.astype(jnp.float32), 0)
    grad_act = right_transposed(grad_branch, down_back)
    grad_pre = gelu_pull(grad_act)[0].astype(jnp.bfloat16)
    grad_up_w = rows_contract(second_in, grad_pre)
    grad_up_b = jnp.sum(grad_pre.astype(jnp.float32), 0)
    grad_second = right_transposed(grad_pre, up_back)
    grad_scale_two = jnp.sum(grad_second * normed_two, 0)
    grad_shift_two = jnp.sum(grad_second, 0)
    grad_hidden = grad_top + norm_backward(
        grad_second, normed_two, inverse_two, scale_two_back.astype(jnp.float32)
    )
    ffn_parts = (
        lax.psum_scatter(grad_scale_two, "fsdp", scatter_dimension=0, tiled=True),
        lax.psum_scatter(grad_shift_two, "fsdp", scatter_dimension=0, tiled=True),
        lax.psum_scatter(grad_up_w, "fsdp", scatter_dimension=0, tiled=True),
        lax.psum_scatter(grad_up_b, "fsdp", scatter_dimension=0, tiled=True),
        lax.psum_scatter(grad_down_w, "fsdp", scatter_dimension=0, tiled=True),
        lax.psum_scatter(grad_down_b, "fsdp", scatter_dimension=0, tiled=True),
    )
    scale_one_back, qkv_back, out_back = (
        lax.all_gather(ln1_scale, "fsdp", axis=0, tiled=True),
        lax.all_gather(qkv_weight, "fsdp", axis=0, tiled=True),
        lax.all_gather(out_weight, "fsdp", axis=0, tiled=True),
    )
    grad_attn = grad_hidden.astype(jnp.bfloat16)
    grad_out_w = rows_contract(attended, grad_attn)
    grad_out_b = jnp.sum(grad_attn.astype(jnp.float32), 0)
    grad_attended = right_transposed(grad_attn, out_back).astype(jnp.bfloat16)
    grad_heads = lax.all_to_all(grad_attended, "seq", split_axis=1, concat_axis=0, tiled=True)
    cos_all, sin_all = tables(all_pos, HD // 2)
    grad_packed = attend_back(
        head_side,
        log_sums,
        grad_heads.reshape(total_rows, -1, HD),
        row_blocks,
        clean_rows,
        cos_all,
        sin_all,
    )
    grad_linear = lax.all_to_all(
        grad_packed, "seq", split_axis=0, concat_axis=1, tiled=True
    ).reshape(local_rows, 3 * width)
    grad_qkv_w = rows_contract(first_in, grad_linear)
    grad_qkv_b = jnp.sum(grad_linear.astype(jnp.float32), 0)
    grad_first = right_transposed(grad_linear, qkv_back)
    grad_scale_one = jnp.sum(grad_first * normed_one, 0)
    grad_shift_one = jnp.sum(grad_first, 0)
    grad_rows = grad_hidden + norm_backward(
        grad_first, normed_one, inverse_one, scale_one_back.astype(jnp.float32)
    )
    att_parts = (
        lax.psum_scatter(grad_scale_one, "fsdp", scatter_dimension=0, tiled=True),
        lax.psum_scatter(grad_shift_one, "fsdp", scatter_dimension=0, tiled=True),
        lax.psum_scatter(grad_qkv_w, "fsdp", scatter_dimension=0, tiled=True),
        lax.psum_scatter(grad_qkv_b, "fsdp", scatter_dimension=0, tiled=True),
        lax.psum_scatter(grad_out_w, "fsdp", scatter_dimension=0, tiled=True),
        lax.psum_scatter(grad_out_b, "fsdp", scatter_dimension=0, tiled=True),
    )
    summed = lax.psum(att_parts + ffn_parts, "seq")
    return (
        result.astype(jnp.bfloat16)[None],
        grad_rows[None],
        summed[0],
        summed[1],
        summed[2],
        summed[3],
        summed[4],
        summed[5],
        summed[6],
        summed[7],
        summed[8],
        summed[9],
        summed[10],
        summed[11],
    )


def solution(mesh):
    in_specs = (
        P("fsdp", "seq", None),
        P("fsdp", None),
        P("fsdp"),
        P("fsdp"),
        P("fsdp", None),
        P("fsdp"),
        P("fsdp", None),
        P("fsdp"),
        P("fsdp"),
        P("fsdp"),
        P("fsdp", None),
        P("fsdp"),
        P("fsdp", None),
        P("fsdp"),
        P("fsdp", "seq", None),
    )
    out_specs = (
        P("fsdp", "seq", None),
        P("fsdp", "seq", None),
        P("fsdp"),
        P("fsdp"),
        P("fsdp", None),
        P("fsdp"),
        P("fsdp", None),
        P("fsdp"),
        P("fsdp"),
        P("fsdp"),
        P("fsdp", None),
        P("fsdp"),
        P("fsdp", None),
        P("fsdp"),
    )
    return jax.shard_map(
        on_device, mesh=mesh, in_specs=in_specs, out_specs=out_specs, check_vma=False
    )
```

profile of v0, /device:TPU:13, one launch (start us, length us, event | category | flops | bytes accessed | tf_op | source)
XLA Modules:
  0.0 1817.5 jit_solution(16155817240082679211)
XLA Ops:
  17.9 24.5 %all-reduce.18 = (bf16[768]{0:T(1024)(128)(2,1)}, bf16[2304]{0:T(1024)(128)(2,1)S(1)}, bf16[768]{0:T(1024)(128)(2,1)S(1)}, bf16[768]{0:T(1024)(128)(2,1)S(1)}, b...) all-reduce(bf16[768]{0:T(1024)(128)(2,1)S(1)} %dynamic-update-slice, ...), channel_id=1, replica_groups=mesh['seq'=4,'fsdp'=8] {'fsdp'}, use_global_device_ids=true, to_apply=%add.6 | all-reduce | flops 6912 | bytes 27648
  46.0 28.0 %all-gather.6.cloned.1.call-done = bf16[768,2304]{1,0:T(8,128)(2,1)} async-done(((bf16[96,2304]{1,0:T(8,128)(2,1)}), bf16[768,2304]{1,0:T(8,128)(2,1)}) %all-gather.6.cloned.1.call-update) | async-done | bytes 3538960 | tf_op jit(solution)/shard_map/all_gather | solution.py:202
  82.6 9.7 copy.84
  112.2 52.3 %all-to-all-done = bf16[1024,12,192]{0,2,1:T(8,128)(2,1)} async-done(((bf16[1024,12,192]{0,2,1:T(8,128)(2,1)}), bf16[1024,12,192]{0,2,1:T(8,128)(2,1)}, u32[]{:S(2)}, u32[]{:S(2)}) %all-to-all-start) | async-done | bytes 4718624 | tf_op jit(solution)/shard_map/all_to_all | solution.py:224
  177.7 278.8 %while.62 = (s32[]{:T(128)}, bf16[3,4096,64]{2,1,0:T(8,128)(2,1)}, f32[3,4096]{1,0:T(4,128)S(1)}, bf16[3,4096,192]{2,1,0:T(8,128)(2,1)}, s32[4096]{0:T(1024)S(1)...) while((s32[]{:T(128)}, bf16[3,4096,64]{2,1,0:T(8,128)(2,1)}, ...), condition=%wide.region_7.8_spmd.clone.clone, body=%wide.region_2.7_spmd.clone.clone.sunk | while | flops 566267392 | bytes 35966912 | solution.py:121
  180.1 87.7 %while.65 = (s32[]{:T(128)}, bf16[8,512,64]{1,2,0:T(8,128)(2,1)}, f32[8,512]{1,0:T(8,128)S(1)}, s32[8]{0:T(128)S(1)}, pred[4096]{0:T(1024)(128)(4,1)S(1)}, /*ind...) while((s32[]{:T(128)}, bf16[8,512,64]{1,2,0:T(8,128)(2,1)}, ...), condition=%wide.region_6.6_spmd.clone, body=%wide.region_3.5_spmd.clone.sunk | while | flops 566263296 | bytes 26984128 | solution.py:118
  273.0 87.6 %while.65 = (s32[]{:T(128)}, bf16[8,512,64]{1,2,0:T(8,128)(2,1)}, f32[8,512]{1,0:T(8,128)S(1)}, s32[8]{0:T(128)S(1)}, pred[4096]{0:T(1024)(128)(4,1)S(1)}, /*ind...) while((s32[]{:T(128)}, bf16[8,512,64]{1,2,0:T(8,128)(2,1)}, ...), condition=%wide.region_6.6_spmd.clone, body=%wide.region_3.5_spmd.clone.sunk | while | flops 566263296 | bytes 26984128 | solution.py:118
  365.9 87.6 %while.65 = (s32[]{:T(128)}, bf16[8,512,64]{1,2,0:T(8,128)(2,1)}, f32[8,512]{1,0:T(8,128)S(1)}, s32[8]{0:T(128)S(1)}, pred[4096]{0:T(1024)(128)(4,1)S(1)}, /*ind...) while((s32[]{:T(128)}, bf16[8,512,64]{1,2,0:T(8,128)(2,1)}, ...), condition=%wide.region_6.6_spmd.clone, body=%wide.region_3.5_spmd.clone.sunk | while | flops 566263296 | bytes 26984128 | solution.py:118
  467.0 19.1 %all-gather = bf16[8,1,384]{2,1,0:T(2,128)(2,1)S(1)} all-gather(bf16[1,1,384]{2,1,0:T(2,128)(2,1)S(1)} %reshape.338), channel_id=1, replica_groups=mesh['seq'=4,'fsdp'=8] {'fsdp'}, dimensions={0}, use_global_device_ids=true | all-gather | bytes 6912 | tf_op jit(solution)/shard_map/all_gather | solution.py:238
  493.2 11.3 fusion.111
  504.5 17.4 convert_reduce_fusion
  543.2 13.5 fusion.82
  561.5 9.1 all-to-all-start.2
  570.6 10.6 fusion.110
  594.8 867.8 %while.64 = (s32[]{:T(128)}, bf16[3,4096,192]{1,2,0:T(8,128)(2,1)}, bf16[3,4096,192]{2,1,0:T(8,128)(2,1)}, bf16[3,4096,64]{1,2,0:T(8,128)(2,1)}, f32[3,4096]{1,0...) while((s32[]{:T(128)}, bf16[3,4096,192]{1,2,0:T(8,128)(2,1)}, ...), condition=%wide.region_16.17_spmd.clone.clone.clone, body=%wide.region_12.16_spmd.clone.clone.clone.sunk | while | flops 1377865216 | bytes 128724736 | solution.py:164
  601.5 271.9 %while.66 = (s32[]{:T(128)}, f32[4096,64]{0,1:T(8,128)S(1)}, f32[4096,64]{0,1:T(8,128)S(1)}, f32[8,512,64]{1,0,2:T(8,128)}, s32[8]{0:T(128)S(1)}, /*index=5*/pre...) while((s32[]{:T(128)}, f32[4096,64]{0,1:T(8,128)S(1)}, ...), condition=%wide.region_15.15_spmd.clone.clone, body=%wide.region_13.14_spmd.clone.clone.sunk | while | flops 1374977536 | bytes 108173136 | solution.py:153
  607.0 8.6 multiply_reduce_fusion.7
  640.7 8.6 multiply_reduce_fusion.7
  674.8 8.6 multiply_reduce_fusion.7
  708.9 8.6 multiply_reduce_fusion.7
  742.9 8.6 multiply_reduce_fusion.7
  776.8 8.6 multiply_reduce_fusion.7
  810.7 8.6 multiply_reduce_fusion.7
  892.0 270.1 %while.66 = (s32[]{:T(128)}, f32[4096,64]{0,1:T(8,128)S(1)}, f32[4096,64]{0,1:T(8,128)S(1)}, f32[8,512,64]{1,0,2:T(8,128)}, s32[8]{0:T(128)S(1)}, /*index=5*/pre...) while((s32[]{:T(128)}, f32[4096,64]{0,1:T(8,128)S(1)}, ...), condition=%wide.region_15.15_spmd.clone.clone, body=%wide.region_13.14_spmd.clone.clone.sunk | while | flops 1374977536 | bytes 108173136 | solution.py:153
  931.5 8.6 multiply_reduce_fusion.7
  965.2 8.6 multiply_reduce_fusion.7
  999.0 8.6 multiply_reduce_fusion.7
  1032.7 8.6 multiply_reduce_fusion.7
  1066.4 8.6 multiply_reduce_fusion.7
  1100.1 8.6 multiply_reduce_fusion.7
  1180.6 269.7 %while.66 = (s32[]{:T(128)}, f32[4096,64]{0,1:T(8,128)S(1)}, f32[4096,64]{0,1:T(8,128)S(1)}, f32[8,512,64]{1,0,2:T(8,128)}, s32[8]{0:T(128)S(1)}, /*index=5*/pre...) while((s32[]{:T(128)}, f32[4096,64]{0,1:T(8,128)S(1)}, ...), condition=%wide.region_15.15_spmd.clone.clone, body=%wide.region_13.14_spmd.clone.clone.sunk | while | flops 1374977536 | bytes 108173136 | solution.py:153
  1219.7 8.6 multiply_reduce_fusion.7
  1253.4 8.6 multiply_reduce_fusion.7
  1287.2 8.6 multiply_reduce_fusion.7
  1320.9 8.6 multiply_reduce_fusion.7
  1354.6 8.6 multiply_reduce_fusion.7
  1388.3 8.6 multiply_reduce_fusion.7
  1462.6 12.7 copy.96
  1475.4 100.5 %all_to_all.68 = bf16[4096,3,192]{2,1,0:T(4,128)(2,1)} all-to-all(bf16[4096,3,192]{2,1,0:T(4,128)(2,1)} %bitcast.213), channel_id=1, replica_groups=mesh['seq'=4,'fsdp'=8] {'seq'}, dimensions={0} | all-to-all | bytes 9437184 | tf_op jit(solution)/shard_map/all_to_all | solution.py:305
  1575.9 12.9 copy.98
  1588.8 8.6 fusion.79
  1599.7 11.8 fusion.93
  1614.1 13.7 copy.106
  1627.8 9.2 fusion.117
  1637.0 89.9 %reduce-scatter.5.cloned.1.call-done = f32[96,2304]{1,0:T(8,128)} async-done(((f32[768,2304]{1,0:T(8,128)}), f32[96,2304]{1,0:T(8,128)}) %reduce-scatter.5.cloned.1.call-update) | async-done | bytes 884752 | tf_op jit(solution)/shard_map/reduce_scatter | solution.py:319
  1738.7 24.2 %all-reduce.15 = (f32[768]{0:T(1024)S(1)}, f32[768]{0:T(1024)S(1)}, f32[2304]{0:T(1024)S(1)}, f32[768]{0:T(1024)S(1)}, f32[768]{0:T(1024)S(1)}, /*index=5*/f32[7...) all-reduce(f32[768]{0:T(1024)S(1)} %get-tuple-element.590, ...), channel_id=2, replica_groups=mesh['seq'=4,'fsdp'=8] {'fsdp'}, use_global_device_ids=true, to_apply=%region_20.21.clone | all-reduce | flops 9984 | bytes 79872
  1772.6 12.9 all-reduce.16
  1785.4 19.3 %all-reduce.21.cloned.1.call-done = (f32[96,2304]{1,0:T(8,128)}, f32[96,768]{1,0:T(8,128)}, f32[96,3072]{1,0:T(8,128)}, f32[384,768]{1,0:T(8,128)}) async-done(((f32[96,2304]{1,0:T(8,128)}, f32[96,768]{1,0:T(8,128)}, f32[96,3072]{1,0:T(8,128)}, f32[384,768]{1,0:T(8,128)}), (f32[96,2304]{1,0:T(8,128)}, f32[96,768]{1,0:T(8,128)}, f32[96,3072]{1,0:T(8,128)}, ...) | async-done | bytes 3538960 | tf_op jit(solution)/shard_map/psum | solution.py:324
  (875 shorter events, 1029.3 us)
Async XLA Ops:
  7.2 66.9 %all-gather.6.cloned.1.call-start = ((), (), s32[]{:S(2)}) async-start(), calls=%async_computation.8 | async-start | bytes 3981312 | tf_op jit(solution)/shard_map/all_gather | solution.py:202
  7.9 479.9 %all-gather.8.cloned.1.call-start = ((), (), s32[]{:S(2)}) async-start(), calls=%async_computation.9 | async-start | bytes 1327104 | tf_op jit(solution)/shard_map/all_gather | solution.py:204
  8.7 484.5 %all-gather.10.cloned.1.call-start = ((), (), s32[]{:S(2)}) async-start(), calls=%async_computation.10 | async-start | bytes 5308416 | tf_op jit(solution)/shard_map/all_gather | solution.py:237
  42.4 31.6 %copy-start.21 = (f32[768]{0:T(1024)}, f32[768]{0:T(1024)S(1)}, u32[]{:S(2)}) copy-start(f32[768]{0:T(1024)S(1)} %convert_element_type.125) | copy-start | bytes 9220
  42.4 31.6 %copy-start.33 = (f32[768]{0:T(1024)}, f32[768]{0:T(1024)S(1)}, u32[]{:S(2)}) copy-start(f32[768]{0:T(1024)S(1)} %convert_element_type.126) | copy-start | bytes 9220
  44.4 38.1 %copy-start.5 = (bf16[1,1024,768]{1,2,0:T(8,128)(2,1)}, bf16[1,1024,768]{1,2,0:T(8,128)(2,1)S(1)}, u32[]{:S(2)}) copy-start(bf16[1,1024,768]{1,2,0:T(8,128)(2,1)S(1)} %copy.83) | copy-start | bytes 4718596
  44.8 37.8 %copy-start.19 = (f32[1024]{0:T(1024)}, f32[1024]{0:T(1024)S(1)}, u32[]{:S(2)}) copy-start(f32[1024]{0:T(1024)S(1)} %broadcast_multiply_fusion.5) | copy-start | bytes 12292
  45.5 37.1 %copy-start.23 = (f32[1024]{0:T(1024)}, f32[1024]{0:T(1024)S(1)}, u32[]{:S(2)}) copy-start(f32[1024]{0:T(1024)S(1)} %add_rsqrt_fusion.1) | copy-start | bytes 12292
  104.2 60.3 %all-to-all-start = ((bf16[1024,12,192]{0,2,1:T(8,128)(2,1)}), bf16[1024,12,192]{0,2,1:T(8,128)(2,1)}, u32[]{:S(2)}, u32[]{:S(2)}) async-start(bf16[1024,12,192]{0,2,1:T(8,128)(2,1)} %fusion.77), calls=%async_computation | async-start | bytes 9437184 | tf_op jit(solution)/shard_map/all_to_all | solution.py:224
  111.6 392.9 %all-gather.12.cloned.1.call-start = ((), (), s32[]{:S(2)}) async-start(), calls=%async_computation.11 | async-start | bytes 5308416 | tf_op jit(solution)/shard_map/all_gather | solution.py:239
  460.8 25.3 %copy-start.12 = (bf16[1,1024,768]{2,1,0:T(8,128)(2,1)S(1)}, bf16[1,1024,768]{2,1,0:T(8,128)(2,1)}, u32[]{:S(2)}) copy-start(bf16[1,1024,768]{2,1,0:T(8,128)(2,1)} %param.37) | copy-start | bytes 4718596
  462.4 25.4 %all-to-all-start.1 = ((bf16[4,1024,192]{1,2,0:T(8,128)(2,1)}), bf16[4,1024,192]{1,2,0:T(8,128)(2,1)S(1)}, u32[]{:S(2)}, u32[]{:S(2)}) async-start(bf16[4,1024,192]{1,2,0:T(8,128)(2,1)} %copy.89), calls=%async_computation.1 | async-start | bytes 3145728 | tf_op jit(solution)/shard_map/all_to_all | solution.py:226
  466.9 1170.1 %reduce-scatter.7.cloned.1.call-start = ((), (), s32[]{:S(2)}) async-start(), calls=%async_computation.13 | async-start | bytes 2654208 | tf_op jit(solution)/shard_map/reduce_scatter | solution.py:321
  486.1 57.1 %copy-start.28 = (f32[8,1,384]{2,1,0:T(1,128)}, f32[8,1,384]{2,1,0:T(1,128)S(1)}, u32[]{:S(2)}) copy-start(f32[8,1,384]{2,1,0:T(1,128)S(1)} %convert_element_type.152) | copy-start | bytes 36868
  492.7 77.8 %copy-start.3 = (f32[1024,768]{0,1:T(8,128)}, f32[1024,768]{0,1:T(8,128)S(1)}, u32[]{:S(2)}) copy-start(f32[1024,768]{0,1:T(8,128)S(1)} %get-tuple-element.709) | copy-start | bytes 9437188
  504.4 17.4 copy-start.11
  543.1 1093.9 %reduce-scatter.11.cloned.1.call-start = ((), (), s32[]{:S(2)}) async-start(), calls=%async_computation.15 | async-start | bytes 10616832 | tf_op jit(solution)/shard_map/reduce_scatter | solution.py:282
  561.5 28.2 %all-to-all-start.2 = ((bf16[1024,4,192]{0,2,1:T(8,128)(2,1)}), bf16[1024,4,192]{0,2,1:T(8,128)(2,1)}, u32[]{:S(2)}, u32[]{:S(2)}) async-start(bf16[1024,4,192]{0,2,1:T(8,128)(2,1)} %bitcast.225), calls=%async_computation.2 | async-start | bytes 3145728 | tf_op jit(solution)/shard_map/all_to_all | solution.py:294
  570.6 1066.4 %reduce-scatter.9.cloned.1.call-start = ((), (), s32[]{:S(2)}) async-start(), calls=%async_computation.14 | async-start | bytes 10616832 | tf_op jit(solution)/shard_map/reduce_scatter | solution.py:280
  581.2 1145.7 %reduce-scatter.5.cloned.1.call-start = ((), (), s32[]{:S(2)}) async-start(), calls=%async_computation.12 | async-start | bytes 7962624 | tf_op jit(solution)/shard_map/reduce_scatter | solution.py:319
  607.0 8.6 copy-start
  640.7 8.6 copy-start
  674.8 8.6 copy-start
  708.9 8.6 copy-start
  742.8 8.6 copy-start
  776.8 8.6 copy-start
  810.6 8.6 copy-start
  844.9 8.6 copy-start
  931.5 8.6 copy-start
  965.2 8.6 copy-start
  999.0 8.6 copy-start
  1032.7 8.6 copy-start
  1066.4 8.6 copy-start
  1100.1 8.6 copy-start
  1133.8 8.6 copy-start
  1219.7 8.6 copy-start
  1253.4 8.6 copy-start
  1287.1 8.6 copy-start
  1320.9 8.6 copy-start
  1354.6 8.6 copy-start
  1388.3 8.6 copy-start
  1422.0 8.6 copy-start
  1575.9 12.9 copy-start.6
  1575.9 12.9 copy-start.20
  1575.9 12.9 copy-start.22
  1575.9 12.9 copy-start.24
  1575.9 12.9 copy-start.34
  1597.4 207.2 %all-reduce.21.cloned.1.call-start = ((), (), s32[]{:S(2)}) async-start(), calls=%async_computation.16 | async-start | bytes 7077888 | tf_op jit(solution)/shard_map/psum | solution.py:324
  (74 other events, 288.0 us)
Sparse Core Ops, SparseCore 0:
  10.2 63.8 all-gather.5
  76.2 39.8 all-gather.7
  118.3 77.3 all-gather.9
  197.8 77.6 all-gather.11
  543.3 72.6 reduce-scatter.6
  619.4 161.7 reduce-scatter.10
  784.7 161.3 reduce-scatter.8
  1597.6 129.2 reduce-scatter.4
  1729.5 75.1 all-reduce.20
where the time goes:
time: 1830 us; the launch traced here: 1820 us
  matrix products  734 us (40%)
  local copies, waits for them, and re-layouts  290 us (16%)
  other arithmetic  276 us (15%)
  waiting for transfers between devices  200 us (11%)
  blocking collectives  181 us (10%)
  loops' own time  96.6 us (5%)
  starting transfers between devices  21.3 us (1%)
    dot_general x76, matrix products, right_transposed(): lax.dot_general(left, right, (((1,), (1,)), ((), ())), preferred_element_...  405 us
    convert_element_type x24, other arithmetic, one_block(): grad_scores = (probability * (grad_probs - delta_rows)).astype(jnp.bfloat16)  192 us
    dot_general x52, matrix products, rows_contract(): lax.dot_general(left, right, (((0,), (0,)), ((), ())), preferred_element_...  191 us
    all_to_all x1, blocking collectives, on_device(): lax.all_to_all(grad_packed, 'seq', split_axis=0, concat_axis=1, tiled=True)  101 us
    dynamic_update_slice x48, local copies, waits for them, and re-layouts, one_head(): lax.scan(one_block, (zero_rows, zero_rows), starts)  93.3 us
    reduce_scatter x1, waiting for transfers between devices, on_device(): lax.psum_scatter(grad_qkv_w, 'fsdp', scatter_dimension=0, tiled=True)  89.9 us
    dot_general x24, matrix products, one_block(): jnp.dot(probability, values, preferred_element_type=jnp.float32)  68 us
    all_to_all x1, waiting for transfers between devices, on_device(): lax.all_to_all(packed, 'seq', split_axis=1, concat_axis=0, tiled=True)  52.3 us
  transfers between devices with their start and end apart: 12, of which 5 were waited for; matrix products, arithmetic and copies ran while one was open for 69% of the time, Pallas kernels for 0%

commit v1 on v0

v1 whole, which is shorter than its diff:
```python
import functools

import jax
import jax.numpy as jnp
from jax import lax
from jax.experimental import pallas as pl
from jax.experimental.pallas import tpu as pltpu
from jax.sharding import PartitionSpec as P

H = 12
HD = 64
EPSILON = 1e-05
LOG2E = 1.4426950408889634
NEG = -1e30
TQ = 256
TK = 256
TM = 128
BF = jnp.bfloat16
F32 = jnp.float32


def normalize_parts(values):
    mean_value = jnp.mean(values, -1, keepdims=True)
    centred = values - mean_value
    variance = jnp.mean(centred * centred, -1, keepdims=True)
    inverse = lax.rsqrt(variance + EPSILON)
    return (centred * inverse, inverse)


def norm_backward(grad_out, normed, inverse, scale):
    grad_norm = grad_out * scale
    return inverse * (
        grad_norm
        - jnp.mean(grad_norm, -1, keepdims=True)
        - normed * jnp.mean(grad_norm * normed, -1, keepdims=True)
    )


def rows_contract(left, right):
    return lax.dot_general(left, right, (((0,), (0,)), ((), ())), preferred_element_type=F32)


def right_transposed(left, right):
    return lax.dot_general(left, right, (((1,), (1,)), ((), ())), preferred_element_type=F32)


def dot(left, right):
    return jnp.dot(left, right, preferred_element_type=F32)


def qkv_kernel(heads, core_ref, mine, other, cmine, cother, w_ref, vec_ref, bias_ref, cos_ref,
               sin_ref, q_out, k_out, v_out, kc_out, vc_out, a_out, ac_out, wt):
    step = pl.program_id(0)
    span = heads * HD

    @pl.when(step == 0)
    def _():
        whole = jnp.transpose(w_ref[...])
        for h in range(heads):
            for part in range(3):
                wt[part * span + h * HD : part * span + (h + 1) * HD, :] = whole[
                    (3 * h + part) * HD : (3 * h + part + 1) * HD, :
                ]

    def normed(rows):
        values = rows.astype(F32)
        n, _ = normalize_parts(values)
        return (n * vec_ref[0:1, :] + vec_ref[1:2, :]).astype(BF)

    def turn(lin, base, out):
        cos_t, sin_t = cos_ref[...], sin_ref[...]
        half = HD // 2
        for h in range(heads):
            first = lin[base + h * HD : base + h * HD + half, :]
            second = lin[base + h * HD + half : base + (h + 1) * HD, :]
            out[h * HD : h * HD + half, :] = (first * cos_t - second * sin_t).astype(BF)
            out[h * HD + half : (h + 1) * HD, :] = (first * sin_t + second * cos_t).astype(BF)

    quarter = pl.num_programs(0) // 4

    @pl.when(step < 2 * quarter)
    def _():
        a = normed(jnp.where(step < quarter, mine[...], other[...]))
        a_out[...] = a
        lin = right_transposed(wt[...], a) + bias_ref[...]
        turn(lin, 0, q_out)
        turn(lin, span, k_out)
        v_out[...] = lin[2 * span :, :].astype(BF)

    @pl.when(step >= 2 * quarter)
    def _():
        a = normed(jnp.where(step < 3 * quarter, cmine[...], cother[...]))
        ac_out[...] = a
        lin = right_transposed(wt[span:, :], a) + bias_ref[span:, :]
        turn(lin, 0, kc_out)
        vc_out[...] = lin[span:, :].astype(BF)


def project(core, mine, other, cmine, cother, weight, vec, bias, cos_t, sin_t, heads):
    local, width = mine.shape
    span = heads * HD
    tile = 256
    n = local // tile

    def place(t, c):
        mine_first = jnp.where(t % (2 * n) < n, c[0], 1 - c[0])
        return mine_first * n + t % n

    def src(k):
        return pl.BlockSpec((tile, width), lambda t, c: (jnp.clip(t - k * n, 0, n - 1), 0))

    whole = lambda shape: pl.BlockSpec(shape, lambda t, c: (0, 0))
    own = pl.BlockSpec((span, tile), lambda t, c: (0, place(jnp.minimum(t, 2 * n - 1), c)))
    cln = pl.BlockSpec((span, tile), lambda t, c: (0, place(jnp.maximum(t, 2 * n), c)))
    own_a = pl.BlockSpec((tile, width), lambda t, c: (place(jnp.minimum(t, 2 * n - 1), c), 0))
    cln_a = pl.BlockSpec((tile, width), lambda t, c: (place(jnp.maximum(t, 2 * n), c), 0))
    tab = pl.BlockSpec((HD // 2, tile), lambda t, c: (0, place(t, c)))
    head_shape = jax.ShapeDtypeStruct((span, 2 * local), BF)
    row_shape = jax.ShapeDtypeStruct((2 * local, width), BF)
    return pl.pallas_call(
        functools.partial(qkv_kernel, heads),
        grid_spec=pltpu.PrefetchScalarGridSpec(
            num_scalar_prefetch=1,
            grid=(4 * n,),
            in_specs=[src(0), src(1), src(2), src(3), whole((width, 3 * span)), whole(vec.shape),
                      whole(bias.shape), tab, tab],
            out_specs=[own, own, own, cln, cln, own_a, cln_a],
            scratch_shapes=[pltpu.VMEM((3 * span, width), BF)],
        ),
        out_shape=[head_shape] * 5 + [row_shape] * 2,
        name="project",
    )(core, mine, other, cmine, cother, weight, vec, bias, cos_t, sin_t)


def attend_kernel(group, bounds, q, k, v, kc, vc, id_row, id_col, o_out, lse_out, ks, kcs, vs,
                  vcs):
    total = q.shape[1]
    scale = LOG2E * HD**-0.5
    ones = jnp.ones((16, total), BF)
    for h in range(group):
        rows = slice(h * HD, (h + 1) * HD)
        ks[h] = jnp.transpose(k[rows, :])
        kcs[h] = jnp.transpose(kc[rows, :])
        vs[h, :HD] = v[rows, :]
        vcs[h, :HD] = vc[rows, :]
        vs[h, HD:] = ones
        vcs[h, HD:] = ones
    lift = bounds[4, 0]

    def one_tile(i, _):
        at = pl.ds(pl.multiple_of(i * TQ, TQ), TQ)
        queries = [q[h * HD : (h + 1) * HD, at] for h in range(group)]
        q_ids = id_row[0:1, at]

        def update(state, key_ref, val_ref, keys, mask):
            out = []
            for h in range(group):
                m, acc = state[2 * h], state[2 * h + 1]
                s = dot(key_ref[h, keys, :], queries[h])
                if mask is not None:
                    s = jnp.where(mask, s, NEG)
                m_new = jnp.maximum(m, jnp.max(s, 0, keepdims=True))
                p = jnp.exp2((s - m_new) * scale).astype(BF)
                alpha = jnp.exp2((m - m_new) * scale)
                acc = acc * alpha + dot(val_ref[h, :, keys], p)
                out += [m_new, acc]
            return tuple(out)

        def key_ids(keys):
            col = id_col[keys, :]
            return jnp.concatenate([col] * (TQ // 128), 1)

        def band(j, state):
            keys = pl.ds(pl.multiple_of(j * TM, TM), TM)
            return update(state, ks, vs, keys, key_ids(keys) == q_ids)

        def full(j, state):
            keys = pl.ds(pl.multiple_of(j * TK, TK), TK)
            return update(state, kcs, vcs, keys, None)

        def edge(j, state):
            keys = pl.ds(pl.multiple_of(j * TM, TM), TM)
            return update(state, kcs, vcs, keys, key_ids(keys) < q_ids + lift)

        state = (jnp.full((1, TQ), NEG, F32), jnp.zeros((HD + 16, TQ), F32)) * group
        state = lax.fori_loop(bounds[2, i], bounds[3, i], band, state)
        state = lax.fori_loop(0, bounds[0, i], full, state)
        state = lax.fori_loop(bounds[0, i] * (TK // TM), bounds[1, i], edge, state)
        for h in range(group):
            m, acc = state[2 * h], state[2 * h + 1]
            total_w = acc[HD : HD + 1, :]
            o_out[h * HD : (h + 1) * HD, at] = (acc[:HD, :] / total_w).astype(BF)
            lse_out[h, :, at] = jnp.broadcast_to(m * scale + jnp.log2(total_w), (8, TQ))
        return 0

    lax.fori_loop(0, total // TQ, one_tile, 0)


def attend(bounds, q, k, v, kc, vc, id_row, id_col, heads, group):
    total = q.shape[1]
    head = pl.BlockSpec((group * HD, total), lambda g, b: (g, 0))
    whole = lambda shape: pl.BlockSpec(shape, lambda g, b: (0, 0))
    return pl.pallas_call(
        functools.partial(attend_kernel, group),
        grid_spec=pltpu.PrefetchScalarGridSpec(
            num_scalar_prefetch=1,
            grid=(heads // group,),
            in_specs=[head] * 5 + [whole(id_row.shape), whole(id_col.shape)],
            out_specs=[head, pl.BlockSpec((group, 8, total), lambda g, b: (g, 0, 0))],
            scratch_shapes=[pltpu.VMEM((group, total, HD), BF)] * 2
            + [pltpu.VMEM((group, HD + 16, total), BF)] * 2,
        ),
        out_shape=[
            jax.ShapeDtypeStruct((heads * HD, total), BF),
            jax.ShapeDtypeStruct((heads, 8, total), F32),
        ],
        name="attend",
    )(bounds, q, k, v, kc, vc, id_row, id_col)


def attend_back_kernel(group, bounds, q, k, v, kc, vc, o, lse, do_mine, do_other, id_row, id_col,
                       cos_ref, sin_ref, own_out, cln_out, ks, vs, kcs, vcs, qs, dos, dot_s,
                       dk_acc, dv_acc, dkc_acc, dvc_acc, dq_acc):
    total = q.shape[1]
    half_rows = total // 2
    scale = LOG2E * HD**-0.5
    lift = bounds[4, 0]
    core = bounds[4, 1]
    near = pl.ds(pl.multiple_of(core * half_rows, 128), half_rows)
    far = pl.ds(pl.multiple_of((1 - core) * half_rows, 128), half_rows)
    dot_s[:, near] = do_mine[...]
    dot_s[:, far] = do_other[...]
    for h in range(group):
        rows = slice(h * HD, (h + 1) * HD)
        ks[h] = jnp.transpose(k[rows, :])
        vs[h] = jnp.transpose(v[rows, :])
        kcs[h] = jnp.transpose(kc[rows, :])
        vcs[h] = jnp.transpose(vc[rows, :])
        qs[h] = jnp.transpose(q[rows, :])
        dos[h] = jnp.transpose(dot_s[rows, :])
    for ref in (dk_acc, dv_acc, dkc_acc, dvc_acc):
        ref[...] = jnp.zeros_like(ref)

    def one_tile(i, _):
        at = pl.ds(pl.multiple_of(i * TQ, TQ), TQ)
        q_ids = id_row[0:1, at]
        queries, grads, deltas, sums, q_rows, g_rows = [], [], [], [], [], []
        for h in range(group):
            rows = slice(h * HD, (h + 1) * HD)
            queries.append(q[rows, at])
            g = dot_s[rows, at]
            grads.append(g)
            deltas.append(jnp.sum(g.astype(F32) * o[rows, at].astype(F32), 0, keepdims=True))
            sums.append(lse[h, 0:1, at])
            q_rows.append(qs[h, at, :])
            g_rows.append(dos[h, at, :])

        def update(state, key_ref, val_ref, key_cols, dk, dv, keys, mask):
            out = []
            for h in range(group):
                s = dot(key_ref[h, keys, :], queries[h])
                p = jnp.exp2(s * scale - sums[h])
                if mask is not None:
                    p = jnp.where(mask, p, 0.0)
                dp = dot(val_ref[h, keys, :], grads[h])
                ds = (p * (dp - deltas[h])).astype(BF)
                dv[h, keys, :] += dot(p.astype(BF), g_rows[h])
                dk[h, keys, :] += dot(ds, q_rows[h])
                out.append(state[h] + dot(key_cols[h * HD : (h + 1) * HD, keys], ds))
            return tuple(out)

        def key_ids(keys):
            col = id_col[keys, :]
            return jnp.concatenate([col] * (TQ // 128), 1)

        def band(j, state):
            keys = pl.ds(pl.multiple_of(j * TM, TM), TM)
            return update(state, ks, vs, k, dk_acc, dv_acc, keys, key_ids(keys) == q_ids)

        def full(j, state):
            keys = pl.ds(pl.multiple_of(j * TK, TK), TK)
            return update(state, kcs, vcs, kc, dkc_acc, dvc_acc, keys, None)

        def edge(j, state):
            keys = pl.ds(pl.multiple_of(j * TM, TM), TM)
            mask = key_ids(keys) < q_ids + lift
            return update(state, kcs, vcs, kc, dkc_acc, dvc_acc, keys, mask)

        state = (jnp.zeros((HD, TQ), F32),) * group
        state = lax.fori_loop(bounds[2, i], bounds[3, i], band, state)
        state = lax.fori_loop(0, bounds[0, i], full, state)
        state = lax.fori_loop(bounds[0, i] * (TK // TM), bounds[1, i], edge, state)
        for h in range(group):
            dq_acc[h * HD : (h + 1) * HD, at] = state[h]
        return 0

    lax.fori_loop(0, total // TQ, one_tile, 0)

    half = HD // 2
    cos_t, sin_t = cos_ref[...], sin_ref[...]
    noisy = lift == 0

    def back_turn(w, out, base):
        first, second = w[:half, :], w[half:, :]
        out[base : base + half, :] = (first * cos_t + second * sin_t).astype(BF)
        out[base + half : base + HD, :] = (second * cos_t - first * sin_t).astype(BF)

    for h in range(group):
        back_turn(dq_acc[h * HD : (h + 1) * HD, :] * HD**-0.5, own_out, 3 * h * HD)
        band_k = jnp.where(noisy, dk_acc[h], dkc_acc[h])
        band_v = jnp.where(noisy, dv_acc[h], dvc_acc[h])
        back_turn(jnp.transpose(band_k) * HD**-0.5, own_out, (3 * h + 1) * HD)
        own_out[(3 * h + 2) * HD : (3 * h + 3) * HD, :] = jnp.transpose(band_v).astype(BF)
        back_turn(jnp.transpose(dkc_acc[h]) * HD**-0.5, cln_out, 2 * h * HD)
        cln_out[(2 * h + 1) * HD : (2 * h + 2) * HD, :] = jnp.transpose(dvc_acc[h]).astype(BF)


def attend_back(bounds, q, k, v, kc, vc, o, lse, do_mine, do_other, id_row, id_col, cos_t, sin_t,
                heads, group):
    total = q.shape[1]
    head = pl.BlockSpec((group * HD, total), lambda g, b: (g, 0))
    halfhead = pl.BlockSpec((group * HD, total // 2), lambda g, b: (g, 0))
    whole = lambda shape: pl.BlockSpec(shape, lambda g, b: (0, 0))
    rows16 = pltpu.VMEM((group, total, HD), BF)
    rows32 = pltpu.VMEM((group, total, HD), F32)
    return pl.pallas_call(
        functools.partial(attend_back_kernel, group),
        grid_spec=pltpu.PrefetchScalarGridSpec(
            num_scalar_prefetch=1,
            grid=(heads // group,),
            in_specs=[head] * 6
            + [pl.BlockSpec((group, 8, total), lambda g, b: (g, 0, 0)), halfhead, halfhead]
            + [whole(id_row.shape), whole(id_col.shape), whole(cos_t.shape), whole(sin_t.shape)],
            out_specs=[
                pl.BlockSpec((group * 3 * HD, total), lambda g, b: (g, 0)),
                pl.BlockSpec((group * 2 * HD, total), lambda g, b: (g, 0)),
            ],
            scratch_shapes=[rows16] * 6
            + [pltpu.VMEM((group * HD, total), BF)]
            + [rows32] * 4
            + [pltpu.VMEM((group * HD, total), F32)],
        ),
        out_shape=[
            jax.ShapeDtypeStruct((heads * 3 * HD, total), BF),
            jax.ShapeDtypeStruct((heads * 2 * HD, total), BF),
        ],
        name="attend_back",
    )(bounds, q, k, v, kc, vc, o, lse, do_mine, do_other, id_row, id_col, cos_t, sin_t)


def on_device(
    tokens,
    block_ids,
    ln1_scale,
    ln1_bias,
    qkv_weight,
    qkv_bias,
    out_weight,
    out_bias,
    ln2_scale,
    ln2_bias,
    up_weight,
    up_bias,
    down_weight,
    down_bias,
    cotangent,
):
    tok = tokens[0]
    local_rows, width = tok.shape
    ids = block_ids[0].astype(jnp.int32)
    length = ids.shape[0]
    shard = ln1_scale.shape[0]
    heads = H // 2
    span = heads * HD
    me = lax.axis_index("seq")
    core = me % 2
    noisy = me < 2
    swap = [(0, 1), (1, 0), (2, 3), (3, 2)]
    other = lax.ppermute(tok, "seq", swap)
    clean_in = lax.ppermute(tok, "seq", [(2, 0), (3, 1)])
    clean_mine = jnp.where(noisy, clean_in, tok)
    clean_other = lax.ppermute(clean_mine, "seq", swap)

    q_cols = lax.dynamic_slice_in_dim(qkv_weight, core * 3 * span, 3 * span, 1)
    small = jnp.concatenate(
        [
            ln1_scale.reshape(1, shard),
            ln1_bias.reshape(1, shard),
            out_bias.reshape(1, shard),
            ln2_scale.reshape(1, shard),
            ln2_bias.reshape(1, shard),
            down_bias.reshape(1, shard),
            qkv_bias.reshape(-1, shard),
            up_bias.reshape(-1, shard),
        ],
        0,
    )
    n_small = small.shape[0]
    small = jnp.pad(small, ((0, 128 - n_small), (0, 0))).T
    gathered = lax.all_gather(
        jnp.concatenate([q_cols, small], 1), "fsdp", axis=0, tiled=True
    )
    n_fsdp = width // shard
    vectors = gathered[:, 3 * span :].reshape(n_fsdp, shard, 128)[:, :, :n_small]
    vectors = jnp.transpose(vectors, (2, 0, 1)).astype(F32)
    flat = vectors[:6].reshape(6, width)
    qkv_b = jnp.transpose(vectors[6:9], (1, 0, 2)).reshape(-1)
    up_b = jnp.transpose(vectors[9:], (1, 0, 2)).reshape(-1)
    scale_one, shift_one, out_shift, scale_two, shift_two, down_shift = [flat[i] for i in range(6)]

    out_full = lax.all_gather(out_weight, "fsdp", axis=0, tiled=True)
    up_full = lax.all_gather(up_weight, "fsdp", axis=0, tiled=True)
    down_full = lax.all_gather(down_weight, "fsdp", axis=0, tiled=True)

    frequency = jnp.exp(-jnp.log(10000.0) * jnp.arange(HD // 2, dtype=F32) / (HD // 2))
    angles = frequency[:, None] * jnp.arange(length, dtype=F32)[None, :]
    cos_t, sin_t = jnp.cos(angles), jnp.sin(angles)

    first = ids[::TQ][:, None]
    last = ids[TQ - 1 :: TQ][:, None]
    before = lambda edge: jnp.sum((ids[None, :] < edge).astype(jnp.int32), 1)
    start_first, end_first = before(first), before(first + 1)
    start_last, end_last = before(last), before(last + 1)
    ceil_m = lambda value: (value + TM - 1) // TM
    lift = jnp.where(noisy, 0, 1)
    zero = jnp.zeros_like(start_first)
    bounds = jnp.stack(
        [
            jnp.where(noisy, start_first, end_first) // TK,
            ceil_m(jnp.where(noisy, start_last, end_last)),
            jnp.where(noisy, start_first // TM, zero),
            jnp.where(noisy, ceil_m(end_last), zero),
            zero + jnp.where(jnp.arange(zero.shape[0]) == 0, lift, core),
        ]
    ).astype(jnp.int32)
    id_row = jnp.broadcast_to(ids[None, :], (8, length))
    id_col = jnp.broadcast_to(ids[:, None], (length, 128))

    vec = jnp.concatenate([scale_one[None], shift_one[None], jnp.zeros((6, width), F32)], 0)
    bias_own = lax.dynamic_slice_in_dim(qkv_b, core * 3 * span, 3 * span, 0)
    bias_own = jnp.transpose(bias_own.reshape(heads, 3, HD), (1, 0, 2)).reshape(3 * span, 1)
    q, k, v, kc, vc, a_own, a_clean = project(
        core.reshape(1).astype(jnp.int32), tok, other, clean_mine, clean_other, gathered, vec,
        bias_own, cos_t, sin_t, heads
    )
    o, lse = attend(bounds, q, k, v, kc, vc, id_row, id_col, heads, 2)
    cut = lambda value, which: lax.dynamic_slice_in_dim(value, which * local_rows, local_rows, 1)
    o_mine = cut(o, core)
    o_in = lax.ppermute(cut(o, 1 - core), "seq", swap)
    attended = jnp.where(
        core == 0, jnp.concatenate([o_mine, o_in], 0), jnp.concatenate([o_in, o_mine], 0)
    )

    rows_in = tok.astype(F32)
    hidden = rows_in + rows_contract(attended, out_full) + out_shift
    normed_two, inverse_two = normalize_parts(hidden)
    second_in = (normed_two * scale_two + shift_two).astype(BF)
    pre_act = dot(second_in, up_full) + up_b
    activated, gelu_pull = jax.vjp(
        lambda pre_value: jax.nn.gelu(pre_value, approximate=True), pre_act
    )
    act_low = activated.astype(BF)
    result = hidden + dot(act_low, down_full) + down_shift

    grad_branch = cotangent[0]
    grad_top = grad_branch.astype(F32)
    grad_down_w = rows_contract(act_low, grad_branch)
    grad_down_b = jnp.sum(grad_top, 0)
    grad_act = right_transposed(grad_branch, down_full)
    grad_pre = gelu_pull(grad_act)[0].astype(BF)
    grad_up_w = rows_contract(second_in, grad_pre)
    grad_up_b = jnp.sum(grad_pre.astype(F32), 0)
    grad_second = right_transposed(grad_pre, up_full)
    grad_scale_two = jnp.sum(grad_second * normed_two, 0)
    grad_shift_two = jnp.sum(grad_second, 0)
    grad_hidden = grad_top + norm_backward(grad_second, normed_two, inverse_two, scale_two)

    grad_attn = grad_hidden.astype(BF)
    grad_out_w = dot(attended, grad_attn)
    grad_out_b = jnp.sum(grad_attn.astype(F32), 0)
    grad_o = right_transposed(out_full, grad_attn).astype(BF)
    cut_heads = lambda which: lax.dynamic_slice_in_dim(grad_o, which * span, span, 0)
    do_mine = cut_heads(core)
    do_in = lax.ppermute(cut_heads(1 - core), "seq", swap)
    down_part = lax.psum_scatter(grad_down_w.astype(BF), "fsdp", scatter_dimension=0, tiled=True)
    up_part = lax.psum_scatter(grad_up_w.astype(BF), "fsdp", scatter_dimension=0, tiled=True)
    out_part = lax.psum_scatter(grad_out_w.astype(BF), "fsdp", scatter_dimension=0, tiled=True)

    own_grad, clean_grad = attend_back(
        bounds, q, k, v, kc, vc, o, lse, do_mine, do_in, id_row, id_col, cos_t, sin_t, heads, 2
    )
    from_noisy = lax.ppermute(clean_grad, "seq", [(0, 2), (1, 3)])
    own_grad = own_grad.reshape(heads, 3 * HD, length)
    own_grad = own_grad.at[:, HD:].add(from_noisy.reshape(heads, 2 * HD, length))
    own_grad = own_grad.reshape(3 * span, length)
    grad_qkv_w = lax.dot_general(
        a_own, own_grad, (((0,), (1,)), ((), ())), preferred_element_type=F32
    )
    grad_qkv_b = jnp.sum(own_grad.astype(F32), 1)
    qkv_part = lax.psum_scatter(grad_qkv_w.astype(BF), "fsdp", scatter_dimension=0, tiled=True)
    grad_first = lax.dot_general(
        own_grad, gathered[:, : 3 * span], (((0,), (1,)), ((), ())), preferred_element_type=F32
    )
    cut_rows = lambda which: lax.dynamic_slice_in_dim(grad_first, which * local_rows, local_rows, 0)
    grad_first = cut_rows(core) + lax.ppermute(
        cut_rows(1 - core).astype(BF), "seq", swap
    ).astype(F32)
    normed_one, inverse_one = normalize_parts(rows_in)
    grad_scale_one = jnp.sum(grad_first * normed_one, 0)
    grad_shift_one = jnp.sum(grad_first, 0)
    grad_rows = grad_hidden + norm_backward(grad_first, normed_one, inverse_one, scale_one)

    grad_qkv_b = lax.dynamic_update_slice_in_dim(
        jnp.zeros((2 * 3 * span,), F32), grad_qkv_b, core * 3 * span, 0
    )
    pieces = [
        grad_scale_one, grad_shift_one, grad_qkv_b, grad_out_b, grad_scale_two, grad_shift_two,
        grad_up_b, grad_down_b,
    ]
    sizes = [piece.shape[0] for piece in pieces]
    packed = lax.psum(jnp.concatenate(pieces), ("fsdp", "seq"))
    index = lax.axis_index("fsdp")
    small_out, at = [], 0
    for size in sizes:
        mine = size // n_fsdp
        small_out.append(lax.dynamic_slice_in_dim(packed, at + index * mine, mine, 0))
        at += size

    qkv_wide = lax.dynamic_update_slice_in_dim(
        jnp.zeros((shard, 2 * 3 * span), F32), qkv_part.astype(F32), core * 3 * span, 1
    )
    qkv_g, out_g, up_g, down_g = lax.psum(
        (qkv_wide, out_part.astype(F32), up_part.astype(F32), down_part.astype(F32)), "seq"
    )
    return (
        result.astype(BF)[None],
        grad_rows[None],
        small_out[0],
        small_out[1],
        qkv_g,
        small_out[2],
        out_g,
        small_out[3],
        small_out[4],
        small_out[5],
        up_g,
        small_out[6],
        down_g,
        small_out[7],
    )


def solution(mesh):
    row, mat, vec = P("fsdp", "seq", None), P("fsdp", None), P("fsdp")
    in_specs = (row, mat, vec, vec, mat, vec, mat, vec, vec, vec, mat, vec, mat, vec, row)
    out_specs = (row, row, vec, vec, mat, vec, mat, vec, vec, vec, mat, vec, mat, vec)
    return jax.shard_map(
        on_device, mesh=mesh, in_specs=in_specs, out_specs=out_specs, check_vma=False
    )
```

time: 1830 us -> 876 us (0.48)
  matrix products: 734 us -> 95.4 us
  Pallas kernels: 0 us -> 305 us
  local copies, waits for them, and re-layouts: 290 us -> 27.2 us
  other arithmetic: 276 us -> 26.6 us
  loops' own time: 96.6 us -> 0 us
  waiting for transfers between devices: 200 us -> 278 us
  blocking collectives: 181 us -> 108 us
    dot_general x76 -> x3, matrix products: 405 us -> 24.1 us  [right_transposed(): lax.dot_general(left, right, (((1,), (1,)), ((), ())), preferred_element_...]
    pallas_call x0 -> x3, Pallas kernels: none -> 305 us  [the longest x1 143 us: attend_back(): pl.pallas_call(functools.partial(attend_back_kernel, group), grid_spec=pl...]
    convert_element_type x34 -> x1, other arithmetic: 192 us -> 0.01 us  [on_device(): vectors = jnp.transpose(vectors, (2, 0, 1)).astype(F32)]
    dot_general x52 -> x3, matrix products: 191 us -> 26.8 us  [rows_contract(): lax.dot_general(left, right, (((0,), (0,)), ((), ())), preferred_element_...]
    dynamic_update_slice x81 -> x1, local copies, waits for them, and re-layouts: 102 us -> 0.24 us  [on_device(): lax.dynamic_update_slice_in_dim(jnp.zeros((2 * 3 * span,), F32), grad_qkv...]
    all_to_all x1 -> x0, blocking collectives: 101 us -> none  [on_device(): lax.all_to_all(grad_packed, 'seq', split_axis=0, concat_axis=1, tiled=True)]
    ppermute x0 -> x7, waiting for transfers between devices: none -> 97.3 us  [the longest x1 60.6 us: on_device(): from_noisy = lax.ppermute(clean_grad, 'seq', [(0, 2), (1, 3)])]
    another operation x8 -> x0, loops' own time: 96.6 us -> none  [the longest x3 48.4 us: one_head(): lax.scan(one_block, (zero_rows, zero_rows), starts)]
  transfers between devices with their start and end apart: 12 -> 16, of which waited for: 5 -> 9; matrix products, arithmetic and copies ran while one was open for 69% -> 13% of each run, Pallas kernels for 0% -> 19%
where the time goes in v1:
time: 876 us; the launch traced here: 867 us
  Pallas kernels  305 us (35%)
  waiting for transfers between devices  278 us (32%)
  blocking collectives  108 us (12%)
  matrix products  95.4 us (11%)
  local copies, waits for them, and re-layouts  27.2 us (3%)
  other arithmetic  26.6 us (3%)
  between operations  14.8 us (2%)
  starting transfers between devices  11.5 us (1%)
    pallas_call x1, Pallas kernels, attend_back(): pl.pallas_call(functools.partial(attend_back_kernel, group), grid_spec=pl...  143 us
    pallas_call x1, Pallas kernels, attend(): pl.pallas_call(functools.partial(attend_kernel, group), grid_spec=pltpu.P...  140 us
    reduce_scatter x1, waiting for transfers between devices, on_device(): lax.psum_scatter(grad_up_w.astype(BF), 'fsdp', scatter_dimension=0, tiled...  99 us
    psum x1, blocking collectives, on_device(): lax.psum((qkv_wide, out_part.astype(F32), up_part.astype(F32), down_part....  64.5 us
    ppermute x1, waiting for transfers between devices, on_device(): from_noisy = lax.ppermute(clean_grad, 'seq', [(0, 2), (1, 3)])  60.6 us
    reduce_scatter x1, waiting for transfers between devices, on_device(): lax.psum_scatter(grad_down_w.astype(BF), 'fsdp', scatter_dimension=0, til...  54 us
    psum x1, blocking collectives, on_device(): packed = lax.psum(jnp.concatenate(pieces), ('fsdp', 'seq'))  43.4 us
    ppermute x1, waiting for transfers between devices, on_device(): clean_in = lax.ppermute(tok, 'seq', [(2, 0), (3, 1)])  32.8 us
  transfers between devices with their start and end apart: 16, of which 9 were waited for; matrix products, arithmetic and copies ran while one was open for 13% of the time, Pallas kernels for 19%

profile of v1, /device:TPU:13, one launch (start us, length us, event | category | flops | bytes accessed | tf_op | source)
XLA Modules:
  0.0 866.5 jit_solution(13565672476448963091)
XLA Ops:
  12.8 1.3 collective-permute-start.1
  16.5 0.9 convert_reduce_fusion.5
  17.5 32.8 %collective-permute-done.1 = bf16[1024,768]{1,0:T(8,128)(2,1)} collective-permute-done((bf16[1024,768]{1,0:T(8,128)(2,1)}, bf16[1024,768]{1,0:T(8,128)(2,1)}, u32[]{:S(2)}, u32[]{:S(2)}) %collective-permute-start.1) | collective-permute-done | bytes 1572896 | tf_op jit(solution)/shard_map/ppermute | solution.py:380
  50.3 2.8 broadcast_select_fusion.cmine
  53.1 1.5 collective-permute-start.2
  55.2 1.8 fusion.26
  59.5 1.4 reshape.427.bias_ref
  61.6 1.1 copy-done.12
  62.7 21.7 %project.1 = (bf16[384,2048]{1,0:T(8,128)(2,1)}, bf16[384,2048]{1,0:T(8,128)(2,1)}, bf16[384,2048]{1,0:T(8,128)(2,1)}, bf16[384,2048]{1,0:T(8,128)(2,1)}, bf16[3...) custom-call(s32[1]{0:T(128)} %bitcast.6.core_ref, bf16[1024,768]{1,0:T(8,128)(2,1)} %bitcast.93, ...), custom_call_target="tpu_custom_call" | custom-call | tf_op jit(solution)/shard_map/project/pallas_call | solution.py:120
  85.1 1.3 broadcast_in_dim.23.id_col
  86.4 140.3 %attend.1 = (bf16[384,2048]{1,0:T(8,128)(2,1)}, f32[6,8,2048]{2,1,0:T(8,128)}) custom-call(s32[5,8]{1,0:T(8,128)} %stack.2.bounds, bf16[384,2048]{1,0:T(8,128)(2,1)} %get-tuple-element.36.q, bf16[384,2048]{1,0:T(8,128)(2,1)} %get-tuple-element.37.k, bf16[384,2048]{1,0:T(8,128)(2,1)} %get-tuple-element.38.v, bf16[384,2048]{1,0:T(8,128)(2,1)} %get-tuple-element.39.kc, ...), custom_call_target="tpu_custom_call" | custom-call | tf_op jit(solution)/shard_map/attend/pallas_call | solution.py:203
  226.7 2.5 constant_dynamic-slice_fusion.1
  229.2 1.7 collective-permute-start.3
  231.2 1.9 collective-permute-done.3
  233.2 3.5 fusion.36
  236.7 1.7 copy-done.4
  239.0 11.1 %fusion.34 = f32[1024,3072]{1,0:T(8,128)} fusion(bf16[768,3072]{1,0:T(8,128)(2,1)} %all-gather.9.cloned.1.call-done, f32[1024,768]{1,0:T(8,128)} %copy-done.4, f32[768]{0:T(1024)S(1)} %add.247, f32[768]{0:T(1024)S(1)} %mul.213, f32[1024]{0:T(1024)S(1)} %add_rsqrt_fusion.1, f32[1024]{0:T(1024)S(1)} %broadcast_multiply_fusion.5), kind=kOutput, calls=%fused_computation.128 | convolution fusion | flops 4835770368 | bytes 20461568 | tf_op jit(solution)/shard_map/dot_general | solution.py:48
  250.1 9.2 %all-gather.11.cloned.1.call-done = bf16[3072,768]{1,0:T(8,128)(2,1)} async-done(((bf16[384,768]{1,0:T(8,128)(2,1)}), bf16[3072,768]{1,0:T(8,128)(2,1)}) %all-gather.11.cloned.1.call-update) | async-done | bytes 4718608 | tf_op jit(solution)/shard_map/all_gather | solution.py:413
  259.3 16.9 %convert_reduce_fusion = (f32[3072]{0:T(1024)S(1)}, bf16[1024,3072]{1,0:T(8,128)(2,1)S(1)}) fusion(f32[1024,3072]{1,0:T(8,128)} %fusion.34, f32[3072]{0:T(1024)S(1)} %add.250, bf16[3072,768]{1,0:T(8,128)(2,1)} %all-gather.11.cloned.1.call-done, bf16[1,1024,768]{2,1,0:T(8,128)(2,1)} %param.31), kind=kOutput, calls=%fused_computation.9 | convolution fusion | flops 4904186880 | bytes 25190400 | tf_op jit(solution)/shard_map/dot_general | solution.py:44
  276.2 5.8 multiply_reduce_fusion
  282.1 1.7 convert_reduce_fusion.4
  283.9 1.4 convolution_convert_fusion.3
  285.5 1.0 dynamic-slice_bitcast_fusion
  286.5 2.0 collective-permute-start.4
  288.5 1.9 collective-permute-done.4.do_other
  291.2 142.9 %attend_back.1 = (bf16[1152,2048]{1,0:T(8,128)(2,1)}, bf16[768,2048]{1,0:T(8,128)(2,1)}) custom-call(s32[5,8]{1,0:T(8,128)} %stack.2.bounds, bf16[384,2048]{1,0:T(8,128)(2,1)} %get-tuple-element.36.q, bf16[384,2048]{1,0:T(8,128)(2,1)} %get-tuple-element.37.k, bf16[384,2048]{1,0:T(8,128)(2,1)} %get-tuple-element.38.v, ...), custom_call_target="tpu_custom_call" | custom-call | tf_op jit(solution)/shard_map/attend_back/pallas_call | solution.py:326
  434.1 3.0 collective-permute-start.5
  437.1 5.3 convolution_convert_fusion.4
  442.4 60.6 %collective-permute-done.5 = bf16[768,2048]{1,0:T(8,128)(2,1)} collective-permute-done((bf16[768,2048]{1,0:T(8,128)(2,1)}, bf16[768,2048]{1,0:T(8,128)(2,1)}, u32[]{:S(2)}, u32[]{:S(2)}) %collective-permute-start.5) | collective-permute-done | bytes 3145760 | tf_op jit(solution)/shard_map/ppermute | solution.py:492
  503.1 6.2 fusion.20
  509.3 8.0 convolution_convert_fusion.2
  517.3 12.8 %convolution_convert_fusion = bf16[3072,768]{1,0:T(8,128)(2,1)} fusion(bf16[1,1024,768]{2,1,0:T(8,128)(2,1)} %param.31, f32[1024,3072]{1,0:T(8,128)} %fusion.34, f32[3072]{0:T(1024)S(1)} %add.250), kind=kOutput, calls=%fused_computation.12 | convolution fusion | flops 4865654784 | bytes 18886656 | tf_op jit(solution)/shard_map/dot_general | solution.py:40
  530.2 10.5 %convolution_convert_fusion.1 = bf16[768,3072]{1,0:T(8,128)(2,1)} fusion(bf16[1024,3072]{1,0:T(8,128)(2,1)} %copy-done.20, f32[1024,768]{1,0:T(8,128)} %copy-done.4, f32[768]{0:T(1024)S(1)} %add.247, f32[768]{0:T(1024)S(1)} %mul.213, f32[1024]{0:T(1024)S(1)} %add_rsqrt_fusion.1, f32[1024]{0:T(1024)S(1)} %broadcast_multiply_fusion.5), kind=kOutput, calls=%fused_computation.13 | convolution fusion | flops 4838129664 | bytes 14170112 | tf_op jit(solution)/shard_map/dot_general | solution.py:40
  541.8 7.0 fusion.21
  548.9 2.6 copy-done.9
  551.5 1.3 dynamic-slice_convert_fusion
  552.8 1.0 collective-permute-start.6
  554.0 13.1 %fusion.25 = bf16[1,1024,768]{2,1,0:T(8,128)(2,1)} fusion(f32[768]{0:T(1024)S(1)} %add.256, f32[1024,768]{1,0:T(8,128)S(1)} %copy-done.6, bf16[3072,768]{1,0:T(8,128)(2,1)} %all-gather.11.cloned.1.call-done, f32[1024,3072]{1,0:T(8,128)} %fusion.34, f32[3072]{0:T(1024)S(1)} %add.250), kind=kOutput, calls=%fused_computation.54 | convolution fusion | flops 4865654784 | bytes 22035456 | tf_op jit(solution)/shard_map/dot_general | solution.py:48
  567.1 3.1 convert_reduce_fusion.1
  570.5 3.8 fusion.17
  574.4 2.4 fusion.16
  576.9 15.8 %reduce-scatter.5.cloned.1.call-done = bf16[96,1152]{1,0:T(8,128)(2,1)} async-done(((bf16[768,1152]{1,0:T(8,128)(2,1)}), bf16[96,1152]{1,0:T(8,128)(2,1)}) %reduce-scatter.5.cloned.1.call-update) | async-done | bytes 221200 | tf_op jit(solution)/shard_map/reduce_scatter | solution.py:500
  592.7 1.0 convert_dynamic-update-slice_fusion
  594.6 43.4 %psum.35 = f32[9984]{0:T(1024)S(1)} all-reduce(f32[9984]{0:T(1024)S(1)} %constant_dynamic-update-slice_fusion), channel_id=1, replica_groups=mesh['seq'=4,'fsdp'=8] {'fsdp','seq'}, use_global_device_ids=true, to_apply=%region_20.21 | all-reduce | flops 9984 | bytes 79872 | tf_op jit(solution)/shard_map/psum | solution.py:521
  639.9 54.0 %reduce-scatter.11.cloned.1.call-done = bf16[384,768]{1,0:T(8,128)(2,1)} async-done(((bf16[3072,768]{1,0:T(8,128)(2,1)}), bf16[384,768]{1,0:T(8,128)(2,1)}) %reduce-scatter.11.cloned.1.call-update) | async-done | bytes 589840 | tf_op jit(solution)/shard_map/reduce_scatter | solution.py:485
  693.9 99.0 %reduce-scatter.9.cloned.1.call-done = bf16[96,3072]{1,0:T(8,128)(2,1)} async-done(((bf16[768,3072]{1,0:T(8,128)(2,1)}), bf16[96,3072]{1,0:T(8,128)(2,1)}) %reduce-scatter.9.cloned.1.call-update) | async-done | bytes 589840 | tf_op jit(solution)/shard_map/reduce_scatter | solution.py:486
  792.9 64.5 %all-reduce.6 = (f32[96,768]{1,0:T(8,128)}, f32[96,3072]{1,0:T(8,128)}, f32[384,768]{1,0:T(8,128)}) all-reduce(bf16[96,768]{1,0:T(8,128)(2,1)S(1)} %copy-done.15, bf16[96,3072]{1,0:T(8,128)(2,1)} %reduce-scatter.9.cloned.1.call-done, bf16[384,768]{1,0:T(8,128)(2,1)} %reduce-scatter.11.cloned.1.call-done), channel_id=1, replica_groups=mesh['seq'=4,'fsdp'=8] {'seq'}, use_global_device_ids=true, to_apply=%region_24.25 | all-reduce | flops 663552 | bytes 3981312 | tf_op jit(solution)/shard_map/psum | solution.py:532
  857.4 2.1 copy.78
  (130 shorter events, 19.1 us)
Async XLA Ops:
  7.2 2.8 copy-start
  7.2 43.1 %copy-start.2 = (bf16[1,1024,768]{2,1,0:T(8,128)(2,1)S(1)}, bf16[1,1024,768]{2,1,0:T(8,128)(2,1)}, u32[]{:S(2)}) copy-start(bf16[1,1024,768]{2,1,0:T(8,128)(2,1)} %param.17) | copy-start | bytes 4718596
  7.2 50.7 %all-gather.5.cloned.1.call-start = ((), (), s32[]{:S(2)}) async-start(), calls=%async_computation.4 | async-start | bytes 2211840 | tf_op jit(solution)/shard_map/all_gather | solution.py:400
  10.7 220.5 %all-gather.7.cloned.1.call-start = ((), (), s32[]{:S(2)}) async-start(), calls=%async_computation.5 | async-start | bytes 1327104 | tf_op jit(solution)/shard_map/all_gather | solution.py:411
  11.5 227.5 %all-gather.9.cloned.1.call-start = ((), (), s32[]{:S(2)}) async-start(), calls=%async_computation.6 | async-start | bytes 5308416 | tf_op jit(solution)/shard_map/all_gather | solution.py:412
  12.2 247.1 %all-gather.11.cloned.1.call-start = ((), (), s32[]{:S(2)}) async-start(), calls=%async_computation.7 | async-start | bytes 5308416 | tf_op jit(solution)/shard_map/all_gather | solution.py:413
  12.8 554.3 %reduce-scatter.7.cloned.1.call-start = ((), (), s32[]{:S(2)}) async-start(), calls=%async_computation.10 | async-start | bytes 1327104 | tf_op jit(solution)/shard_map/reduce_scatter | solution.py:487
  12.8 37.5 %collective-permute-start.1 = (bf16[1024,768]{1,0:T(8,128)(2,1)}, bf16[1024,768]{1,0:T(8,128)(2,1)}, u32[]{:S(2)}, u32[]{:S(2)}) collective-permute-start(bf16[1024,768]{1,0:T(8,128)(2,1)} %bitcast.91), channel_id=1, source_target_pairs={{16,0},{24,8},{17,1},{25,9},{18,2},{26,10},{19,3},{27,11},{20,4},{... | collective-permute-start | bytes 4718600 | tf_op jit(solution)/shard_map/ppermute | solution.py:380
  14.1 47.4 %collective-permute-start = (bf16[1024,768]{1,0:T(8,128)(2,1)}, bf16[1024,768]{1,0:T(8,128)(2,1)}, u32[]{:S(2)}, u32[]{:S(2)}) collective-permute-start(bf16[1024,768]{1,0:T(8,128)(2,1)} %bitcast.92), channel_id=1, source_target_pairs={{0,8},{8,0},{16,24},{24,16},{1,9},{9,1},{17,25},{25,17},{2,10},{10... | collective-permute-start | bytes 4718600 | tf_op jit(solution)/shard_map/ppermute | solution.py:379
  53.1 8.5 collective-permute-start.2
  61.6 1.1 copy-start.12
  62.7 21.7 %copy-start.16 = (s32[1,2048]{1,0:T(1,128)S(1)}, s32[1,2048]{1,0:T(1,128)}, u32[]{:S(2)}) copy-start(s32[1,2048]{1,0:T(1,128)} %param.18) | copy-start | bytes 24580
  226.7 6.5 copy-start.3
  229.2 7.5 copy-start.14
  229.2 3.9 collective-permute-start.3
  236.7 1.7 copy-start.4
  259.3 16.9 %copy-start.5 = (f32[1024,768]{1,0:T(8,128)S(1)}, f32[1024,768]{1,0:T(8,128)}, u32[]{:S(2)}) copy-start(f32[1024,768]{1,0:T(8,128)} %copy-done.4) | copy-start | bytes 9437188
  259.3 16.9 %copy-start.17 = (bf16[768,3072]{1,0:T(8,128)(2,1)S(1)}, bf16[768,3072]{1,0:T(8,128)(2,1)}, u32[]{:S(2)}) copy-start(bf16[768,3072]{1,0:T(8,128)(2,1)} %all-gather.9.cloned.1.call-done) | copy-start | bytes 14155780
  276.2 5.8 copy-start.20
  276.2 5.8 copy-start.11
  282.1 1.8 copy-start.19
  283.8 1.6 copy-start.7
  286.5 3.9 collective-permute-start.4
  290.4 0.9 copy-start.13
  434.1 69.0 %collective-permute-start.5 = (bf16[768,2048]{1,0:T(8,128)(2,1)}, bf16[768,2048]{1,0:T(8,128)(2,1)}, u32[]{:S(2)}, u32[]{:S(2)}) collective-permute-start(bf16[768,2048]{1,0:T(8,128)(2,1)} %get-tuple-element.44), channel_id=1, source_target_pairs={{0,16},{8,24},{1,17},{9,25},{2,18},{10,26},{3,19},{11,27},{4,20},{... | collective-permute-start | bytes 9437192 | tf_op jit(solution)/shard_map/ppermute | solution.py:492
  442.4 150.2 %reduce-scatter.5.cloned.1.call-start = ((), (), s32[]{:S(2)}) async-start(), calls=%async_computation.8 | async-start | bytes 1990656 | tf_op jit(solution)/shard_map/reduce_scatter | solution.py:500
  503.1 6.2 copy-start.18
  517.3 176.6 %reduce-scatter.11.cloned.1.call-start = ((), (), s32[]{:S(2)}) async-start(), calls=%async_computation.12 | async-start | bytes 5308416 | tf_op jit(solution)/shard_map/reduce_scatter | solution.py:485
  530.2 262.7 %reduce-scatter.9.cloned.1.call-start = ((), (), s32[]{:S(2)}) async-start(), calls=%async_computation.11 | async-start | bytes 5308416 | tf_op jit(solution)/shard_map/reduce_scatter | solution.py:486
  540.7 316.7 %all-reduce.5.cloned.1.call-start = ((), (), s32[]{:S(2)}) async-start(), calls=%async_computation.9 | async-start | bytes 1769472 | tf_op jit(solution)/shard_map/psum | solution.py:532
  548.9 2.6 copy-start.9
  551.5 2.5 copy-start.6
  552.8 17.7 %collective-permute-start.6 = (bf16[1024,768]{1,0:T(8,128)(2,1)}, bf16[1024,768]{1,0:T(8,128)(2,1)}, u32[]{:S(2)}, u32[]{:S(2)}) collective-permute-start(bf16[1024,768]{1,0:T(8,128)(2,1)} %dynamic-slice_convert_fusion), channel_id=1, source_target_pairs={{0,8},{8,0},{16,24},{24,16},{1,9},{9,1},{17,25},{25,17},{2,10},{10... | collective-permute-start | bytes 4718600 | tf_op jit(solution)/shard_map/ppermute | solution.py:505
  570.5 3.9 copy-start.8
  574.4 218.5 %copy-start.15 = (bf16[96,768]{1,0:T(8,128)(2,1)S(1)}, bf16[96,768]{1,0:T(8,128)(2,1)}, u32[]{:S(2)}) copy-start(bf16[96,768]{1,0:T(8,128)(2,1)} %reduce-scatter.7.cloned.1.call-done) | copy-start | bytes 442372
  574.4 285.1 %copy-start.1 = (bf16[96,2304]{1,0:T(8,128)(2,1)S(1)}, bf16[96,2304]{1,0:T(8,128)(2,1)}, u32[]{:S(2)}) copy-start(bf16[96,2304]{1,0:T(8,128)(2,1)} %param.21) | copy-start | bytes 1327108
  593.6 0.9 copy-start.10
Sparse Core Ops, SparseCore 0:
  10.8 47.0 all-gather.4
  60.1 39.1 all-gather.6
  101.5 77.4 all-gather.8
  181.0 78.2 all-gather.10
  442.5 70.8 reduce-scatter.6
  517.4 75.1 reduce-scatter.4
  596.2 97.6 reduce-scatter.10
  697.5 95.2 reduce-scatter.8
  795.8 42.7 all-reduce.4

commit v2 on v1

--- a/solution.py
+++ b/solution.py
@@ -12,9 +12,9 @@
 EPSILON = 1e-05
 LOG2E = 1.4426950408889634
 NEG = -1e30
-TQ = 256
+TQ = 512
 TK = 256
-TM = 128
+TM = 256
 BF = jnp.bfloat16
 F32 = jnp.float32
 
@@ -311,8 +311,10 @@
         band_v = jnp.where(noisy, dv_acc[h], dvc_acc[h])
         back_turn(jnp.transpose(band_k) * HD**-0.5, own_out, (3 * h + 1) * HD)
         own_out[(3 * h + 2) * HD : (3 * h + 3) * HD, :] = jnp.transpose(band_v).astype(BF)
-        back_turn(jnp.transpose(dkc_acc[h]) * HD**-0.5, cln_out, 2 * h * HD)
-        cln_out[(2 * h + 1) * HD : (2 * h + 2) * HD, :] = jnp.transpose(dvc_acc[h]).astype(BF)
+        part_k = jnp.where(noisy, dkc_acc[h], 0.0)
+        part_v = jnp.where(noisy, dvc_acc[h], 0.0)
+        back_turn(jnp.transpose(part_k) * HD**-0.5, cln_out, 2 * h * HD)
+        cln_out[(2 * h + 1) * HD : (2 * h + 2) * HD, :] = jnp.transpose(part_v).astype(BF)
 
 
 def attend_back(bounds, q, k, v, kc, vc, o, lse, do_mine, do_other, id_row, id_col, cos_t, sin_t,
@@ -346,6 +348,135 @@
         ],
         name="attend_back",
     )(bounds, q, k, v, kc, vc, o, lse, do_mine, do_other, id_row, id_col, cos_t, sin_t)
+
+
+def finish_kernel(n, g, s, up, dn, ou, g_out, s_out, up_out, dn_out, ou_out, g_in, s_in, g_x,
+                  s_x, up_x, dn_x, ou_x, g_t, s_t, s_c, up_t, dn_t, ou_t, send, recv, s_send,
+                  s_recv, x_send, x_recv, c_send, c_recv, local):
+    me = lax.axis_index("fsdp")
+    seat = lax.axis_index("seq")
+    core = lax.rem(seat, 2)
+    across = {"seq": lax.rem(seat + 2, 4)}
+    beside = {"seq": seat + 1 - 2 * core}
+    mesh_id = pl.DeviceIdType.MESH
+    barrier = pltpu.get_barrier_semaphore()
+    peers = [{"fsdp": lax.rem(me + d, n)} for d in range(1, n)]
+    for where in peers + [across, beside]:
+        pl.semaphore_signal(barrier, inc=1, device_id=where, device_id_type=mesh_id)
+    pl.semaphore_wait(barrier, n + 1)
+
+    def push(src, dst, one, two, where):
+        copy = pltpu.make_async_remote_copy(
+            src_ref=src, dst_ref=dst, send_sem=one, recv_sem=two, device_id=where,
+            device_id_type=mesh_id,
+        )
+        copy.start()
+        return copy
+
+    def settle(tmp, out, sem):
+        copy = pltpu.make_async_copy(tmp, out, sem)
+        copy.start()
+        copy.wait()
+
+    first = []
+    for d in range(1, n):
+        to = lax.rem(me + d, n)
+        first.append(push(g.at[to], g_in.at[d - 1], send.at[d - 1], recv.at[d - 1], peers[d - 1]))
+        first.append(
+            push(s.at[to], s_in.at[d - 1], s_send.at[d - 1], s_recv.at[d - 1], peers[d - 1])
+        )
+    shards = [(up, up_x, up_t, up_out), (dn, dn_x, dn_t, dn_out), (ou, ou_x, ou_t, ou_out)]
+    over = [
+        push(src, land, x_send.at[i], x_recv.at[i], across)
+        for i, (src, land, _, _) in enumerate(shards)
+    ]
+    near = []
+    for i, (src, land, tmp, out) in enumerate(shards):
+        over[i].wait()
+        tmp[...] = (src[...].astype(F32) + land[...].astype(F32)).astype(BF)
+        settle(tmp, out.at[core], local.at[i])
+        near.append(push(out.at[core], out.at[core], c_send.at[i], c_recv.at[i], beside))
+    for copy in first:
+        copy.wait()
+
+    rows = g.shape[1]
+    block = 16 if rows % 16 == 0 else rows
+
+    def add_rows(i, _):
+        at = pl.ds(pl.multiple_of(i * block, block), block)
+        total = g[me, at, :].astype(F32)
+        for d in range(n - 1):
+            total = total + g_in[d, at, :].astype(F32)
+        g_t[at, :] = total.astype(BF)
+        return 0
+
+    lax.fori_loop(0, rows // block, add_rows, 0)
+    total = s[me]
+    for d in range(n - 1):
+        total = total + s_in[d]
+    s_t[0] = total
+    settle(g_t, g_x.at[0], local.at[3])
+    settle(s_t.at[0], s_x.at[0], local.at[4])
+    far_g = push(g_x.at[0], g_x.at[1], x_send.at[3], x_recv.at[3], across)
+    far_s = push(s_x.at[0], s_x.at[1], x_send.at[4], x_recv.at[4], across)
+    far_s.wait()
+    s_t[1] = s_x[0] + s_x[1]
+    settle(s_t.at[1], s_c.at[0], local.at[5])
+    near_s = push(s_c.at[0], s_c.at[1], c_send.at[4], c_recv.at[4], beside)
+    far_g.wait()
+    g_t[...] = (g_x[0].astype(F32) + g_x[1].astype(F32)).astype(BF)
+    settle(g_t, g_out.at[core], local.at[6])
+    near.append(push(g_out.at[core], g_out.at[core], c_send.at[3], c_recv.at[3], beside))
+    near_s.wait()
+    s_out[...] = s_c[0] + s_c[1]
+    for copy in near:
+        copy.wait()
+
+
+def finish(g, s, up, dn, ou):
+    n = g.shape[0]
+    vm = pl.BlockSpec(memory_space=pltpu.VMEM)
+    pair = lambda a: jax.ShapeDtypeStruct((2,) + a.shape, BF)
+    one = lambda a: pltpu.VMEM(a.shape, a.dtype)
+    dma = pltpu.SemaphoreType.DMA
+    return pl.pallas_call(
+        functools.partial(finish_kernel, n),
+        in_specs=[vm] * 5,
+        out_specs=[vm] * 5,
+        out_shape=[
+            jax.ShapeDtypeStruct((2,) + g.shape[1:], BF),
+            jax.ShapeDtypeStruct(s.shape[1:], F32),
+            pair(up),
+            pair(dn),
+            pair(ou),
+        ],
+        scratch_shapes=[
+            pltpu.VMEM((n - 1,) + g.shape[1:], BF),
+            pltpu.VMEM((n - 1,) + s.shape[1:], F32),
+            pltpu.VMEM((2,) + g.shape[1:], BF),
+            pltpu.VMEM((2,) + s.shape[1:], F32),
+            one(up),
+            one(dn),
+            one(ou),
+            pltpu.VMEM(g.shape[1:], BF),
+            pltpu.VMEM((2,) + s.shape[1:], F32),
+            pltpu.VMEM((2,) + s.shape[1:], F32),
+            one(up),
+            one(dn),
+            one(ou),
+            dma((n - 1,)),
+            dma((n - 1,)),
+            dma((n - 1,)),
+            dma((n - 1,)),
+            dma((5,)),
+            dma((5,)),
+            dma((5,)),
+            dma((5,)),
+            dma((7,)),
+        ],
+        compiler_params=pltpu.CompilerParams(collective_id=1, has_side_effects=True),
+        name="finish",
+    )(g, s, up, dn, ou)
 
 
 def on_device(
@@ -405,12 +536,25 @@
     vectors = jnp.transpose(vectors, (2, 0, 1)).astype(F32)
     flat = vectors[:6].reshape(6, width)
     qkv_b = jnp.transpose(vectors[6:9], (1, 0, 2)).reshape(-1)
-    up_b = jnp.transpose(vectors[9:], (1, 0, 2)).reshape(-1)
     scale_one, shift_one, out_shift, scale_two, shift_two, down_shift = [flat[i] for i in range(6)]
 
-    out_full = lax.all_gather(out_weight, "fsdp", axis=0, tiled=True)
-    up_full = lax.all_gather(up_weight, "fsdp", axis=0, tiled=True)
-    down_full = lax.all_gather(down_weight, "fsdp", axis=0, tiled=True)
+    inner = up_bias.shape[0] // 2
+    up_b = jnp.transpose(vectors[9:], (1, 0, 2)).reshape(n_fsdp, 2, inner)
+    up_b = lax.dynamic_index_in_dim(up_b, core, 1, False).reshape(-1)
+    up_cols = lax.dynamic_index_in_dim(
+        up_weight.reshape(shard, n_fsdp, 2, inner), core, 2, False
+    ).reshape(shard, n_fsdp * inner)
+    down_rows = lax.dynamic_slice_in_dim(down_weight, core * inner, inner, 0)
+    out_cols = lax.dynamic_slice_in_dim(out_weight, core * span, span, 1)
+    out_near = lax.all_gather(out_cols, "fsdp", axis=0, tiled=True)
+    up_own = lax.all_gather(up_cols, "fsdp", axis=0, tiled=True)
+    down_own = lax.all_gather(down_rows, "fsdp", axis=0, tiled=True)
+    out_far = lax.ppermute(out_near, "seq", swap)
+    in_order = lambda near, far, axis: jnp.where(
+        core == 0, jnp.concatenate([near, far], axis), jnp.concatenate([far, near], axis)
+    )
+    out_full = in_order(out_near, out_far, 1)
+    cot_both = jnp.concatenate([cotangent[0], lax.ppermute(cotangent[0], "seq", swap)], 0)
 
     frequency = jnp.exp(-jnp.log(10000.0) * jnp.arange(HD // 2, dtype=F32) / (HD // 2))
     angles = frequency[:, None] * jnp.arange(length, dtype=F32)[None, :]
@@ -447,105 +591,138 @@
     cut = lambda value, which: lax.dynamic_slice_in_dim(value, which * local_rows, local_rows, 1)
     o_mine = cut(o, core)
     o_in = lax.ppermute(cut(o, 1 - core), "seq", swap)
-    attended = jnp.where(
-        core == 0, jnp.concatenate([o_mine, o_in], 0), jnp.concatenate([o_in, o_mine], 0)
-    )
+    attended = in_order(o_mine, o_in, 0)
 
     rows_in = tok.astype(F32)
     hidden = rows_in + rows_contract(attended, out_full) + out_shift
     normed_two, inverse_two = normalize_parts(hidden)
     second_in = (normed_two * scale_two + shift_two).astype(BF)
-    pre_act = dot(second_in, up_full) + up_b
+    both_in = jnp.concatenate([second_in, lax.ppermute(second_in, "seq", swap)], 0)
+
+    def join(partial):
+        return partial[:local_rows] + lax.ppermute(
+            partial[local_rows:].astype(BF), "seq", swap
+        ).astype(F32)
+
+    pre_act = dot(both_in, up_own) + up_b
     activated, gelu_pull = jax.vjp(
         lambda pre_value: jax.nn.gelu(pre_value, approximate=True), pre_act
     )
     act_low = activated.astype(BF)
-    result = hidden + dot(act_low, down_full) + down_shift
-
-    grad_branch = cotangent[0]
-    grad_top = grad_branch.astype(F32)
-    grad_down_w = rows_contract(act_low, grad_branch)
+    result = hidden + join(dot(act_low, down_own)) + down_shift
+
+    grad_top = cotangent[0].astype(F32)
     grad_down_b = jnp.sum(grad_top, 0)
-    grad_act = right_transposed(grad_branch, down_full)
-    grad_pre = gelu_pull(grad_act)[0].astype(BF)
-    grad_up_w = rows_contract(second_in, grad_pre)
+    grad_pre = gelu_pull(right_transposed(cot_both, down_own))[0].astype(BF)
+    grad_second = join(right_transposed(grad_pre, up_own))
     grad_up_b = jnp.sum(grad_pre.astype(F32), 0)
-    grad_second = right_transposed(grad_pre, up_full)
+    grad_down_w = rows_contract(act_low, cot_both).astype(BF)
+    grad_up_w = rows_contract(both_in, grad_pre).astype(BF)
     grad_scale_two = jnp.sum(grad_second * normed_two, 0)
     grad_shift_two = jnp.sum(grad_second, 0)
     grad_hidden = grad_top + norm_backward(grad_second, normed_two, inverse_two, scale_two)
 
     grad_attn = grad_hidden.astype(BF)
-    grad_out_w = dot(attended, grad_attn)
+    grad_out_w = dot(attended, grad_attn).astype(BF)
     grad_out_b = jnp.sum(grad_attn.astype(F32), 0)
     grad_o = right_transposed(out_full, grad_attn).astype(BF)
     cut_heads = lambda which: lax.dynamic_slice_in_dim(grad_o, which * span, span, 0)
     do_mine = cut_heads(core)
     do_in = lax.ppermute(cut_heads(1 - core), "seq", swap)
-    down_part = lax.psum_scatter(grad_down_w.astype(BF), "fsdp", scatter_dimension=0, tiled=True)
-    up_part = lax.psum_scatter(grad_up_w.astype(BF), "fsdp", scatter_dimension=0, tiled=True)
-    out_part = lax.psum_scatter(grad_out_w.astype(BF), "fsdp", scatter_dimension=0, tiled=True)
+    cut_cols = lambda which: lax.dynamic_slice_in_dim(grad_out_w, which * span, span, 1)
+    out_sum = (
+        cut_cols(core).astype(F32) + lax.ppermute(cut_cols(1 - core), "seq", swap).astype(F32)
+    ).astype(BF)
+    do_mine, do_in, grad_down_w, grad_up_w, out_sum = lax.optimization_barrier(
+        (do_mine, do_in, grad_down_w, grad_up_w, out_sum)
+    )
+    scatter = lambda grad: lax.psum_scatter(grad, "fsdp", scatter_dimension=0, tiled=True)
+    down_part = scatter(grad_down_w)
+    up_out_part = scatter(jnp.concatenate([grad_up_w, out_sum], 1))
+    up_part, out_part = up_out_part[:, : n_fsdp * inner], up_out_part[:, n_fsdp * inner :]
 
     own_grad, clean_grad = attend_back(
         bounds, q, k, v, kc, vc, o, lse, do_mine, do_in, id_row, id_col, cos_t, sin_t, heads, 2
     )
-    from_noisy = lax.ppermute(clean_grad, "seq", [(0, 2), (1, 3)])
-    own_grad = own_grad.reshape(heads, 3 * HD, length)
-    own_grad = own_grad.at[:, HD:].add(from_noisy.reshape(heads, 2 * HD, length))
-    own_grad = own_grad.reshape(3 * span, length)
-    grad_qkv_w = lax.dot_general(
-        a_own, own_grad, (((0,), (1,)), ((), ())), preferred_element_type=F32
-    )
-    grad_qkv_b = jnp.sum(own_grad.astype(F32), 1)
-    qkv_part = lax.psum_scatter(grad_qkv_w.astype(BF), "fsdp", scatter_dimension=0, tiled=True)
-    grad_first = lax.dot_general(
-        own_grad, gathered[:, : 3 * span], (((0,), (1,)), ((), ())), preferred_element_type=F32
-    )
-    cut_rows = lambda which: lax.dynamic_slice_in_dim(grad_first, which * local_rows, local_rows, 0)
-    grad_first = cut_rows(core) + lax.ppermute(
-        cut_rows(1 - core).astype(BF), "seq", swap
-    ).astype(F32)
+    weight = gathered[:, : 3 * span]
+    weight_kv = weight.reshape(width, heads, 3 * HD)[:, :, HD:].reshape(width, 2 * span)
+    back = lambda grad, w: lax.dot_general(
+        grad, w, (((0,), (1,)), ((), ())), preferred_element_type=F32
+    )
+    first_clean = back(clean_grad, weight_kv)
+    first_own = back(own_grad, weight)
+    cut_rows = lambda value, which: lax.dynamic_slice_in_dim(
+        value, which * local_rows, local_rows, 0
+    )
+    send_rows = jnp.concatenate(
+        [cut_rows(first_clean, 1 - core), cut_rows(first_own, 1 - core)], 0
+    ).astype(BF)
+    got_rows = lax.ppermute(send_rows, "seq", swap).astype(F32)
+    clean_sum = (cut_rows(first_clean, core) + got_rows[:local_rows]).astype(BF)
+    from_noisy = lax.ppermute(clean_sum, "seq", [(0, 2), (1, 3)])
+    grad_first = cut_rows(first_own, core) + got_rows[local_rows:]
+
+    by_rows = lambda a, grad: lax.dot_general(
+        a, grad, (((0,), (1,)), ((), ())), preferred_element_type=F32
+    )
+    grad_qkv_w = by_rows(a_own, own_grad).reshape(width, heads, 3 * HD)
+    grad_kv = by_rows(a_clean, clean_grad).reshape(width, heads, 2 * HD)
+    grad_qkv_w = grad_qkv_w.at[:, :, HD:].add(grad_kv).astype(BF)
+    grad_qkv_w = grad_qkv_w.reshape(n_fsdp, shard, 3 * span)
+    grad_qkv_b = jnp.sum(own_grad.astype(F32), 1).reshape(heads, 3 * HD)
+    kv_b = jnp.sum(clean_grad.astype(F32), 1).reshape(heads, 2 * HD)
+    grad_qkv_b = grad_qkv_b.at[:, HD:].add(kv_b).reshape(3 * span)
+
     normed_one, inverse_one = normalize_parts(rows_in)
-    grad_scale_one = jnp.sum(grad_first * normed_one, 0)
-    grad_shift_one = jnp.sum(grad_first, 0)
+    normed_clean, _ = normalize_parts(clean_mine.astype(F32))
+    clean_wide = clean_sum.astype(F32)
+    grad_scale_one = jnp.sum(grad_first * normed_one + clean_wide * normed_clean, 0)
+    grad_shift_one = jnp.sum(grad_first + clean_wide, 0)
+    grad_first = grad_first + from_noisy.astype(F32)
     grad_rows = grad_hidden + norm_backward(grad_first, normed_one, inverse_one, scale_one)
 
-    grad_qkv_b = lax.dynamic_update_slice_in_dim(
+    qkv_b_wide = lax.dynamic_update_slice_in_dim(
         jnp.zeros((2 * 3 * span,), F32), grad_qkv_b, core * 3 * span, 0
     )
+    up_b_wide = lax.dynamic_update_slice_in_dim(
+        jnp.zeros((n_fsdp, 2, inner), F32), grad_up_b.reshape(n_fsdp, 1, inner), core, 1
+    )
     pieces = [
-        grad_scale_one, grad_shift_one, grad_qkv_b, grad_out_b, grad_scale_two, grad_shift_two,
-        grad_up_b, grad_down_b,
+        piece.reshape(n_fsdp, -1)
+        for piece in (
+            grad_scale_one, grad_shift_one, qkv_b_wide, grad_out_b, grad_scale_two,
+            grad_shift_two, up_b_wide, grad_down_b,
+        )
     ]
-    sizes = [piece.shape[0] for piece in pieces]
-    packed = lax.psum(jnp.concatenate(pieces), ("fsdp", "seq"))
-    index = lax.axis_index("fsdp")
+    sizes = [piece.shape[1] for piece in pieces]
+    packed = jnp.concatenate(pieces, 1)
+    lines = -(-packed.shape[1] // 128)
+    packed = jnp.pad(packed, ((0, 0), (0, lines * 128 - packed.shape[1])))
+    packed = packed.reshape(n_fsdp, lines, 128)
+    qkv_g, small_sum, up_g, down_g, out_g = finish(
+        grad_qkv_w, packed, up_part, down_part, out_part
+    )
+    small_sum = small_sum.reshape(-1)
     small_out, at = [], 0
     for size in sizes:
-        mine = size // n_fsdp
-        small_out.append(lax.dynamic_slice_in_dim(packed, at + index * mine, mine, 0))
+        small_out.append(small_sum[at : at + size])
         at += size
-
-    qkv_wide = lax.dynamic_update_slice_in_dim(
-        jnp.zeros((shard, 2 * 3 * span), F32), qkv_part.astype(F32), core * 3 * span, 1
-    )
-    qkv_g, out_g, up_g, down_g = lax.psum(
-        (qkv_wide, out_part.astype(F32), up_part.astype(F32), down_part.astype(F32)), "seq"
-    )
+    side = lambda pair: jnp.concatenate([pair[0], pair[1]], 1).astype(F32)
+    up_g = jnp.transpose(up_g.reshape(2, shard, n_fsdp, inner), (1, 2, 0, 3))
     return (
         result.astype(BF)[None],
         grad_rows[None],
         small_out[0],
         small_out[1],
-        qkv_g,
+        side(qkv_g),
         small_out[2],
-        out_g,
+        side(out_g),
         small_out[3],
         small_out[4],
         small_out[5],
-        up_g,
+        up_g.reshape(shard, -1).astype(F32),
         small_out[6],
-        down_g,
+        down_g.reshape(2 * inner, width).astype(F32),
         small_out[7],
     )
 

time: 876 us -> 607 us (0.69)
  waiting for transfers between devices: 278 us -> 79.7 us
  blocking collectives: 108 us -> 23.8 us
  Pallas kernels: 305 us -> 258 us
  local copies, waits for them, and re-layouts: 27.2 us -> 63.5 us
  other arithmetic: 26.6 us -> 47.3 us
    reduce_scatter x4 -> x2, waiting for transfers between devices: 169 us -> 3.7 us  [on_device(): lax.psum_scatter(grad, 'fsdp', scatter_dimension=0, tiled=True)]
    psum x2 -> x0, blocking collectives: 108 us -> none  [the longest x1 64.5 us: on_device(): lax.psum((qkv_wide, out_part.astype(F32), up_part.astype(F32), down_part....]
    pallas_call x1, Pallas kernels: 140 us -> 84 us  [attend(): pl.pallas_call(functools.partial(attend_kernel, group), grid_spec=pltpu.P...]
    pallas_call x0 -> x1, Pallas kernels: none -> 56.1 us  [finish(): pl.pallas_call(functools.partial(finish_kernel, n), in_specs=[vm] * 5, ou...]
    pallas_call x1, Pallas kernels: 143 us -> 96 us  [attend_back(): pl.pallas_call(functools.partial(attend_back_kernel, group), grid_spec=pl...]
    ppermute x2 -> x8, waiting for transfers between devices: 60.6 us -> 20.3 us  [the longest x1 16.7 us: on_device(): from_noisy = lax.ppermute(clean_sum, 'seq', [(0, 2), (1, 3)])]
    all_gather x0 -> x1, blocking collectives: none -> 23.8 us  [on_device(): out_near = lax.all_gather(out_cols, 'fsdp', axis=0, tiled=True)]
    all_gather x3 -> x2, waiting for transfers between devices: 9.26 us -> 26.2 us  [the longest x1 26.2 us: on_device(): down_own = lax.all_gather(down_rows, 'fsdp', axis=0, tiled=True)]
  transfers between devices with their start and end apart: 16 -> 18, of which waited for: 9 -> 7; matrix products, arithmetic and copies ran while one was open for 13% -> 27% of each run, Pallas kernels for 19% -> 34%
where the time goes in v2:
time: 607 us; the launch traced here: 602 us
  Pallas kernels  258 us (43%)
  matrix products  97.5 us (16%)
  waiting for transfers between devices  79.7 us (13%)
  local copies, waits for them, and re-layouts  63.5 us (10%)
  other arithmetic  47.3 us (8%)
  blocking collectives  23.8 us (4%)
  starting transfers between devices  17.4 us (3%)
  between operations  14.7 us (2%)
    pallas_call x1, Pallas kernels, attend_back(): pl.pallas_call(functools.partial(attend_back_kernel, group), grid_spec=pl...  96 us
    pallas_call x1, Pallas kernels, attend(): pl.pallas_call(functools.partial(attend_kernel, group), grid_spec=pltpu.P...  84 us
    pallas_call x1, Pallas kernels, finish(): pl.pallas_call(functools.partial(finish_kernel, n), in_specs=[vm] * 5, ou...  56.1 us
    dot_general x3, matrix products, right_transposed(): lax.dot_general(left, right, (((1,), (1,)), ((), ())), preferred_element_...  28.7 us
    ppermute x1, waiting for transfers between devices, on_device(): clean_in = lax.ppermute(tok, 'seq', [(2, 0), (3, 1)])  27.3 us
    all_gather x1, waiting for transfers between devices, on_device(): down_own = lax.all_gather(down_rows, 'fsdp', axis=0, tiled=True)  26.2 us
    dot_general x3, matrix products, dot(): return jnp.dot(left, right, preferred_element_type=F32)  24.8 us
    all_gather x1, blocking collectives, on_device(): out_near = lax.all_gather(out_cols, 'fsdp', axis=0, tiled=True)  23.8 us
  transfers between devices with their start and end apart: 18, of which 7 were waited for; matrix products, arithmetic and copies ran while one was open for 27% of the time, Pallas kernels for 34%

profile of v2, /device:TPU:13, one launch (start us, length us, event | category | flops | bytes accessed | tf_op | source)
XLA Modules:
  0.0 601.8 jit_solution(14443443385739080239)
XLA Ops:
  13.7 2.9 reshape.528
  16.6 2.5 dynamic-slice_reduce_fusion
  21.9 27.3 %collective-permute-done.1 = bf16[1024,768]{1,0:T(8,128)(2,1)} collective-permute-done((bf16[1024,768]{1,0:T(8,128)(2,1)}, bf16[1024,768]{1,0:T(8,128)(2,1)}, u32[]{:S(2)}, u32[]{:S(2)}) %collective-permute-start.1) | collective-permute-done | bytes 1572896 | tf_op jit(solution)/shard_map/ppermute | solution.py:511
  49.2 4.1 convert_reduce_fusion.4
  54.8 1.8 fusion.33
  56.7 2.2 all-gather.4.cloned.1.call-done.w_ref
  64.2 21.7 %project.1 = (bf16[384,2048]{1,0:T(8,128)(2,1)}, bf16[384,2048]{1,0:T(8,128)(2,1)}, bf16[384,2048]{1,0:T(8,128)(2,1)}, bf16[384,2048]{1,0:T(8,128)(2,1)}, bf16[3...) custom-call(s32[1]{0:T(128)} %bitcast.6.core_ref, bf16[1024,768]{1,0:T(8,128)(2,1)} %bitcast.110, ...), custom_call_target="tpu_custom_call" | custom-call | tf_op jit(solution)/shard_map/project/pallas_call | solution.py:120
  87.8 84.0 %attend.1 = (bf16[384,2048]{1,0:T(8,128)(2,1)}, f32[6,8,2048]{2,1,0:T(8,128)}) custom-call(s32[5,4]{1,0:T(8,128)} %stack.2.bounds, bf16[384,2048]{1,0:T(8,128)(2,1)} %get-tuple-element.59.q, bf16[384,2048]{1,0:T(8,128)(2,1)} %get-tuple-element.60.k, bf16[384,2048]{1,0:T(8,128)(2,1)} %get-tuple-element.61.v, bf16[384,2048]{1,0:T(8,128)(2,1)} %get-tuple-element.62.kc, ...), custom_call_target="tpu_custom_call" | custom-call | tf_op jit(solution)/shard_map/attend/pallas_call | solution.py:203
  171.8 2.4 constant_dynamic-slice_fusion.6
  175.7 23.8 %all_gather.13 = bf16[768,384]{1,0:T(8,128)(2,1)S(1)} all-gather(bf16[96,384]{1,0:T(8,128)(2,1)S(1)} %constant_dynamic-slice_fusion.4), channel_id=1, replica_groups=mesh['seq'=4,'fsdp'=8] {'fsdp'}, dimensions={0}, use_global_device_ids=true | all-gather | bytes 663552 | tf_op jit(solution)/shard_map/all_gather | solution.py:549
  199.5 6.0 collective-permute-start.4
  207.9 4.8 fusion.50
  215.8 3.0 collective-permute-done.5
  218.7 13.4 %multiply_convert_fusion = (bf16[2048,1536]{1,0:T(8,128)(2,1)}, f32[2048,1536]{1,0:T(8,128)}) fusion(f32[1536]{0:T(1024)S(1)} %add.249, bf16[768,1536]{1,0:T(8,128)(2,1)} %all-gather.6.cloned.1.call-done, bf16[1024,768]{1,0:T(8,128)(2,1)} %collective-permute-done.5, bf16[1024,768]{1,0:T(8,128)(2,1)} %add_convert_fusion), kind=kOutput, calls=%fused_computation.10 | convolution fusion | flops 4869586944 | bytes 24385536 | tf_op jit(solution)/shard_map/dot_general | solution.py:48
  232.1 26.2 %all-gather.8.cloned.1.call-done = bf16[1536,768]{1,0:T(8,128)(2,1)} async-done(((bf16[192,768]{1,0:T(8,128)(2,1)}), bf16[1536,768]{1,0:T(8,128)(2,1)}) %all-gather.8.cloned.1.call-update) | async-done | bytes 2359312 | tf_op jit(solution)/shard_map/all_gather | solution.py:551
  258.3 7.8 %fusion.51 = f32[2048,768]{1,0:T(8,128)S(1)} fusion(bf16[2048,1536]{1,0:T(8,128)(2,1)} %get-tuple-element.129, bf16[1536,768]{1,0:T(8,128)(2,1)} %all-gather.8.cloned.1.call-done), kind=kOutput, calls=%fused_computation.168 | convolution fusion | flops 4831838208 | bytes 14942208 | tf_op jit(solution)/shard_map/dot_general | solution.py:48
  266.4 1.9 collective-permute-start.6
  268.2 19.0 %convert_reduce_fusion = (f32[1536]{0:T(1024)}, bf16[2048,1536]{1,0:T(8,128)(2,1)}) fusion(f32[2048,1536]{1,0:T(8,128)} %get-tuple-element.130, f32[1536]{0:T(1024)S(1)} %add.249, bf16[1536,768]{1,0:T(8,128)(2,1)} %all-gather.8.cloned.1.call-done, bf16[1024,768]{1,0:T(8,128)(2,1)} %collective-permute-done.7, bf16[1024,768]{1,0:T(8,128)(2,1)} %bitcast.20), kind=kOutput, calls=%fused_computation.9 | convolution fusion | flops 4910479872 | bytes 24391680 | tf_op jit(solution)/shard_map/dot_general | solution.py:44
  287.2 8.2 %fusion.52 = f32[2048,768]{1,0:T(8,128)S(1)} fusion(bf16[2048,1536]{1,0:T(8,128)(2,1)} %get-tuple-element.132, bf16[768,1536]{1,0:T(8,128)(2,1)S(1)} %copy-done.26), kind=kOutput, calls=%fused_computation.169 | convolution fusion | flops 4831838208 | bytes 14942208 | tf_op jit(solution)/shard_map/dot_general | solution.py:44
  295.7 8.3 %convolution_convert_fusion = bf16[768,1536]{1,0:T(8,128)(2,1)} fusion(bf16[2048,1536]{1,0:T(8,128)(2,1)S(1)} %copy-done.29, bf16[1024,768]{1,0:T(8,128)(2,1)} %collective-permute-done.5, bf16[1024,768]{1,0:T(8,128)(2,1)} %add_convert_fusion), kind=kOutput, calls=%fused_computation.29 | convolution fusion | flops 4839309312 | bytes 11796480 | tf_op jit(solution)/shard_map/dot_general | solution.py:40
  304.1 1.9 multiply_reduce_fusion
  306.0 4.8 convert_reduce_fusion.6
  313.5 3.6 convolution_convert_fusion.3
  318.5 8.5 %convolution_convert_fusion.1 = bf16[1536,768]{1,0:T(8,128)(2,1)} fusion(bf16[2048,1536]{1,0:T(8,128)(2,1)S(1)} %bitcast.135, bf16[1024,768]{1,0:T(8,128)(2,1)} %collective-permute-done.7, bf16[1024,768]{1,0:T(8,128)(2,1)} %bitcast.20), kind=kOutput, calls=%fused_computation.30 | convolution fusion | flops 4839309312 | bytes 11796480 | tf_op jit(solution)/shard_map/dot_general | solution.py:40
  328.2 1.8 pad_maximum_fusion.3
  333.7 96.0 %attend_back.1 = (bf16[1152,2048]{1,0:T(8,128)(2,1)}, bf16[768,2048]{1,0:T(8,128)(2,1)}) custom-call(s32[5,4]{1,0:T(8,128)} %stack.2.bounds, bf16[384,2048]{1,0:T(8,128)(2,1)} %get-tuple-element.59.q, bf16[384,2048]{1,0:T(8,128)(2,1)} %get-tuple-element.60.k, bf16[384,2048]{1,0:T(8,128)(2,1)} %get-tuple-element.61.v, ...), custom_call_target="tpu_custom_call" | custom-call | tf_op jit(solution)/shard_map/attend_back/pallas_call | solution.py:328
  429.7 6.5 %fusion.46 = f32[2048,768]{1,0:T(8,128)S(1)} fusion(bf16[1152,2048]{1,0:T(8,128)(2,1)} %get-tuple-element.68, bf16[768,1280]{1,0:T(8,128)(2,1)S(1)} %copy-done.6), kind=kOutput, calls=%fused_computation.163 | convolution fusion | flops 3623878656 | bytes 12779520 | tf_op jit(solution)/shard_map/dot_general | solution.py:649
  436.4 3.0 copy-done.8
  440.4 2.8 fusion.53
  443.2 2.6 copy-done.7
  446.1 1.9 pad_maximum_fusion.2
  448.4 2.0 fusion.22
  451.0 3.0 convert_reduce_fusion.1
  454.7 6.2 %fusion.55 = f32[768,768]{0,1:T(8,128)} fusion(bf16[768,2048]{1,0:T(8,128)(2,1)S(1)} %copy-done.9, bf16[2048,768]{1,0:T(8,128)(2,1)} %get-tuple-element.71), kind=kOutput, calls=%fused_computation.172 | convolution fusion | flops 2415919104 | bytes 8650752 | tf_op jit(solution)/shard_map/dot_general | solution.py:665
  460.8 2.4 convert_element_type.149
  463.3 2.6 copy-done.4
  467.3 2.5 collective-permute-start.12
  470.9 6.9 %fusion.54 = f32[768,1152]{0,1:T(8,128)S(1)} fusion(bf16[1152,2048]{1,0:T(8,128)(2,1)} %get-tuple-element.68, bf16[2048,768]{1,0:T(8,128)(2,1)} %get-tuple-element.70), kind=kOutput, calls=%fused_computation.171 | convolution fusion | flops 3623878656 | bytes 11403264 | tf_op jit(solution)/shard_map/dot_general | solution.py:665
  478.5 3.5 reshape.535
  482.0 4.3 copy.72.g
  486.3 16.7 %collective-permute-done.12 = bf16[1024,768]{1,0:T(8,128)(2,1)} collective-permute-done((bf16[1024,768]{1,0:T(8,128)(2,1)}, bf16[1024,768]{1,0:T(8,128)(2,1)}, u32[]{:S(2)}, u32[]{:S(2)}) %collective-permute-start.12) | collective-permute-done | bytes 1572896 | tf_op jit(solution)/shard_map/ppermute | solution.py:662
  503.0 6.6 %fusion.20 = (f32[768]{0:T(1024)S(1)}, f32[1024]{0:T(1024)S(1)}, f32[1024]{0:T(1024)S(1)}, f32[768]{0:T(1024)S(1)}, f32[1024,768]{1,0:T(8,128)}) fusion(bf16[1024,768]{1,0:T(8,128)(2,1)} %get-tuple-element.102.cmine, bf16[1024,768]{1,0:T(8,128)(2,1)} %fusion.25, f32[1024]{0:T(1024)S(1)} %add_rsqrt_fusion, f32[1024]{0:T(1024)S(1)} %broadcast_multiply_fusion, ...), kind=kLoop, calls=%fused_computation.37 | loop fusion | flops 15725056 | bytes 15762436 | tf_op jit(solution)/shard_map/reduce_sum | solution.py:679
  510.5 5.0 fusion.18
  518.7 3.7 reduce-scatter.5.cloned.1.call-done.dn
  522.4 56.1 %finish.1 = (bf16[2,96,1152]{2,1,0:T(8,128)(2,1)}, f32[10,128]{1,0:T(8,128)}, bf16[2,96,1536]{2,1,0:T(8,128)(2,1)}, bf16[2,192,768]{2,1,0:T(8,128)(2,1)}, bf16[2,96,384]{2,1,0:T(8,128)(2,1)}) custom-call(bf16[8,96,1152]{2,1,0:T(8,128)(2,1)} %copy.72.g, f32[8,10,128]{2,1,0:T(8,128)} %copy.73.s, bf16[96,1536]{1,0:T(8,128)(2,1)} %slice.226.up, ...), custom_call_target="tpu_custom_call" | custom-call | tf_op jit(solution)/shard_map/finish/pallas_call | solution.py:442
  584.7 2.2 bitcast_convert_fusion
  587.4 2.4 copy.74
  589.8 3.5 reshape.550
  (203 shorter events, 52.9 us)
Async XLA Ops:
  7.2 198.3 %copy-start = (bf16[384,768]{1,0:T(8,128)(2,1)S(1)}, bf16[384,768]{1,0:T(8,128)(2,1)}, u32[]{:S(2)}) copy-start(bf16[384,768]{1,0:T(8,128)(2,1)} %param.31) | copy-start | bytes 1769476
  7.2 14.4 %copy-start.2 = (bf16[1,1024,768]{2,1,0:T(8,128)(2,1)S(1)}, bf16[1,1024,768]{2,1,0:T(8,128)(2,1)}, u32[]{:S(2)}) copy-start(bf16[1,1024,768]{2,1,0:T(8,128)(2,1)} %param.19) | copy-start | bytes 4718596
  7.2 13.2 %copy-start.18 = (s32[1,2048]{1,0:T(1,128)S(1)}, s32[1,2048]{1,0:T(1,128)}, u32[]{:S(2)}) copy-start(s32[1,2048]{1,0:T(1,128)} %param.20) | copy-start | bytes 24580
  7.2 51.6 %all-gather.4.cloned.1.call-start = ((), (), s32[]{:S(2)}) async-start(), calls=%async_computation.2 | async-start | bytes 2211840 | tf_op jit(solution)/shard_map/all_gather | solution.py:531
  11.7 204.1 %all-gather.6.cloned.1.call-start = ((), (), s32[]{:S(2)}) async-start(), calls=%async_computation.3 | async-start | bytes 2654208 | tf_op jit(solution)/shard_map/all_gather | solution.py:550
  11.7 37.5 %collective-permute-start.1 = (bf16[1024,768]{1,0:T(8,128)(2,1)}, bf16[1024,768]{1,0:T(8,128)(2,1)}, u32[]{:S(2)}, u32[]{:S(2)}) collective-permute-start(bf16[1024,768]{1,0:T(8,128)(2,1)} %bitcast.108), channel_id=1, source_target_pairs={{16,0},{24,8},{17,1},{25,9},{18,2},{26,10},{19,3},{27,11},{20,4},{... | collective-permute-start | bytes 4718600 | tf_op jit(solution)/shard_map/ppermute | solution.py:511
  13.0 50.0 %collective-permute-start = (bf16[1024,768]{1,0:T(8,128)(2,1)}, bf16[1024,768]{1,0:T(8,128)(2,1)}, u32[]{:S(2)}, u32[]{:S(2)}) collective-permute-start(bf16[1024,768]{1,0:T(8,128)(2,1)} %bitcast.109), channel_id=1, source_target_pairs={{0,8},{8,0},{16,24},{24,16},{1,9},{9,1},{17,25},{25,17},{2,10},{10... | collective-permute-start | bytes 4718600 | tf_op jit(solution)/shard_map/ppermute | solution.py:510
  20.2 238.2 %all-gather.8.cloned.1.call-start = ((), (), s32[]{:S(2)}) async-start(), calls=%async_computation.4 | async-start | bytes 2654208 | tf_op jit(solution)/shard_map/all_gather | solution.py:551
  21.6 33.2 %copy-start.21 = (bf16[96,768]{1,0:T(8,128)(2,1)S(1)}, bf16[96,768]{1,0:T(8,128)(2,1)}, u32[]{:S(2)}) copy-start(bf16[96,768]{1,0:T(8,128)(2,1)} %param.25) | copy-start | bytes 442372
  21.9 34.8 %copy-start.19 = (f32[1024]{0:T(1024)}, f32[1024]{0:T(1024)S(1)}, u32[]{:S(2)}) copy-start(f32[1024]{0:T(1024)S(1)} %broadcast_multiply_fusion.3) | copy-start | bytes 12292
  53.3 9.7 %collective-permute-start.2 = (bf16[1024,768]{1,0:T(8,128)(2,1)}, bf16[1024,768]{1,0:T(8,128)(2,1)S(1)}, u32[]{:S(2)}, u32[]{:S(2)}) collective-permute-start(bf16[1024,768]{1,0:T(8,128)(2,1)} %get-tuple-element.102.cmine), channel_id=1, source_target_pairs={{0,8},{8,0},{16,24},{24,16},{1,9},{9,1},{17,25},{25,17},{2,10},{10... | collective-permute-start | bytes 4718600 | tf_op jit(solution)/shard_map/ppermute | solution.py:513
  174.2 32.9 %collective-permute-start.3 = (bf16[384,1024]{1,0:T(8,128)(2,1)S(1)}, bf16[384,1024]{1,0:T(8,128)(2,1)}, u32[]{:S(2)}, u32[]{:S(2)}) collective-permute-start(bf16[384,1024]{1,0:T(8,128)(2,1)S(1)} %get-tuple-element.109), channel_id=1, source_target_pairs={{0,8},{8,0},{16,24},{24,16},{1,9},{9,1},{17,25},{25,17},{2,10},{10... | collective-permute-start | bytes 2359304 | tf_op jit(solution)/shard_map/ppermute | solution.py:593
  199.5 7.6 %copy-start.15 = (bf16[768,384]{1,0:T(8,128)(2,1)}, bf16[768,384]{1,0:T(8,128)(2,1)S(1)}, u32[]{:S(2)}) copy-start(bf16[768,384]{1,0:T(8,128)(2,1)S(1)} %all_gather.13) | copy-start | bytes 1769476
  199.5 7.6 %collective-permute-start.4 = (bf16[768,384]{1,0:T(8,128)(2,1)S(1)}, bf16[768,384]{1,0:T(8,128)(2,1)S(1)}, u32[]{:S(2)}, u32[]{:S(2)}) collective-permute-start(bf16[768,384]{1,0:T(8,128)(2,1)S(1)} %all_gather.13), channel_id=1, source_target_pairs={{0,8},{8,0},{16,24},{24,16},{1,9},{9,1},{17,25},{25,17},{2,10},{10... | collective-permute-start | bytes 1769480 | tf_op jit(solution)/shard_map/ppermute | solution.py:552
  206.2 309.3 %reduce-scatter.3.cloned.1.call-start = ((), (), s32[]{:S(2)}) async-start(), calls=%async_computation.5 | async-start | bytes 3317760 | tf_op jit(solution)/shard_map/reduce_scatter | solution.py:639
  215.0 3.8 collective-permute-start.5
  215.3 52.9 %collective-permute-start.7 = (bf16[1024,768]{1,0:T(8,128)(2,1)}, bf16[1024,768]{1,0:T(8,128)(2,1)}, u32[]{:S(2)}, u32[]{:S(2)}) collective-permute-start(bf16[1024,768]{1,0:T(8,128)(2,1)} %bitcast.20), channel_id=1, source_target_pairs={{0,8},{8,0},{16,24},{24,16},{1,9},{9,1},{17,25},{25,17},{2,10},{10... | collective-permute-start | bytes 4718600 | tf_op jit(solution)/shard_map/ppermute | solution.py:557
  266.4 39.6 %collective-permute-start.6 = (bf16[1024,768]{1,0:T(8,128)(2,1)S(1)}, bf16[1024,768]{1,0:T(8,128)(2,1)S(1)}, u32[]{:S(2)}, u32[]{:S(2)}) collective-permute-start(bf16[1024,768]{1,0:T(8,128)(2,1)S(1)} %slice.281), channel_id=1, source_target_pairs={{0,8},{8,0},{16,24},{24,16},{1,9},{9,1},{17,25},{25,17},{2,10},{10... | collective-permute-start | bytes 4718600 | tf_op jit(solution)/shard_map/ppermute | solution.py:603
  268.2 19.0 %copy-start.26 = (bf16[768,1536]{1,0:T(8,128)(2,1)S(1)}, bf16[768,1536]{1,0:T(8,128)(2,1)}, u32[]{:S(2)}) copy-start(bf16[768,1536]{1,0:T(8,128)(2,1)} %all-gather.6.cloned.1.call-done) | copy-start | bytes 7077892
  287.2 8.5 %copy-start.29 = (bf16[2048,1536]{1,0:T(8,128)(2,1)S(1)}, bf16[2048,1536]{1,0:T(8,128)(2,1)}, u32[]{:S(2)}) copy-start(bf16[2048,1536]{1,0:T(8,128)(2,1)} %get-tuple-element.132) | copy-start | bytes 18874372
  295.6 8.4 %collective-permute-start.8 = (bf16[1024,768]{1,0:T(8,128)(2,1)S(1)}, bf16[1024,768]{1,0:T(8,128)(2,1)S(1)}, u32[]{:S(2)}, u32[]{:S(2)}) collective-permute-start(bf16[1024,768]{1,0:T(8,128)(2,1)S(1)} %slice.280), channel_id=1, source_target_pairs={{0,8},{8,0},{16,24},{24,16},{1,9},{9,1},{17,25},{25,17},{2,10},{10... | collective-permute-start | bytes 4718600 | tf_op jit(solution)/shard_map/ppermute | solution.py:603
  305.9 4.8 copy-start.16
  306.0 4.8 copy-start.28
  310.7 6.4 %copy-start.5 = (f32[1024,768]{1,0:T(8,128)}, f32[1024,768]{1,0:T(8,128)S(1)}, u32[]{:S(2)}) copy-start(f32[1024,768]{1,0:T(8,128)S(1)} %get-tuple-element.99) | copy-start | bytes 9437188
  312.2 6.3 %slice-start.3 = ((s8[6291456]{0:T(1024)(128)(4,1)}), s8[4194304]{0:T(1024)(128)(4,1)S(1)}, s32[]{:S(2)}) async-start(s8[6291456]{0:T(1024)(128)(4,1)} %bitcast.134), calls=%async_computation.10 | async-start | bytes 8388608
  313.5 5.0 slice-start.4
  318.0 9.0 %collective-permute-start.10 = (bf16[768,384]{1,0:T(8,128)(2,1)}, bf16[768,384]{1,0:T(8,128)(2,1)}, u32[]{:S(2)}, u32[]{:S(2)}) collective-permute-start(bf16[768,384]{1,0:T(8,128)(2,1)} %constant_dynamic-slice_fusion), channel_id=1, source_target_pairs={{0,8},{8,0},{16,24},{24,16},{1,9},{9,1},{17,25},{25,17},{2,10},{10... | collective-permute-start | bytes 1769480 | tf_op jit(solution)/shard_map/ppermute | solution.py:634
  318.4 9.8 %collective-permute-start.9 = (bf16[384,1024]{1,0:T(8,128)(2,1)}, bf16[384,1024]{1,0:T(8,128)(2,1)}, u32[]{:S(2)}, u32[]{:S(2)}) collective-permute-start(bf16[384,1024]{1,0:T(8,128)(2,1)} %get-tuple-element.106), channel_id=1, source_target_pairs={{0,8},{8,0},{16,24},{24,16},{1,9},{9,1},{17,25},{25,17},{2,10},{10... | collective-permute-start | bytes 2359304 | tf_op jit(solution)/shard_map/ppermute | solution.py:631
  318.5 9.7 %copy-start.11 = (bf16[768,1536]{1,0:T(8,128)(2,1)S(1)}, bf16[768,1536]{1,0:T(8,128)(2,1)}, u32[]{:S(2)}) copy-start(bf16[768,1536]{1,0:T(8,128)(2,1)} %convolution_convert_fusion) | copy-start | bytes 7077892
  330.1 192.4 %reduce-scatter.5.cloned.1.call-start = ((), (), s32[]{:S(2)}) async-start(), calls=%async_computation.6 | async-start | bytes 2654208 | tf_op jit(solution)/shard_map/reduce_scatter | solution.py:639
  333.7 96.0 %copy-start.6 = (bf16[768,1280]{1,0:T(8,128)(2,1)S(1)}, bf16[768,1280]{1,0:T(8,128)(2,1)}, u32[]{:S(2)}) copy-start(bf16[768,1280]{1,0:T(8,128)(2,1)} %all-gather.4.cloned.1.call-done.w_ref) | copy-start | bytes 5898244
  429.7 9.7 %copy-start.13 = (bf16[768,6,128]{0,2,1:T(8,128)(2,1)S(1)}, bf16[768,6,128]{0,2,1:T(8,128)(2,1)}, u32[]{:S(2)}) copy-start(bf16[768,6,128]{0,2,1:T(8,128)(2,1)} %slice.221) | copy-start | bytes 3538948
  436.3 3.2 copy-start.8
  436.3 4.2 copy-start.9
  443.2 2.7 copy-start.7
  446.0 2.4 copy-start.24
  446.0 4.4 copy-start.22
  446.0 4.5 copy-start.25
  447.9 12.9 %collective-permute-start.11 = (bf16[2048,768]{1,0:T(8,128)(2,1)}, bf16[2048,768]{1,0:T(8,128)(2,1)}, u32[]{:S(2)}, u32[]{:S(2)}) collective-permute-start(bf16[2048,768]{1,0:T(8,128)(2,1)} %pad_maximum_fusion.2), channel_id=1, source_target_pairs={{0,8},{8,0},{16,24},{24,16},{1,9},{9,1},{17,25},{25,17},{2,10},{10... | collective-permute-start | bytes 9437192 | tf_op jit(solution)/shard_map/ppermute | solution.py:660
  454.2 11.7 %slice-start.1 = ((s8[6291456]{0:T(1024)(128)(4,1)}), s8[4194304]{0:T(1024)(128)(4,1)S(1)}, s32[]{:S(2)}) async-start(s8[6291456]{0:T(1024)(128)(4,1)} %bitcast.114), calls=%async_computation.8 | async-start | bytes 8388608
  454.7 11.2 %slice-start.2 = ((s8[6291456]{0:T(1024)(128)(4,1)}), s8[2097152]{0:T(1024)(128)(4,1)S(1)}, s32[]{:S(2)}) async-start(s8[6291456]{0:T(1024)(128)(4,1)} %bitcast.114), calls=%async_computation.9 | async-start | bytes 4194304
  463.3 2.6 copy-start.4
  467.3 35.6 %collective-permute-start.12 = (bf16[1024,768]{1,0:T(8,128)(2,1)}, bf16[1024,768]{1,0:T(8,128)(2,1)}, u32[]{:S(2)}, u32[]{:S(2)}) collective-permute-start(bf16[1024,768]{1,0:T(8,128)(2,1)} %fusion.25), channel_id=1, source_target_pairs={{0,16},{8,24},{1,17},{9,25},{2,18},{10,26},{3,19},{11,27},{4,20},{... | collective-permute-start | bytes 4718600 | tf_op jit(solution)/shard_map/ppermute | solution.py:662
  470.9 6.9 %copy-start.10 = (f32[768,768]{0,1:T(8,128)S(1)}, f32[768,768]{0,1:T(8,128)}, u32[]{:S(2)}) copy-start(f32[768,768]{0,1:T(8,128)} %fusion.55) | copy-start | bytes 7077892
  478.5 24.4 %copy-start.3 = (bf16[1,1024,768]{2,1,0:T(8,128)(2,1)S(1)}, bf16[1,1024,768]{2,1,0:T(8,128)(2,1)}, u32[]{:S(2)}) copy-start(bf16[1,1024,768]{2,1,0:T(8,128)(2,1)} %param.19) | copy-start | bytes 4718596
  478.5 24.4 %copy-start.20 = (f32[1024]{0:T(1024)S(1)}, f32[1024]{0:T(1024)}, u32[]{:S(2)}) copy-start(f32[1024]{0:T(1024)} %copy-done.19) | copy-start | bytes 12292
  578.5 8.3 %copy-start.17 = (bf16[2,96,1536]{2,1,0:T(8,128)(2,1)S(1)}, bf16[2,96,1536]{2,1,0:T(8,128)(2,1)}, u32[]{:S(2)}) copy-start(bf16[2,96,1536]{2,1,0:T(8,128)(2,1)} %get-tuple-element.78) | copy-start | bytes 1769476
  587.4 7.6 %copy-start.1 = (bf16[384,768]{1,0:T(8,128)(2,1)S(1)}, bf16[384,768]{1,0:T(8,128)(2,1)}, u32[]{:S(2)}) copy-start(bf16[384,768]{1,0:T(8,128)(2,1)} %param.31) | copy-start | bytes 1769476
  (5 other events, 7.1 us)
Sparse Core Ops, SparseCore 0:
  11.8 47.0 all-gather.3
  61.6 50.3 all-gather.5
  206.4 51.9 all-gather.7
  330.2 71.2 reduce-scatter.2
  454.3 68.1 reduce-scatter.4

commit v3 on v2

--- a/solution.py
+++ b/solution.py
@@ -1,4 +1,5 @@
 import functools
+import math
 
 import jax
 import jax.numpy as jnp
@@ -49,7 +50,7 @@
 
 
 def qkv_kernel(heads, core_ref, mine, other, cmine, cother, w_ref, vec_ref, bias_ref, cos_ref,
-               sin_ref, q_out, k_out, v_out, kc_out, vc_out, a_out, ac_out, wt):
+               sin_ref, q_out, k_out, v_out, kc_out, vc_out, a_out, wt):
     step = pl.program_id(0)
     span = heads * HD
 
@@ -90,7 +91,6 @@
     @pl.when(step >= 2 * quarter)
     def _():
         a = normed(jnp.where(step < 3 * quarter, cmine[...], cother[...]))
-        ac_out[...] = a
         lin = right_transposed(wt[span:, :], a) + bias_ref[span:, :]
         turn(lin, 0, kc_out)
         vc_out[...] = lin[span:, :].astype(BF)
@@ -112,8 +112,7 @@
     whole = lambda shape: pl.BlockSpec(shape, lambda t, c: (0, 0))
     own = pl.BlockSpec((span, tile), lambda t, c: (0, place(jnp.minimum(t, 2 * n - 1), c)))
     cln = pl.BlockSpec((span, tile), lambda t, c: (0, place(jnp.maximum(t, 2 * n), c)))
-    own_a = pl.BlockSpec((tile, width), lambda t, c: (place(jnp.minimum(t, 2 * n - 1), c), 0))
-    cln_a = pl.BlockSpec((tile, width), lambda t, c: (place(jnp.maximum(t, 2 * n), c), 0))
+    own_a = pl.BlockSpec((tile, width), lambda t, c: (jnp.minimum(t, 2 * n - 1), 0))
     tab = pl.BlockSpec((HD // 2, tile), lambda t, c: (0, place(t, c)))
     head_shape = jax.ShapeDtypeStruct((span, 2 * local), BF)
     row_shape = jax.ShapeDtypeStruct((2 * local, width), BF)
@@ -124,10 +123,10 @@
             grid=(4 * n,),
             in_specs=[src(0), src(1), src(2), src(3), whole((width, 3 * span)), whole(vec.shape),
                       whole(bias.shape), tab, tab],
-            out_specs=[own, own, own, cln, cln, own_a, cln_a],
+            out_specs=[own, own, own, cln, cln, own_a],
             scratch_shapes=[pltpu.VMEM((3 * span, width), BF)],
         ),
-        out_shape=[head_shape] * 5 + [row_shape] * 2,
+        out_shape=[head_shape] * 5 + [row_shape],
         name="project",
     )(core, mine, other, cmine, cother, weight, vec, bias, cos_t, sin_t)
 
@@ -147,53 +146,88 @@
         vcs[h, HD:] = ones
     lift = bounds[4, 0]
 
-    def one_tile(i, _):
+    lead = jnp.ones((8, HD), BF)
+    top = lambda ref, rows: jnp.max(dot(lead, ref[rows, :] * ref[rows, :]))
+    limit = jnp.float32(0.9 * (96.0 / scale) ** 2)
+    small = None
+    for h in range(group):
+        rows = slice(h * HD, (h + 1) * HD)
+        fits = top(q, rows) * jnp.maximum(top(k, rows), top(kc, rows)) < limit
+        small = fits if small is None else jnp.logical_and(small, fits)
+
+    def key_ids(keys):
+        col = id_col[keys, :]
+        return jnp.concatenate([col] * (TQ // 128), 1)
+
+    def sweep(i, q_ids, update, state):
+        def band(j, state):
+            keys = pl.ds(pl.multiple_of(j * TM, TM), TM)
+            return update(state, ks, vs, keys, key_ids(keys) == q_ids)
+
+        def full(j, state):
+            keys = pl.ds(pl.multiple_of(j * TK, TK), TK)
+            return update(state, kcs, vcs, keys, None)
+
+        def edge(j, state):
+            keys = pl.ds(pl.multiple_of(j * TM, TM), TM)
+            return update(state, kcs, vcs, keys, key_ids(keys) < q_ids + lift)
+
+        state = lax.fori_loop(bounds[2, i], bounds[3, i], band, state)
+        state = lax.fori_loop(0, bounds[0, i], full, state)
+        return lax.fori_loop(bounds[0, i] * (TK // TM), bounds[1, i], edge, state)
+
+    def store(h, at, acc, log_shift):
+        total_w = acc[HD : HD + 1, :]
+        o_out[h * HD : (h + 1) * HD, at] = (acc[:HD, :] / total_w).astype(BF)
+        lse_out[h, :, at] = jnp.broadcast_to(log_shift + jnp.log2(total_w), (8, TQ))
+
+    def plain_tile(i, _):
         at = pl.ds(pl.multiple_of(i * TQ, TQ), TQ)
         queries = [q[h * HD : (h + 1) * HD, at] for h in range(group)]
-        q_ids = id_row[0:1, at]
 
         def update(state, key_ref, val_ref, keys, mask):
             out = []
             for h in range(group):
-                m, acc = state[2 * h], state[2 * h + 1]
-                s = dot(key_ref[h, keys, :], queries[h])
+                p = jnp.exp2(dot(key_ref[h, keys, :], queries[h]) * scale)
+                if mask is not None:
+                    p = jnp.where(mask, p, 0.0)
+                out.append(state[h] + dot(val_ref[h, :, keys], p.astype(BF)))
+            return tuple(out)
+
+        state = (jnp.zeros((HD + 16, TQ), F32),) * group
+        state = sweep(i, id_row[0:1, at], update, state)
+        for h in range(group):
+            store(h, at, state[h], 0.0)
+        return 0
+
+    def shifted_tile(i, _):
+        at = pl.ds(pl.multiple_of(i * TQ, TQ), TQ)
+        q_ids = id_row[0:1, at]
+        for h in range(group):
+            query = q[h * HD : (h + 1) * HD, at]
+
+            def update(state, key_ref, val_ref, keys, mask):
+                m, acc = state
+                s = dot(key_ref[h, keys, :], query)
                 if mask is not None:
                     s = jnp.where(mask, s, NEG)
                 m_new = jnp.maximum(m, jnp.max(s, 0, keepdims=True))
                 p = jnp.exp2((s - m_new) * scale).astype(BF)
                 alpha = jnp.exp2((m - m_new) * scale)
-                acc = acc * alpha + dot(val_ref[h, :, keys], p)
-                out += [m_new, acc]
-            return tuple(out)
-
-        def key_ids(keys):
-            col = id_col[keys, :]
-            return jnp.concatenate([col] * (TQ // 128), 1)
-
-        def band(j, state):
-            keys = pl.ds(pl.multiple_of(j * TM, TM), TM)
-            return update(state, ks, vs, keys, key_ids(keys) == q_ids)
-
-        def full(j, state):
-            keys = pl.ds(pl.multiple_of(j * TK, TK), TK)
-            return update(state, kcs, vcs, keys, None)
-
-        def edge(j, state):
-            keys = pl.ds(pl.multiple_of(j * TM, TM), TM)
-            return update(state, kcs, vcs, keys, key_ids(keys) < q_ids + lift)
-
-        state = (jnp.full((1, TQ), NEG, F32), jnp.zeros((HD + 16, TQ), F32)) * group
-        state = lax.fori_loop(bounds[2, i], bounds[3, i], band, state)
-        state = lax.fori_loop(0, bounds[0, i], full, state)
-        state = lax.fori_loop(bounds[0, i] * (TK // TM), bounds[1, i], edge, state)
-        for h in range(group):
-            m, acc = state[2 * h], state[2 * h + 1]
-            total_w = acc[HD : HD + 1, :]
-            o_out[h * HD : (h + 1) * HD, at] = (acc[:HD, :] / total_w).astype(BF)
-            lse_out[h, :, at] = jnp.broadcast_to(m * scale + jnp.log2(total_w), (8, TQ))
+                return m_new, acc * alpha + dot(val_ref[h, :, keys], p)
+
+            state = (jnp.full((1, TQ), NEG, F32), jnp.zeros((HD + 16, TQ), F32))
+            m, acc = sweep(i, q_ids, update, state)
+            store(h, at, acc, m * scale)
         return 0
 
-    lax.fori_loop(0, total // TQ, one_tile, 0)
+    @pl.when(small)
+    def _():
+        lax.fori_loop(0, total // TQ, plain_tile, 0)
+
+    @pl.when(jnp.logical_not(small))
+    def _():
+        lax.fori_loop(0, total // TQ, shifted_tile, 0)
 
 
 def attend(bounds, q, k, v, kc, vc, id_row, id_col, heads, group):
@@ -214,6 +248,9 @@
             jax.ShapeDtypeStruct((heads * HD, total), BF),
             jax.ShapeDtypeStruct((heads, 8, total), F32),
         ],
+        cost_estimate=pl.CostEstimate(
+            flops=16 * heads * HD * total * total, bytes_accessed=2**24, transcendentals=0
+        ),
         name="attend",
     )(bounds, q, k, v, kc, vc, id_row, id_col)
 
@@ -300,59 +337,59 @@
     cos_t, sin_t = cos_ref[...], sin_ref[...]
     noisy = lift == 0
 
-    def back_turn(w, out, base):
+    def spread(out, value, base):
+        rows = slice(base, base + value.shape[0])
+        out[rows, near] = value[:, :half_rows].astype(BF)
+        out[rows, far] = value[:, half_rows:].astype(BF)
+
+    def back_turn(out, w, base):
         first, second = w[:half, :], w[half:, :]
-        out[base : base + half, :] = (first * cos_t + second * sin_t).astype(BF)
-        out[base + half : base + HD, :] = (second * cos_t - first * sin_t).astype(BF)
+        spread(out, first * cos_t + second * sin_t, base)
+        spread(out, second * cos_t - first * sin_t, base + half)
 
     for h in range(group):
-        back_turn(dq_acc[h * HD : (h + 1) * HD, :] * HD**-0.5, own_out, 3 * h * HD)
+        back_turn(own_out, dq_acc[h * HD : (h + 1) * HD, :] * HD**-0.5, 3 * h * HD)
         band_k = jnp.where(noisy, dk_acc[h], dkc_acc[h])
         band_v = jnp.where(noisy, dv_acc[h], dvc_acc[h])
-        back_turn(jnp.transpose(band_k) * HD**-0.5, own_out, (3 * h + 1) * HD)
-        own_out[(3 * h + 2) * HD : (3 * h + 3) * HD, :] = jnp.transpose(band_v).astype(BF)
-        part_k = jnp.where(noisy, dkc_acc[h], 0.0)
-        part_v = jnp.where(noisy, dvc_acc[h], 0.0)
-        back_turn(jnp.transpose(part_k) * HD**-0.5, cln_out, 2 * h * HD)
-        cln_out[(2 * h + 1) * HD : (2 * h + 2) * HD, :] = jnp.transpose(part_v).astype(BF)
+        back_turn(own_out, jnp.transpose(band_k) * HD**-0.5, (3 * h + 1) * HD)
+        spread(own_out, jnp.transpose(band_v), (3 * h + 2) * HD)
+        back_turn(cln_out, jnp.transpose(dkc_acc[h]) * HD**-0.5, 2 * h * HD)
+        spread(cln_out, jnp.transpose(dvc_acc[h]), (2 * h + 1) * HD)
 
 
 def attend_back(bounds, q, k, v, kc, vc, o, lse, do_mine, do_other, id_row, id_col, cos_t, sin_t,
-                heads, group):
+                pair, group):
     total = q.shape[1]
-    head = pl.BlockSpec((group * HD, total), lambda g, b: (g, 0))
-    halfhead = pl.BlockSpec((group * HD, total // 2), lambda g, b: (g, 0))
+    head = pl.BlockSpec((group * HD, total), lambda g, b: (pair, 0))
+    halfhead = pl.BlockSpec((group * HD, total // 2), lambda g, b: (pair, 0))
     whole = lambda shape: pl.BlockSpec(shape, lambda g, b: (0, 0))
     rows16 = pltpu.VMEM((group, total, HD), BF)
     rows32 = pltpu.VMEM((group, total, HD), F32)
+    outs = [(group * 3 * HD, total), (group * 2 * HD, total)]
     return pl.pallas_call(
         functools.partial(attend_back_kernel, group),
         grid_spec=pltpu.PrefetchScalarGridSpec(
             num_scalar_prefetch=1,
-            grid=(heads // group,),
+            grid=(1,),
             in_specs=[head] * 6
-            + [pl.BlockSpec((group, 8, total), lambda g, b: (g, 0, 0)), halfhead, halfhead]
+            + [pl.BlockSpec((group, 8, total), lambda g, b: (pair, 0, 0)), halfhead, halfhead]
             + [whole(id_row.shape), whole(id_col.shape), whole(cos_t.shape), whole(sin_t.shape)],
-            out_specs=[
-                pl.BlockSpec((group * 3 * HD, total), lambda g, b: (g, 0)),
-                pl.BlockSpec((group * 2 * HD, total), lambda g, b: (g, 0)),
-            ],
+            out_specs=[whole(shape) for shape in outs],
             scratch_shapes=[rows16] * 6
             + [pltpu.VMEM((group * HD, total), BF)]
             + [rows32] * 4
             + [pltpu.VMEM((group * HD, total), F32)],
         ),
-        out_shape=[
-            jax.ShapeDtypeStruct((heads * 3 * HD, total), BF),
-            jax.ShapeDtypeStruct((heads * 2 * HD, total), BF),
-        ],
+        out_shape=[jax.ShapeDtypeStruct(shape, BF) for shape in outs],
+        cost_estimate=pl.CostEstimate(
+            flops=20 * group * HD * total * total, bytes_accessed=8 * 2**20, transcendentals=0
+        ),
         name="attend_back",
     )(bounds, q, k, v, kc, vc, o, lse, do_mine, do_other, id_row, id_col, cos_t, sin_t)
 
 
-def finish_kernel(n, g, s, up, dn, ou, g_out, s_out, up_out, dn_out, ou_out, g_in, s_in, g_x,
-                  s_x, up_x, dn_x, ou_x, g_t, s_t, s_c, up_t, dn_t, ou_t, send, recv, s_send,
-                  s_recv, x_send, x_recv, c_send, c_recv, local):
+def finish_kernel(n, g, w, s, g_out, s_out, w_in, s_in, g_x, w_x, s_x, g_c, s_c, g_t, w_t, s_t,
+                  w_send, w_recv, s_send, s_recv, x_send, x_recv, c_send, c_recv, local):
     me = lax.axis_index("fsdp")
     seat = lax.axis_index("seq")
     core = lax.rem(seat, 2)
@@ -378,105 +415,97 @@
         copy.start()
         copy.wait()
 
-    first = []
+    first_s, first_w = [], []
     for d in range(1, n):
         to = lax.rem(me + d, n)
-        first.append(push(g.at[to], g_in.at[d - 1], send.at[d - 1], recv.at[d - 1], peers[d - 1]))
-        first.append(
+        first_s.append(
             push(s.at[to], s_in.at[d - 1], s_send.at[d - 1], s_recv.at[d - 1], peers[d - 1])
         )
-    shards = [(up, up_x, up_t, up_out), (dn, dn_x, dn_t, dn_out), (ou, ou_x, ou_t, ou_out)]
-    over = [
-        push(src, land, x_send.at[i], x_recv.at[i], across)
-        for i, (src, land, _, _) in enumerate(shards)
-    ]
-    near = []
-    for i, (src, land, tmp, out) in enumerate(shards):
-        over[i].wait()
-        tmp[...] = (src[...].astype(F32) + land[...].astype(F32)).astype(BF)
-        settle(tmp, out.at[core], local.at[i])
-        near.append(push(out.at[core], out.at[core], c_send.at[i], c_recv.at[i], beside))
-    for copy in first:
+        first_w.append(
+            push(w.at[to], w_in.at[d - 1], w_send.at[d - 1], w_recv.at[d - 1], peers[d - 1])
+        )
+    far_g = push(g, g_x, x_send.at[0], x_recv.at[0], across)
+    for copy in first_s:
         copy.wait()
-
-    rows = g.shape[1]
-    block = 16 if rows % 16 == 0 else rows
-
-    def add_rows(i, _):
-        at = pl.ds(pl.multiple_of(i * block, block), block)
-        total = g[me, at, :].astype(F32)
-        for d in range(n - 1):
-            total = total + g_in[d, at, :].astype(F32)
-        g_t[at, :] = total.astype(BF)
-        return 0
-
-    lax.fori_loop(0, rows // block, add_rows, 0)
     total = s[me]
     for d in range(n - 1):
         total = total + s_in[d]
     s_t[0] = total
-    settle(g_t, g_x.at[0], local.at[3])
-    settle(s_t.at[0], s_x.at[0], local.at[4])
-    far_g = push(g_x.at[0], g_x.at[1], x_send.at[3], x_recv.at[3], across)
-    far_s = push(s_x.at[0], s_x.at[1], x_send.at[4], x_recv.at[4], across)
+    settle(s_t.at[0], s_x.at[0], local.at[0])
+    far_s = push(s_x.at[0], s_x.at[1], x_send.at[1], x_recv.at[1], across)
+    split = g.shape[1]
+    span = split + w.shape[2]
+    far_g.wait()
+    g_t[:, :split] = (g[...].astype(F32) + g_x[...].astype(F32)).astype(BF)
     far_s.wait()
     s_t[1] = s_x[0] + s_x[1]
-    settle(s_t.at[1], s_c.at[0], local.at[5])
-    near_s = push(s_c.at[0], s_c.at[1], c_send.at[4], c_recv.at[4], beside)
-    far_g.wait()
-    g_t[...] = (g_x[0].astype(F32) + g_x[1].astype(F32)).astype(BF)
-    settle(g_t, g_out.at[core], local.at[6])
-    near.append(push(g_out.at[core], g_out.at[core], c_send.at[3], c_recv.at[3], beside))
+    settle(s_t.at[1], s_c.at[0], local.at[1])
+    near_s = push(s_c.at[0], s_c.at[1], c_send.at[1], c_recv.at[1], beside)
+    for copy in first_w:
+        copy.wait()
+    rows = w.shape[1]
+    block = 16 if rows % 16 == 0 else rows
+
+    def add_rows(i, _):
+        at = pl.ds(pl.multiple_of(i * block, block), block)
+        total = w[me, at, :].astype(F32)
+        for d in range(n - 1):
+            total = total + w_in[d, at, :].astype(F32)
+        w_t[at, :] = total.astype(BF)
+        return 0
+
+    lax.fori_loop(0, rows // block, add_rows, 0)
+    settle(w_t, w_x.at[0], local.at[2])
+    far_w = push(w_x.at[0], w_x.at[1], x_send.at[2], x_recv.at[2], across)
+    far_w.wait()
+    g_t[:, split:] = (w_x[0].astype(F32) + w_x[1].astype(F32)).astype(BF)
+    settle(g_t, g_c.at[core], local.at[3])
+    near_g = push(g_c.at[core], g_c.at[core], c_send.at[0], c_recv.at[0], beside)
     near_s.wait()
     s_out[...] = s_c[0] + s_c[1]
-    for copy in near:
-        copy.wait()
-
-
-def finish(g, s, up, dn, ou):
-    n = g.shape[0]
+    near_g.wait()
+    for c in range(2):
+        g_out[:, c * span : (c + 1) * span] = g_c[c].astype(F32)
+
+
+def finish(g, w, s):
+    n, rows, last = w.shape
+    span = g.shape[1] + last
     vm = pl.BlockSpec(memory_space=pltpu.VMEM)
-    pair = lambda a: jax.ShapeDtypeStruct((2,) + a.shape, BF)
-    one = lambda a: pltpu.VMEM(a.shape, a.dtype)
     dma = pltpu.SemaphoreType.DMA
+    pair = pltpu.VMEM((2,) + s.shape[1:], F32)
     return pl.pallas_call(
         functools.partial(finish_kernel, n),
-        in_specs=[vm] * 5,
-        out_specs=[vm] * 5,
+        in_specs=[vm] * 3,
+        out_specs=[vm] * 2,
         out_shape=[
-            jax.ShapeDtypeStruct((2,) + g.shape[1:], BF),
+            jax.ShapeDtypeStruct((rows, 2 * span), F32),
             jax.ShapeDtypeStruct(s.shape[1:], F32),
-            pair(up),
-            pair(dn),
-            pair(ou),
         ],
         scratch_shapes=[
-            pltpu.VMEM((n - 1,) + g.shape[1:], BF),
+            pltpu.VMEM((n - 1, rows, last), BF),
             pltpu.VMEM((n - 1,) + s.shape[1:], F32),
-            pltpu.VMEM((2,) + g.shape[1:], BF),
-            pltpu.VMEM((2,) + s.shape[1:], F32),
-            one(up),
-            one(dn),
-            one(ou),
-            pltpu.VMEM(g.shape[1:], BF),
-            pltpu.VMEM((2,) + s.shape[1:], F32),
-            pltpu.VMEM((2,) + s.shape[1:], F32),
-            one(up),
-            one(dn),
-            one(ou),
+            pltpu.VMEM(g.shape, BF),
+            pltpu.VMEM((2, rows, last), BF),
+            pair,
+            pltpu.VMEM((2, rows, span), BF),
+            pair,
+            pltpu.VMEM((rows, span), BF),
+            pltpu.VMEM((rows, last), BF),
+            pair,
             dma((n - 1,)),
             dma((n - 1,)),
             dma((n - 1,)),
             dma((n - 1,)),
-            dma((5,)),
-            dma((5,)),
-            dma((5,)),
-            dma((5,)),
-            dma((7,)),
+            dma((3,)),
+            dma((3,)),
+            dma((2,)),
+            dma((2,)),
+            dma((4,)),
         ],
         compiler_params=pltpu.CompilerParams(collective_id=1, has_side_effects=True),
         name="finish",
-    )(g, s, up, dn, ou)
+    )(g, w, s)
 
 
 def on_device(
@@ -546,15 +575,14 @@
     ).reshape(shard, n_fsdp * inner)
     down_rows = lax.dynamic_slice_in_dim(down_weight, core * inner, inner, 0)
     out_cols = lax.dynamic_slice_in_dim(out_weight, core * span, span, 1)
-    out_near = lax.all_gather(out_cols, "fsdp", axis=0, tiled=True)
-    up_own = lax.all_gather(up_cols, "fsdp", axis=0, tiled=True)
+    out_up = lax.all_gather(
+        jnp.concatenate([out_cols, up_cols], 1), "fsdp", axis=0, tiled=True
+    )
     down_own = lax.all_gather(down_rows, "fsdp", axis=0, tiled=True)
-    out_far = lax.ppermute(out_near, "seq", swap)
     in_order = lambda near, far, axis: jnp.where(
         core == 0, jnp.concatenate([near, far], axis), jnp.concatenate([far, near], axis)
     )
-    out_full = in_order(out_near, out_far, 1)
-    cot_both = jnp.concatenate([cotangent[0], lax.ppermute(cotangent[0], "seq", swap)], 0)
+    cot_far = lax.ppermute(cotangent[0], "seq", swap)
 
     frequency = jnp.exp(-jnp.log(10000.0) * jnp.arange(HD // 2, dtype=F32) / (HD // 2))
     angles = frequency[:, None] * jnp.arange(length, dtype=F32)[None, :]
@@ -583,11 +611,15 @@
     vec = jnp.concatenate([scale_one[None], shift_one[None], jnp.zeros((6, width), F32)], 0)
     bias_own = lax.dynamic_slice_in_dim(qkv_b, core * 3 * span, 3 * span, 0)
     bias_own = jnp.transpose(bias_own.reshape(heads, 3, HD), (1, 0, 2)).reshape(3 * span, 1)
-    q, k, v, kc, vc, a_own, a_clean = project(
+    q, k, v, kc, vc, a_own = project(
         core.reshape(1).astype(jnp.int32), tok, other, clean_mine, clean_other, gathered, vec,
         bias_own, cos_t, sin_t, heads
     )
     o, lse = attend(bounds, q, k, v, kc, vc, id_row, id_col, heads, 2)
+    o, lse, out_up, cot_far = lax.optimization_barrier((o, lse, out_up, cot_far))
+    cot_both = jnp.concatenate([cotangent[0], cot_far], 0)
+    out_near, up_own = out_up[:, :span], out_up[:, span:]
+    out_full = in_order(out_near, lax.ppermute(out_near, "seq", swap), 1)
     cut = lambda value, which: lax.dynamic_slice_in_dim(value, which * local_rows, local_rows, 1)
     o_mine = cut(o, core)
     o_in = lax.ppermute(cut(o, 1 - core), "seq", swap)
@@ -597,6 +629,7 @@
     hidden = rows_in + rows_contract(attended, out_full) + out_shift
     normed_two, inverse_two = normalize_parts(hidden)
     second_in = (normed_two * scale_two + shift_two).astype(BF)
+    second_in, down_own = lax.optimization_barrier((second_in, down_own))
     both_in = jnp.concatenate([second_in, lax.ppermute(second_in, "seq", swap)], 0)
 
     def join(partial):
@@ -605,18 +638,26 @@
         ).astype(F32)
 
     pre_act = dot(both_in, up_own) + up_b
-    activated, gelu_pull = jax.vjp(
-        lambda pre_value: jax.nn.gelu(pre_value, approximate=True), pre_act
-    )
-    act_low = activated.astype(BF)
+    root = (2 / math.pi) ** 0.5
+    square = pre_act * pre_act
+    bend = jnp.tanh(root * pre_act * (1 + 0.044715 * square))
+    rise = 0.5 * (1 + bend)
+    act_low = (pre_act * rise).astype(BF)
+    curve = 0.5 * pre_act * (1 - bend * bend) * (1 + 3 * 0.044715 * square)
+    slope = (rise + root * curve).astype(BF)
+    grad_down_w = rows_contract(act_low, cot_both).astype(BF)
+    scatter = lambda grad: lax.psum_scatter(grad, "fsdp", scatter_dimension=0, tiled=True)
+    act_low, slope, grad_down_w, cot_both = lax.optimization_barrier(
+        (act_low, slope, grad_down_w, cot_both)
+    )
+    down_part = scatter(grad_down_w)
     result = hidden + join(dot(act_low, down_own)) + down_shift
 
     grad_top = cotangent[0].astype(F32)
     grad_down_b = jnp.sum(grad_top, 0)
-    grad_pre = gelu_pull(right_transposed(cot_both, down_own))[0].astype(BF)
+    grad_pre = (right_transposed(cot_both, down_own) * slope.astype(F32)).astype(BF)
     grad_second = join(right_transposed(grad_pre, up_own))
     grad_up_b = jnp.sum(grad_pre.astype(F32), 0)
-    grad_down_w = rows_contract(act_low, cot_both).astype(BF)
     grad_up_w = rows_contract(both_in, grad_pre).astype(BF)
     grad_scale_two = jnp.sum(grad_second * normed_two, 0)
     grad_shift_two = jnp.sum(grad_second, 0)
@@ -633,52 +674,72 @@
     out_sum = (
         cut_cols(core).astype(F32) + lax.ppermute(cut_cols(1 - core), "seq", swap).astype(F32)
     ).astype(BF)
-    do_mine, do_in, grad_down_w, grad_up_w, out_sum = lax.optimization_barrier(
-        (do_mine, do_in, grad_down_w, grad_up_w, out_sum)
-    )
-    scatter = lambda grad: lax.psum_scatter(grad, "fsdp", scatter_dimension=0, tiled=True)
-    down_part = scatter(grad_down_w)
-    up_out_part = scatter(jnp.concatenate([grad_up_w, out_sum], 1))
-    up_part, out_part = up_out_part[:, : n_fsdp * inner], up_out_part[:, n_fsdp * inner :]
-
-    own_grad, clean_grad = attend_back(
-        bounds, q, k, v, kc, vc, o, lse, do_mine, do_in, id_row, id_col, cos_t, sin_t, heads, 2
-    )
-    weight = gathered[:, : 3 * span]
-    weight_kv = weight.reshape(width, heads, 3 * HD)[:, :, HD:].reshape(width, 2 * span)
-    back = lambda grad, w: lax.dot_general(
-        grad, w, (((0,), (1,)), ((), ())), preferred_element_type=F32
-    )
-    first_clean = back(clean_grad, weight_kv)
-    first_own = back(own_grad, weight)
-    cut_rows = lambda value, which: lax.dynamic_slice_in_dim(
-        value, which * local_rows, local_rows, 0
-    )
-    send_rows = jnp.concatenate(
-        [cut_rows(first_clean, 1 - core), cut_rows(first_own, 1 - core)], 0
-    ).astype(BF)
-    got_rows = lax.ppermute(send_rows, "seq", swap).astype(F32)
-    clean_sum = (cut_rows(first_clean, core) + got_rows[:local_rows]).astype(BF)
-    from_noisy = lax.ppermute(clean_sum, "seq", [(0, 2), (1, 3)])
-    grad_first = cut_rows(first_own, core) + got_rows[local_rows:]
-
-    by_rows = lambda a, grad: lax.dot_general(
-        a, grad, (((0,), (1,)), ((), ())), preferred_element_type=F32
-    )
-    grad_qkv_w = by_rows(a_own, own_grad).reshape(width, heads, 3 * HD)
-    grad_kv = by_rows(a_clean, clean_grad).reshape(width, heads, 2 * HD)
-    grad_qkv_w = grad_qkv_w.at[:, :, HD:].add(grad_kv).astype(BF)
-    grad_qkv_w = grad_qkv_w.reshape(n_fsdp, shard, 3 * span)
-    grad_qkv_b = jnp.sum(own_grad.astype(F32), 1).reshape(heads, 3 * HD)
-    kv_b = jnp.sum(clean_grad.astype(F32), 1).reshape(heads, 2 * HD)
-    grad_qkv_b = grad_qkv_b.at[:, HD:].add(kv_b).reshape(3 * span)
-
+    do_mine, do_in, grad_up_w, out_sum = lax.optimization_barrier(
+        (do_mine, do_in, grad_up_w, out_sum)
+    )
+    out_up_part = scatter(jnp.concatenate([out_sum, grad_up_w], 1))
+
+    back_args = lambda mine: (
+        bounds, q, k, v, kc, vc, o, lse, mine, do_in, id_row, id_col, cos_t, sin_t
+    )
+    hold = lax.optimization_barrier
+    cross = [(0, 2), (1, 3), (2, 0), (3, 1)]
+    to_clean = lambda send: lax.ppermute(send, "seq", [(0, 2), (1, 3)])
+    pair_w = 2 * 3 * HD
+
+    def joined(own, got):
+        own = own.reshape(2, 3, HD, -1)
+        key_value = own[:, 1:].astype(F32) + got.reshape(2, 2, HD, -1).astype(F32)
+        return jnp.concatenate([own[:, :1], key_value.astype(BF)], 1).reshape(pair_w, -1)
+
+    def weight_grad(own):
+        return lax.dot_general(
+            a_own, own, (((0,), (1,)), ((), ())), preferred_element_type=F32
+        ).astype(BF)
+
+    def back(own, first, count):
+        cols = gathered[:, first * pair_w : (first + count) * pair_w]
+        return lax.dot_general(
+            own, cols, (((0,), (1,)), ((), ())), preferred_element_type=F32
+        )
+
+    own_0, send_0 = attend_back(*back_args(do_mine), 0, 2)
+    send_0, do_mine = hold((send_0, do_mine))
+    got_0 = to_clean(send_0)
+    own_1, send_1 = attend_back(*back_args(do_mine), 1, 2)
+    own_1, send_1, got_0, down_part = hold((own_1, send_1, got_0, down_part))
+    got_1, down_far = to_clean(send_1), lax.ppermute(down_part, "seq", cross)
+    own_0 = joined(own_0, got_0)
+    grad_0, do_mine = hold((weight_grad(own_0), do_mine))
+    own_2, send_2 = attend_back(*back_args(do_mine), 2, 2)
+    own_2, send_2, got_1, down_far, out_up_part = hold(
+        (own_2, send_2, got_1, down_far, out_up_part)
+    )
+    got_2 = to_clean(send_2)
+    own_1 = joined(own_1, got_1)
+    grad_01, own_1 = hold((jnp.concatenate([grad_0, weight_grad(own_1)], 1), own_1))
+    part_01 = scatter(grad_01)
+    own_01 = jnp.concatenate([own_0, own_1], 0)
+    first_01 = back(own_01, 0, 2)
+    got_2, out_up_part, first_01 = hold((got_2, out_up_part, first_01))
+    own_2 = joined(own_2, got_2)
+    far_rows = first_01[local_rows:] + back(own_2[:, local_rows:], 2, 1)
+    got_rows = lax.ppermute(far_rows.astype(BF), "seq", swap).astype(F32)
+    grad_first = first_01[:local_rows] + back(own_2[:, :local_rows], 2, 1) + got_rows
+    grad_2 = weight_grad(own_2)
+
+    def gather_cores(part, far):
+        total = (part.astype(F32) + far.astype(F32)).astype(BF)
+        return in_order(total[None], lax.ppermute(total, "seq", swap)[None], 0)
+
+    down_g = gather_cores(down_part, down_far)
+    out_up_g = gather_cores(out_up_part, lax.ppermute(out_up_part, "seq", cross))
+
+    sum_cols = lambda own: jnp.sum(own.astype(F32), 1)
+    grad_qkv_b = jnp.concatenate([sum_cols(own_01), sum_cols(own_2)])
     normed_one, inverse_one = normalize_parts(rows_in)
-    normed_clean, _ = normalize_parts(clean_mine.astype(F32))
-    clean_wide = clean_sum.astype(F32)
-    grad_scale_one = jnp.sum(grad_first * normed_one + clean_wide * normed_clean, 0)
-    grad_shift_one = jnp.sum(grad_first + clean_wide, 0)
-    grad_first = grad_first + from_noisy.astype(F32)
+    grad_scale_one = jnp.sum(grad_first * normed_one, 0)
+    grad_shift_one = jnp.sum(grad_first, 0)
     grad_rows = grad_hidden + norm_backward(grad_first, normed_one, inverse_one, scale_one)
 
     qkv_b_wide = lax.dynamic_update_slice_in_dim(
@@ -699,22 +760,24 @@
     lines = -(-packed.shape[1] // 128)
     packed = jnp.pad(packed, ((0, 0), (0, lines * 128 - packed.shape[1])))
     packed = packed.reshape(n_fsdp, lines, 128)
-    qkv_g, small_sum, up_g, down_g, out_g = finish(
-        grad_qkv_w, packed, up_part, down_part, out_part
-    )
+    grad_rows, out_up_g, down_g, packed, part_01 = hold(
+        (grad_rows, out_up_g, down_g, packed, part_01)
+    )
+    qkv_g, small_sum = finish(part_01, grad_2.reshape(n_fsdp, shard, pair_w), packed)
     small_sum = small_sum.reshape(-1)
     small_out, at = [], 0
     for size in sizes:
         small_out.append(small_sum[at : at + size])
         at += size
     side = lambda pair: jnp.concatenate([pair[0], pair[1]], 1).astype(F32)
+    out_g, up_g = out_up_g[:, :, :span], out_up_g[:, :, span:]
     up_g = jnp.transpose(up_g.reshape(2, shard, n_fsdp, inner), (1, 2, 0, 3))
     return (
         result.astype(BF)[None],
         grad_rows[None],
         small_out[0],
         small_out[1],
-        side(qkv_g),
+        qkv_g,
         small_out[2],
         side(out_g),
         small_out[3],

time: 607 us -> 508 us (0.84)
  Pallas kernels: 258 us -> 212 us
  blocking collectives: 23.8 us -> 0 us
  matrix products: 97.5 us -> 80.9 us
  local copies, waits for them, and re-layouts: 63.5 us -> 52.4 us
  waiting for transfers between devices: 79.7 us -> 69.6 us
    pallas_call x1, Pallas kernels: 56.1 us -> 27.4 us  [finish(): pl.pallas_call(functools.partial(finish_kernel, n), in_specs=[vm] * 3, ou...]
    all_gather x1 -> x0, blocking collectives: 23.8 us -> none  [on_device(): out_near = lax.all_gather(out_cols, 'fsdp', axis=0, tiled=True)]
    all_gather x1, waiting for transfers between devices: 26.2 us -> 5.88 us  [on_device(): down_own = lax.all_gather(down_rows, 'fsdp', axis=0, tiled=True)]
    pallas_call x1, Pallas kernels: 84 us -> 64 us  [attend(): pl.pallas_call(functools.partial(attend_kernel, group), grid_spec=pltpu.P...]
    reduce_scatter x2 -> x3, waiting for transfers between devices: 3.7 us -> 20.4 us  [on_device(): lax.psum_scatter(grad, 'fsdp', scatter_dimension=0, tiled=True)]
    dot_general x3, matrix products: 28.7 us -> 17.3 us  [right_transposed(): lax.dot_general(left, right, (((1,), (1,)), ((), ())), preferred_element_...]
    reshape x4 -> x0, local copies, waits for them, and re-layouts: 7.87 us -> none  [the longest x2 7.72 us: on_device(): grad_qkv_w = grad_qkv_w.reshape(n_fsdp, shard, 3 * span)]
    ppermute x4 -> x10, waiting for transfers between devices: 17.3 us -> 9.6 us  [the longest x3 8.04 us: on_device(): to_clean = lambda send: lax.ppermute(send, 'seq', [(0, 2), (1, 3)])]
  transfers between devices with their start and end apart: 18 -> 25, of which waited for: 7 -> 6; matrix products, arithmetic and copies ran while one was open for 27% -> 22% of each run, Pallas kernels for 34% -> 37%
where the time goes in v3:
time: 508 us; the launch traced here: 502 us
  Pallas kernels  212 us (42%)
  matrix products  80.9 us (16%)
  waiting for transfers between devices  69.6 us (14%)
  local copies, waits for them, and re-layouts  52.4 us (10%)
  other arithmetic  49.4 us (10%)
  starting transfers between devices  22.4 us (4%)
  between operations  15.3 us (3%)
    pallas_call x3, Pallas kernels, attend_back(): pl.pallas_call(functools.partial(attend_back_kernel, group), grid_spec=pl...  99.8 us
    pallas_call x1, Pallas kernels, attend(): pl.pallas_call(functools.partial(attend_kernel, group), grid_spec=pltpu.P...  64 us
    ppermute x1, waiting for transfers between devices, on_device(): clean_in = lax.ppermute(tok, 'seq', [(2, 0), (3, 1)])  33.5 us
    pallas_call x1, Pallas kernels, finish(): pl.pallas_call(functools.partial(finish_kernel, n), in_specs=[vm] * 3, ou...  27.4 us
    dot_general x3, matrix products, dot(): return jnp.dot(left, right, preferred_element_type=F32)  25.1 us
    pallas_call x1, Pallas kernels, project(): pl.pallas_call(functools.partial(qkv_kernel, heads), grid_spec=pltpu.Pref...  21.3 us
    reduce_scatter x3, waiting for transfers between devices, on_device(): lax.psum_scatter(grad, 'fsdp', scatter_dimension=0, tiled=True)  20.4 us
    dot_general x3, matrix products, right_transposed(): lax.dot_general(left, right, (((1,), (1,)), ((), ())), preferred_element_...  17.3 us
  transfers between devices with their start and end apart: 25, of which 6 were waited for; matrix products, arithmetic and copies ran while one was open for 22% of the time, Pallas kernels for 37%

profile of v3, /device:TPU:13, one launch (start us, length us, event | category | flops | bytes accessed | tf_op | source)
XLA Modules:
  0.0 502.4 jit_solution(13143472815244584569)
XLA Ops:
  11.7 2.9 reshape.468
  14.6 2.5 dynamic-slice_reduce_fusion
  22.1 33.5 %collective-permute-done.1 = bf16[1024,768]{1,0:T(8,128)(2,1)} collective-permute-done((bf16[1024,768]{1,0:T(8,128)(2,1)S(1)}, bf16[1024,768]{1,0:T(8,128)(2,1)}, u32[]{:S(2)}, u32[]{:S(2)}) %collective-permute-start.1) | collective-permute-done | bytes 1572896 | tf_op jit(solution)/shard_map/ppermute | solution.py:540
  55.6 2.7 broadcast_select_fusion.cmine
  60.5 1.8 fusion.33
  65.9 21.3 %project.1 = (bf16[384,2048]{1,0:T(8,128)(2,1)}, bf16[384,2048]{1,0:T(8,128)(2,1)}, bf16[384,2048]{1,0:T(8,128)(2,1)}, bf16[384,2048]{1,0:T(8,128)(2,1)}, bf16[3...) custom-call(s32[1]{0:T(128)} %bitcast.6.core_ref, bf16[1024,768]{1,0:T(8,128)(2,1)} %bitcast.111, ...), custom_call_target="tpu_custom_call" | custom-call | tf_op jit(solution)/shard_map/project/pallas_call | solution.py:119
  89.2 64.0 %attend.1 = (bf16[384,2048]{1,0:T(8,128)(2,1)}, f32[6,8,2048]{2,1,0:T(8,128)}) custom-call(s32[5,4]{1,0:T(8,128)} %stack.2.bounds, bf16[384,2048]{1,0:T(8,128)(2,1)} %get-tuple-element.67.q, bf16[384,2048]{1,0:T(8,128)(2,1)} %get-tuple-element.68.k, bf16[384,2048]{1,0:T(8,128)(2,1)} %get-tuple-element.69.v, bf16[384,2048]{1,0:T(8,128)(2,1)} %get-tuple-element.70.kc, ...), custom_call_target="tpu_custom_call" | custom-call | flops 25769803776 | bytes 16777216 | tf_op jit(solution)/shard_map/attend/pallas_call | solution.py:237
  153.2 2.5 constant_dynamic-slice_fusion.5
  159.2 3.5 fusion.45
  164.3 1.7 add_convert_fusion.2
  166.0 5.9 %all-gather.8.cloned.1.call-done = bf16[1536,768]{1,0:T(8,128)(2,1)} async-done(((bf16[192,768]{1,0:T(8,128)(2,1)}), bf16[1536,768]{1,0:T(8,128)(2,1)}) %all-gather.8.cloned.1.call-update) | async-done | bytes 2359312 | tf_op jit(solution)/shard_map/all_gather | solution.py:581
  171.9 1.7 collective-permute-start.6
  173.8 3.9 pad_maximum_fusion
  180.0 15.8 %add_convert_fusion = (bf16[2048,1536]{1,0:T(8,128)(2,1)}, bf16[2048,1536]{1,0:T(8,128)(2,1)S(1)}) fusion(f32[1536]{0:T(1024)S(1)} %add.240, bf16[2048,768]{1,0:T(8,128)(2,1)S(1)} %constant_dynamic-update-slice_fusion, bf16[768,1920]{1,0:T(8,128)(2,1)S(1)} %copy-done.26), kind=kOutput, calls=%fused_computation.2 | convolution fusion | flops 4894752768 | bytes 18096128 | tf_op jit(solution)/shard_map/dot_general | solution.py:49
  195.8 2.6 copy-done.36
  198.4 7.9 %convolution_convert_fusion.1 = bf16[1536,768]{1,0:T(8,128)(2,1)} fusion(bf16[2048,1536]{1,0:T(8,128)(2,1)S(1)} %get-tuple-element.78, bf16[1024,768]{1,0:T(8,128)(2,1)} %collective-permute-done.3, bf16[1024,768]{1,0:T(8,128)(2,1)S(1)} %bitcast.116), kind=kOutput, calls=%fused_computation.18 | convolution fusion | flops 4839309312 | bytes 11796480 | tf_op jit(solution)/shard_map/dot_general | solution.py:41
  206.3 9.2 %convert_reduce_fusion = (f32[1536]{0:T(1024)S(1)}, bf16[2048,1536]{1,0:T(8,128)(2,1)S(1)}) fusion(bf16[2048,1536]{1,0:T(8,128)(2,1)} %get-tuple-element.81, bf16[2048,768]{1,0:T(8,128)(2,1)} %pad_maximum_fusion, bf16[1536,768]{1,0:T(8,128)(2,1)} %all-gather.8.cloned.1.call-done), kind=kOutput, calls=%fused_computation | convolution fusion | flops 4847565312 | bytes 18094080 | tf_op jit(solution)/shard_map/dot_general | solution.py:45
  215.5 5.3 %fusion.18 = f32[2048,768]{1,0:T(8,128)S(1)} fusion(bf16[2048,1536]{1,0:T(8,128)(2,1)S(1)} %get-tuple-element.167, bf16[768,1920]{1,0:T(8,128)(2,1)S(1)} %copy-done.27), kind=kOutput, calls=%fused_computation.53 | convolution fusion | flops 4831838208 | bytes 14942208 | tf_op jit(solution)/shard_map/dot_general | solution.py:45
  222.2 2.1 copy-done.33
  224.2 5.3 %fusion.46 = f32[2048,768]{1,0:T(8,128)S(1)} fusion(bf16[2048,1536]{1,0:T(8,128)(2,1)S(1)} %bitcast.159, bf16[1536,768]{1,0:T(8,128)(2,1)S(1)} %copy-done.33), kind=kOutput, calls=%fused_computation.168 | convolution fusion | flops 4831838208 | bytes 14942208 | tf_op jit(solution)/shard_map/dot_general | solution.py:49
  232.9 4.5 multiply_reduce_fusion
  237.5 5.9 %convert_reduce_fusion.4 = (f32[768]{0:T(1024)S(1)}, f32[1024,768]{1,0:T(8,128)S(1)}, bf16[1,1024,768]{2,1,0:T(8,128)(2,1)}, f32[768]{0:T(1024)S(1)}) fusion(f32[1024]{0:T(1024)S(1)} %broadcast_multiply_fusion.3, f32[1024,768]{1,0:T(8,128)S(1)} %copy-done.5, f32[1024]{0:T(1024)S(1)} %broadcast_multiply_fusion.5, f32[1024]{0:T(1024)S(1)} %broadcast_multiply_fusion.4, ...), kind=kLoop, calls=%fused_computation.36 | loop fusion | flops 15727104 | bytes 18903040 | tf_op jit(solution)/shard_map/reduce_sum | solution.py:668
  243.4 4.0 convolution_convert_fusion.3
  248.1 2.8 convolution_convert_fusion.2
  253.1 5.4 %convolution_convert_fusion = bf16[768,1536]{1,0:T(8,128)(2,1)S(1)} fusion(bf16[2048,768]{1,0:T(8,128)(2,1)S(1)} %copy-done.22, bf16[2048,1536]{1,0:T(8,128)(2,1)S(1)} %bitcast.157), kind=kOutput, calls=%fused_computation.17 | convolution fusion | flops 4833017856 | bytes 11796480 | tf_op jit(solution)/shard_map/dot_general | solution.py:41
  258.7 1.8 pad_maximum_fusion.2
  261.6 33.5 %attend_back.3 = (bf16[384,2048]{1,0:T(8,128)(2,1)}, bf16[256,2048]{1,0:T(8,128)(2,1)}) custom-call(s32[5,4]{1,0:T(8,128)} %stack.2.bounds, bf16[384,2048]{1,0:T(8,128)(2,1)} %get-tuple-element.67.q, bf16[384,2048]{1,0:T(8,128)(2,1)} %get-tuple-element.68.k, bf16[384,2048]{1,0:T(8,128)(2,1)} %get-tuple-element.69.v, bf16[384,2048]{1,0:T(8,128)(2,1)} %get-tuple-element.70.kc, ...), custom_call_target="tpu_custom_call" | custom-call | flops 10737418240 | bytes 8388608 | tf_op jit(solution)/shard_map/attend_back/pallas_call | solution.py:369
  298.1 33.0 %attend_back.4 = (bf16[384,2048]{1,0:T(8,128)(2,1)}, bf16[256,2048]{1,0:T(8,128)(2,1)}) custom-call(s32[5,4]{1,0:T(8,128)} %stack.2.bounds, bf16[384,2048]{1,0:T(8,128)(2,1)} %get-tuple-element.67.q, bf16[384,2048]{1,0:T(8,128)(2,1)} %get-tuple-element.68.k, bf16[384,2048]{1,0:T(8,128)(2,1)} %get-tuple-element.69.v, bf16[384,2048]{1,0:T(8,128)(2,1)} %get-tuple-element.70.kc, ...), custom_call_target="tpu_custom_call" | custom-call | flops 10737418240 | bytes 8388608 | tf_op jit(solution)/shard_map/attend_back/pallas_call | solution.py:369
  331.2 4.5 collective-permute-start.12
  335.8 1.8 fusion.17
  338.9 2.7 convolution_convert_fusion.6
  341.6 33.2 %attend_back.5 = (bf16[384,2048]{1,0:T(8,128)(2,1)}, bf16[256,2048]{1,0:T(8,128)(2,1)}) custom-call(s32[5,4]{1,0:T(8,128)} %stack.2.bounds, bf16[384,2048]{1,0:T(8,128)(2,1)} %get-tuple-element.67.q, bf16[384,2048]{1,0:T(8,128)(2,1)} %get-tuple-element.68.k, bf16[384,2048]{1,0:T(8,128)(2,1)} %get-tuple-element.69.v, bf16[384,2048]{1,0:T(8,128)(2,1)} %get-tuple-element.70.kc, ...), custom_call_target="tpu_custom_call" | custom-call | flops 10737418240 | bytes 8388608 | tf_op jit(solution)/shard_map/attend_back/pallas_call | solution.py:369
  376.3 2.1 fusion.16
  379.8 3.4 collective-permute-start.14
  383.4 1.8 convolution_convert_fusion.5
  387.5 7.7 %fusion.22 = f32[2048,768]{1,0:T(8,128)} fusion(bf16[384,2048]{1,0:T(8,128)(2,1)} %bitcast.121, bf16[384,2048]{1,0:T(8,128)(2,1)} %bitcast.118, bf16[768,1280]{1,0:T(8,128)(2,1)} %all-gather.4.cloned.1.call-done.w_ref), kind=kOutput, calls=%fused_computation.57 | convolution fusion | flops 2422210560 | bytes 10616832 | tf_op jit(solution)/shard_map/dot_general | solution.py:702
  395.8 2.0 maximum_select_fusion.3
  397.7 8.0 %collective-permute-done.14 = bf16[256,2048]{1,0:T(8,128)(2,1)S(1)} collective-permute-done((bf16[256,2048]{1,0:T(8,128)(2,1)}, bf16[256,2048]{1,0:T(8,128)(2,1)S(1)}, u32[]{:S(2)}, u32[]{:S(2)}) %collective-permute-start.14) | collective-permute-done | bytes 1048608 | tf_op jit(solution)/shard_map/ppermute | solution.py:687
  407.8 2.1 collective-permute-start.16
  410.0 4.6 add_convert_fusion.1
  415.7 2.7 convolution_convert_fusion.4
  420.1 2.3 fusion.29
  422.6 5.1 %fusion.9 = (f32[768]{0:T(1024)S(1)}, f32[1024]{0:T(1024)S(1)}, f32[1024]{0:T(1024)S(1)}, f32[768]{0:T(1024)S(1)}, f32[1024,768]{1,0:T(8,128)}) fusion(f32[1024]{0:T(1024)S(1)} %add_rsqrt_fusion, f32[1024]{0:T(1024)S(1)} %broadcast_multiply_fusion.2, bf16[1,1024,768]{2,1,0:T(8,128)(2,1)S(1)} %copy-done.3, f32[768]{0:T(1024)S(1)} %mul.254, ...), kind=kLoop, calls=%fused_computation.23 | loop fusion | flops 10220032 | bytes 12608512 | tf_op jit(solution)/shard_map/reduce_sum | solution.py:741
  427.9 4.6 fusion.8
  432.5 20.1 %reduce-scatter.8.cloned.1.call-done.g = bf16[96,768]{1,0:T(8,128)(2,1)} async-done(((bf16[768,768]{1,0:T(8,128)(2,1)}), bf16[96,768]{1,0:T(8,128)(2,1)}) %reduce-scatter.8.cloned.1.call-update) | async-done | bytes 147472 | tf_op jit(solution)/shard_map/reduce_scatter | solution.py:649
  453.3 27.4 %finish.1 = (f32[96,2304]{1,0:T(8,128)}, f32[10,128]{1,0:T(8,128)}) custom-call(bf16[96,768]{1,0:T(8,128)(2,1)} %reduce-scatter.8.cloned.1.call-done.g, bf16[8,96,384]{2,1,0:T(8,128)(2,1)} %bitcast.139, f32[8,10,128]{2,1,0:T(8,128)} %copy.71.s), custom_call_target="tpu_custom_call" | custom-call | tf_op jit(solution)/shard_map/finish/pallas_call | solution.py:477
  486.5 2.4 copy.72
  488.9 3.5 reshape.492
  (234 shorter events, 58.0 us)
Async XLA Ops:
  7.2 13.3 %copy-start = (bf16[384,768]{1,0:T(8,128)(2,1)S(1)}, bf16[384,768]{1,0:T(8,128)(2,1)}, u32[]{:S(2)}) copy-start(bf16[384,768]{1,0:T(8,128)(2,1)} %param.27) | copy-start | bytes 1769476
  7.2 10.3 %copy-start.29 = (bf16[96,768]{1,0:T(8,128)(2,1)S(1)}, bf16[96,768]{1,0:T(8,128)(2,1)}, u32[]{:S(2)}) copy-start(bf16[96,768]{1,0:T(8,128)(2,1)} %param.21) | copy-start | bytes 442372
  7.2 11.1 %copy-start.2 = (bf16[1,1024,768]{2,1,0:T(8,128)(2,1)S(1)}, bf16[1,1024,768]{2,1,0:T(8,128)(2,1)}, u32[]{:S(2)}) copy-start(bf16[1,1024,768]{2,1,0:T(8,128)(2,1)} %param.15) | copy-start | bytes 4718596
  7.2 55.1 %all-gather.4.cloned.1.call-start = ((), (), s32[]{:S(2)}) async-start(), calls=%async_computation.3 | async-start | bytes 2211840 | tf_op jit(solution)/shard_map/all_gather | solution.py:560
  10.9 10.6 %copy-start.28 = (s32[1,2048]{1,0:T(1,128)S(1)}, s32[1,2048]{1,0:T(1,128)}, u32[]{:S(2)}) copy-start(s32[1,2048]{1,0:T(1,128)} %param.16) | copy-start | bytes 24580
  11.7 141.5 %all-gather.6.cloned.1.call-start = ((), (), s32[]{:S(2)}) async-start(), calls=%async_computation.4 | async-start | bytes 3317760 | tf_op jit(solution)/shard_map/all_gather | solution.py:578
  18.3 153.6 %all-gather.8.cloned.1.call-start = ((), (), s32[]{:S(2)}) async-start(), calls=%async_computation.5 | async-start | bytes 2654208 | tf_op jit(solution)/shard_map/all_gather | solution.py:581
  18.3 37.3 %collective-permute-start.1 = (bf16[1024,768]{1,0:T(8,128)(2,1)S(1)}, bf16[1024,768]{1,0:T(8,128)(2,1)}, u32[]{:S(2)}, u32[]{:S(2)}) collective-permute-start(bf16[1024,768]{1,0:T(8,128)(2,1)S(1)} %bitcast.112), channel_id=1, source_target_pairs={{16,0},{24,8},{17,1},{25,9},{18,2},{26,10},{19,3},{27,11},{20,4},{... | collective-permute-start | bytes 4718600 | tf_op jit(solution)/shard_map/ppermute | solution.py:540
  19.6 46.3 %collective-permute-start = (bf16[1024,768]{1,0:T(8,128)(2,1)S(1)}, bf16[1024,768]{1,0:T(8,128)(2,1)}, u32[]{:S(2)}, u32[]{:S(2)}) collective-permute-start(bf16[1024,768]{1,0:T(8,128)(2,1)S(1)} %bitcast.113), channel_id=1, source_target_pairs={{0,8},{8,0},{16,24},{24,16},{1,9},{9,1},{17,25},{25,17},{2,10},{10... | collective-permute-start | bytes 4718600 | tf_op jit(solution)/shard_map/ppermute | solution.py:539
  20.4 132.8 %collective-permute-start.3 = (bf16[1024,768]{1,0:T(8,128)(2,1)}, bf16[1024,768]{1,0:T(8,128)(2,1)}, u32[]{:S(2)}, u32[]{:S(2)}) collective-permute-start(bf16[1024,768]{1,0:T(8,128)(2,1)} %bitcast.114), channel_id=1, source_target_pairs={{0,8},{8,0},{16,24},{24,16},{1,9},{9,1},{17,25},{25,17},{2,10},{10... | collective-permute-start | bytes 4718600 | tf_op jit(solution)/shard_map/ppermute | solution.py:585
  21.2 309.9 %reduce-scatter.4.cloned.1.call-start = ((), (), s32[]{:S(2)}) async-start(), calls=%async_computation.6 | async-start | bytes 2654208 | tf_op jit(solution)/shard_map/reduce_scatter | solution.py:649
  58.3 7.6 %collective-permute-start.2 = (bf16[1024,768]{1,0:T(8,128)(2,1)}, bf16[1024,768]{1,0:T(8,128)(2,1)}, u32[]{:S(2)}, u32[]{:S(2)}) collective-permute-start(bf16[1024,768]{1,0:T(8,128)(2,1)} %broadcast_select_fusion.cmine), channel_id=1, source_target_pairs={{0,8},{8,0},{16,24},{24,16},{1,9},{9,1},{17,25},{25,17},{2,10},{10... | collective-permute-start | bytes 4718600 | tf_op jit(solution)/shard_map/ppermute | solution.py:542
  153.1 6.0 %copy-start.3 = (bf16[1,1024,768]{2,1,0:T(8,128)(2,1)S(1)}, bf16[1,1024,768]{2,1,0:T(8,128)(2,1)}, u32[]{:S(2)}) copy-start(bf16[1,1024,768]{2,1,0:T(8,128)(2,1)} %param.15) | copy-start | bytes 4718596
  155.7 3.5 collective-permute-start.4
  156.8 2.3 collective-permute-start.5
  171.9 5.9 %collective-permute-start.6 = (bf16[1024,768]{1,0:T(8,128)(2,1)}, bf16[1024,768]{1,0:T(8,128)(2,1)}, u32[]{:S(2)}, u32[]{:S(2)}) collective-permute-start(bf16[1024,768]{1,0:T(8,128)(2,1)} %add_convert_fusion.2), channel_id=1, source_target_pairs={{0,8},{8,0},{16,24},{24,16},{1,9},{9,1},{17,25},{25,17},{2,10},{10... | collective-permute-start | bytes 4718600 | tf_op jit(solution)/shard_map/ppermute | solution.py:633
  180.0 15.8 %copy-start.21 = (bf16[2048,768]{1,0:T(8,128)(2,1)}, bf16[2048,768]{1,0:T(8,128)(2,1)S(1)}, u32[]{:S(2)}) copy-start(bf16[2048,768]{1,0:T(8,128)(2,1)S(1)} %constant_dynamic-update-slice_fusion) | copy-start | bytes 9437188
  180.0 18.4 %copy-start.8 = (bf16[1,1024,768]{2,1,0:T(8,128)(2,1)S(1)}, bf16[1,1024,768]{2,1,0:T(8,128)(2,1)}, u32[]{:S(2)}) copy-start(bf16[1,1024,768]{2,1,0:T(8,128)(2,1)} %param.29) | copy-start | bytes 4718596
  206.3 9.2 %copy-start.27 = (bf16[768,1920]{1,0:T(8,128)(2,1)S(1)}, bf16[768,1920]{1,0:T(8,128)(2,1)}, u32[]{:S(2)}) copy-start(bf16[768,1920]{1,0:T(8,128)(2,1)} %all-gather.6.cloned.1.call-done) | copy-start | bytes 8847364
  206.3 15.9 %slice-start.2 = ((s8[6291456]{0:T(1024)(128)(4,1)}), s8[4194304]{0:T(1024)(128)(4,1)S(1)}, s32[]{:S(2)}) async-start(s8[6291456]{0:T(1024)(128)(4,1)} %bitcast.158), calls=%async_computation.11 | async-start | bytes 8388608
  215.5 6.7 %slice-start.3 = ((s8[6291456]{0:T(1024)(128)(4,1)}), s8[2097152]{0:T(1024)(128)(4,1)S(1)}, s32[]{:S(2)}) async-start(s8[6291456]{0:T(1024)(128)(4,1)} %bitcast.158), calls=%async_computation.12 | async-start | bytes 4194304
  220.8 8.7 %copy-start.7 = (f32[2048,768]{1,0:T(8,128)}, f32[2048,768]{1,0:T(8,128)S(1)}, u32[]{:S(2)}) copy-start(f32[2048,768]{1,0:T(8,128)S(1)} %fusion.18) | copy-start | bytes 18874372
  222.2 10.7 %collective-permute-start.8 = (bf16[1024,768]{1,0:T(8,128)(2,1)}, bf16[1024,768]{1,0:T(8,128)(2,1)}, u32[]{:S(2)}, u32[]{:S(2)}) collective-permute-start(bf16[1024,768]{1,0:T(8,128)(2,1)} %slice.279), channel_id=1, source_target_pairs={{0,8},{8,0},{16,24},{24,16},{1,9},{9,1},{17,25},{25,17},{2,10},{10... | collective-permute-start | bytes 4718600 | tf_op jit(solution)/shard_map/ppermute | solution.py:636
  232.7 4.7 collective-permute-start.7
  232.8 143.5 %reduce-scatter.6.cloned.1.call-start = ((), (), s32[]{:S(2)}) async-start(), calls=%async_computation.7 | async-start | bytes 3317760 | tf_op jit(solution)/shard_map/reduce_scatter | solution.py:649
  243.4 8.5 %slice-start = ((s8[6291456]{0:T(1024)(128)(4,1)}), s8[4194304]{0:T(1024)(128)(4,1)S(1)}, s32[]{:S(2)}) async-start(s8[6291456]{0:T(1024)(128)(4,1)} %bitcast.156), calls=%async_computation.9 | async-start | bytes 8388608
  247.5 11.0 %collective-permute-start.10 = (bf16[768,384]{1,0:T(8,128)(2,1)S(1)}, bf16[768,384]{1,0:T(8,128)(2,1)S(1)}, u32[]{:S(2)}, u32[]{:S(2)}) collective-permute-start(bf16[768,384]{1,0:T(8,128)(2,1)S(1)} %constant_dynamic-slice_fusion), channel_id=1, source_target_pairs={{0,8},{8,0},{16,24},{24,16},{1,9},{9,1},{17,25},{25,17},{2,10},{10... | collective-permute-start | bytes 1769480 | tf_op jit(solution)/shard_map/ppermute | solution.py:675
  251.9 6.8 %collective-permute-start.9 = (bf16[384,1024]{1,0:T(8,128)(2,1)S(1)}, bf16[384,1024]{1,0:T(8,128)(2,1)S(1)}, u32[]{:S(2)}, u32[]{:S(2)}) collective-permute-start(bf16[384,1024]{1,0:T(8,128)(2,1)S(1)} %get-tuple-element.145), channel_id=1, source_target_pairs={{0,8},{8,0},{16,24},{24,16},{1,9},{9,1},{17,25},{25,17},{2,10},{10... | collective-permute-start | bytes 2359304 | tf_op jit(solution)/shard_map/ppermute | solution.py:672
  260.6 192.0 %reduce-scatter.8.cloned.1.call-start = ((), (), s32[]{:S(2)}) async-start(), calls=%async_computation.8 | async-start | bytes 1327104 | tf_op jit(solution)/shard_map/reduce_scatter | solution.py:649
  295.0 36.1 %collective-permute-start.11 = (bf16[256,2048]{1,0:T(8,128)(2,1)}, bf16[256,2048]{1,0:T(8,128)(2,1)S(1)}, u32[]{:S(2)}, u32[]{:S(2)}) collective-permute-start(bf16[256,2048]{1,0:T(8,128)(2,1)} %get-tuple-element.91), channel_id=1, source_target_pairs={{0,16},{8,24},{1,17},{9,25},{2,18},{10,26},{3,19},{11,27},{4,20},{... | collective-permute-start | bytes 3145736 | tf_op jit(solution)/shard_map/ppermute | solution.py:687
  331.2 44.8 %collective-permute-start.13 = (bf16[192,768]{1,0:T(8,128)(2,1)}, bf16[192,768]{1,0:T(8,128)(2,1)S(1)}, u32[]{:S(2)}, u32[]{:S(2)}) collective-permute-start(bf16[192,768]{1,0:T(8,128)(2,1)} %reduce-scatter.4.cloned.1.call-done), channel_id=1, source_target_pairs={{0,16},{8,24},{16,0},{24,8},{1,17},{9,25},{17,1},{25,9},{2,18},{10... | collective-permute-start | bytes 884744 | tf_op jit(solution)/shard_map/ppermute | solution.py:711
  331.2 44.7 %collective-permute-start.12 = (bf16[256,2048]{1,0:T(8,128)(2,1)}, bf16[256,2048]{1,0:T(8,128)(2,1)}, u32[]{:S(2)}, u32[]{:S(2)}) collective-permute-start(bf16[256,2048]{1,0:T(8,128)(2,1)} %get-tuple-element.97), channel_id=1, source_target_pairs={{0,16},{8,24},{1,17},{9,25},{2,18},{10,26},{3,19},{11,27},{4,20},{... | collective-permute-start | bytes 3145736 | tf_op jit(solution)/shard_map/ppermute | solution.py:687
  341.6 34.7 %copy-start.25 = (bf16[192,768]{1,0:T(8,128)(2,1)S(1)}, bf16[192,768]{1,0:T(8,128)(2,1)}, u32[]{:S(2)}) copy-start(bf16[192,768]{1,0:T(8,128)(2,1)} %reduce-scatter.4.cloned.1.call-done) | copy-start | bytes 884740
  376.3 7.1 %copy-start.31 = (bf16[2048,768]{1,0:T(8,128)(2,1)S(1)}, bf16[2048,768]{1,0:T(8,128)(2,1)}, u32[]{:S(2)}) copy-start(bf16[2048,768]{1,0:T(8,128)(2,1)} %get-tuple-element.83) | copy-start | bytes 9437188
  378.4 17.3 %collective-permute-start.18 = (bf16[192,768]{1,0:T(8,128)(2,1)S(1)}, bf16[192,768]{1,0:T(8,128)(2,1)}, u32[]{:S(2)}, u32[]{:S(2)}) collective-permute-start(bf16[192,768]{1,0:T(8,128)(2,1)S(1)} %add_convert_fusion.5), channel_id=1, source_target_pairs={{0,8},{8,0},{16,24},{24,16},{1,9},{9,1},{17,25},{25,17},{2,10},{10... | collective-permute-start | bytes 884744 | tf_op jit(solution)/shard_map/ppermute | solution.py:733
  379.8 25.9 %collective-permute-start.14 = (bf16[256,2048]{1,0:T(8,128)(2,1)}, bf16[256,2048]{1,0:T(8,128)(2,1)S(1)}, u32[]{:S(2)}, u32[]{:S(2)}) collective-permute-start(bf16[256,2048]{1,0:T(8,128)(2,1)} %get-tuple-element.101), channel_id=1, source_target_pairs={{0,16},{8,24},{1,17},{9,25},{2,18},{10,26},{3,19},{11,27},{4,20},{... | collective-permute-start | bytes 3145736 | tf_op jit(solution)/shard_map/ppermute | solution.py:687
  387.5 7.8 %copy-start.11 = (bf16[2,3,64,2048]{3,2,1,0:T(8,128)(2,1)S(1)}, bf16[2,3,64,2048]{3,2,1,0:T(8,128)(2,1)}, u32[]{:S(2)}) copy-start(bf16[2,3,64,2048]{3,2,1,0:T(8,128)(2,1)} %copy-done.10) | copy-start | bytes 4718596
  387.5 7.7 %copy-start.13 = (bf16[2,3,64,2048]{3,2,1,0:T(8,128)(2,1)S(1)}, bf16[2,3,64,2048]{3,2,1,0:T(8,128)(2,1)}, u32[]{:S(2)}) copy-start(bf16[2,3,64,2048]{3,2,1,0:T(8,128)(2,1)} %copy-done.12) | copy-start | bytes 4718596
  395.3 10.5 %copy-start.19 = (bf16[384,2048]{1,0:T(8,128)(2,1)S(1)}, bf16[384,2048]{1,0:T(8,128)(2,1)}, u32[]{:S(2)}) copy-start(bf16[384,2048]{1,0:T(8,128)(2,1)} %get-tuple-element.108) | copy-start | bytes 4718596
  407.8 7.9 %copy-start.14 = (bf16[2,3,64,2048]{3,2,1,0:T(8,128)(2,1)S(1)}, bf16[2,3,64,2048]{3,2,1,0:T(8,128)(2,1)}, u32[]{:S(2)}) copy-start(bf16[2,3,64,2048]{3,2,1,0:T(8,128)(2,1)} %pad_maximum_fusion.6) | copy-start | bytes 4718596
  407.8 7.9 %copy-start.32 = (bf16[2048,768]{1,0:T(8,128)(2,1)S(1)}, bf16[2048,768]{1,0:T(8,128)(2,1)}, u32[]{:S(2)}) copy-start(bf16[2048,768]{1,0:T(8,128)(2,1)} %get-tuple-element.83) | copy-start | bytes 9437188
  407.8 10.5 %collective-permute-start.16 = (bf16[96,1920]{1,0:T(8,128)(2,1)S(1)}, bf16[96,1920]{1,0:T(8,128)(2,1)S(1)}, u32[]{:S(2)}, u32[]{:S(2)}) collective-permute-start(bf16[96,1920]{1,0:T(8,128)(2,1)S(1)} %copy-done.24), channel_id=1, source_target_pairs={{0,16},{8,24},{16,0},{24,8},{1,17},{9,25},{17,1},{25,9},{2,18},{10... | collective-permute-start | bytes 1105928 | tf_op jit(solution)/shard_map/ppermute | solution.py:736
  414.5 8.0 %collective-permute-start.15 = (bf16[1024,768]{1,0:T(8,128)(2,1)}, bf16[1024,768]{1,0:T(8,128)(2,1)}, u32[]{:S(2)}, u32[]{:S(2)}) collective-permute-start(bf16[1024,768]{1,0:T(8,128)(2,1)} %add_convert_fusion.1), channel_id=1, source_target_pairs={{0,8},{8,0},{16,24},{24,16},{1,9},{9,1},{17,25},{25,17},{2,10},{10... | collective-permute-start | bytes 4718600 | tf_op jit(solution)/shard_map/ppermute | solution.py:727
  418.5 4.0 collective-permute-start.17
  422.6 62.2 %copy-start.17 = (bf16[2,96,1920]{2,1,0:T(8,128)(2,1)}, bf16[2,96,1920]{2,1,0:T(8,128)(2,1)S(1)}, u32[]{:S(2)}) copy-start(bf16[2,96,1920]{2,1,0:T(8,128)(2,1)S(1)} %maximum_select_fusion.2) | copy-start | bytes 2211844
  486.5 6.0 %copy-start.18 = (bf16[2,192,768]{2,1,0:T(8,128)(2,1)S(1)}, bf16[2,192,768]{2,1,0:T(8,128)(2,1)}, u32[]{:S(2)}) copy-start(bf16[2,192,768]{2,1,0:T(8,128)(2,1)} %maximum_select_fusion.3) | copy-start | bytes 1769476
  486.5 8.8 %copy-start.1 = (bf16[384,768]{1,0:T(8,128)(2,1)S(1)}, bf16[384,768]{1,0:T(8,128)(2,1)}, u32[]{:S(2)}) copy-start(bf16[384,768]{1,0:T(8,128)(2,1)} %param.27) | copy-start | bytes 1769476
  488.9 5.4 %copy-start.20 = (f32[96,2304]{1,0:T(8,128)S(1)}, f32[96,2304]{1,0:T(8,128)}, u32[]{:S(2)}) copy-start(f32[96,2304]{1,0:T(8,128)} %get-tuple-element.188) | copy-start | bytes 2654212
  (18 other events, 55.7 us)
Sparse Core Ops, SparseCore 0:
  11.8 47.1 all-gather.3
  61.7 56.1 all-gather.5
  120.7 51.1 all-gather.7
  232.9 66.6 reduce-scatter.3
  303.0 73.1 reduce-scatter.5
  387.6 64.9 reduce-scatter.7

commit v4 on v3

--- a/solution.py
+++ b/solution.py
@@ -508,6 +508,40 @@
     )(g, w, s)
 
 
+def assemble_kernel(span, inner, core_ref, mine, other, d_mine, d_other, out_ref, up_ref, down_ref):
+    first_core = core_ref[0] == 0
+    pick = lambda one, two: (
+        jnp.where(first_core, one, two).astype(F32), jnp.where(first_core, two, one).astype(F32)
+    )
+    first, second = pick(mine[...].astype(F32), other[...].astype(F32))
+    out_ref[:, :span] = first[:, :span]
+    out_ref[:, span:] = second[:, :span]
+    for i in range((first.shape[1] - span) // inner):
+        cols = slice(span + i * inner, span + (i + 1) * inner)
+        up_ref[:, 2 * i * inner : 2 * (i + 1) * inner] = jnp.concatenate(
+            [first[:, cols], second[:, cols]], 1
+        )
+    first, second = pick(d_mine[...].astype(F32), d_other[...].astype(F32))
+    down_ref[: first.shape[0], :] = first
+    down_ref[first.shape[0] :, :] = second
+
+
+def assemble(core, mine, other, d_mine, d_other, span, inner):
+    rows, width = mine.shape
+    vm = pl.BlockSpec(memory_space=pltpu.VMEM)
+    return pl.pallas_call(
+        functools.partial(assemble_kernel, span, inner),
+        in_specs=[pl.BlockSpec(memory_space=pltpu.SMEM)] + [vm] * 4,
+        out_specs=[vm] * 3,
+        out_shape=[
+            jax.ShapeDtypeStruct((rows, 2 * span), F32),
+            jax.ShapeDtypeStruct((rows, 2 * (width - span)), F32),
+            jax.ShapeDtypeStruct((2 * d_mine.shape[0], d_mine.shape[1]), F32),
+        ],
+        name="assemble",
+    )(core, mine, other, d_mine, d_other)
+
+
 def on_device(
     tokens,
     block_ids,
@@ -538,8 +572,7 @@
     swap = [(0, 1), (1, 0), (2, 3), (3, 2)]
     other = lax.ppermute(tok, "seq", swap)
     clean_in = lax.ppermute(tok, "seq", [(2, 0), (3, 1)])
-    clean_mine = jnp.where(noisy, clean_in, tok)
-    clean_other = lax.ppermute(clean_mine, "seq", swap)
+    cot_far = lax.ppermute(cotangent[0], "seq", swap)
 
     q_cols = lax.dynamic_slice_in_dim(qkv_weight, core * 3 * span, 3 * span, 1)
     small = jnp.concatenate(
@@ -582,7 +615,6 @@
     in_order = lambda near, far, axis: jnp.where(
         core == 0, jnp.concatenate([near, far], axis), jnp.concatenate([far, near], axis)
     )
-    cot_far = lax.ppermute(cotangent[0], "seq", swap)
 
     frequency = jnp.exp(-jnp.log(10000.0) * jnp.arange(HD // 2, dtype=F32) / (HD // 2))
     angles = frequency[:, None] * jnp.arange(length, dtype=F32)[None, :]
@@ -608,6 +640,13 @@
     id_row = jnp.broadcast_to(ids[None, :], (8, length))
     id_col = jnp.broadcast_to(ids[:, None], (length, 128))
 
+    cot_both = jnp.concatenate([cotangent[0], cot_far], 0)
+    clean_in, cot_both, cos_t, sin_t, bounds, id_row, id_col = lax.optimization_barrier(
+        (clean_in, cot_both, cos_t, sin_t, bounds, id_row, id_col)
+    )
+    clean_mine = jnp.where(noisy, clean_in, tok)
+    clean_other = lax.ppermute(clean_mine, "seq", swap)
+
     vec = jnp.concatenate([scale_one[None], shift_one[None], jnp.zeros((6, width), F32)], 0)
     bias_own = lax.dynamic_slice_in_dim(qkv_b, core * 3 * span, 3 * span, 0)
     bias_own = jnp.transpose(bias_own.reshape(heads, 3, HD), (1, 0, 2)).reshape(3 * span, 1)
@@ -616,8 +655,7 @@
         bias_own, cos_t, sin_t, heads
     )
     o, lse = attend(bounds, q, k, v, kc, vc, id_row, id_col, heads, 2)
-    o, lse, out_up, cot_far = lax.optimization_barrier((o, lse, out_up, cot_far))
-    cot_both = jnp.concatenate([cotangent[0], cot_far], 0)
+    o, lse, out_up = lax.optimization_barrier((o, lse, out_up))
     out_near, up_own = out_up[:, :span], out_up[:, span:]
     out_full = in_order(out_near, lax.ppermute(out_near, "seq", swap), 1)
     cut = lambda value, which: lax.dynamic_slice_in_dim(value, which * local_rows, local_rows, 1)
@@ -718,22 +756,30 @@
     got_2 = to_clean(send_2)
     own_1 = joined(own_1, got_1)
     grad_01, own_1 = hold((jnp.concatenate([grad_0, weight_grad(own_1)], 1), own_1))
-    part_01 = scatter(grad_01)
+    exchange = lambda grad: lax.all_to_all(
+        grad.reshape(n_fsdp, shard, grad.shape[1]), "fsdp", 0, 0
+    )
+    piece_sum = lambda pieces: functools.reduce(
+        jnp.add, [pieces[d].astype(F32) for d in range(n_fsdp)]
+    ).astype(BF)
+    pieces_01 = exchange(grad_01)
     own_01 = jnp.concatenate([own_0, own_1], 0)
     first_01 = back(own_01, 0, 2)
     got_2, out_up_part, first_01 = hold((got_2, out_up_part, first_01))
     own_2 = joined(own_2, got_2)
-    far_rows = first_01[local_rows:] + back(own_2[:, local_rows:], 2, 1)
-    got_rows = lax.ppermute(far_rows.astype(BF), "seq", swap).astype(F32)
+    far_rows = (first_01[local_rows:] + back(own_2[:, local_rows:], 2, 1)).astype(BF)
+    got_rows = lax.ppermute(far_rows, "seq", swap).astype(F32)
+    grad_2 = weight_grad(own_2)
     grad_first = first_01[:local_rows] + back(own_2[:, :local_rows], 2, 1) + got_rows
-    grad_2 = weight_grad(own_2)
-
-    def gather_cores(part, far):
+
+    def chip_sum(part, far):
         total = (part.astype(F32) + far.astype(F32)).astype(BF)
-        return in_order(total[None], lax.ppermute(total, "seq", swap)[None], 0)
-
-    down_g = gather_cores(down_part, down_far)
-    out_up_g = gather_cores(out_up_part, lax.ppermute(out_up_part, "seq", cross))
+        return total, lax.ppermute(total, "seq", swap)
+
+    out_up_both = chip_sum(out_up_part, lax.ppermute(out_up_part, "seq", cross))
+    out_g, up_g, down_g = assemble(
+        core.reshape(1).astype(jnp.int32), *out_up_both, *chip_sum(down_part, down_far), span, inner
+    )
 
     sum_cols = lambda own: jnp.sum(own.astype(F32), 1)
     grad_qkv_b = jnp.concatenate([sum_cols(own_01), sum_cols(own_2)])
@@ -760,8 +806,9 @@
     lines = -(-packed.shape[1] // 128)
     packed = jnp.pad(packed, ((0, 0), (0, lines * 128 - packed.shape[1])))
     packed = packed.reshape(n_fsdp, lines, 128)
-    grad_rows, out_up_g, down_g, packed, part_01 = hold(
-        (grad_rows, out_up_g, down_g, packed, part_01)
+    part_01 = piece_sum(pieces_01)
+    grad_rows, out_g, up_g, down_g, packed, part_01 = hold(
+        (grad_rows, out_g, up_g, down_g, packed, part_01)
     )
     qkv_g, small_sum = finish(part_01, grad_2.reshape(n_fsdp, shard, pair_w), packed)
     small_sum = small_sum.reshape(-1)
@@ -769,9 +816,6 @@
     for size in sizes:
         small_out.append(small_sum[at : at + size])
         at += size
-    side = lambda pair: jnp.concatenate([pair[0], pair[1]], 1).astype(F32)
-    out_g, up_g = out_up_g[:, :, :span], out_up_g[:, :, span:]
-    up_g = jnp.transpose(up_g.reshape(2, shard, n_fsdp, inner), (1, 2, 0, 3))
     return (
         result.astype(BF)[None],
         grad_rows[None],
@@ -779,13 +823,13 @@
         small_out[1],
         qkv_g,
         small_out[2],
-        side(out_g),
+        out_g,
         small_out[3],
         small_out[4],
         small_out[5],
-        up_g.reshape(shard, -1).astype(F32),
+        up_g,
         small_out[6],
-        down_g.reshape(2 * inner, width).astype(F32),
+        down_g,
         small_out[7],
     )
 

time: 508 us -> 492 us (0.969)
  waiting for transfers between devices: 69.6 us -> 37.7 us
  Pallas kernels: 212 us -> 227 us
    reduce_scatter x3 -> x2, waiting for transfers between devices: 20.4 us -> 0.03 us  [on_device(): lax.psum_scatter(grad, 'fsdp', scatter_dimension=0, tiled=True)]
    pallas_call x3, Pallas kernels: 99.8 us -> 107 us  [attend_back(): pl.pallas_call(functools.partial(attend_back_kernel, group), grid_spec=pl...]
    convert_element_type x3 -> x0, local copies, waits for them, and re-layouts: 6.43 us -> none  [on_device(): up_g.reshape(shard, -1).astype(F32)]
    all_to_all x0 -> x1, starting transfers between devices: none -> 5.45 us  [on_device(): lax.all_to_all(grad.reshape(n_fsdp, shard, grad.shape[1]), 'fsdp', 0, 0)]
    pallas_call x1, Pallas kernels: 64 us -> 69.1 us  [attend(): pl.pallas_call(functools.partial(attend_kernel, group), grid_spec=pltpu.P...]
    unnamed x85 -> x83, local copies, waits for them, and re-layouts: 11.7 us -> 14.7 us
  transfers between devices with their start and end apart: 25 -> 25, of which waited for: 6 -> 5; matrix products, arithmetic and copies ran while one was open for 22% -> 21% of each run, Pallas kernels for 37% -> 41%
where the time goes in v4:
time: 492 us; the launch traced here: 485 us
  Pallas kernels  227 us (46%)
  matrix products  80.8 us (16%)
  other arithmetic  49.4 us (10%)
  local copies, waits for them, and re-layouts  48.6 us (10%)
  waiting for transfers between devices  37.7 us (8%)
  starting transfers between devices  26.8 us (5%)
  between operations  14.9 us (3%)
    pallas_call x3, Pallas kernels, attend_back(): pl.pallas_call(functools.partial(attend_back_kernel, group), grid_spec=pl...  107 us
    pallas_call x1, Pallas kernels, attend(): pl.pallas_call(functools.partial(attend_kernel, group), grid_spec=pltpu.P...  69.1 us
    ppermute x1, waiting for transfers between devices, on_device(): clean_in = lax.ppermute(tok, 'seq', [(2, 0), (3, 1)])  29.5 us
    pallas_call x1, Pallas kernels, finish(): pl.pallas_call(functools.partial(finish_kernel, n), in_specs=[vm] * 3, ou...  26.9 us
    dot_general x3, matrix products, dot(): return jnp.dot(left, right, preferred_element_type=F32)  24.7 us
    pallas_call x1, Pallas kernels, project(): pl.pallas_call(functools.partial(qkv_kernel, heads), grid_spec=pltpu.Pref...  21.3 us
    dot_general x3, matrix products, right_transposed(): lax.dot_general(left, right, (((1,), (1,)), ((), ())), preferred_element_...  17.6 us
    dot_general x3, matrix products, back(): lax.dot_general(own, cols, (((0,), (1,)), ((), ())), preferred_element_ty...  16.1 us
  transfers between devices with their start and end apart: 25, of which 5 were waited for; matrix products, arithmetic and copies ran while one was open for 21% of the time, Pallas kernels for 41%

profile of v4, /device:TPU:13, one launch (start us, length us, event | category | flops | bytes accessed | tf_op | source)
XLA Modules:
  0.0 485.2 jit_solution(1822981638597324572)
XLA Ops:
  11.7 2.9 reshape.478
  14.6 2.5 dynamic-slice_reduce_fusion
  21.5 1.8 fusion.33
  23.4 3.8 pad_maximum_fusion
  27.1 29.5 %collective-permute-done = bf16[1024,768]{1,0:T(8,128)(2,1)} collective-permute-done((bf16[1024,768]{1,0:T(8,128)(2,1)S(1)}, bf16[1024,768]{1,0:T(8,128)(2,1)}, u32[]{:S(2)}, u32[]{:S(2)}) %collective-permute-start) | collective-permute-done | bytes 1572896 | tf_op jit(solution)/shard_map/ppermute | solution.py:574
  58.6 2.7 broadcast_select_fusion.cmine
  67.3 21.3 %project.1 = (bf16[384,2048]{1,0:T(8,128)(2,1)}, bf16[384,2048]{1,0:T(8,128)(2,1)}, bf16[384,2048]{1,0:T(8,128)(2,1)}, bf16[384,2048]{1,0:T(8,128)(2,1)}, bf16[3...) custom-call(s32[1]{0:T(128)} %bitcast.7.core_ref, bf16[1024,768]{1,0:T(8,128)(2,1)} %bitcast.103, ...), custom_call_target="tpu_custom_call" | custom-call | tf_op jit(solution)/shard_map/project/pallas_call | solution.py:119
  88.7 69.1 %attend.1 = (bf16[384,2048]{1,0:T(8,128)(2,1)}, f32[6,8,2048]{2,1,0:T(8,128)}) custom-call(s32[5,4]{1,0:T(8,128)} %stack.2.bounds, bf16[384,2048]{1,0:T(8,128)(2,1)} %get-tuple-element.81.q, bf16[384,2048]{1,0:T(8,128)(2,1)} %get-tuple-element.82.k, bf16[384,2048]{1,0:T(8,128)(2,1)} %get-tuple-element.83.v, bf16[384,2048]{1,0:T(8,128)(2,1)} %get-tuple-element.84.kc, ...), custom_call_target="tpu_custom_call" | custom-call | flops 25769803776 | bytes 16777216 | tf_op jit(solution)/shard_map/attend/pallas_call | solution.py:237
  157.8 2.5 constant_dynamic-slice_fusion.5
  163.8 3.5 fusion.46
  168.9 1.7 add_convert_fusion.2
  171.8 1.7 collective-permute-start.6
  178.4 15.5 %add_convert_fusion = (bf16[2048,1536]{1,0:T(8,128)(2,1)}, bf16[2048,1536]{1,0:T(8,128)(2,1)S(1)}) fusion(f32[1536]{0:T(1024)S(1)} %add.264, bf16[2048,768]{1,0:T(8,128)(2,1)S(1)} %constant_dynamic-update-slice_fusion, bf16[768,1920]{1,0:T(8,128)(2,1)S(1)} %copy-done.25), kind=kOutput, calls=%fused_computation.2 | convolution fusion | flops 4894752768 | bytes 18096128 | tf_op jit(solution)/shard_map/dot_general | solution.py:49
  193.9 2.6 copy-done.34
  196.5 6.5 %convolution_convert_fusion.1 = bf16[1536,768]{1,0:T(8,128)(2,1)} fusion(bf16[2048,1536]{1,0:T(8,128)(2,1)S(1)} %get-tuple-element.94, bf16[2048,768]{1,0:T(8,128)(2,1)S(1)} %copy-done.14), kind=kOutput, calls=%fused_computation.18 | convolution fusion | flops 4833017856 | bytes 11796480 | tf_op jit(solution)/shard_map/dot_general | solution.py:41
  203.0 9.5 %convert_reduce_fusion = (f32[1536]{0:T(1024)S(1)}, bf16[2048,1536]{1,0:T(8,128)(2,1)S(1)}) fusion(bf16[2048,1536]{1,0:T(8,128)(2,1)} %get-tuple-element.97, bf16[2048,768]{1,0:T(8,128)(2,1)} %pad_maximum_fusion, bf16[1536,768]{1,0:T(8,128)(2,1)} %all-gather.8.cloned.1.call-done), kind=kOutput, calls=%fused_computation | convolution fusion | flops 4847565312 | bytes 18094080 | tf_op jit(solution)/shard_map/dot_general | solution.py:45
  212.6 5.2 %fusion.18 = f32[2048,768]{1,0:T(8,128)S(1)} fusion(bf16[2048,1536]{1,0:T(8,128)(2,1)S(1)} %get-tuple-element.185, bf16[768,1920]{1,0:T(8,128)(2,1)S(1)} %copy-done.26), kind=kOutput, calls=%fused_computation.53 | convolution fusion | flops 4831838208 | bytes 14942208 | tf_op jit(solution)/shard_map/dot_general | solution.py:45
  219.5 1.7 copy-done.32
  221.2 5.2 %fusion.47 = f32[2048,768]{1,0:T(8,128)S(1)} fusion(bf16[2048,1536]{1,0:T(8,128)(2,1)S(1)} %bitcast.143, bf16[1536,768]{1,0:T(8,128)(2,1)S(1)} %copy-done.32), kind=kOutput, calls=%fused_computation.163 | convolution fusion | flops 4831838208 | bytes 14942208 | tf_op jit(solution)/shard_map/dot_general | solution.py:49
  230.1 4.5 multiply_reduce_fusion
  234.7 5.9 %convert_reduce_fusion.4 = (f32[768]{0:T(1024)S(1)}, f32[1024,768]{1,0:T(8,128)S(1)}, bf16[1,1024,768]{2,1,0:T(8,128)(2,1)}, f32[768]{0:T(1024)S(1)}) fusion(f32[1024]{0:T(1024)S(1)} %broadcast_multiply_fusion.3, f32[1024,768]{1,0:T(8,128)S(1)} %copy-done.5, f32[1024]{0:T(1024)S(1)} %broadcast_multiply_fusion.5, f32[1024]{0:T(1024)S(1)} %broadcast_multiply_fusion.4, ...), kind=kLoop, calls=%fused_computation.36 | loop fusion | flops 15727104 | bytes 18903040 | tf_op jit(solution)/shard_map/reduce_sum | solution.py:706
  240.6 4.0 convolution_convert_fusion.3
  244.9 2.8 convolution_convert_fusion.2
  250.0 5.4 %convolution_convert_fusion = bf16[768,1536]{1,0:T(8,128)(2,1)S(1)} fusion(bf16[2048,768]{1,0:T(8,128)(2,1)S(1)} %copy-done.19, bf16[2048,1536]{1,0:T(8,128)(2,1)S(1)} %bitcast.145), kind=kOutput, calls=%fused_computation.17 | convolution fusion | flops 4833017856 | bytes 11796480 | tf_op jit(solution)/shard_map/dot_general | solution.py:41
  255.6 1.9 pad_maximum_fusion.2
  258.4 35.7 %attend_back.3 = (bf16[384,2048]{1,0:T(8,128)(2,1)}, bf16[256,2048]{1,0:T(8,128)(2,1)}) custom-call(s32[5,4]{1,0:T(8,128)} %stack.2.bounds, bf16[384,2048]{1,0:T(8,128)(2,1)} %get-tuple-element.81.q, bf16[384,2048]{1,0:T(8,128)(2,1)} %get-tuple-element.82.k, bf16[384,2048]{1,0:T(8,128)(2,1)} %get-tuple-element.83.v, bf16[384,2048]{1,0:T(8,128)(2,1)} %get-tuple-element.84.kc, ...), custom_call_target="tpu_custom_call" | custom-call | flops 10737418240 | bytes 8388608 | tf_op jit(solution)/shard_map/attend_back/pallas_call | solution.py:369
  297.2 35.4 %attend_back.4 = (bf16[384,2048]{1,0:T(8,128)(2,1)}, bf16[256,2048]{1,0:T(8,128)(2,1)}) custom-call(s32[5,4]{1,0:T(8,128)} %stack.2.bounds, bf16[384,2048]{1,0:T(8,128)(2,1)} %get-tuple-element.81.q, bf16[384,2048]{1,0:T(8,128)(2,1)} %get-tuple-element.82.k, bf16[384,2048]{1,0:T(8,128)(2,1)} %get-tuple-element.83.v, bf16[384,2048]{1,0:T(8,128)(2,1)} %get-tuple-element.84.kc, ...), custom_call_target="tpu_custom_call" | custom-call | flops 10737418240 | bytes 8388608 | tf_op jit(solution)/shard_map/attend_back/pallas_call | solution.py:369
  332.7 4.7 collective-permute-start.12
  337.4 1.8 fusion.17
  340.5 2.7 convolution_convert_fusion.6
  343.2 35.7 %attend_back.5 = (bf16[384,2048]{1,0:T(8,128)(2,1)}, bf16[256,2048]{1,0:T(8,128)(2,1)}) custom-call(s32[5,4]{1,0:T(8,128)} %stack.2.bounds, bf16[384,2048]{1,0:T(8,128)(2,1)} %get-tuple-element.81.q, bf16[384,2048]{1,0:T(8,128)(2,1)} %get-tuple-element.82.k, bf16[384,2048]{1,0:T(8,128)(2,1)} %get-tuple-element.83.v, bf16[384,2048]{1,0:T(8,128)(2,1)} %get-tuple-element.84.kc, ...), custom_call_target="tpu_custom_call" | custom-call | flops 10737418240 | bytes 8388608 | tf_op jit(solution)/shard_map/attend_back/pallas_call | solution.py:369
  381.8 2.1 fusion.16
  386.1 2.3 collective-permute-start.14
  388.5 1.8 convolution_convert_fusion.5
  391.5 5.4 %all-to-all-start = ((bf16[8,96,768]{2,1,0:T(8,128)(2,1)}), bf16[8,96,768]{2,1,0:T(8,128)(2,1)}, u32[]{:S(2)}, u32[]{:S(2)}) async-start(bf16[8,96,768]{2,1,0:T(8,128)(2,1)} %bitcast.31), calls=%async_computation.2 | async-start | bytes 2359296 | tf_op jit(solution)/shard_map/all_to_all | solution.py:759
  397.0 2.5 convert_reduce_fusion.1
  399.5 7.2 %fusion.22 = f32[2048,768]{1,0:T(8,128)} fusion(bf16[384,2048]{1,0:T(8,128)(2,1)S(1)} %bitcast.113, bf16[384,2048]{1,0:T(8,128)(2,1)} %bitcast.110, bf16[768,1280]{1,0:T(8,128)(2,1)} %all-gather.4.cloned.1.call-done.w_ref), kind=kOutput, calls=%fused_computation.57 | convolution fusion | flops 2422210560 | bytes 10616832 | tf_op jit(solution)/shard_map/dot_general | solution.py:740
  406.7 3.7 collective-permute-done.14
  412.4 2.2 collective-permute-start.16
  414.8 4.9 %add_convert_fusion.1 = bf16[1024,768]{1,0:T(8,128)(2,1)} fusion(f32[2048,768]{1,0:T(8,128)} %fusion.22, bf16[384,2048]{1,0:T(8,128)(2,1)S(1)} %bitcast.114, bf16[768,1280]{1,0:T(8,128)(2,1)} %all-gather.4.cloned.1.call-done.w_ref), kind=kOutput, calls=%fused_computation.39 | convolution fusion | flops 605552640 | bytes 6094848 | tf_op jit(solution)/shard_map/dot_general | solution.py:740
  420.6 2.7 convolution_convert_fusion.4
  424.7 4.0 fusion.29
  429.5 2.9 assemble.1
  432.4 2.1 fusion.35.g
  434.6 5.3 %fusion.9 = (f32[768]{0:T(1024)S(1)}, f32[1024]{0:T(1024)S(1)}, f32[1024]{0:T(1024)S(1)}, f32[768]{0:T(1024)S(1)}, f32[1024,768]{1,0:T(8,128)}) fusion(f32[1024]{0:T(1024)S(1)} %add_rsqrt_fusion, f32[1024]{0:T(1024)S(1)} %broadcast_multiply_fusion.2, bf16[1,1024,768]{2,1,0:T(8,128)(2,1)S(1)} %copy-done.3, f32[768]{0:T(1024)S(1)} %mul.218, ...), kind=kLoop, calls=%fused_computation.23 | loop fusion | flops 10220032 | bytes 12608512 | tf_op jit(solution)/shard_map/reduce_sum | solution.py:787
  440.2 4.6 fusion.8
  445.4 26.9 %finish.1 = (f32[96,2304]{1,0:T(8,128)}, f32[10,128]{1,0:T(8,128)}) custom-call(bf16[96,768]{1,0:T(8,128)(2,1)} %fusion.35.g, bf16[8,96,384]{2,1,0:T(8,128)(2,1)} %bitcast.126, f32[8,10,128]{2,1,0:T(8,128)} %copy.68.s), custom_call_target="tpu_custom_call" | custom-call | tf_op jit(solution)/shard_map/finish/pallas_call | solution.py:477
  476.4 2.1 copy.77
  (224 shorter events, 57.9 us)
Async XLA Ops:
  7.2 55.4 %copy-start = (bf16[384,768]{1,0:T(8,128)(2,1)S(1)}, bf16[384,768]{1,0:T(8,128)(2,1)}, u32[]{:S(2)}) copy-start(bf16[384,768]{1,0:T(8,128)(2,1)} %param.27) | copy-start | bytes 1769476
  7.2 10.3 %copy-start.28 = (bf16[96,768]{1,0:T(8,128)(2,1)S(1)}, bf16[96,768]{1,0:T(8,128)(2,1)}, u32[]{:S(2)}) copy-start(bf16[96,768]{1,0:T(8,128)(2,1)} %param.21) | copy-start | bytes 442372
  7.2 11.9 %copy-start.2 = (bf16[1,1024,768]{2,1,0:T(8,128)(2,1)S(1)}, bf16[1,1024,768]{2,1,0:T(8,128)(2,1)}, u32[]{:S(2)}) copy-start(bf16[1,1024,768]{2,1,0:T(8,128)(2,1)} %param.15) | copy-start | bytes 4718596
  7.2 13.2 %copy-start.27 = (s32[1,2048]{1,0:T(1,128)S(1)}, s32[1,2048]{1,0:T(1,128)}, u32[]{:S(2)}) copy-start(s32[1,2048]{1,0:T(1,128)} %param.16) | copy-start | bytes 24580
  7.2 56.5 %all-gather.4.cloned.1.call-start = ((), (), s32[]{:S(2)}) async-start(), calls=%async_computation.3 | async-start | bytes 2211840 | tf_op jit(solution)/shard_map/all_gather | solution.py:593
  11.7 146.1 %all-gather.6.cloned.1.call-start = ((), (), s32[]{:S(2)}) async-start(), calls=%async_computation.4 | async-start | bytes 3317760 | tf_op jit(solution)/shard_map/all_gather | solution.py:611
  18.3 153.6 %all-gather.8.cloned.1.call-start = ((), (), s32[]{:S(2)}) async-start(), calls=%async_computation.5 | async-start | bytes 2654208 | tf_op jit(solution)/shard_map/all_gather | solution.py:614
  18.3 5.0 %collective-permute-start.1 = (bf16[1024,768]{1,0:T(8,128)(2,1)}, bf16[1024,768]{1,0:T(8,128)(2,1)}, u32[]{:S(2)}, u32[]{:S(2)}) collective-permute-start(bf16[1024,768]{1,0:T(8,128)(2,1)} %bitcast.106), channel_id=1, source_target_pairs={{0,8},{8,0},{16,24},{24,16},{1,9},{9,1},{17,25},{25,17},{2,10},{10... | collective-permute-start | bytes 4718600 | tf_op jit(solution)/shard_map/ppermute | solution.py:575
  19.1 48.3 %collective-permute-start.2 = (bf16[1024,768]{1,0:T(8,128)(2,1)S(1)}, bf16[1024,768]{1,0:T(8,128)(2,1)}, u32[]{:S(2)}, u32[]{:S(2)}) collective-permute-start(bf16[1024,768]{1,0:T(8,128)(2,1)S(1)} %bitcast.104), channel_id=1, source_target_pairs={{0,8},{8,0},{16,24},{24,16},{1,9},{9,1},{17,25},{25,17},{2,10},{10... | collective-permute-start | bytes 4718600 | tf_op jit(solution)/shard_map/ppermute | solution.py:573
  19.2 37.5 %collective-permute-start = (bf16[1024,768]{1,0:T(8,128)(2,1)S(1)}, bf16[1024,768]{1,0:T(8,128)(2,1)}, u32[]{:S(2)}, u32[]{:S(2)}) collective-permute-start(bf16[1024,768]{1,0:T(8,128)(2,1)S(1)} %bitcast.105), channel_id=1, source_target_pairs={{16,0},{24,8},{17,1},{25,9},{18,2},{26,10},{19,3},{27,11},{20,4},{... | collective-permute-start | bytes 4718600 | tf_op jit(solution)/shard_map/ppermute | solution.py:574
  61.3 6.0 %collective-permute-start.3 = (bf16[1024,768]{1,0:T(8,128)(2,1)}, bf16[1024,768]{1,0:T(8,128)(2,1)}, u32[]{:S(2)}, u32[]{:S(2)}) collective-permute-start(bf16[1024,768]{1,0:T(8,128)(2,1)} %broadcast_select_fusion.cmine), channel_id=1, source_target_pairs={{0,8},{8,0},{16,24},{24,16},{1,9},{9,1},{17,25},{25,17},{2,10},{10... | collective-permute-start | bytes 4718600 | tf_op jit(solution)/shard_map/ppermute | solution.py:648
  63.4 269.2 %reduce-scatter.3.cloned.1.call-start = ((), (), s32[]{:S(2)}) async-start(), calls=%async_computation.6 | async-start | bytes 2654208 | tf_op jit(solution)/shard_map/reduce_scatter | solution.py:687
  157.8 6.0 %copy-start.3 = (bf16[1,1024,768]{2,1,0:T(8,128)(2,1)S(1)}, bf16[1,1024,768]{2,1,0:T(8,128)(2,1)}, u32[]{:S(2)}) copy-start(bf16[1,1024,768]{2,1,0:T(8,128)(2,1)} %param.15) | copy-start | bytes 4718596
  160.3 3.5 collective-permute-start.4
  161.4 2.3 collective-permute-start.5
  171.8 5.1 %collective-permute-start.6 = (bf16[1024,768]{1,0:T(8,128)(2,1)}, bf16[1024,768]{1,0:T(8,128)(2,1)}, u32[]{:S(2)}, u32[]{:S(2)}) collective-permute-start(bf16[1024,768]{1,0:T(8,128)(2,1)} %add_convert_fusion.2), channel_id=1, source_target_pairs={{0,8},{8,0},{16,24},{24,16},{1,9},{9,1},{17,25},{25,17},{2,10},{10... | collective-permute-start | bytes 4718600 | tf_op jit(solution)/shard_map/ppermute | solution.py:671
  173.7 4.7 copy-start.25
  178.4 15.5 %copy-start.18 = (bf16[2048,768]{1,0:T(8,128)(2,1)}, bf16[2048,768]{1,0:T(8,128)(2,1)S(1)}, u32[]{:S(2)}) copy-start(bf16[2048,768]{1,0:T(8,128)(2,1)S(1)} %constant_dynamic-update-slice_fusion) | copy-start | bytes 9437188
  178.4 18.1 %copy-start.14 = (bf16[2048,768]{1,0:T(8,128)(2,1)S(1)}, bf16[2048,768]{1,0:T(8,128)(2,1)}, u32[]{:S(2)}) copy-start(bf16[2048,768]{1,0:T(8,128)(2,1)} %pad_maximum_fusion) | copy-start | bytes 9437188
  203.0 9.5 %copy-start.26 = (bf16[768,1920]{1,0:T(8,128)(2,1)S(1)}, bf16[768,1920]{1,0:T(8,128)(2,1)}, u32[]{:S(2)}) copy-start(bf16[768,1920]{1,0:T(8,128)(2,1)} %all-gather.6.cloned.1.call-done) | copy-start | bytes 8847364
  203.0 16.5 %slice-start = ((s8[6291456]{0:T(1024)(128)(4,1)}), s8[4194304]{0:T(1024)(128)(4,1)S(1)}, s32[]{:S(2)}) async-start(s8[6291456]{0:T(1024)(128)(4,1)} %bitcast.142), calls=%async_computation.8 | async-start | bytes 8388608
  212.5 5.3 %copy-start.35 = (bf16[2048,1536]{1,0:T(8,128)(2,1)}, bf16[2048,1536]{1,0:T(8,128)(2,1)S(1)}, u32[]{:S(2)}) copy-start(bf16[2048,1536]{1,0:T(8,128)(2,1)S(1)} %get-tuple-element.185) | copy-start | bytes 18874372
  212.5 7.0 %slice-start.1 = ((s8[6291456]{0:T(1024)(128)(4,1)}), s8[2097152]{0:T(1024)(128)(4,1)S(1)}, s32[]{:S(2)}) async-start(s8[6291456]{0:T(1024)(128)(4,1)} %bitcast.142), calls=%async_computation.9 | async-start | bytes 4194304
  217.8 8.6 %copy-start.7 = (f32[2048,768]{1,0:T(8,128)}, f32[2048,768]{1,0:T(8,128)S(1)}, u32[]{:S(2)}) copy-start(f32[2048,768]{1,0:T(8,128)S(1)} %fusion.18) | copy-start | bytes 18874372
  219.1 10.9 %collective-permute-start.8 = (bf16[1024,768]{1,0:T(8,128)(2,1)}, bf16[1024,768]{1,0:T(8,128)(2,1)}, u32[]{:S(2)}, u32[]{:S(2)}) collective-permute-start(bf16[1024,768]{1,0:T(8,128)(2,1)} %slice.309), channel_id=1, source_target_pairs={{0,8},{8,0},{16,24},{24,16},{1,9},{9,1},{17,25},{25,17},{2,10},{10... | collective-permute-start | bytes 4718600 | tf_op jit(solution)/shard_map/ppermute | solution.py:674
  229.5 5.1 %collective-permute-start.7 = (bf16[1024,768]{1,0:T(8,128)(2,1)}, bf16[1024,768]{1,0:T(8,128)(2,1)}, u32[]{:S(2)}, u32[]{:S(2)}) collective-permute-start(bf16[1024,768]{1,0:T(8,128)(2,1)} %slice.310), channel_id=1, source_target_pairs={{0,8},{8,0},{16,24},{24,16},{1,9},{9,1},{17,25},{25,17},{2,10},{10... | collective-permute-start | bytes 4718600 | tf_op jit(solution)/shard_map/ppermute | solution.py:674
  230.0 150.1 %reduce-scatter.5.cloned.1.call-start = ((), (), s32[]{:S(2)}) async-start(), calls=%async_computation.7 | async-start | bytes 3317760 | tf_op jit(solution)/shard_map/reduce_scatter | solution.py:687
  230.0 4.7 copy-start.8
  240.6 8.6 %slice-start.2 = ((s8[6291456]{0:T(1024)(128)(4,1)}), s8[4194304]{0:T(1024)(128)(4,1)S(1)}, s32[]{:S(2)}) async-start(s8[6291456]{0:T(1024)(128)(4,1)} %bitcast.144), calls=%async_computation.10 | async-start | bytes 8388608
  244.7 10.7 %collective-permute-start.10 = (bf16[768,384]{1,0:T(8,128)(2,1)S(1)}, bf16[768,384]{1,0:T(8,128)(2,1)S(1)}, u32[]{:S(2)}, u32[]{:S(2)}) collective-permute-start(bf16[768,384]{1,0:T(8,128)(2,1)S(1)} %constant_dynamic-slice_fusion), channel_id=1, source_target_pairs={{0,8},{8,0},{16,24},{24,16},{1,9},{9,1},{17,25},{25,17},{2,10},{10... | collective-permute-start | bytes 1769480 | tf_op jit(solution)/shard_map/ppermute | solution.py:713
  248.7 6.8 %collective-permute-start.9 = (bf16[384,1024]{1,0:T(8,128)(2,1)S(1)}, bf16[384,1024]{1,0:T(8,128)(2,1)S(1)}, u32[]{:S(2)}, u32[]{:S(2)}) collective-permute-start(bf16[384,1024]{1,0:T(8,128)(2,1)S(1)} %get-tuple-element.165), channel_id=1, source_target_pairs={{0,8},{8,0},{16,24},{24,16},{1,9},{9,1},{17,25},{25,17},{2,10},{10... | collective-permute-start | bytes 2359304 | tf_op jit(solution)/shard_map/ppermute | solution.py:710
  294.1 38.5 %collective-permute-start.11 = (bf16[256,2048]{1,0:T(8,128)(2,1)}, bf16[256,2048]{1,0:T(8,128)(2,1)S(1)}, u32[]{:S(2)}, u32[]{:S(2)}) collective-permute-start(bf16[256,2048]{1,0:T(8,128)(2,1)} %get-tuple-element.107), channel_id=1, source_target_pairs={{0,16},{8,24},{1,17},{9,25},{2,18},{10,26},{3,19},{11,27},{4,20},{... | collective-permute-start | bytes 3145736 | tf_op jit(solution)/shard_map/ppermute | solution.py:725
  332.6 47.4 %collective-permute-start.13 = (bf16[192,768]{1,0:T(8,128)(2,1)}, bf16[192,768]{1,0:T(8,128)(2,1)S(1)}, u32[]{:S(2)}, u32[]{:S(2)}) collective-permute-start(bf16[192,768]{1,0:T(8,128)(2,1)} %reduce-scatter.3.cloned.1.call-done), channel_id=1, source_target_pairs={{0,16},{8,24},{16,0},{24,8},{1,17},{9,25},{17,1},{25,9},{2,18},{10... | collective-permute-start | bytes 884744 | tf_op jit(solution)/shard_map/ppermute | solution.py:749
  332.7 47.3 %collective-permute-start.12 = (bf16[256,2048]{1,0:T(8,128)(2,1)}, bf16[256,2048]{1,0:T(8,128)(2,1)}, u32[]{:S(2)}, u32[]{:S(2)}) collective-permute-start(bf16[256,2048]{1,0:T(8,128)(2,1)} %get-tuple-element.113), channel_id=1, source_target_pairs={{0,16},{8,24},{1,17},{9,25},{2,18},{10,26},{3,19},{11,27},{4,20},{... | collective-permute-start | bytes 3145736 | tf_op jit(solution)/shard_map/ppermute | solution.py:725
  343.2 37.5 %copy-start.23 = (bf16[192,768]{1,0:T(8,128)(2,1)S(1)}, bf16[192,768]{1,0:T(8,128)(2,1)}, u32[]{:S(2)}) copy-start(bf16[192,768]{1,0:T(8,128)(2,1)} %reduce-scatter.3.cloned.1.call-done) | copy-start | bytes 884740
  381.7 6.7 %copy-start.17 = (bf16[192,768]{1,0:T(8,128)(2,1)}, bf16[192,768]{1,0:T(8,128)(2,1)S(1)}, u32[]{:S(2)}) copy-start(bf16[192,768]{1,0:T(8,128)(2,1)S(1)} %add_convert_fusion.5.d_mine) | copy-start | bytes 884740
  381.7 6.8 %copy-start.30 = (bf16[2048,768]{1,0:T(8,128)(2,1)S(1)}, bf16[2048,768]{1,0:T(8,128)(2,1)}, u32[]{:S(2)}) copy-start(bf16[2048,768]{1,0:T(8,128)(2,1)} %get-tuple-element.99) | copy-start | bytes 9437188
  383.8 44.9 %collective-permute-start.18 = (bf16[192,768]{1,0:T(8,128)(2,1)S(1)}, bf16[192,768]{1,0:T(8,128)(2,1)}, u32[]{:S(2)}, u32[]{:S(2)}) collective-permute-start(bf16[192,768]{1,0:T(8,128)(2,1)S(1)} %add_convert_fusion.5.d_mine), channel_id=1, source_target_pairs={{0,8},{8,0},{16,24},{24,16},{1,9},{9,1},{17,25},{25,17},{2,10},{10... | collective-permute-start | bytes 884744 | tf_op jit(solution)/shard_map/ppermute | solution.py:777
  386.1 24.4 %collective-permute-start.14 = (bf16[256,2048]{1,0:T(8,128)(2,1)}, bf16[256,2048]{1,0:T(8,128)(2,1)}, u32[]{:S(2)}, u32[]{:S(2)}) collective-permute-start(bf16[256,2048]{1,0:T(8,128)(2,1)} %get-tuple-element.117), channel_id=1, source_target_pairs={{0,16},{8,24},{1,17},{9,25},{2,18},{10,26},{3,19},{11,27},{4,20},{... | collective-permute-start | bytes 3145736 | tf_op jit(solution)/shard_map/ppermute | solution.py:725
  391.5 40.9 %all-to-all-start = ((bf16[8,96,768]{2,1,0:T(8,128)(2,1)}), bf16[8,96,768]{2,1,0:T(8,128)(2,1)}, u32[]{:S(2)}, u32[]{:S(2)}) async-start(bf16[8,96,768]{2,1,0:T(8,128)(2,1)} %bitcast.31), calls=%async_computation.2 | async-start | bytes 2359296 | tf_op jit(solution)/shard_map/all_to_all | solution.py:759
  399.5 10.9 %copy-start.15 = (bf16[384,2048]{1,0:T(8,128)(2,1)S(1)}, bf16[384,2048]{1,0:T(8,128)(2,1)}, u32[]{:S(2)}) copy-start(bf16[384,2048]{1,0:T(8,128)(2,1)} %get-tuple-element.124) | copy-start | bytes 4718596
  412.4 10.8 %collective-permute-start.16 = (bf16[96,1920]{1,0:T(8,128)(2,1)}, bf16[96,1920]{1,0:T(8,128)(2,1)S(1)}, u32[]{:S(2)}, u32[]{:S(2)}) collective-permute-start(bf16[96,1920]{1,0:T(8,128)(2,1)} %reduce-scatter.5.cloned.1.call-done), channel_id=1, source_target_pairs={{0,16},{8,24},{16,0},{24,8},{1,17},{9,25},{17,1},{25,9},{2,18},{10... | collective-permute-start | bytes 1105928 | tf_op jit(solution)/shard_map/ppermute | solution.py:779
  414.8 8.4 %copy-start.12 = (bf16[2,3,64,2048]{3,2,1,0:T(8,128)(2,1)}, bf16[2,3,64,2048]{3,2,1,0:T(8,128)(2,1)S(1)}, u32[]{:S(2)}) copy-start(bf16[2,3,64,2048]{3,2,1,0:T(8,128)(2,1)S(1)} %pad_maximum_fusion.6) | copy-start | bytes 4718596
  414.8 5.8 %copy-start.31 = (bf16[2048,768]{1,0:T(8,128)(2,1)S(1)}, bf16[2048,768]{1,0:T(8,128)(2,1)}, u32[]{:S(2)}) copy-start(bf16[2048,768]{1,0:T(8,128)(2,1)} %get-tuple-element.99) | copy-start | bytes 9437188
  419.7 14.9 %collective-permute-start.15 = (bf16[1024,768]{1,0:T(8,128)(2,1)}, bf16[1024,768]{1,0:T(8,128)(2,1)}, u32[]{:S(2)}, u32[]{:S(2)}) collective-permute-start(bf16[1024,768]{1,0:T(8,128)(2,1)} %add_convert_fusion.1), channel_id=1, source_target_pairs={{0,8},{8,0},{16,24},{24,16},{1,9},{9,1},{17,25},{25,17},{2,10},{10... | collective-permute-start | bytes 4718600 | tf_op jit(solution)/shard_map/ppermute | solution.py:771
  423.3 5.4 %copy-start.16 = (bf16[96,1920]{1,0:T(8,128)(2,1)}, bf16[96,1920]{1,0:T(8,128)(2,1)S(1)}, u32[]{:S(2)}) copy-start(bf16[96,1920]{1,0:T(8,128)(2,1)S(1)} %add_convert_fusion.4.mine) | copy-start | bytes 1105924
  423.3 5.4 %collective-permute-start.17 = (bf16[96,1920]{1,0:T(8,128)(2,1)S(1)}, bf16[96,1920]{1,0:T(8,128)(2,1)S(1)}, u32[]{:S(2)}, u32[]{:S(2)}) collective-permute-start(bf16[96,1920]{1,0:T(8,128)(2,1)S(1)} %add_convert_fusion.4.mine), channel_id=1, source_target_pairs={{0,8},{8,0},{16,24},{24,16},{1,9},{9,1},{17,25},{25,17},{2,10},{10... | collective-permute-start | bytes 1105928 | tf_op jit(solution)/shard_map/ppermute | solution.py:777
  440.2 38.4 %copy-start.1 = (bf16[384,768]{1,0:T(8,128)(2,1)S(1)}, bf16[384,768]{1,0:T(8,128)(2,1)}, u32[]{:S(2)}) copy-start(bf16[384,768]{1,0:T(8,128)(2,1)} %param.27) | copy-start | bytes 1769476
  (17 other events, 43.8 us)
Sparse Core Ops, SparseCore 0:
  11.8 47.1 all-gather.3
  61.7 56.1 all-gather.5
  120.7 51.1 all-gather.7
  230.1 66.3 reduce-scatter.2
  299.9 73.2 reduce-scatter.4

commit v5 on v4

--- a/solution.py
+++ b/solution.py
@@ -16,6 +16,7 @@
 TQ = 512
 TK = 256
 TM = 256
+FK = 1024
 BF = jnp.bfloat16
 F32 = jnp.float32
 
@@ -49,7 +50,7 @@
     return jnp.dot(left, right, preferred_element_type=F32)
 
 
-def qkv_kernel(heads, core_ref, mine, other, cmine, cother, w_ref, vec_ref, bias_ref, cos_ref,
+def qkv_kernel(heads, core_ref, mine, other, mine_c, other_c, sent, sent_other, w_ref, vec_ref, bias_ref, cos_ref,
                sin_ref, q_out, k_out, v_out, kc_out, vc_out, a_out, wt):
     step = pl.program_id(0)
     span = heads * HD
@@ -90,13 +91,15 @@
 
     @pl.when(step >= 2 * quarter)
     def _():
-        a = normed(jnp.where(step < 3 * quarter, cmine[...], cother[...]))
+        here = jnp.where(step < 3 * quarter, mine_c[...], other_c[...])
+        there = jnp.where(step < 3 * quarter, sent[...], sent_other[...])
+        a = normed(jnp.where(core_ref[1] == 1, there, here))
         lin = right_transposed(wt[span:, :], a) + bias_ref[span:, :]
         turn(lin, 0, kc_out)
         vc_out[...] = lin[span:, :].astype(BF)
 
 
-def project(core, mine, other, cmine, cother, weight, vec, bias, cos_t, sin_t, heads):
+def project(core, mine, other, sent, sent_other, weight, vec, bias, cos_t, sin_t, heads):
     local, width = mine.shape
     span = heads * HD
     tile = 256
@@ -121,14 +124,14 @@
         grid_spec=pltpu.PrefetchScalarGridSpec(
             num_scalar_prefetch=1,
             grid=(4 * n,),
-            in_specs=[src(0), src(1), src(2), src(3), whole((width, 3 * span)), whole(vec.shape),
+            in_specs=[src(0), src(1)] + [src(2), src(3)] * 2 + [whole((width, 3 * span)), whole(vec.shape),
                       whole(bias.shape), tab, tab],
             out_specs=[own, own, own, cln, cln, own_a],
             scratch_shapes=[pltpu.VMEM((3 * span, width), BF)],
         ),
         out_shape=[head_shape] * 5 + [row_shape],
         name="project",
-    )(core, mine, other, cmine, cother, weight, vec, bias, cos_t, sin_t)
+    )(core, mine, other, mine, other, sent, sent_other, weight, vec, bias, cos_t, sin_t)
 
 
 def attend_kernel(group, bounds, q, k, v, kc, vc, id_row, id_col, o_out, lse_out, ks, kcs, vs,
@@ -161,20 +164,20 @@
 
     def sweep(i, q_ids, update, state):
         def band(j, state):
-            keys = pl.ds(pl.multiple_of(j * TM, TM), TM)
+            keys = pl.ds(pl.multiple_of(j * FK, FK), FK)
             return update(state, ks, vs, keys, key_ids(keys) == q_ids)
 
         def full(j, state):
-            keys = pl.ds(pl.multiple_of(j * TK, TK), TK)
+            keys = pl.ds(pl.multiple_of(j * FK, FK), FK)
             return update(state, kcs, vcs, keys, None)
 
         def edge(j, state):
-            keys = pl.ds(pl.multiple_of(j * TM, TM), TM)
+            keys = pl.ds(pl.multiple_of(j * FK, FK), FK)
             return update(state, kcs, vcs, keys, key_ids(keys) < q_ids + lift)
 
         state = lax.fori_loop(bounds[2, i], bounds[3, i], band, state)
         state = lax.fori_loop(0, bounds[0, i], full, state)
-        return lax.fori_loop(bounds[0, i] * (TK // TM), bounds[1, i], edge, state)
+        return lax.fori_loop(bounds[0, i], bounds[1, i], edge, state)
 
     def store(h, at, acc, log_shift):
         total_w = acc[HD : HD + 1, :]
@@ -388,8 +391,8 @@
     )(bounds, q, k, v, kc, vc, o, lse, do_mine, do_other, id_row, id_col, cos_t, sin_t)
 
 
-def finish_kernel(n, g, w, s, g_out, s_out, w_in, s_in, g_x, w_x, s_x, g_c, s_c, g_t, w_t, s_t,
-                  w_send, w_recv, s_send, s_recv, x_send, x_recv, c_send, c_recv, local):
+def finish_kernel(n, g, s, g_out, s_out, s_in, g_x, s_x, g_c, s_c, g_t, s_t, s_send, s_recv,
+                  x_send, x_recv, c_send, c_recv, local):
     me = lax.axis_index("fsdp")
     seat = lax.axis_index("seq")
     core = lax.rem(seat, 2)
@@ -415,17 +418,13 @@
         copy.start()
         copy.wait()
 
-    first_s, first_w = [], []
-    for d in range(1, n):
-        to = lax.rem(me + d, n)
-        first_s.append(
-            push(s.at[to], s_in.at[d - 1], s_send.at[d - 1], s_recv.at[d - 1], peers[d - 1])
-        )
-        first_w.append(
-            push(w.at[to], w_in.at[d - 1], w_send.at[d - 1], w_recv.at[d - 1], peers[d - 1])
-        )
+    first = [
+        push(s.at[lax.rem(me + d, n)], s_in.at[d - 1], s_send.at[d - 1], s_recv.at[d - 1],
+             peers[d - 1])
+        for d in range(1, n)
+    ]
     far_g = push(g, g_x, x_send.at[0], x_recv.at[0], across)
-    for copy in first_s:
+    for copy in first:
         copy.wait()
     total = s[me]
     for d in range(n - 1):
@@ -433,79 +432,53 @@
     s_t[0] = total
     settle(s_t.at[0], s_x.at[0], local.at[0])
     far_s = push(s_x.at[0], s_x.at[1], x_send.at[1], x_recv.at[1], across)
-    split = g.shape[1]
-    span = split + w.shape[2]
     far_g.wait()
-    g_t[:, :split] = (g[...].astype(F32) + g_x[...].astype(F32)).astype(BF)
+    g_t[...] = (g[...].astype(F32) + g_x[...].astype(F32)).astype(BF)
+    settle(g_t, g_c.at[core], local.at[1])
+    near_g = push(g_c.at[core], g_c.at[core], c_send.at[0], c_recv.at[0], beside)
     far_s.wait()
     s_t[1] = s_x[0] + s_x[1]
-    settle(s_t.at[1], s_c.at[0], local.at[1])
+    settle(s_t.at[1], s_c.at[0], local.at[2])
     near_s = push(s_c.at[0], s_c.at[1], c_send.at[1], c_recv.at[1], beside)
-    for copy in first_w:
-        copy.wait()
-    rows = w.shape[1]
-    block = 16 if rows % 16 == 0 else rows
-
-    def add_rows(i, _):
-        at = pl.ds(pl.multiple_of(i * block, block), block)
-        total = w[me, at, :].astype(F32)
-        for d in range(n - 1):
-            total = total + w_in[d, at, :].astype(F32)
-        w_t[at, :] = total.astype(BF)
-        return 0
-
-    lax.fori_loop(0, rows // block, add_rows, 0)
-    settle(w_t, w_x.at[0], local.at[2])
-    far_w = push(w_x.at[0], w_x.at[1], x_send.at[2], x_recv.at[2], across)
-    far_w.wait()
-    g_t[:, split:] = (w_x[0].astype(F32) + w_x[1].astype(F32)).astype(BF)
-    settle(g_t, g_c.at[core], local.at[3])
-    near_g = push(g_c.at[core], g_c.at[core], c_send.at[0], c_recv.at[0], beside)
+    near_g.wait()
+    span = g.shape[1]
+    for c in range(2):
+        g_out[:, c * span : (c + 1) * span] = g_c[c].astype(F32)
     near_s.wait()
     s_out[...] = s_c[0] + s_c[1]
-    near_g.wait()
-    for c in range(2):
-        g_out[:, c * span : (c + 1) * span] = g_c[c].astype(F32)
-
-
-def finish(g, w, s):
-    n, rows, last = w.shape
-    span = g.shape[1] + last
+
+
+def finish(g, s):
+    n = s.shape[0]
     vm = pl.BlockSpec(memory_space=pltpu.VMEM)
     dma = pltpu.SemaphoreType.DMA
-    pair = pltpu.VMEM((2,) + s.shape[1:], F32)
     return pl.pallas_call(
         functools.partial(finish_kernel, n),
-        in_specs=[vm] * 3,
+        in_specs=[vm] * 2,
         out_specs=[vm] * 2,
         out_shape=[
-            jax.ShapeDtypeStruct((rows, 2 * span), F32),
+            jax.ShapeDtypeStruct((g.shape[0], 2 * g.shape[1]), F32),
             jax.ShapeDtypeStruct(s.shape[1:], F32),
         ],
         scratch_shapes=[
-            pltpu.VMEM((n - 1, rows, last), BF),
             pltpu.VMEM((n - 1,) + s.shape[1:], F32),
             pltpu.VMEM(g.shape, BF),
-            pltpu.VMEM((2, rows, last), BF),
-            pair,
-            pltpu.VMEM((2, rows, span), BF),
-            pair,
-            pltpu.VMEM((rows, span), BF),
-            pltpu.VMEM((rows, last), BF),
-            pair,
+            pltpu.VMEM((2,) + s.shape[1:], F32),
+            pltpu.VMEM((2,) + g.shape, BF),
+            pltpu.VMEM((2,) + s.shape[1:], F32),
+            pltpu.VMEM(g.shape, BF),
+            pltpu.VMEM((2,) + s.shape[1:], F32),
             dma((n - 1,)),
             dma((n - 1,)),
-            dma((n - 1,)),
-            dma((n - 1,)),
-            dma((3,)),
-            dma((3,)),
             dma((2,)),
             dma((2,)),
-            dma((4,)),
+            dma((2,)),
+            dma((2,)),
+            dma((3,)),
         ],
         compiler_params=pltpu.CompilerParams(collective_id=1, has_side_effects=True),
         name="finish",
-    )(g, w, s)
+    )(g, s)
 
 
 def assemble_kernel(span, inner, core_ref, mine, other, d_mine, d_other, out_ref, up_ref, down_ref):
@@ -625,36 +598,41 @@
     before = lambda edge: jnp.sum((ids[None, :] < edge).astype(jnp.int32), 1)
     start_first, end_first = before(first), before(first + 1)
     start_last, end_last = before(last), before(last + 1)
-    ceil_m = lambda value: (value + TM - 1) // TM
     lift = jnp.where(noisy, 0, 1)
     zero = jnp.zeros_like(start_first)
-    bounds = jnp.stack(
-        [
-            jnp.where(noisy, start_first, end_first) // TK,
-            ceil_m(jnp.where(noisy, start_last, end_last)),
-            jnp.where(noisy, start_first // TM, zero),
-            jnp.where(noisy, ceil_m(end_last), zero),
-            zero + jnp.where(jnp.arange(zero.shape[0]) == 0, lift, core),
-        ]
-    ).astype(jnp.int32)
+
+    def key_bounds(full, masked):
+        ceil_m = lambda value: (value + masked - 1) // masked
+        return jnp.stack(
+            [
+                jnp.where(noisy, start_first, end_first) // full,
+                ceil_m(jnp.where(noisy, start_last, end_last)),
+                jnp.where(noisy, start_first // masked, zero),
+                jnp.where(noisy, ceil_m(end_last), zero),
+                zero + jnp.where(jnp.arange(zero.shape[0]) == 0, lift, core),
+            ]
+        ).astype(jnp.int32)
+
+    bounds, wide_bounds = key_bounds(TK, TM), key_bounds(FK, FK)
     id_row = jnp.broadcast_to(ids[None, :], (8, length))
     id_col = jnp.broadcast_to(ids[:, None], (length, 128))
 
     cot_both = jnp.concatenate([cotangent[0], cot_far], 0)
-    clean_in, cot_both, cos_t, sin_t, bounds, id_row, id_col = lax.optimization_barrier(
-        (clean_in, cot_both, cos_t, sin_t, bounds, id_row, id_col)
-    )
-    clean_mine = jnp.where(noisy, clean_in, tok)
-    clean_other = lax.ppermute(clean_mine, "seq", swap)
+    clean_in, cot_both, cos_t, sin_t, bounds, wide_bounds, id_row, id_col = (
+        lax.optimization_barrier(
+            (clean_in, cot_both, cos_t, sin_t, bounds, wide_bounds, id_row, id_col)
+        )
+    )
+    clean_far = lax.ppermute(clean_in, "seq", swap)
 
     vec = jnp.concatenate([scale_one[None], shift_one[None], jnp.zeros((6, width), F32)], 0)
     bias_own = lax.dynamic_slice_in_dim(qkv_b, core * 3 * span, 3 * span, 0)
     bias_own = jnp.transpose(bias_own.reshape(heads, 3, HD), (1, 0, 2)).reshape(3 * span, 1)
     q, k, v, kc, vc, a_own = project(
-        core.reshape(1).astype(jnp.int32), tok, other, clean_mine, clean_other, gathered, vec,
+        jnp.stack([core, noisy.astype(core.dtype)]), tok, other, clean_in, clean_far, gathered, vec,
         bias_own, cos_t, sin_t, heads
     )
-    o, lse = attend(bounds, q, k, v, kc, vc, id_row, id_col, heads, 2)
+    o, lse = attend(wide_bounds, q, k, v, kc, vc, id_row, id_col, heads, 1)
     o, lse, out_up = lax.optimization_barrier((o, lse, out_up))
     out_near, up_own = out_up[:, :span], out_up[:, span:]
     out_full = in_order(out_near, lax.ppermute(out_near, "seq", swap), 1)
@@ -670,31 +648,30 @@
     second_in, down_own = lax.optimization_barrier((second_in, down_own))
     both_in = jnp.concatenate([second_in, lax.ppermute(second_in, "seq", swap)], 0)
 
-    def join(partial):
-        return partial[:local_rows] + lax.ppermute(
-            partial[local_rows:].astype(BF), "seq", swap
-        ).astype(F32)
+    def join(product, rows):
+        far = product(rows[local_rows:]).astype(BF)
+        return product(rows[:local_rows]) + lax.ppermute(far, "seq", swap).astype(F32)
 
     pre_act = dot(both_in, up_own) + up_b
     root = (2 / math.pi) ** 0.5
     square = pre_act * pre_act
-    bend = jnp.tanh(root * pre_act * (1 + 0.044715 * square))
-    rise = 0.5 * (1 + bend)
+    bend = jnp.tanh(pre_act * (root + 0.044715 * root * square))
+    rise = 0.5 + 0.5 * bend
     act_low = (pre_act * rise).astype(BF)
-    curve = 0.5 * pre_act * (1 - bend * bend) * (1 + 3 * 0.044715 * square)
-    slope = (rise + root * curve).astype(BF)
+    curve = pre_act * (1 - bend * bend) * (0.5 * root + 1.5 * 0.044715 * root * square)
+    slope = (rise + curve).astype(BF)
     grad_down_w = rows_contract(act_low, cot_both).astype(BF)
     scatter = lambda grad: lax.psum_scatter(grad, "fsdp", scatter_dimension=0, tiled=True)
     act_low, slope, grad_down_w, cot_both = lax.optimization_barrier(
         (act_low, slope, grad_down_w, cot_both)
     )
     down_part = scatter(grad_down_w)
-    result = hidden + join(dot(act_low, down_own)) + down_shift
+    result = hidden + join(lambda rows: dot(rows, down_own), act_low) + down_shift
 
     grad_top = cotangent[0].astype(F32)
     grad_down_b = jnp.sum(grad_top, 0)
     grad_pre = (right_transposed(cot_both, down_own) * slope.astype(F32)).astype(BF)
-    grad_second = join(right_transposed(grad_pre, up_own))
+    grad_second = join(lambda rows: right_transposed(rows, up_own), grad_pre)
     grad_up_b = jnp.sum(grad_pre.astype(F32), 0)
     grad_up_w = rows_contract(both_in, grad_pre).astype(BF)
     grad_scale_two = jnp.sum(grad_second * normed_two, 0)
@@ -768,8 +745,9 @@
     got_2, out_up_part, first_01 = hold((got_2, out_up_part, first_01))
     own_2 = joined(own_2, got_2)
     far_rows = (first_01[local_rows:] + back(own_2[:, local_rows:], 2, 1)).astype(BF)
+    grad_2, far_rows, pieces_01 = hold((weight_grad(own_2), far_rows, pieces_01))
+    pieces_2 = exchange(grad_2)
     got_rows = lax.ppermute(far_rows, "seq", swap).astype(F32)
-    grad_2 = weight_grad(own_2)
     grad_first = first_01[:local_rows] + back(own_2[:, :local_rows], 2, 1) + got_rows
 
     def chip_sum(part, far):
@@ -807,10 +785,11 @@
     packed = jnp.pad(packed, ((0, 0), (0, lines * 128 - packed.shape[1])))
     packed = packed.reshape(n_fsdp, lines, 128)
     part_01 = piece_sum(pieces_01)
-    grad_rows, out_g, up_g, down_g, packed, part_01 = hold(
-        (grad_rows, out_g, up_g, down_g, packed, part_01)
-    )
-    qkv_g, small_sum = finish(part_01, grad_2.reshape(n_fsdp, shard, pair_w), packed)
+    grad_rows, out_g, up_g, down_g, packed, part_01, pieces_2 = hold(
+        (grad_rows, out_g, up_g, down_g, packed, part_01, pieces_2)
+    )
+    qkv_part = jnp.concatenate([part_01, piece_sum(pieces_2)], 1)
+    qkv_g, small_sum = finish(qkv_part, packed)
     small_sum = small_sum.reshape(-1)
     small_out, at = [], 0
     for size in sizes:

time: 492 us -> 486 us (0.988)
  Pallas kernels: 227 us -> 193 us
  waiting for transfers between devices: 37.7 us -> 66.4 us
  other arithmetic: 49.4 us -> 35.3 us
  matrix products: 80.8 us -> 93.6 us
  local copies, waits for them, and re-layouts: 48.6 us -> 42.1 us
    all_gather x1, waiting for transfers between devices: 1.21 us -> 20.7 us  [on_device(): down_own = lax.all_gather(down_rows, 'fsdp', axis=0, tiled=True)]
    pallas_call x1, Pallas kernels: 69.1 us -> 50.9 us  [attend(): pl.pallas_call(functools.partial(attend_kernel, group), grid_spec=pltpu.P...]
    pallas_call x1, Pallas kernels: 26.9 us -> 12.9 us  [finish(): pl.pallas_call(functools.partial(finish_kernel, n), in_specs=[vm] * 2, ou...]
    all_to_all x1 -> x2, starting transfers between devices: 5.45 us -> 15.3 us  [on_device(): lax.all_to_all(grad.reshape(n_fsdp, shard, grad.shape[1]), 'fsdp', 0, 0)]
    reduce_sum x2 -> x0, other arithmetic: 9.8 us -> none  [the longest x1 5.33 us: on_device(): grad_scale_one = jnp.sum(grad_first * normed_one, 0)]
    all_to_all x1 -> x2, waiting for transfers between devices: 0.01 us -> 8.78 us  [on_device(): lax.all_to_all(grad.reshape(n_fsdp, shard, grad.shape[1]), 'fsdp', 0, 0)]
    dot_general x3 -> x4, matrix products: 24.7 us -> 31.9 us  [dot(): return jnp.dot(left, right, preferred_element_type=F32)]
    dot_general x3 -> x4, matrix products: 17.6 us -> 23.9 us  [right_transposed(): lax.dot_general(left, right, (((1,), (1,)), ((), ())), preferred_element_...]
  transfers between devices with their start and end apart: 25 -> 26, of which waited for: 5 -> 9; matrix products, arithmetic and copies ran while one was open for 21% -> 25% of each run, Pallas kernels for 41% -> 38%
where the time goes in v5:
time: 486 us; the launch traced here: 477 us
  Pallas kernels  193 us (40%)
  matrix products  93.6 us (19%)
  waiting for transfers between devices  66.4 us (14%)
  local copies, waits for them, and re-layouts  42.1 us (9%)
  other arithmetic  35.3 us (7%)
  starting transfers between devices  31.3 us (6%)
  between operations  15.1 us (3%)
    pallas_call x3, Pallas kernels, attend_back(): pl.pallas_call(functools.partial(attend_back_kernel, group), grid_spec=pl...  104 us
    pallas_call x1, Pallas kernels, attend(): pl.pallas_call(functools.partial(attend_kernel, group), grid_spec=pltpu.P...  50.9 us
    dot_general x4, matrix products, dot(): return jnp.dot(left, right, preferred_element_type=F32)  31.9 us
    ppermute x1, waiting for transfers between devices, on_device(): clean_in = lax.ppermute(tok, 'seq', [(2, 0), (3, 1)])  26.1 us
    dot_general x4, matrix products, right_transposed(): lax.dot_general(left, right, (((1,), (1,)), ((), ())), preferred_element_...  23.9 us
    pallas_call x1, Pallas kernels, project(): pl.pallas_call(functools.partial(qkv_kernel, heads), grid_spec=pltpu.Pref...  22.3 us
    all_gather x1, waiting for transfers between devices, on_device(): down_own = lax.all_gather(down_rows, 'fsdp', axis=0, tiled=True)  20.7 us
    dot_general x3, matrix products, rows_contract(): lax.dot_general(left, right, (((0,), (0,)), ((), ())), preferred_element_...  15.6 us
  transfers between devices with their start and end apart: 26, of which 9 were waited for; matrix products, arithmetic and copies ran while one was open for 25% of the time, Pallas kernels for 38%

profile of v5, /device:TPU:13, one launch (start us, length us, event | category | flops | bytes accessed | tf_op | source)
XLA Modules:
  0.0 477.2 jit_solution(6048390469345982645)
XLA Ops:
  11.7 2.9 reshape.679
  14.6 2.5 dynamic-slice_reduce_fusion
  22.2 1.8 fusion.54
  24.0 1.8 collective-permute-done.1
  25.8 3.7 pad_maximum_fusion
  29.5 26.1 %collective-permute-done.sent = bf16[1024,768]{1,0:T(8,128)(2,1)} collective-permute-done((bf16[1024,768]{1,0:T(8,128)(2,1)S(1)}, bf16[1024,768]{1,0:T(8,128)(2,1)}, u32[]{:S(2)}, u32[]{:S(2)}) %collective-permute-start) | collective-permute-done | bytes 1572896 | tf_op jit(solution)/shard_map/ppermute | solution.py:547
  64.4 22.3 %project.1 = (bf16[384,2048]{1,0:T(8,128)(2,1)}, bf16[384,2048]{1,0:T(8,128)(2,1)}, bf16[384,2048]{1,0:T(8,128)(2,1)}, bf16[384,2048]{1,0:T(8,128)(2,1)}, bf16[3...) custom-call(s32[2]{0:T(128)} %pad_add_fusion.core_ref, bf16[1024,768]{1,0:T(8,128)(2,1)} %bitcast.131, ...), custom_call_target="tpu_custom_call" | custom-call | tf_op jit(solution)/shard_map/project/pallas_call | solution.py:122
  86.7 50.9 %attend.1 = (bf16[384,2048]{1,0:T(8,128)(2,1)}, f32[6,8,2048]{2,1,0:T(8,128)}) custom-call(s32[5,4]{1,0:T(8,128)} %stack.14.bounds, bf16[384,2048]{1,0:T(8,128)(2,1)} %get-tuple-element.86.q, bf16[384,2048]{1,0:T(8,128)(2,1)} %get-tuple-element.87.k, bf16[384,2048]{1,0:T(8,128)(2,1)} %get-tuple-element.88.v, bf16[384,2048]{1,0:T(8,128)(2,1)} %get-tuple-element.89.kc, ...), custom_call_target="tpu_custom_call" | custom-call | flops 25769803776 | bytes 16777216 | tf_op jit(solution)/shard_map/attend/pallas_call | solution.py:240
  137.6 2.5 constant_dynamic-slice_fusion.5
  143.6 3.7 fusion.65
  150.7 20.7 %all-gather.8.cloned.1.call-done = bf16[1536,768]{1,0:T(8,128)(2,1)} async-done(((bf16[192,768]{1,0:T(8,128)(2,1)}), bf16[1536,768]{1,0:T(8,128)(2,1)}) %all-gather.8.cloned.1.call-update) | async-done | bytes 2359312 | tf_op jit(solution)/shard_map/all_gather | solution.py:587
  171.4 1.8 collective-permute-start.6
  178.1 14.2 %add_convert_fusion = (bf16[2048,1536]{1,0:T(8,128)(2,1)}, bf16[2048,1536]{1,0:T(8,128)(2,1)S(1)}) fusion(f32[1536]{0:T(1024)S(1)} %add.354, bf16[2048,768]{1,0:T(8,128)(2,1)S(1)} %constant_dynamic-update-slice_fusion, bf16[768,1920]{1,0:T(8,128)(2,1)S(1)} %copy-done.20), kind=kOutput, calls=%fused_computation.2 | convolution fusion | flops 4885315584 | bytes 18096128 | tf_op jit(solution)/shard_map/dot_general | solution.py:50
  192.4 2.6 copy-done.28
  195.0 6.5 %convolution_convert_fusion.1 = bf16[1536,768]{1,0:T(8,128)(2,1)} fusion(bf16[2048,1536]{1,0:T(8,128)(2,1)S(1)} %get-tuple-element.99, bf16[2048,768]{1,0:T(8,128)(2,1)S(1)} %copy-done.11), kind=kOutput, calls=%fused_computation.19 | convolution fusion | flops 4833017856 | bytes 11796480 | tf_op jit(solution)/shard_map/dot_general | solution.py:42
  201.5 9.0 %convert_reduce_fusion = (f32[1536]{0:T(1024)S(1)}, bf16[2048,1536]{1,0:T(8,128)(2,1)S(1)}) fusion(bf16[2048,1536]{1,0:T(8,128)(2,1)} %get-tuple-element.102, bf16[2048,768]{1,0:T(8,128)(2,1)} %pad_maximum_fusion, bf16[1536,768]{1,0:T(8,128)(2,1)} %all-gather.8.cloned.1.call-done), kind=kOutput, calls=%fused_computation | convolution fusion | flops 4847565312 | bytes 18094080 | tf_op jit(solution)/shard_map/dot_general | solution.py:46
  210.5 3.7 fusion.35
  214.8 3.3 collective-permute-done.8
  218.0 7.5 %multiply_reduce_fusion = (f32[768]{0:T(1024)S(1)}, f32[1024]{0:T(1024)S(1)}, f32[1024]{0:T(1024)S(1)}, f32[768]{0:T(1024)S(1)}, f32[1024,768]{1,0:T(8,128)S(1)}) fusion(f32[1024,768]{1,0:T(8,128)} %copy-done.4, f32[1024]{0:T(1024)S(1)} %add_rsqrt_fusion.1, f32[1024]{0:T(1024)S(1)} %broadcast_multiply_fusion.5, f32[768]{0:T(1024)S(1)} %mul.182, ...), kind=kOutput, calls=%fused_computation.33 | convolution fusion | flops 2424566272 | bytes 13394944 | tf_op jit(solution)/shard_map/dot_general | solution.py:46
  225.6 1.9 convert_reduce_fusion.4
  227.6 3.6 convolution_convert_fusion.2
  232.6 3.6 convolution_convert_fusion.3
  236.4 5.4 %convolution_convert_fusion = bf16[768,1536]{1,0:T(8,128)(2,1)S(1)} fusion(bf16[2048,768]{1,0:T(8,128)(2,1)S(1)} %copy-done.17, bf16[2048,1536]{1,0:T(8,128)(2,1)S(1)} %bitcast.173), kind=kOutput, calls=%fused_computation.18 | convolution fusion | flops 4833017856 | bytes 11796480 | tf_op jit(solution)/shard_map/dot_general | solution.py:42
  242.9 1.8 pad_maximum_fusion.2
  245.7 34.8 %attend_back.3 = (bf16[384,2048]{1,0:T(8,128)(2,1)}, bf16[256,2048]{1,0:T(8,128)(2,1)}) custom-call(s32[5,4]{1,0:T(8,128)} %stack.13.bounds, bf16[384,2048]{1,0:T(8,128)(2,1)} %get-tuple-element.86.q, bf16[384,2048]{1,0:T(8,128)(2,1)} %get-tuple-element.87.k, bf16[384,2048]{1,0:T(8,128)(2,1)} %get-tuple-element.88.v, ...), custom_call_target="tpu_custom_call" | custom-call | flops 10737418240 | bytes 8388608 | tf_op jit(solution)/shard_map/attend_back/pallas_call | solution.py:372
  281.9 6.4 %fusion.32 = bf16[1024,768]{1,0:T(8,128)(2,1)} fusion(bf16[1536,768]{1,0:T(8,128)(2,1)} %all-gather.8.cloned.1.call-done, bf16[2048,1536]{1,0:T(8,128)(2,1)} %copy-done.28), kind=kOutput, calls=%fused_computation.62 | convolution fusion | flops 2416705536 | bytes 7077888 | tf_op jit(solution)/shard_map/dot_general | solution.py:50
  290.1 34.6 %attend_back.4 = (bf16[384,2048]{1,0:T(8,128)(2,1)}, bf16[256,2048]{1,0:T(8,128)(2,1)}) custom-call(s32[5,4]{1,0:T(8,128)} %stack.13.bounds, bf16[384,2048]{1,0:T(8,128)(2,1)} %get-tuple-element.86.q, bf16[384,2048]{1,0:T(8,128)(2,1)} %get-tuple-element.87.k, bf16[384,2048]{1,0:T(8,128)(2,1)} %get-tuple-element.88.v, ...), custom_call_target="tpu_custom_call" | custom-call | flops 10737418240 | bytes 8388608 | tf_op jit(solution)/shard_map/attend_back/pallas_call | solution.py:372
  327.3 2.1 fusion.22
  329.8 2.6 convolution_convert_fusion.6
  332.5 34.8 %attend_back.5 = (bf16[384,2048]{1,0:T(8,128)(2,1)}, bf16[256,2048]{1,0:T(8,128)(2,1)}) custom-call(s32[5,4]{1,0:T(8,128)} %stack.13.bounds, bf16[384,2048]{1,0:T(8,128)(2,1)} %get-tuple-element.86.q, bf16[384,2048]{1,0:T(8,128)(2,1)} %get-tuple-element.87.k, bf16[384,2048]{1,0:T(8,128)(2,1)} %get-tuple-element.88.v, ...), custom_call_target="tpu_custom_call" | custom-call | flops 10737418240 | bytes 8388608 | tf_op jit(solution)/shard_map/attend_back/pallas_call | solution.py:372
  368.4 2.3 collective-permute-start.14
  372.9 1.8 convolution_convert_fusion.5
  377.0 8.4 %all-to-all-start = ((bf16[8,96,768]{2,1,0:T(8,128)(2,1)}), bf16[8,96,768]{2,1,0:T(8,128)(2,1)}, u32[]{:S(2)}, u32[]{:S(2)}) async-start(bf16[8,96,768]{2,1,0:T(8,128)(2,1)} %bitcast.33), calls=%async_computation.2 | async-start | bytes 2359296 | tf_op jit(solution)/shard_map/all_to_all | solution.py:736
  385.4 4.8 %fusion.23 = f32[2048,768]{1,0:T(8,128)S(1)} fusion(bf16[384,2048]{1,0:T(8,128)(2,1)} %bitcast.139, bf16[384,2048]{1,0:T(8,128)(2,1)} %bitcast.136, bf16[768,1280]{1,0:T(8,128)(2,1)} %all-gather.4.cloned.1.call-done.w_ref), kind=kOutput, calls=%fused_computation.57 | convolution fusion | flops 2422210560 | bytes 10616832 | tf_op jit(solution)/shard_map/dot_general | solution.py:717
  390.2 2.5 collective-permute-done.14
  392.7 2.2 collective-permute-start.16
  396.7 3.9 add_convert_fusion.1
  400.6 2.6 convolution_convert_fusion.4
  403.2 8.2 %all-to-all-done = bf16[8,96,768]{2,1,0:T(8,128)(2,1)} async-done(((bf16[8,96,768]{2,1,0:T(8,128)(2,1)}), bf16[8,96,768]{2,1,0:T(8,128)(2,1)}, u32[]{:S(2)}, u32[]{:S(2)}) %all-to-all-start) | async-done | bytes 1179680 | tf_op jit(solution)/shard_map/all_to_all | solution.py:736
  411.8 7.7 %fusion.40 = bf16[1,1024,768]{2,1,0:T(8,128)(2,1)} fusion(f32[1024,768]{1,0:T(8,128)} %copy-done.4, bf16[1024,768]{1,0:T(8,128)(2,1)} %collective-permute-done.7, f32[768]{0:T(1024)S(1)} %add.365, bf16[1536,768]{1,0:T(8,128)(2,1)} %all-gather.8.cloned.1.call-done, bf16[2048,1536]{1,0:T(8,128)(2,1)} %copy-done.28), kind=kOutput, calls=%fused_computation.65 | convolution fusion | flops 2419851264 | bytes 11799552 | tf_op jit(solution)/shard_map/dot_general | solution.py:50
  419.9 1.9 add_convert_fusion.5.mine
  423.5 2.4 convert_reduce_fusion.1
  426.4 2.9 assemble.1
  429.4 6.9 %all-to-all-start.1 = ((bf16[8,96,384]{2,1,0:T(8,128)(2,1)}), bf16[8,96,384]{2,1,0:T(8,128)(2,1)S(1)}, u32[]{:S(2)}, u32[]{:S(2)}) async-start(bf16[8,96,384]{2,1,0:T(8,128)(2,1)} %bitcast.156), calls=%async_computation.3 | async-start | bytes 1179648 | tf_op jit(solution)/shard_map/all_to_all | solution.py:736
  437.8 6.3 %fusion.9 = (f32[768]{0:T(1024)S(1)}, f32[1024]{0:T(1024)S(1)}, f32[1024]{0:T(1024)S(1)}, f32[768]{0:T(1024)S(1)}, f32[1024,768]{1,0:T(8,128)}) fusion(f32[1024]{0:T(1024)S(1)} %add_rsqrt_fusion, f32[1024]{0:T(1024)S(1)} %broadcast_multiply_fusion.2, bf16[1,1024,768]{2,1,0:T(8,128)(2,1)S(1)} %copy-done.3, f32[768]{0:T(1024)S(1)} %mul.206, ...), kind=kOutput, calls=%fused_computation.24 | convolution fusion | flops 614199808 | bytes 10839040 | tf_op jit(solution)/shard_map/dot_general | solution.py:717
  444.4 4.6 fusion.8
  451.0 12.9 %finish.1 = (f32[96,2304]{1,0:T(8,128)}, f32[10,128]{1,0:T(8,128)}) custom-call(bf16[96,1152]{1,0:T(8,128)(2,1)} %pad_maximum_fusion.10.g, f32[8,10,128]{2,1,0:T(8,128)} %copy.68.s), custom_call_target="tpu_custom_call" | custom-call | tf_op jit(solution)/shard_map/finish/pallas_call | solution.py:455
  468.0 2.1 copy.77
  (211 shorter events, 58.1 us)
Async XLA Ops:
  7.2 51.9 %copy-start = (bf16[384,768]{1,0:T(8,128)(2,1)S(1)}, bf16[384,768]{1,0:T(8,128)(2,1)}, u32[]{:S(2)}) copy-start(bf16[384,768]{1,0:T(8,128)(2,1)} %param.27) | copy-start | bytes 1769476
  7.2 10.3 %copy-start.23 = (bf16[96,768]{1,0:T(8,128)(2,1)S(1)}, bf16[96,768]{1,0:T(8,128)(2,1)}, u32[]{:S(2)}) copy-start(bf16[96,768]{1,0:T(8,128)(2,1)} %param.21) | copy-start | bytes 442372
  7.2 11.1 %copy-start.2 = (bf16[1,1024,768]{2,1,0:T(8,128)(2,1)S(1)}, bf16[1,1024,768]{2,1,0:T(8,128)(2,1)}, u32[]{:S(2)}) copy-start(bf16[1,1024,768]{2,1,0:T(8,128)(2,1)} %param.15) | copy-start | bytes 4718596
  7.2 13.2 %copy-start.22 = (s32[1,2048]{1,0:T(1,128)S(1)}, s32[1,2048]{1,0:T(1,128)}, u32[]{:S(2)}) copy-start(s32[1,2048]{1,0:T(1,128)} %param.16) | copy-start | bytes 24580
  7.2 53.5 %all-gather.4.cloned.1.call-start = ((), (), s32[]{:S(2)}) async-start(), calls=%async_computation.4 | async-start | bytes 2211840 | tf_op jit(solution)/shard_map/all_gather | solution.py:566
  11.7 125.9 %all-gather.6.cloned.1.call-start = ((), (), s32[]{:S(2)}) async-start(), calls=%async_computation.5 | async-start | bytes 3317760 | tf_op jit(solution)/shard_map/all_gather | solution.py:584
  18.3 153.2 %all-gather.8.cloned.1.call-start = ((), (), s32[]{:S(2)}) async-start(), calls=%async_computation.6 | async-start | bytes 2654208 | tf_op jit(solution)/shard_map/all_gather | solution.py:587
  18.3 37.3 %collective-permute-start = (bf16[1024,768]{1,0:T(8,128)(2,1)S(1)}, bf16[1024,768]{1,0:T(8,128)(2,1)}, u32[]{:S(2)}, u32[]{:S(2)}) collective-permute-start(bf16[1024,768]{1,0:T(8,128)(2,1)S(1)} %bitcast.133), channel_id=1, source_target_pairs={{16,0},{24,8},{17,1},{25,9},{18,2},{26,10},{19,3},{27,11},{20,4},{... | collective-permute-start | bytes 4718600 | tf_op jit(solution)/shard_map/ppermute | solution.py:547
  19.6 44.7 %collective-permute-start.2 = (bf16[1024,768]{1,0:T(8,128)(2,1)S(1)}, bf16[1024,768]{1,0:T(8,128)(2,1)}, u32[]{:S(2)}, u32[]{:S(2)}) collective-permute-start(bf16[1024,768]{1,0:T(8,128)(2,1)S(1)} %bitcast.134), channel_id=1, source_target_pairs={{0,8},{8,0},{16,24},{24,16},{1,9},{9,1},{17,25},{25,17},{2,10},{10... | collective-permute-start | bytes 4718600 | tf_op jit(solution)/shard_map/ppermute | solution.py:546
  20.4 5.4 %collective-permute-start.1 = (bf16[1024,768]{1,0:T(8,128)(2,1)}, bf16[1024,768]{1,0:T(8,128)(2,1)}, u32[]{:S(2)}, u32[]{:S(2)}) collective-permute-start(bf16[1024,768]{1,0:T(8,128)(2,1)} %bitcast.141), channel_id=1, source_target_pairs={{0,8},{8,0},{16,24},{24,16},{1,9},{9,1},{17,25},{25,17},{2,10},{10... | collective-permute-start | bytes 4718600 | tf_op jit(solution)/shard_map/ppermute | solution.py:548
  57.5 6.8 %collective-permute-start.3 = (bf16[1024,768]{1,0:T(8,128)(2,1)}, bf16[1024,768]{1,0:T(8,128)(2,1)}, u32[]{:S(2)}, u32[]{:S(2)}) collective-permute-start(bf16[1024,768]{1,0:T(8,128)(2,1)} %collective-permute-done.sent), channel_id=1, source_target_pairs={{0,8},{8,0},{16,24},{24,16},{1,9},{9,1},{17,25},{25,17},{2,10},{10... | collective-permute-start | bytes 4718600 | tf_op jit(solution)/shard_map/ppermute | solution.py:626
  59.8 264.9 %reduce-scatter.3.cloned.1.call-start = ((), (), s32[]{:S(2)}) async-start(), calls=%async_computation.7 | async-start | bytes 2654208 | tf_op jit(solution)/shard_map/reduce_scatter | solution.py:664
  137.6 6.0 %copy-start.3 = (bf16[1,1024,768]{2,1,0:T(8,128)(2,1)S(1)}, bf16[1,1024,768]{2,1,0:T(8,128)(2,1)}, u32[]{:S(2)}) copy-start(bf16[1,1024,768]{2,1,0:T(8,128)(2,1)} %param.15) | copy-start | bytes 4718596
  140.1 3.5 collective-permute-start.4
  141.3 2.3 collective-permute-start.5
  171.4 5.2 %collective-permute-start.6 = (bf16[1024,768]{1,0:T(8,128)(2,1)}, bf16[1024,768]{1,0:T(8,128)(2,1)}, u32[]{:S(2)}, u32[]{:S(2)}) collective-permute-start(bf16[1024,768]{1,0:T(8,128)(2,1)} %add_convert_fusion.3), channel_id=1, source_target_pairs={{0,8},{8,0},{16,24},{24,16},{1,9},{9,1},{17,25},{25,17},{2,10},{10... | collective-permute-start | bytes 4718600 | tf_op jit(solution)/shard_map/ppermute | solution.py:649
  173.4 4.7 copy-start.20
  178.1 14.2 %copy-start.16 = (bf16[2048,768]{1,0:T(8,128)(2,1)}, bf16[2048,768]{1,0:T(8,128)(2,1)S(1)}, u32[]{:S(2)}) copy-start(bf16[2048,768]{1,0:T(8,128)(2,1)S(1)} %constant_dynamic-update-slice_fusion) | copy-start | bytes 9437188
  178.1 16.9 %copy-start.11 = (bf16[2048,768]{1,0:T(8,128)(2,1)S(1)}, bf16[2048,768]{1,0:T(8,128)(2,1)}, u32[]{:S(2)}) copy-start(bf16[2048,768]{1,0:T(8,128)(2,1)} %pad_maximum_fusion) | copy-start | bytes 9437188
  201.5 9.0 %copy-start.21 = (bf16[768,1920]{1,0:T(8,128)(2,1)S(1)}, bf16[768,1920]{1,0:T(8,128)(2,1)}, u32[]{:S(2)}) copy-start(bf16[768,1920]{1,0:T(8,128)(2,1)} %all-gather.6.cloned.1.call-done) | copy-start | bytes 8847364
  210.5 3.8 copy-start.29
  214.3 3.8 collective-permute-start.8
  214.7 153.7 %reduce-scatter.5.cloned.1.call-start = ((), (), s32[]{:S(2)}) async-start(), calls=%async_computation.8 | async-start | bytes 3317760 | tf_op jit(solution)/shard_map/reduce_scatter | solution.py:664
  214.7 10.9 %copy-start.5 = (f32[1024,768]{1,0:T(8,128)S(1)}, f32[1024,768]{1,0:T(8,128)}, u32[]{:S(2)}) copy-start(f32[1024,768]{1,0:T(8,128)} %copy-done.4) | copy-start | bytes 9437188
  214.7 10.9 %copy-start.9 = (bf16[1,1024,768]{2,1,0:T(8,128)(2,1)S(1)}, bf16[1,1024,768]{2,1,0:T(8,128)(2,1)}, u32[]{:S(2)}) copy-start(bf16[1,1024,768]{2,1,0:T(8,128)(2,1)} %param.29) | copy-start | bytes 4718596
  227.6 5.0 %copy-start.6 = (f32[1024,768]{1,0:T(8,128)}, f32[1024,768]{1,0:T(8,128)S(1)}, u32[]{:S(2)}) copy-start(f32[1024,768]{1,0:T(8,128)S(1)} %get-tuple-element.169) | copy-start | bytes 9437188
  231.2 5.1 %slice-start = ((s8[6291456]{0:T(1024)(128)(4,1)}), s8[4194304]{0:T(1024)(128)(4,1)S(1)}, s32[]{:S(2)}) async-start(s8[6291456]{0:T(1024)(128)(4,1)} %bitcast.172), calls=%async_computation.9 | async-start | bytes 8388608
  232.2 4.1 copy-start.17
  232.2 4.1 slice-start.1
  232.2 9.7 %collective-permute-start.9 = (bf16[384,1024]{1,0:T(8,128)(2,1)S(1)}, bf16[384,1024]{1,0:T(8,128)(2,1)S(1)}, u32[]{:S(2)}, u32[]{:S(2)}) collective-permute-start(bf16[384,1024]{1,0:T(8,128)(2,1)S(1)} %get-tuple-element.175), channel_id=1, source_target_pairs={{0,8},{8,0},{16,24},{24,16},{1,9},{9,1},{17,25},{25,17},{2,10},{10... | collective-permute-start | bytes 2359304 | tf_op jit(solution)/shard_map/ppermute | solution.py:687
  236.2 5.6 %collective-permute-start.10 = (bf16[768,384]{1,0:T(8,128)(2,1)S(1)}, bf16[768,384]{1,0:T(8,128)(2,1)S(1)}, u32[]{:S(2)}, u32[]{:S(2)}) collective-permute-start(bf16[768,384]{1,0:T(8,128)(2,1)S(1)} %constant_dynamic-slice_fusion), channel_id=1, source_target_pairs={{0,8},{8,0},{16,24},{24,16},{1,9},{9,1},{17,25},{25,17},{2,10},{10... | collective-permute-start | bytes 1769480 | tf_op jit(solution)/shard_map/ppermute | solution.py:690
  280.6 44.2 %collective-permute-start.11 = (bf16[256,2048]{1,0:T(8,128)(2,1)}, bf16[256,2048]{1,0:T(8,128)(2,1)S(1)}, u32[]{:S(2)}, u32[]{:S(2)}) collective-permute-start(bf16[256,2048]{1,0:T(8,128)(2,1)} %get-tuple-element.113), channel_id=1, source_target_pairs={{0,16},{8,24},{1,17},{9,25},{2,18},{10,26},{3,19},{11,27},{4,20},{... | collective-permute-start | bytes 3145736 | tf_op jit(solution)/shard_map/ppermute | solution.py:702
  288.3 123.5 %collective-permute-start.7 = (bf16[1024,768]{1,0:T(8,128)(2,1)}, bf16[1024,768]{1,0:T(8,128)(2,1)}, u32[]{:S(2)}, u32[]{:S(2)}) collective-permute-start(bf16[1024,768]{1,0:T(8,128)(2,1)} %fusion.32), channel_id=1, source_target_pairs={{0,8},{8,0},{16,24},{24,16},{1,9},{9,1},{17,25},{25,17},{2,10},{10... | collective-permute-start | bytes 4718600 | tf_op jit(solution)/shard_map/ppermute | solution.py:653
  325.7 42.7 %collective-permute-start.12 = (bf16[256,2048]{1,0:T(8,128)(2,1)}, bf16[256,2048]{1,0:T(8,128)(2,1)S(1)}, u32[]{:S(2)}, u32[]{:S(2)}) collective-permute-start(bf16[256,2048]{1,0:T(8,128)(2,1)} %get-tuple-element.119), channel_id=1, source_target_pairs={{0,16},{8,24},{1,17},{9,25},{2,18},{10,26},{3,19},{11,27},{4,20},{... | collective-permute-start | bytes 3145736 | tf_op jit(solution)/shard_map/ppermute | solution.py:702
  332.4 35.9 %collective-permute-start.13 = (bf16[192,768]{1,0:T(8,128)(2,1)S(1)}, bf16[192,768]{1,0:T(8,128)(2,1)}, u32[]{:S(2)}, u32[]{:S(2)}) collective-permute-start(bf16[192,768]{1,0:T(8,128)(2,1)S(1)} %copy-done.19), channel_id=1, source_target_pairs={{0,16},{8,24},{16,0},{24,8},{1,17},{9,25},{17,1},{25,9},{2,18},{10... | collective-permute-start | bytes 884744 | tf_op jit(solution)/shard_map/ppermute | solution.py:726
  368.4 24.3 %collective-permute-start.14 = (bf16[256,2048]{1,0:T(8,128)(2,1)}, bf16[256,2048]{1,0:T(8,128)(2,1)}, u32[]{:S(2)}, u32[]{:S(2)}) collective-permute-start(bf16[256,2048]{1,0:T(8,128)(2,1)} %get-tuple-element.123), channel_id=1, source_target_pairs={{0,16},{8,24},{1,17},{9,25},{2,18},{10,26},{3,19},{11,27},{4,20},{... | collective-permute-start | bytes 3145736 | tf_op jit(solution)/shard_map/ppermute | solution.py:702
  377.0 34.4 %all-to-all-start = ((bf16[8,96,768]{2,1,0:T(8,128)(2,1)}), bf16[8,96,768]{2,1,0:T(8,128)(2,1)}, u32[]{:S(2)}, u32[]{:S(2)}) async-start(bf16[8,96,768]{2,1,0:T(8,128)(2,1)} %bitcast.33), calls=%async_computation.2 | async-start | bytes 2359296 | tf_op jit(solution)/shard_map/all_to_all | solution.py:736
  385.4 9.5 %copy-start.13 = (bf16[384,2048]{1,0:T(8,128)(2,1)S(1)}, bf16[384,2048]{1,0:T(8,128)(2,1)}, u32[]{:S(2)}) copy-start(bf16[384,2048]{1,0:T(8,128)(2,1)} %get-tuple-element.130) | copy-start | bytes 4718596
  390.2 6.5 %copy-start.12 = (f32[2048,768]{1,0:T(8,128)}, f32[2048,768]{1,0:T(8,128)S(1)}, u32[]{:S(2)}) copy-start(f32[2048,768]{1,0:T(8,128)S(1)} %fusion.23) | copy-start | bytes 18874372
  392.7 27.2 %collective-permute-start.16 = (bf16[96,1920]{1,0:T(8,128)(2,1)}, bf16[96,1920]{1,0:T(8,128)(2,1)}, u32[]{:S(2)}, u32[]{:S(2)}) collective-permute-start(bf16[96,1920]{1,0:T(8,128)(2,1)} %reduce-scatter.5.cloned.1.call-done), channel_id=1, source_target_pairs={{0,16},{8,24},{16,0},{24,8},{1,17},{9,25},{17,1},{25,9},{2,18},{10... | collective-permute-start | bytes 1105928 | tf_op jit(solution)/shard_map/ppermute | solution.py:757
  396.7 3.9 copy-start.10
  396.7 3.9 copy-start.26
  411.4 26.4 %collective-permute-start.15 = (bf16[1024,768]{1,0:T(8,128)(2,1)}, bf16[1024,768]{1,0:T(8,128)(2,1)}, u32[]{:S(2)}, u32[]{:S(2)}) collective-permute-start(bf16[1024,768]{1,0:T(8,128)(2,1)} %add_convert_fusion.1), channel_id=1, source_target_pairs={{0,8},{8,0},{16,24},{24,16},{1,9},{9,1},{17,25},{25,17},{2,10},{10... | collective-permute-start | bytes 4718600 | tf_op jit(solution)/shard_map/ppermute | solution.py:750
  421.8 4.6 collective-permute-start.17
  423.0 3.5 copy-start.14
  423.0 3.4 collective-permute-start.18
  429.4 20.2 %all-to-all-start.1 = ((bf16[8,96,384]{2,1,0:T(8,128)(2,1)}), bf16[8,96,384]{2,1,0:T(8,128)(2,1)S(1)}, u32[]{:S(2)}, u32[]{:S(2)}) async-start(bf16[8,96,384]{2,1,0:T(8,128)(2,1)} %bitcast.156), calls=%async_computation.3 | async-start | bytes 1179648 | tf_op jit(solution)/shard_map/all_to_all | solution.py:736
  444.4 25.8 %copy-start.1 = (bf16[384,768]{1,0:T(8,128)(2,1)S(1)}, bf16[384,768]{1,0:T(8,128)(2,1)}, u32[]{:S(2)}) copy-start(bf16[384,768]{1,0:T(8,128)(2,1)} %param.27) | copy-start | bytes 1769476
  (10 other events, 20.5 us)
Sparse Core Ops, SparseCore 0:
  11.8 47.1 all-gather.3
  61.7 56.1 all-gather.5
  120.7 50.6 all-gather.7
  214.8 66.5 reduce-scatter.2
  284.8 73.1 reduce-scatter.4

commit v6 on v5

--- a/solution.py
+++ b/solution.py
@@ -481,35 +481,44 @@
     )(g, s)
 
 
-def assemble_kernel(span, inner, core_ref, mine, other, d_mine, d_other, out_ref, up_ref, down_ref):
+def assemble_kernel(span, n, core_ref, mine, other, d_mine, d_other, out_ref, up_ref, down_ref):
     first_core = core_ref[0] == 0
     pick = lambda one, two: (
         jnp.where(first_core, one, two).astype(F32), jnp.where(first_core, two, one).astype(F32)
     )
-    first, second = pick(mine[...].astype(F32), other[...].astype(F32))
-    out_ref[:, :span] = first[:, :span]
-    out_ref[:, span:] = second[:, :span]
-    for i in range((first.shape[1] - span) // inner):
-        cols = slice(span + i * inner, span + (i + 1) * inner)
-        up_ref[:, 2 * i * inner : 2 * (i + 1) * inner] = jnp.concatenate(
-            [first[:, cols], second[:, cols]], 1
+    pair = pick(mine[...].astype(F32), other[...].astype(F32))
+    rows = pair[0].shape[0]
+    half = (pair[0].shape[1] - span) // (2 * n)
+    for c in range(2):
+        out_ref[:, c * span : (c + 1) * span] = pair[c][:, :span]
+    for i in range(n):
+        up_ref[:, 4 * i * half : 4 * (i + 1) * half] = jnp.concatenate(
+            [
+                part[:, span + (j * n + i) * half : span + (j * n + i + 1) * half]
+                for part in pair
+                for j in range(2)
+            ],
+            1,
         )
-    first, second = pick(d_mine[...].astype(F32), d_other[...].astype(F32))
-    down_ref[: first.shape[0], :] = first
-    down_ref[first.shape[0] :, :] = second
-
-
-def assemble(core, mine, other, d_mine, d_other, span, inner):
+    pair = pick(d_mine[...].astype(F32), d_other[...].astype(F32))
+    width = down_ref.shape[1]
+    for c in range(2):
+        for j in range(2):
+            at = (2 * c + j) * rows
+            down_ref[at : at + rows, :] = pair[c][:, j * width : (j + 1) * width]
+
+
+def assemble(core, mine, other, d_mine, d_other, span, n):
     rows, width = mine.shape
     vm = pl.BlockSpec(memory_space=pltpu.VMEM)
     return pl.pallas_call(
-        functools.partial(assemble_kernel, span, inner),
+        functools.partial(assemble_kernel, span, n),
         in_specs=[pl.BlockSpec(memory_space=pltpu.SMEM)] + [vm] * 4,
         out_specs=[vm] * 3,
         out_shape=[
             jax.ShapeDtypeStruct((rows, 2 * span), F32),
             jax.ShapeDtypeStruct((rows, 2 * (width - span)), F32),
-            jax.ShapeDtypeStruct((2 * d_mine.shape[0], d_mine.shape[1]), F32),
+            jax.ShapeDtypeStruct((4 * rows, d_mine.shape[1] // 2), F32),
         ],
         name="assemble",
     )(core, mine, other, d_mine, d_other)
@@ -575,16 +584,17 @@
 
     inner = up_bias.shape[0] // 2
     up_b = jnp.transpose(vectors[9:], (1, 0, 2)).reshape(n_fsdp, 2, inner)
-    up_b = lax.dynamic_index_in_dim(up_b, core, 1, False).reshape(-1)
-    up_cols = lax.dynamic_index_in_dim(
-        up_weight.reshape(shard, n_fsdp, 2, inner), core, 2, False
+    by_half = lambda a: jnp.swapaxes(a.reshape(-1, n_fsdp, 2, inner // 2), 1, 2)
+    up_b = by_half(lax.dynamic_index_in_dim(up_b, core, 1, False)).reshape(-1)
+    up_cols = by_half(
+        lax.dynamic_index_in_dim(up_weight.reshape(shard, n_fsdp, 2, inner), core, 2, False)
     ).reshape(shard, n_fsdp * inner)
     down_rows = lax.dynamic_slice_in_dim(down_weight, core * inner, inner, 0)
+    beside = lambda a: jnp.concatenate([a[: a.shape[0] // 2], a[a.shape[0] // 2 :]], 1)
     out_cols = lax.dynamic_slice_in_dim(out_weight, core * span, span, 1)
-    out_up = lax.all_gather(
-        jnp.concatenate([out_cols, up_cols], 1), "fsdp", axis=0, tiled=True
-    )
-    down_own = lax.all_gather(down_rows, "fsdp", axis=0, tiled=True)
+    ffn = lax.all_gather(
+        jnp.concatenate([out_cols, up_cols, beside(down_rows)], 1), "fsdp", axis=0, tiled=True
+    )
     in_order = lambda near, far, axis: jnp.where(
         core == 0, jnp.concatenate([near, far], axis), jnp.concatenate([far, near], axis)
     )
@@ -633,8 +643,10 @@
         bias_own, cos_t, sin_t, heads
     )
     o, lse = attend(wide_bounds, q, k, v, kc, vc, id_row, id_col, heads, 1)
-    o, lse, out_up = lax.optimization_barrier((o, lse, out_up))
-    out_near, up_own = out_up[:, :span], out_up[:, span:]
+    o, lse, ffn = lax.optimization_barrier((o, lse, ffn))
+    at = span + n_fsdp * inner
+    out_near, up_own = ffn[:, :span], ffn[:, span:at]
+    down_own = jnp.concatenate([ffn[:, at : at + width], ffn[:, at + width :]], 0)
     out_full = in_order(out_near, lax.ppermute(out_near, "seq", swap), 1)
     cut = lambda value, which: lax.dynamic_slice_in_dim(value, which * local_rows, local_rows, 1)
     o_mine = cut(o, core)
@@ -645,7 +657,6 @@
     hidden = rows_in + rows_contract(attended, out_full) + out_shift
     normed_two, inverse_two = normalize_parts(hidden)
     second_in = (normed_two * scale_two + shift_two).astype(BF)
-    second_in, down_own = lax.optimization_barrier((second_in, down_own))
     both_in = jnp.concatenate([second_in, lax.ppermute(second_in, "seq", swap)], 0)
 
     def join(product, rows):
@@ -660,7 +671,7 @@
     act_low = (pre_act * rise).astype(BF)
     curve = pre_act * (1 - bend * bend) * (0.5 * root + 1.5 * 0.044715 * root * square)
     slope = (rise + curve).astype(BF)
-    grad_down_w = rows_contract(act_low, cot_both).astype(BF)
+    grad_down_w = beside(rows_contract(act_low, cot_both).astype(BF))
     scatter = lambda grad: lax.psum_scatter(grad, "fsdp", scatter_dimension=0, tiled=True)
     act_low, slope, grad_down_w, cot_both = lax.optimization_barrier(
         (act_low, slope, grad_down_w, cot_both)
@@ -756,7 +767,7 @@
 
     out_up_both = chip_sum(out_up_part, lax.ppermute(out_up_part, "seq", cross))
     out_g, up_g, down_g = assemble(
-        core.reshape(1).astype(jnp.int32), *out_up_both, *chip_sum(down_part, down_far), span, inner
+        core.reshape(1).astype(jnp.int32), *out_up_both, *chip_sum(down_part, down_far), span, n_fsdp
     )
 
     sum_cols = lambda own: jnp.sum(own.astype(F32), 1)
@@ -770,7 +781,10 @@
         jnp.zeros((2 * 3 * span,), F32), grad_qkv_b, core * 3 * span, 0
     )
     up_b_wide = lax.dynamic_update_slice_in_dim(
-        jnp.zeros((n_fsdp, 2, inner), F32), grad_up_b.reshape(n_fsdp, 1, inner), core, 1
+        jnp.zeros((n_fsdp, 2, inner), F32),
+        jnp.swapaxes(grad_up_b.reshape(2, n_fsdp, inner // 2), 0, 1).reshape(n_fsdp, 1, inner),
+        core,
+        1,
     )
     pieces = [
         piece.reshape(n_fsdp, -1)

time: 486 us -> 473 us (0.973)
  waiting for transfers between devices: 66.4 us -> 50.7 us
    all_gather x2 -> x1, waiting for transfers between devices: 20.7 us -> 6.3 us  [on_device(): lax.all_gather(jnp.concatenate([out_cols, up_cols, beside(down_rows)], 1)...]
    unnamed x67 -> x74, local copies, waits for them, and re-layouts: 10.2 us -> 3.9 us
  transfers between devices with their start and end apart: 26 -> 25, of which waited for: 9 -> 9; matrix products, arithmetic and copies ran while one was open for 25% -> 24% of each run, Pallas kernels for 38% -> 39%
where the time goes in v6:
time: 473 us; the launch traced here: 465 us
  Pallas kernels  196 us (41%)
  matrix products  95.2 us (20%)
  waiting for transfers between devices  50.7 us (11%)
  local copies, waits for them, and re-layouts  38.3 us (8%)
  other arithmetic  37.5 us (8%)
  starting transfers between devices  31.9 us (7%)
  between operations  14.9 us (3%)
    pallas_call x3, Pallas kernels, attend_back(): pl.pallas_call(functools.partial(attend_back_kernel, group), grid_spec=pl...  107 us
    pallas_call x1, Pallas kernels, attend(): pl.pallas_call(functools.partial(attend_kernel, group), grid_spec=pltpu.P...  51.3 us
    dot_general x4, matrix products, dot(): return jnp.dot(left, right, preferred_element_type=F32)  31.5 us
    dot_general x4, matrix products, right_transposed(): lax.dot_general(left, right, (((1,), (1,)), ((), ())), preferred_element_...  26.2 us
    ppermute x1, waiting for transfers between devices, on_device(): clean_in = lax.ppermute(tok, 'seq', [(2, 0), (3, 1)])  25.8 us
    pallas_call x1, Pallas kernels, project(): pl.pallas_call(functools.partial(qkv_kernel, heads), grid_spec=pltpu.Pref...  22.3 us
    dot_general x3, matrix products, rows_contract(): lax.dot_general(left, right, (((0,), (0,)), ((), ())), preferred_element_...  16.2 us
    dot_general x3, matrix products, back(): lax.dot_general(own, cols, (((0,), (1,)), ((), ())), preferred_element_ty...  15 us
  transfers between devices with their start and end apart: 25, of which 9 were waited for; matrix products, arithmetic and copies ran while one was open for 24% of the time, Pallas kernels for 39%

profile of v6, /device:TPU:13, one launch (start us, length us, event | category | flops | bytes accessed | tf_op | source)
XLA Modules:
  0.0 465.0 jit_solution(15070843552132775970)
XLA Ops:
  10.7 3.5 reshape.688
  14.2 2.1 constant_dynamic-slice_fusion.7
  27.1 3.8 pad_maximum_fusion
  30.8 25.8 %collective-permute-done.sent = bf16[1024,768]{1,0:T(8,128)(2,1)} collective-permute-done((bf16[1024,768]{1,0:T(8,128)(2,1)S(1)}, bf16[1024,768]{1,0:T(8,128)(2,1)}, u32[]{:S(2)}, u32[]{:S(2)}) %collective-permute-start) | collective-permute-done | bytes 1572896 | tf_op jit(solution)/shard_map/ppermute | solution.py:556
  64.5 22.3 %project.1 = (bf16[384,2048]{1,0:T(8,128)(2,1)}, bf16[384,2048]{1,0:T(8,128)(2,1)}, bf16[384,2048]{1,0:T(8,128)(2,1)}, bf16[384,2048]{1,0:T(8,128)(2,1)}, bf16[3...) custom-call(s32[2]{0:T(128)} %pad_add_fusion.core_ref, bf16[1024,768]{1,0:T(8,128)(2,1)} %bitcast.135, ...), custom_call_target="tpu_custom_call" | custom-call | tf_op jit(solution)/shard_map/project/pallas_call | solution.py:122
  86.9 51.3 %attend.1 = (bf16[384,2048]{1,0:T(8,128)(2,1)}, f32[6,8,2048]{2,1,0:T(8,128)}) custom-call(s32[5,4]{1,0:T(8,128)} %stack.14.bounds, bf16[384,2048]{1,0:T(8,128)(2,1)} %get-tuple-element.84.q, bf16[384,2048]{1,0:T(8,128)(2,1)} %get-tuple-element.85.k, bf16[384,2048]{1,0:T(8,128)(2,1)} %get-tuple-element.86.v, bf16[384,2048]{1,0:T(8,128)(2,1)} %get-tuple-element.87.kc, ...), custom_call_target="tpu_custom_call" | custom-call | flops 25769803776 | bytes 16777216 | tf_op jit(solution)/shard_map/attend/pallas_call | solution.py:240
  138.2 6.3 %all-gather.5.cloned.1.call-done = bf16[768,3456]{1,0:T(8,128)(2,1)} async-done(((bf16[96,3456]{1,0:T(8,128)(2,1)}), bf16[768,3456]{1,0:T(8,128)(2,1)}) %all-gather.5.cloned.1.call-update) | async-done | bytes 5308432 | tf_op jit(solution)/shard_map/all_gather | solution.py:595
  144.5 2.4 constant_dynamic-slice_fusion.5
  146.9 2.2 collective-permute-start.4
  152.4 3.5 fusion.72
  158.8 2.8 fusion.69
  161.9 14.7 %add_convert_fusion = (bf16[2048,1536]{1,0:T(8,128)(2,1)}, bf16[2048,1536]{1,0:T(8,128)(2,1)S(1)}) fusion(f32[1536]{0:T(1024)S(1)} %add.354, bf16[768,3456]{1,0:T(8,128)(2,1)} %all-gather.5.cloned.1.call-done, bf16[1024,768]{1,0:T(8,128)(2,1)} %collective-permute-done.6, bf16[1024,768]{1,0:T(8,128)(2,1)} %add_convert_fusion.3), kind=kOutput, calls=%fused_computation.2 | convolution fusion | flops 4891607040 | bytes 18094080 | tf_op jit(solution)/shard_map/dot_general | solution.py:50
  176.7 5.4 %convolution_convert_fusion.1 = bf16[1536,768]{1,0:T(8,128)(2,1)S(1)} fusion(bf16[2048,1536]{1,0:T(8,128)(2,1)S(1)} %get-tuple-element.96, bf16[2048,768]{1,0:T(8,128)(2,1)S(1)} %copy-done.12), kind=kOutput, calls=%fused_computation.19 | convolution fusion | flops 4833017856 | bytes 11796480 | tf_op jit(solution)/shard_map/dot_general | solution.py:42
  183.9 8.0 %convert_reduce_fusion = (f32[1536]{0:T(1024)S(1)}, bf16[2048,1536]{1,0:T(8,128)(2,1)S(1)}) fusion(bf16[2048,1536]{1,0:T(8,128)(2,1)} %get-tuple-element.98, bf16[2048,768]{1,0:T(8,128)(2,1)} %pad_maximum_fusion, bf16[768,768]{1,0:T(8,128)(2,1)} %get-tuple-element.171, bf16[768,768]{1,0:T(8,128)(2,1)S(1)} %get-tuple-element.170), kind=kOutput, calls=%fused_computation | convolution fusion | flops 4852283904 | bytes 18094080 | tf_op jit(solution)/shard_map/dot_general | solution.py:46
  192.0 7.2 %fusion.35 = bf16[1024,768]{1,0:T(8,128)(2,1)} fusion(bf16[768,3456]{1,0:T(8,128)(2,1)} %all-gather.5.cloned.1.call-done, bf16[2048,1536]{1,0:T(8,128)(2,1)S(1)} %get-tuple-element.203), kind=kOutput, calls=%fused_computation.66 | convolution fusion | flops 2416705536 | bytes 7077888 | tf_op jit(solution)/shard_map/dot_general | solution.py:46
  199.6 3.3 collective-permute-done.8
  202.9 7.4 %multiply_reduce_fusion = (f32[768]{0:T(1024)S(1)}, f32[1024]{0:T(1024)S(1)}, f32[1024]{0:T(1024)S(1)}, f32[768]{0:T(1024)S(1)}, f32[1024,768]{1,0:T(8,128)S(1)}) fusion(f32[1024,768]{1,0:T(8,128)} %copy-done.4, f32[1024]{0:T(1024)S(1)} %add_rsqrt_fusion.1, f32[1024]{0:T(1024)S(1)} %broadcast_multiply_fusion.5, f32[768]{0:T(1024)S(1)} %mul.183, ...), kind=kOutput, calls=%fused_computation.34 | convolution fusion | flops 2424566272 | bytes 13394944 | tf_op jit(solution)/shard_map/dot_general | solution.py:46
  212.1 3.6 convolution_convert_fusion.2
  217.1 3.0 convolution_convert_fusion.3
  220.5 7.3 %convolution_convert_fusion = bf16[768,1536]{1,0:T(8,128)(2,1)S(1)} fusion(bf16[2048,1536]{1,0:T(8,128)(2,1)S(1)} %bitcast.178, bf16[1024,768]{1,0:T(8,128)(2,1)} %collective-permute-done.6, bf16[1024,768]{1,0:T(8,128)(2,1)} %add_convert_fusion.3), kind=kOutput, calls=%fused_computation.18 | convolution fusion | flops 4839309312 | bytes 11796480 | tf_op jit(solution)/shard_map/dot_general | solution.py:42
  228.9 1.9 pad_maximum_fusion.3
  231.9 35.7 %attend_back.3 = (bf16[384,2048]{1,0:T(8,128)(2,1)}, bf16[256,2048]{1,0:T(8,128)(2,1)}) custom-call(s32[5,4]{1,0:T(8,128)} %stack.13.bounds, bf16[384,2048]{1,0:T(8,128)(2,1)} %get-tuple-element.84.q, bf16[384,2048]{1,0:T(8,128)(2,1)} %get-tuple-element.85.k, bf16[384,2048]{1,0:T(8,128)(2,1)} %get-tuple-element.86.v, ...), custom_call_target="tpu_custom_call" | custom-call | flops 10737418240 | bytes 8388608 | tf_op jit(solution)/shard_map/attend_back/pallas_call | solution.py:372
  267.5 2.3 collective-permute-start.11
  269.8 6.0 %fusion.32 = bf16[1024,768]{1,0:T(8,128)(2,1)} fusion(bf16[2048,1536]{1,0:T(8,128)(2,1)} %copy-done.32, bf16[768,768]{1,0:T(8,128)(2,1)} %get-tuple-element.171, bf16[768,768]{1,0:T(8,128)(2,1)S(1)} %get-tuple-element.170), kind=kOutput, calls=%fused_computation.65 | convolution fusion | flops 2421424128 | bytes 7077888 | tf_op jit(solution)/shard_map/dot_general | solution.py:50
  277.5 35.7 %attend_back.4 = (bf16[384,2048]{1,0:T(8,128)(2,1)}, bf16[256,2048]{1,0:T(8,128)(2,1)}) custom-call(s32[5,4]{1,0:T(8,128)} %stack.13.bounds, bf16[384,2048]{1,0:T(8,128)(2,1)} %get-tuple-element.84.q, bf16[384,2048]{1,0:T(8,128)(2,1)} %get-tuple-element.85.k, bf16[384,2048]{1,0:T(8,128)(2,1)} %get-tuple-element.86.v, ...), custom_call_target="tpu_custom_call" | custom-call | flops 10737418240 | bytes 8388608 | tf_op jit(solution)/shard_map/attend_back/pallas_call | solution.py:372
  313.2 2.6 collective-permute-start.12
  315.9 2.1 fusion.22
  318.5 1.8 convolution_convert_fusion.6
  320.4 35.5 %attend_back.5 = (bf16[384,2048]{1,0:T(8,128)(2,1)}, bf16[256,2048]{1,0:T(8,128)(2,1)}) custom-call(s32[5,4]{1,0:T(8,128)} %stack.13.bounds, bf16[384,2048]{1,0:T(8,128)(2,1)} %get-tuple-element.84.q, bf16[384,2048]{1,0:T(8,128)(2,1)} %get-tuple-element.85.k, bf16[384,2048]{1,0:T(8,128)(2,1)} %get-tuple-element.86.v, ...), custom_call_target="tpu_custom_call" | custom-call | flops 10737418240 | bytes 8388608 | tf_op jit(solution)/shard_map/attend_back/pallas_call | solution.py:372
  357.0 2.3 collective-permute-start.14
  359.3 2.1 fusion.21
  361.8 1.8 convolution_convert_fusion.5
  364.8 1.9 slice.283
  366.7 6.4 %all-to-all-start = ((bf16[8,96,768]{2,1,0:T(8,128)(2,1)}), bf16[8,96,768]{2,1,0:T(8,128)(2,1)}, u32[]{:S(2)}, u32[]{:S(2)}) async-start(bf16[8,96,768]{2,1,0:T(8,128)(2,1)} %bitcast.36), calls=%async_computation.2 | async-start | bytes 2359296 | tf_op jit(solution)/shard_map/all_to_all | solution.py:747
  373.1 4.8 %fusion.23 = f32[2048,768]{1,0:T(8,128)S(1)} fusion(bf16[384,2048]{1,0:T(8,128)(2,1)} %bitcast.143, bf16[384,2048]{1,0:T(8,128)(2,1)} %bitcast.140, bf16[768,1280]{1,0:T(8,128)(2,1)} %all-gather.3.cloned.1.call-done.w_ref), kind=kOutput, calls=%fused_computation.60 | convolution fusion | flops 2422210560 | bytes 10616832 | tf_op jit(solution)/shard_map/dot_general | solution.py:728
  378.0 3.2 collective-permute-done.14
  381.2 2.2 collective-permute-start.16
  385.2 3.8 add_convert_fusion.1
  389.1 2.6 convolution_convert_fusion.4
  391.7 7.4 %all-to-all-done = bf16[8,96,768]{2,1,0:T(8,128)(2,1)} async-done(((bf16[8,96,768]{2,1,0:T(8,128)(2,1)}), bf16[8,96,768]{2,1,0:T(8,128)(2,1)}, u32[]{:S(2)}, u32[]{:S(2)}) %all-to-all-start) | async-done | bytes 1179680 | tf_op jit(solution)/shard_map/all_to_all | solution.py:747
  399.6 7.7 %fusion.40 = bf16[1,1024,768]{2,1,0:T(8,128)(2,1)} fusion(f32[1024,768]{1,0:T(8,128)} %copy-done.4, bf16[1024,768]{1,0:T(8,128)(2,1)} %collective-permute-done.7, f32[768]{0:T(1024)S(1)} %add.365, bf16[2048,1536]{1,0:T(8,128)(2,1)} %copy-done.32, bf16[768,768]{1,0:T(8,128)(2,1)} %get-tuple-element.171, bf16[768,768]{1,0:T(8,128)(2,1)} %copy-done.17), kind=kOutput, calls=%fused_computation.68 | convolution fusion | flops 2424569856 | bytes 11799552 | tf_op jit(solution)/shard_map/dot_general | solution.py:50
  410.5 2.4 convert_reduce_fusion.1
  414.5 3.1 assemble.1
  417.5 6.8 %all-to-all-start.1 = ((bf16[8,96,384]{2,1,0:T(8,128)(2,1)}), bf16[8,96,384]{2,1,0:T(8,128)(2,1)S(1)}, u32[]{:S(2)}, u32[]{:S(2)}) async-start(bf16[8,96,384]{2,1,0:T(8,128)(2,1)} %bitcast.159), calls=%async_computation.3 | async-start | bytes 1179648 | tf_op jit(solution)/shard_map/all_to_all | solution.py:747
  425.9 6.3 %fusion.9 = (f32[768]{0:T(1024)S(1)}, f32[1024]{0:T(1024)S(1)}, f32[1024]{0:T(1024)S(1)}, f32[768]{0:T(1024)S(1)}, f32[1024,768]{1,0:T(8,128)}) fusion(f32[1024]{0:T(1024)S(1)} %add_rsqrt_fusion, f32[1024]{0:T(1024)S(1)} %broadcast_multiply_fusion.2, bf16[1,1024,768]{2,1,0:T(8,128)(2,1)S(1)} %copy-done.3, f32[768]{0:T(1024)S(1)} %mul.206, ...), kind=kOutput, calls=%fused_computation.24 | convolution fusion | flops 614199808 | bytes 10839040 | tf_op jit(solution)/shard_map/dot_general | solution.py:728
  432.5 4.6 fusion.8
  439.1 12.9 %finish.1 = (f32[96,2304]{1,0:T(8,128)}, f32[10,128]{1,0:T(8,128)}) custom-call(bf16[96,1152]{1,0:T(8,128)(2,1)} %pad_maximum_fusion.18.g, f32[8,10,128]{2,1,0:T(8,128)} %copy.95.s), custom_call_target="tpu_custom_call" | custom-call | tf_op jit(solution)/shard_map/finish/pallas_call | solution.py:455
  456.1 2.1 copy.102
  (223 shorter events, 55.9 us)
Async XLA Ops:
  7.2 53.7 %all-gather.3.cloned.1.call-start = ((), (), s32[]{:S(2)}) async-start(), calls=%async_computation.4 | async-start | bytes 2211840 | tf_op jit(solution)/shard_map/all_gather | solution.py:575
  9.9 8.5 %copy-start.27 = (bf16[96,768]{1,0:T(8,128)(2,1)S(1)}, bf16[96,768]{1,0:T(8,128)(2,1)}, u32[]{:S(2)}) copy-start(bf16[96,768]{1,0:T(8,128)(2,1)} %param.21) | copy-start | bytes 442372
  9.9 8.5 %copy-start.25 = (bf16[384,768]{1,0:T(8,128)(2,1)S(1)}, bf16[384,768]{1,0:T(8,128)(2,1)}, u32[]{:S(2)}) copy-start(bf16[384,768]{1,0:T(8,128)(2,1)} %param.27) | copy-start | bytes 1769476
  10.7 133.8 %all-gather.5.cloned.1.call-start = ((), (), s32[]{:S(2)}) async-start(), calls=%async_computation.5 | async-start | bytes 5971968 | tf_op jit(solution)/shard_map/all_gather | solution.py:595
  14.2 5.2 %copy-start.2 = (bf16[1,1024,768]{2,1,0:T(8,128)(2,1)S(1)}, bf16[1,1024,768]{2,1,0:T(8,128)(2,1)}, u32[]{:S(2)}) copy-start(bf16[1,1024,768]{2,1,0:T(8,128)(2,1)} %param.15) | copy-start | bytes 4718596
  14.2 7.5 %copy-start.26 = (s32[1,2048]{1,0:T(1,128)S(1)}, s32[1,2048]{1,0:T(1,128)}, u32[]{:S(2)}) copy-start(s32[1,2048]{1,0:T(1,128)} %param.16) | copy-start | bytes 24580
  19.3 293.9 %reduce-scatter.3.cloned.1.call-start = ((), (), s32[]{:S(2)}) async-start(), calls=%async_computation.6 | async-start | bytes 2654208 | tf_op jit(solution)/shard_map/reduce_scatter | solution.py:675
  19.4 37.3 %collective-permute-start = (bf16[1024,768]{1,0:T(8,128)(2,1)S(1)}, bf16[1024,768]{1,0:T(8,128)(2,1)}, u32[]{:S(2)}, u32[]{:S(2)}) collective-permute-start(bf16[1024,768]{1,0:T(8,128)(2,1)S(1)} %bitcast.137), channel_id=1, source_target_pairs={{16,0},{24,8},{17,1},{25,9},{18,2},{26,10},{19,3},{27,11},{20,4},{... | collective-permute-start | bytes 4718600 | tf_op jit(solution)/shard_map/ppermute | solution.py:556
  20.9 43.6 %collective-permute-start.2 = (bf16[1024,768]{1,0:T(8,128)(2,1)S(1)}, bf16[1024,768]{1,0:T(8,128)(2,1)}, u32[]{:S(2)}, u32[]{:S(2)}) collective-permute-start(bf16[1024,768]{1,0:T(8,128)(2,1)S(1)} %bitcast.138), channel_id=1, source_target_pairs={{0,8},{8,0},{16,24},{24,16},{1,9},{9,1},{17,25},{25,17},{2,10},{10... | collective-permute-start | bytes 4718600 | tf_op jit(solution)/shard_map/ppermute | solution.py:555
  21.7 5.4 %collective-permute-start.1 = (bf16[1024,768]{1,0:T(8,128)(2,1)}, bf16[1024,768]{1,0:T(8,128)(2,1)}, u32[]{:S(2)}, u32[]{:S(2)}) collective-permute-start(bf16[1024,768]{1,0:T(8,128)(2,1)} %bitcast.145), channel_id=1, source_target_pairs={{0,8},{8,0},{16,24},{24,16},{1,9},{9,1},{17,25},{25,17},{2,10},{10... | collective-permute-start | bytes 4718600 | tf_op jit(solution)/shard_map/ppermute | solution.py:557
  58.7 5.8 %collective-permute-start.3 = (bf16[1024,768]{1,0:T(8,128)(2,1)}, bf16[1024,768]{1,0:T(8,128)(2,1)}, u32[]{:S(2)}, u32[]{:S(2)}) collective-permute-start(bf16[1024,768]{1,0:T(8,128)(2,1)} %collective-permute-done.sent), channel_id=1, source_target_pairs={{0,8},{8,0},{16,24},{24,16},{1,9},{9,1},{17,25},{25,17},{2,10},{10... | collective-permute-start | bytes 4718600 | tf_op jit(solution)/shard_map/ppermute | solution.py:636
  138.2 14.2 %copy-start.3 = (bf16[1,1024,768]{2,1,0:T(8,128)(2,1)S(1)}, bf16[1,1024,768]{2,1,0:T(8,128)(2,1)}, u32[]{:S(2)}) copy-start(bf16[1,1024,768]{2,1,0:T(8,128)(2,1)} %param.15) | copy-start | bytes 4718596
  146.9 9.0 %copy-start.18 = (bf16[384,1024]{1,0:T(8,128)(2,1)}, bf16[384,1024]{1,0:T(8,128)(2,1)S(1)}, u32[]{:S(2)}) copy-start(bf16[384,1024]{1,0:T(8,128)(2,1)S(1)} %get-tuple-element.177) | copy-start | bytes 2359300
  146.9 5.5 %collective-permute-start.4 = (bf16[384,1024]{1,0:T(8,128)(2,1)}, bf16[384,1024]{1,0:T(8,128)(2,1)}, u32[]{:S(2)}, u32[]{:S(2)}) collective-permute-start(bf16[384,1024]{1,0:T(8,128)(2,1)} %get-tuple-element.178), channel_id=1, source_target_pairs={{0,8},{8,0},{16,24},{24,16},{1,9},{9,1},{17,25},{25,17},{2,10},{10... | collective-permute-start | bytes 2359304 | tf_op jit(solution)/shard_map/ppermute | solution.py:653
  150.2 5.7 %copy-start.20 = (bf16[768,384]{1,0:T(8,128)(2,1)}, bf16[768,384]{1,0:T(8,128)(2,1)S(1)}, u32[]{:S(2)}) copy-start(bf16[768,384]{1,0:T(8,128)(2,1)S(1)} %slice.212) | copy-start | bytes 1769476
  150.2 2.2 collective-permute-start.5
  158.2 3.8 collective-permute-start.6
  161.6 108.2 %copy-start.17 = (bf16[768,768]{1,0:T(8,128)(2,1)}, bf16[768,768]{1,0:T(8,128)(2,1)S(1)}, u32[]{:S(2)}) copy-start(bf16[768,768]{1,0:T(8,128)(2,1)S(1)} %get-tuple-element.170) | copy-start | bytes 3538948
  161.6 15.1 %copy-start.12 = (bf16[2048,768]{1,0:T(8,128)(2,1)S(1)}, bf16[2048,768]{1,0:T(8,128)(2,1)}, u32[]{:S(2)}) copy-start(bf16[2048,768]{1,0:T(8,128)(2,1)} %pad_maximum_fusion) | copy-start | bytes 9437188
  176.7 5.4 %copy-start.32 = (bf16[2048,1536]{1,0:T(8,128)(2,1)}, bf16[2048,1536]{1,0:T(8,128)(2,1)S(1)}, u32[]{:S(2)}) copy-start(bf16[2048,1536]{1,0:T(8,128)(2,1)S(1)} %get-tuple-element.96) | copy-start | bytes 18874372
  192.0 7.2 %copy-start.33 = (bf16[2048,1536]{1,0:T(8,128)(2,1)}, bf16[2048,1536]{1,0:T(8,128)(2,1)S(1)}, u32[]{:S(2)}) copy-start(bf16[2048,1536]{1,0:T(8,128)(2,1)S(1)} %get-tuple-element.203) | copy-start | bytes 18874372
  199.2 3.8 collective-permute-start.8
  199.5 157.5 %reduce-scatter.5.cloned.1.call-start = ((), (), s32[]{:S(2)}) async-start(), calls=%async_computation.7 | async-start | bytes 3317760 | tf_op jit(solution)/shard_map/reduce_scatter | solution.py:675
  199.6 10.7 %copy-start.5 = (f32[1024,768]{1,0:T(8,128)S(1)}, f32[1024,768]{1,0:T(8,128)}, u32[]{:S(2)}) copy-start(f32[1024,768]{1,0:T(8,128)} %copy-done.4) | copy-start | bytes 9437188
  199.6 10.7 %copy-start.9 = (bf16[1,1024,768]{2,1,0:T(8,128)(2,1)S(1)}, bf16[1,1024,768]{2,1,0:T(8,128)(2,1)}, u32[]{:S(2)}) copy-start(bf16[1,1024,768]{2,1,0:T(8,128)(2,1)} %param.29) | copy-start | bytes 4718596
  212.1 5.0 %copy-start.6 = (f32[1024,768]{1,0:T(8,128)}, f32[1024,768]{1,0:T(8,128)S(1)}, u32[]{:S(2)}) copy-start(f32[1024,768]{1,0:T(8,128)S(1)} %get-tuple-element.165) | copy-start | bytes 9437188
  216.7 11.2 %collective-permute-start.9 = (bf16[384,1024]{1,0:T(8,128)(2,1)S(1)}, bf16[384,1024]{1,0:T(8,128)(2,1)S(1)}, u32[]{:S(2)}, u32[]{:S(2)}) collective-permute-start(bf16[384,1024]{1,0:T(8,128)(2,1)S(1)} %get-tuple-element.175), channel_id=1, source_target_pairs={{0,8},{8,0},{16,24},{24,16},{1,9},{9,1},{17,25},{25,17},{2,10},{10... | collective-permute-start | bytes 2359304 | tf_op jit(solution)/shard_map/ppermute | solution.py:698
  220.2 7.6 %collective-permute-start.10 = (bf16[768,384]{1,0:T(8,128)(2,1)S(1)}, bf16[768,384]{1,0:T(8,128)(2,1)S(1)}, u32[]{:S(2)}, u32[]{:S(2)}) collective-permute-start(bf16[768,384]{1,0:T(8,128)(2,1)S(1)} %constant_dynamic-slice_fusion.1), channel_id=1, source_target_pairs={{0,8},{8,0},{16,24},{24,16},{1,9},{9,1},{17,25},{25,17},{2,10},{10... | collective-permute-start | bytes 1769480 | tf_op jit(solution)/shard_map/ppermute | solution.py:701
  267.5 45.7 %collective-permute-start.11 = (bf16[256,2048]{1,0:T(8,128)(2,1)}, bf16[256,2048]{1,0:T(8,128)(2,1)}, u32[]{:S(2)}, u32[]{:S(2)}) collective-permute-start(bf16[256,2048]{1,0:T(8,128)(2,1)} %get-tuple-element.109), channel_id=1, source_target_pairs={{0,16},{8,24},{1,17},{9,25},{2,18},{10,26},{3,19},{11,27},{4,20},{... | collective-permute-start | bytes 3145736 | tf_op jit(solution)/shard_map/ppermute | solution.py:713
  275.8 123.8 %collective-permute-start.7 = (bf16[1024,768]{1,0:T(8,128)(2,1)}, bf16[1024,768]{1,0:T(8,128)(2,1)}, u32[]{:S(2)}, u32[]{:S(2)}) collective-permute-start(bf16[1024,768]{1,0:T(8,128)(2,1)} %fusion.32), channel_id=1, source_target_pairs={{0,8},{8,0},{16,24},{24,16},{1,9},{9,1},{17,25},{25,17},{2,10},{10... | collective-permute-start | bytes 4718600 | tf_op jit(solution)/shard_map/ppermute | solution.py:664
  313.2 43.7 %collective-permute-start.12 = (bf16[256,2048]{1,0:T(8,128)(2,1)}, bf16[256,2048]{1,0:T(8,128)(2,1)}, u32[]{:S(2)}, u32[]{:S(2)}) collective-permute-start(bf16[256,2048]{1,0:T(8,128)(2,1)} %get-tuple-element.115), channel_id=1, source_target_pairs={{0,16},{8,24},{1,17},{9,25},{2,18},{10,26},{3,19},{11,27},{4,20},{... | collective-permute-start | bytes 3145736 | tf_op jit(solution)/shard_map/ppermute | solution.py:713
  320.3 36.7 %collective-permute-start.13 = (bf16[96,1536]{1,0:T(8,128)(2,1)S(1)}, bf16[96,1536]{1,0:T(8,128)(2,1)S(1)}, u32[]{:S(2)}, u32[]{:S(2)}) collective-permute-start(bf16[96,1536]{1,0:T(8,128)(2,1)S(1)} %copy-done.23), channel_id=1, source_target_pairs={{0,16},{8,24},{16,0},{24,8},{1,17},{9,25},{17,1},{25,9},{2,18},{10... | collective-permute-start | bytes 884744 | tf_op jit(solution)/shard_map/ppermute | solution.py:737
  357.0 4.6 copy-start.24
  357.0 24.2 %collective-permute-start.14 = (bf16[256,2048]{1,0:T(8,128)(2,1)}, bf16[256,2048]{1,0:T(8,128)(2,1)}, u32[]{:S(2)}, u32[]{:S(2)}) collective-permute-start(bf16[256,2048]{1,0:T(8,128)(2,1)} %get-tuple-element.119), channel_id=1, source_target_pairs={{0,16},{8,24},{1,17},{9,25},{2,18},{10,26},{3,19},{11,27},{4,20},{... | collective-permute-start | bytes 3145736 | tf_op jit(solution)/shard_map/ppermute | solution.py:713
  366.7 32.4 %all-to-all-start = ((bf16[8,96,768]{2,1,0:T(8,128)(2,1)}), bf16[8,96,768]{2,1,0:T(8,128)(2,1)}, u32[]{:S(2)}, u32[]{:S(2)}) async-start(bf16[8,96,768]{2,1,0:T(8,128)(2,1)} %bitcast.36), calls=%async_computation.2 | async-start | bytes 2359296 | tf_op jit(solution)/shard_map/all_to_all | solution.py:747
  373.1 8.1 %copy-start.22 = (bf16[96,1920]{1,0:T(8,128)(2,1)S(1)}, bf16[96,1920]{1,0:T(8,128)(2,1)}, u32[]{:S(2)}) copy-start(bf16[96,1920]{1,0:T(8,128)(2,1)} %reduce-scatter.5.cloned.1.call-done) | copy-start | bytes 1105924
  373.1 10.3 %copy-start.14 = (bf16[384,2048]{1,0:T(8,128)(2,1)S(1)}, bf16[384,2048]{1,0:T(8,128)(2,1)}, u32[]{:S(2)}) copy-start(bf16[384,2048]{1,0:T(8,128)(2,1)} %get-tuple-element.126) | copy-start | bytes 4718596
  378.0 7.3 %copy-start.13 = (f32[2048,768]{1,0:T(8,128)}, f32[2048,768]{1,0:T(8,128)S(1)}, u32[]{:S(2)}) copy-start(f32[2048,768]{1,0:T(8,128)S(1)} %fusion.23) | copy-start | bytes 18874372
  378.0 7.1 %copy-start.10 = (bf16[2,1,64,2048]{3,2,1,0:T(8,128)(2,1)S(1)}, bf16[2,1,64,2048]{3,2,1,0:T(8,128)(2,1)}, u32[]{:S(2)}) copy-start(bf16[2,1,64,2048]{3,2,1,0:T(8,128)(2,1)} %slice.283) | copy-start | bytes 1572868
  381.2 26.4 %collective-permute-start.16 = (bf16[96,1920]{1,0:T(8,128)(2,1)S(1)}, bf16[96,1920]{1,0:T(8,128)(2,1)}, u32[]{:S(2)}, u32[]{:S(2)}) collective-permute-start(bf16[96,1920]{1,0:T(8,128)(2,1)S(1)} %copy-done.22), channel_id=1, source_target_pairs={{0,16},{8,24},{16,0},{24,8},{1,17},{9,25},{17,1},{25,9},{2,18},{10... | collective-permute-start | bytes 1105928 | tf_op jit(solution)/shard_map/ppermute | solution.py:768
  385.2 3.9 copy-start.11
  399.1 26.7 %collective-permute-start.15 = (bf16[1024,768]{1,0:T(8,128)(2,1)}, bf16[1024,768]{1,0:T(8,128)(2,1)}, u32[]{:S(2)}, u32[]{:S(2)}) collective-permute-start(bf16[1024,768]{1,0:T(8,128)(2,1)} %add_convert_fusion.1), channel_id=1, source_target_pairs={{0,8},{8,0},{16,24},{24,16},{1,9},{9,1},{17,25},{25,17},{2,10},{10... | collective-permute-start | bytes 4718600 | tf_op jit(solution)/shard_map/ppermute | solution.py:761
  408.7 5.8 %copy-start.15 = (bf16[96,1920]{1,0:T(8,128)(2,1)}, bf16[96,1920]{1,0:T(8,128)(2,1)S(1)}, u32[]{:S(2)}) copy-start(bf16[96,1920]{1,0:T(8,128)(2,1)S(1)} %add_convert_fusion.5.mine) | copy-start | bytes 1105924
  408.7 5.7 %collective-permute-start.17 = (bf16[96,1920]{1,0:T(8,128)(2,1)S(1)}, bf16[96,1920]{1,0:T(8,128)(2,1)}, u32[]{:S(2)}, u32[]{:S(2)}) collective-permute-start(bf16[96,1920]{1,0:T(8,128)(2,1)S(1)} %add_convert_fusion.5.mine), channel_id=1, source_target_pairs={{0,8},{8,0},{16,24},{24,16},{1,9},{9,1},{17,25},{25,17},{2,10},{10... | collective-permute-start | bytes 1105928 | tf_op jit(solution)/shard_map/ppermute | solution.py:766
  410.0 4.5 copy-start.16
  410.0 4.5 collective-permute-start.18
  417.5 20.1 %all-to-all-start.1 = ((bf16[8,96,384]{2,1,0:T(8,128)(2,1)}), bf16[8,96,384]{2,1,0:T(8,128)(2,1)S(1)}, u32[]{:S(2)}, u32[]{:S(2)}) async-start(bf16[8,96,384]{2,1,0:T(8,128)(2,1)} %bitcast.159), calls=%async_computation.3 | async-start | bytes 1179648 | tf_op jit(solution)/shard_map/all_to_all | solution.py:747
  432.4 25.8 %copy-start.1 = (bf16[96,2304]{1,0:T(8,128)(2,1)S(1)}, bf16[96,2304]{1,0:T(8,128)(2,1)}, u32[]{:S(2)}) copy-start(bf16[96,2304]{1,0:T(8,128)(2,1)} %param.19) | copy-start | bytes 1327108
  (13 other events, 31.5 us)
Sparse Core Ops, SparseCore 0:
  10.8 47.0 all-gather.2
  60.6 83.8 all-gather.4
  199.7 67.0 reduce-scatter.2
  270.1 73.6 reduce-scatter.4

commit v7 on v6

--- a/solution.py
+++ b/solution.py
@@ -643,14 +643,14 @@
         bias_own, cos_t, sin_t, heads
     )
     o, lse = attend(wide_bounds, q, k, v, kc, vc, id_row, id_col, heads, 1)
-    o, lse, ffn = lax.optimization_barrier((o, lse, ffn))
+    cut = lambda value, which: lax.dynamic_slice_in_dim(value, which * local_rows, local_rows, 1)
+    o_mine = cut(o, core)
+    o_in = lax.ppermute(cut(o, 1 - core), "seq", swap)
+    o_mine, o_in, ffn = lax.optimization_barrier((o_mine, o_in, ffn))
     at = span + n_fsdp * inner
     out_near, up_own = ffn[:, :span], ffn[:, span:at]
     down_own = jnp.concatenate([ffn[:, at : at + width], ffn[:, at + width :]], 0)
     out_full = in_order(out_near, lax.ppermute(out_near, "seq", swap), 1)
-    cut = lambda value, which: lax.dynamic_slice_in_dim(value, which * local_rows, local_rows, 1)
-    o_mine = cut(o, core)
-    o_in = lax.ppermute(cut(o, 1 - core), "seq", swap)
     attended = in_order(o_mine, o_in, 0)
 
     rows_in = tok.astype(F32)
@@ -756,8 +756,7 @@
     got_2, out_up_part, first_01 = hold((got_2, out_up_part, first_01))
     own_2 = joined(own_2, got_2)
     far_rows = (first_01[local_rows:] + back(own_2[:, local_rows:], 2, 1)).astype(BF)
-    grad_2, far_rows, pieces_01 = hold((weight_grad(own_2), far_rows, pieces_01))
-    pieces_2 = exchange(grad_2)
+    grad_2, far_rows = hold((weight_grad(own_2), far_rows))
     got_rows = lax.ppermute(far_rows, "seq", swap).astype(F32)
     grad_first = first_01[:local_rows] + back(own_2[:, :local_rows], 2, 1) + got_rows
 
@@ -770,6 +769,8 @@
         core.reshape(1).astype(jnp.int32), *out_up_both, *chip_sum(down_part, down_far), span, n_fsdp
     )
 
+    grad_2, pieces_01, out_g, up_g, down_g = hold((grad_2, pieces_01, out_g, up_g, down_g))
+    pieces_2 = exchange(grad_2)
     sum_cols = lambda own: jnp.sum(own.astype(F32), 1)
     grad_qkv_b = jnp.concatenate([sum_cols(own_01), sum_cols(own_2)])
     normed_one, inverse_one = normalize_parts(rows_in)

time: 473 us -> 466 us (0.985)
  waiting for transfers between devices: 50.7 us -> 45.9 us
    all_to_all x2, waiting for transfers between devices: 8.02 us -> 0.61 us  [on_device(): lax.all_to_all(grad.reshape(n_fsdp, shard, grad.shape[1]), 'fsdp', 0, 0)]
  transfers between devices with their start and end apart: 25 -> 25, of which waited for: 9 -> 10; matrix products, arithmetic and copies ran while one was open for 24% -> 24% of each run, Pallas kernels for 39% -> 40%
where the time goes in v7:
time: 466 us; the launch traced here: 458 us
  Pallas kernels  198 us (42%)
  matrix products  93.2 us (20%)
  waiting for transfers between devices  45.9 us (10%)
  other arithmetic  37.9 us (8%)
  local copies, waits for them, and re-layouts  37.6 us (8%)
  starting transfers between devices  30.4 us (7%)
  between operations  15 us (3%)
    pallas_call x3, Pallas kernels, attend_back(): pl.pallas_call(functools.partial(attend_back_kernel, group), grid_spec=pl...  107 us
    pallas_call x1, Pallas kernels, attend(): pl.pallas_call(functools.partial(attend_kernel, group), grid_spec=pltpu.P...  50.9 us
    dot_general x4, matrix products, dot(): return jnp.dot(left, right, preferred_element_type=F32)  29.5 us
    dot_general x4, matrix products, right_transposed(): lax.dot_general(left, right, (((1,), (1,)), ((), ())), preferred_element_...  26.2 us
    ppermute x1, waiting for transfers between devices, on_device(): clean_in = lax.ppermute(tok, 'seq', [(2, 0), (3, 1)])  26 us
    pallas_call x1, Pallas kernels, project(): pl.pallas_call(functools.partial(qkv_kernel, heads), grid_spec=pltpu.Pref...  22.3 us
    dot_general x3, matrix products, rows_contract(): lax.dot_general(left, right, (((0,), (0,)), ((), ())), preferred_element_...  16.2 us
    dot_general x3, matrix products, back(): lax.dot_general(own, cols, (((0,), (1,)), ((), ())), preferred_element_ty...  15 us
  transfers between devices with their start and end apart: 25, of which 10 were waited for; matrix products, arithmetic and copies ran while one was open for 24% of the time, Pallas kernels for 40%

profile of v7, /device:TPU:13, one launch (start us, length us, event | category | flops | bytes accessed | tf_op | source)
XLA Modules:
  0.0 458.1 jit_solution(17043170273840156962)
XLA Ops:
  10.7 3.5 reshape.688
  14.2 2.1 constant_dynamic-slice_fusion.5
  23.2 2.0 fusion.54
  26.9 3.8 pad_maximum_fusion
  30.7 26.0 %collective-permute-done.sent = bf16[1024,768]{1,0:T(8,128)(2,1)} collective-permute-done((bf16[1024,768]{1,0:T(8,128)(2,1)S(1)}, bf16[1024,768]{1,0:T(8,128)(2,1)}, u32[]{:S(2)}, u32[]{:S(2)}) %collective-permute-start) | collective-permute-done | bytes 1572896 | tf_op jit(solution)/shard_map/ppermute | solution.py:556
  64.5 22.3 %project.1 = (bf16[384,2048]{1,0:T(8,128)(2,1)}, bf16[384,2048]{1,0:T(8,128)(2,1)}, bf16[384,2048]{1,0:T(8,128)(2,1)}, bf16[384,2048]{1,0:T(8,128)(2,1)}, bf16[3...) custom-call(s32[2]{0:T(128)} %pad_add_fusion.core_ref, bf16[1024,768]{1,0:T(8,128)(2,1)} %bitcast.135, ...), custom_call_target="tpu_custom_call" | custom-call | tf_op jit(solution)/shard_map/project/pallas_call | solution.py:122
  86.8 50.9 %attend.1 = (bf16[384,2048]{1,0:T(8,128)(2,1)}, f32[6,8,2048]{2,1,0:T(8,128)}) custom-call(s32[5,4]{1,0:T(8,128)} %stack.14.bounds, bf16[384,2048]{1,0:T(8,128)(2,1)} %get-tuple-element.88.q, bf16[384,2048]{1,0:T(8,128)(2,1)} %get-tuple-element.89.k, bf16[384,2048]{1,0:T(8,128)(2,1)} %get-tuple-element.90.v, bf16[384,2048]{1,0:T(8,128)(2,1)} %get-tuple-element.91.kc, ...), custom_call_target="tpu_custom_call" | custom-call | flops 25769803776 | bytes 16777216 | tf_op jit(solution)/shard_map/attend/pallas_call | solution.py:240
  139.4 2.4 collective-permute-done.4
  141.8 3.0 all-gather.5.cloned.1.call-done
  145.9 2.1 collective-permute-start.5
  149.8 3.5 fusion.72
  156.2 2.8 fusion.69
  159.3 15.2 %add_convert_fusion = (bf16[2048,1536]{1,0:T(8,128)(2,1)}, bf16[2048,1536]{1,0:T(8,128)(2,1)S(1)}) fusion(f32[1536]{0:T(1024)S(1)} %add.354, bf16[768,3456]{1,0:T(8,128)(2,1)} %all-gather.5.cloned.1.call-done, bf16[1024,768]{1,0:T(8,128)(2,1)} %collective-permute-done.6, bf16[1024,768]{1,0:T(8,128)(2,1)} %add_convert_fusion.3), kind=kOutput, calls=%fused_computation.2 | convolution fusion | flops 4891607040 | bytes 18094080 | tf_op jit(solution)/shard_map/dot_general | solution.py:50
  174.5 5.4 %convolution_convert_fusion.1 = bf16[1536,768]{1,0:T(8,128)(2,1)S(1)} fusion(bf16[2048,1536]{1,0:T(8,128)(2,1)S(1)} %get-tuple-element.100, bf16[2048,768]{1,0:T(8,128)(2,1)S(1)} %copy-done.13), kind=kOutput, calls=%fused_computation.19 | convolution fusion | flops 4833017856 | bytes 11796480 | tf_op jit(solution)/shard_map/dot_general | solution.py:42
  181.8 8.0 %convert_reduce_fusion = (f32[1536]{0:T(1024)S(1)}, bf16[2048,1536]{1,0:T(8,128)(2,1)S(1)}) fusion(bf16[2048,1536]{1,0:T(8,128)(2,1)} %get-tuple-element.102, bf16[2048,768]{1,0:T(8,128)(2,1)} %pad_maximum_fusion, bf16[768,768]{1,0:T(8,128)(2,1)} %get-tuple-element.179, bf16[768,768]{1,0:T(8,128)(2,1)S(1)} %get-tuple-element.178), kind=kOutput, calls=%fused_computation | convolution fusion | flops 4852283904 | bytes 18094080 | tf_op jit(solution)/shard_map/dot_general | solution.py:46
  189.8 7.2 %fusion.35 = bf16[1024,768]{1,0:T(8,128)(2,1)} fusion(bf16[768,3456]{1,0:T(8,128)(2,1)} %all-gather.5.cloned.1.call-done, bf16[2048,1536]{1,0:T(8,128)(2,1)S(1)} %get-tuple-element.211), kind=kOutput, calls=%fused_computation.66 | convolution fusion | flops 2416705536 | bytes 7077888 | tf_op jit(solution)/shard_map/dot_general | solution.py:46
  197.3 3.5 collective-permute-done.8
  200.8 7.4 %multiply_reduce_fusion = (f32[768]{0:T(1024)S(1)}, f32[1024]{0:T(1024)S(1)}, f32[1024]{0:T(1024)S(1)}, f32[768]{0:T(1024)S(1)}, f32[1024,768]{1,0:T(8,128)S(1)}) fusion(f32[1024,768]{1,0:T(8,128)} %copy-done.4, f32[1024]{0:T(1024)S(1)} %add_rsqrt_fusion.1, f32[1024]{0:T(1024)S(1)} %broadcast_multiply_fusion.5, f32[768]{0:T(1024)S(1)} %mul.183, ...), kind=kOutput, calls=%fused_computation.34 | convolution fusion | flops 2424566272 | bytes 13394944 | tf_op jit(solution)/shard_map/dot_general | solution.py:46
  209.9 3.6 convolution_convert_fusion.2
  214.9 3.0 convolution_convert_fusion.3
  218.2 7.3 %convolution_convert_fusion = bf16[768,1536]{1,0:T(8,128)(2,1)S(1)} fusion(bf16[2048,1536]{1,0:T(8,128)(2,1)S(1)} %bitcast.180, bf16[1024,768]{1,0:T(8,128)(2,1)} %collective-permute-done.6, bf16[1024,768]{1,0:T(8,128)(2,1)} %add_convert_fusion.3), kind=kOutput, calls=%fused_computation.18 | convolution fusion | flops 4839309312 | bytes 11796480 | tf_op jit(solution)/shard_map/dot_general | solution.py:42
  226.6 1.9 pad_maximum_fusion.3
  229.6 35.7 %attend_back.3 = (bf16[384,2048]{1,0:T(8,128)(2,1)}, bf16[256,2048]{1,0:T(8,128)(2,1)}) custom-call(s32[5,4]{1,0:T(8,128)} %stack.13.bounds, bf16[384,2048]{1,0:T(8,128)(2,1)} %get-tuple-element.88.q, bf16[384,2048]{1,0:T(8,128)(2,1)} %get-tuple-element.89.k, bf16[384,2048]{1,0:T(8,128)(2,1)} %get-tuple-element.90.v, ...), custom_call_target="tpu_custom_call" | custom-call | flops 10737418240 | bytes 8388608 | tf_op jit(solution)/shard_map/attend_back/pallas_call | solution.py:372
  265.2 2.3 collective-permute-start.11
  267.5 6.0 %fusion.32 = bf16[1024,768]{1,0:T(8,128)(2,1)} fusion(bf16[2048,1536]{1,0:T(8,128)(2,1)} %copy-done.35, bf16[768,768]{1,0:T(8,128)(2,1)} %get-tuple-element.179, bf16[768,768]{1,0:T(8,128)(2,1)S(1)} %get-tuple-element.178), kind=kOutput, calls=%fused_computation.65 | convolution fusion | flops 2421424128 | bytes 7077888 | tf_op jit(solution)/shard_map/dot_general | solution.py:50
  275.4 35.7 %attend_back.4 = (bf16[384,2048]{1,0:T(8,128)(2,1)}, bf16[256,2048]{1,0:T(8,128)(2,1)}) custom-call(s32[5,4]{1,0:T(8,128)} %stack.13.bounds, bf16[384,2048]{1,0:T(8,128)(2,1)} %get-tuple-element.88.q, bf16[384,2048]{1,0:T(8,128)(2,1)} %get-tuple-element.89.k, bf16[384,2048]{1,0:T(8,128)(2,1)} %get-tuple-element.90.v, ...), custom_call_target="tpu_custom_call" | custom-call | flops 10737418240 | bytes 8388608 | tf_op jit(solution)/shard_map/attend_back/pallas_call | solution.py:372
  311.1 2.6 collective-permute-start.12
  313.8 2.1 fusion.22
  316.3 1.8 convolution_convert_fusion.6
  318.3 35.5 %attend_back.5 = (bf16[384,2048]{1,0:T(8,128)(2,1)}, bf16[256,2048]{1,0:T(8,128)(2,1)}) custom-call(s32[5,4]{1,0:T(8,128)} %stack.13.bounds, bf16[384,2048]{1,0:T(8,128)(2,1)} %get-tuple-element.88.q, bf16[384,2048]{1,0:T(8,128)(2,1)} %get-tuple-element.89.k, bf16[384,2048]{1,0:T(8,128)(2,1)} %get-tuple-element.90.v, ...), custom_call_target="tpu_custom_call" | custom-call | flops 10737418240 | bytes 8388608 | tf_op jit(solution)/shard_map/attend_back/pallas_call | solution.py:372
  354.9 2.3 collective-permute-start.14
  357.2 2.1 fusion.21
  362.7 1.9 slice.283
  364.6 6.4 %all-to-all-start = ((bf16[8,96,768]{2,1,0:T(8,128)(2,1)}), bf16[8,96,768]{2,1,0:T(8,128)(2,1)}, u32[]{:S(2)}, u32[]{:S(2)}) async-start(bf16[8,96,768]{2,1,0:T(8,128)(2,1)} %bitcast.36), calls=%async_computation.2 | async-start | bytes 2359296 | tf_op jit(solution)/shard_map/all_to_all | solution.py:747
  371.0 4.8 %fusion.23 = f32[2048,768]{1,0:T(8,128)S(1)} fusion(bf16[384,2048]{1,0:T(8,128)(2,1)} %bitcast.143, bf16[384,2048]{1,0:T(8,128)(2,1)} %bitcast.140, bf16[768,1280]{1,0:T(8,128)(2,1)} %all-gather.3.cloned.1.call-done.w_ref), kind=kOutput, calls=%fused_computation.60 | convolution fusion | flops 2422210560 | bytes 10616832 | tf_op jit(solution)/shard_map/dot_general | solution.py:728
  375.9 3.4 collective-permute-done.14
  381.2 3.8 add_convert_fusion.1
  385.1 2.6 convolution_convert_fusion.4
  388.4 2.2 collective-permute-start.16
  390.6 5.2 %fusion.40 = bf16[1,1024,768]{2,1,0:T(8,128)(2,1)} fusion(f32[1024,768]{1,0:T(8,128)S(1)} %copy-done.6, bf16[1024,768]{1,0:T(8,128)(2,1)} %collective-permute-done.7, f32[768]{0:T(1024)S(1)} %add.365, bf16[2048,1536]{1,0:T(8,128)(2,1)S(1)} %bitcast.178, bf16[768,768]{1,0:T(8,128)(2,1)S(1)} %copy-done.20, bf16[768,768]{1,0:T(8,128)(2,1)S(1)} %copy-done.19), kind=kOutput, calls=%fused_computation.68 | convolution fusion | flops 2424569856 | bytes 11800576 | tf_op jit(solution)/shard_map/dot_general | solution.py:50
  396.2 3.4 collective-permute-done.16
  402.7 2.4 convert_reduce_fusion.1
  406.7 3.1 assemble.1
  409.7 5.7 %all-to-all-start.1 = ((bf16[8,96,384]{2,1,0:T(8,128)(2,1)}), bf16[8,96,384]{2,1,0:T(8,128)(2,1)S(1)}, u32[]{:S(2)}, u32[]{:S(2)}) async-start(bf16[8,96,384]{2,1,0:T(8,128)(2,1)} %bitcast.159), calls=%async_computation.3 | async-start | bytes 1179648 | tf_op jit(solution)/shard_map/all_to_all | solution.py:747
  416.9 6.3 %fusion.9 = (f32[768]{0:T(1024)S(1)}, f32[1024]{0:T(1024)S(1)}, f32[1024]{0:T(1024)S(1)}, f32[768]{0:T(1024)S(1)}, f32[1024,768]{1,0:T(8,128)}) fusion(f32[1024]{0:T(1024)S(1)} %add_rsqrt_fusion, f32[1024]{0:T(1024)S(1)} %broadcast_multiply_fusion.2, bf16[1,1024,768]{2,1,0:T(8,128)(2,1)S(1)} %copy-done.3, f32[768]{0:T(1024)S(1)} %mul.206, ...), kind=kOutput, calls=%fused_computation.24 | convolution fusion | flops 614199808 | bytes 10839040 | tf_op jit(solution)/shard_map/dot_general | solution.py:728
  423.5 4.6 %fusion.8 = f32[1024,768]{1,0:T(8,128)} fusion(f32[1024,768]{1,0:T(8,128)} %copy-done.7, f32[1024,768]{1,0:T(8,128)} %get-tuple-element.209, f32[1024]{0:T(1024)S(1)} %broadcast_multiply_fusion, f32[1024]{0:T(1024)S(1)} %broadcast_multiply_fusion.1, f32[768]{0:T(1024)S(1)} %mul.206, f32[1024]{0:T(1024)S(1)} %add_rsqrt_fusion, ...), kind=kLoop, calls=%fused_computation.23 | loop fusion | flops 7077888 | bytes 11029504 | tf_op jit(solution)/shard_map/add | solution.py:779
  430.2 14.9 %finish.1 = (f32[96,2304]{1,0:T(8,128)}, f32[10,128]{1,0:T(8,128)}) custom-call(bf16[96,1152]{1,0:T(8,128)(2,1)} %pad_maximum_fusion.18.g, f32[8,10,128]{2,1,0:T(8,128)} %copy.95.s), custom_call_target="tpu_custom_call" | custom-call | tf_op jit(solution)/shard_map/finish/pallas_call | solution.py:455
  449.2 2.1 copy.102
  (234 shorter events, 57.1 us)
Async XLA Ops:
  7.2 53.7 %all-gather.3.cloned.1.call-start = ((), (), s32[]{:S(2)}) async-start(), calls=%async_computation.4 | async-start | bytes 2211840 | tf_op jit(solution)/shard_map/all_gather | solution.py:575
  9.9 8.5 %copy-start.30 = (bf16[96,768]{1,0:T(8,128)(2,1)S(1)}, bf16[96,768]{1,0:T(8,128)(2,1)}, u32[]{:S(2)}) copy-start(bf16[96,768]{1,0:T(8,128)(2,1)} %param.21) | copy-start | bytes 442372
  9.9 8.5 %copy-start.28 = (bf16[384,768]{1,0:T(8,128)(2,1)S(1)}, bf16[384,768]{1,0:T(8,128)(2,1)}, u32[]{:S(2)}) copy-start(bf16[384,768]{1,0:T(8,128)(2,1)} %param.27) | copy-start | bytes 1769476
  10.7 134.1 %all-gather.5.cloned.1.call-start = ((), (), s32[]{:S(2)}) async-start(), calls=%async_computation.5 | async-start | bytes 5971968 | tf_op jit(solution)/shard_map/all_gather | solution.py:595
  14.2 7.3 %copy-start.29 = (s32[1,2048]{1,0:T(1,128)S(1)}, s32[1,2048]{1,0:T(1,128)}, u32[]{:S(2)}) copy-start(s32[1,2048]{1,0:T(1,128)} %param.16) | copy-start | bytes 24580
  19.3 291.8 %reduce-scatter.3.cloned.1.call-start = ((), (), s32[]{:S(2)}) async-start(), calls=%async_computation.6 | async-start | bytes 2654208 | tf_op jit(solution)/shard_map/reduce_scatter | solution.py:675
  19.4 37.3 %collective-permute-start = (bf16[1024,768]{1,0:T(8,128)(2,1)S(1)}, bf16[1024,768]{1,0:T(8,128)(2,1)}, u32[]{:S(2)}, u32[]{:S(2)}) collective-permute-start(bf16[1024,768]{1,0:T(8,128)(2,1)S(1)} %bitcast.137), channel_id=1, source_target_pairs={{16,0},{24,8},{17,1},{25,9},{18,2},{26,10},{19,3},{27,11},{20,4},{... | collective-permute-start | bytes 4718600 | tf_op jit(solution)/shard_map/ppermute | solution.py:556
  20.7 43.8 %collective-permute-start.2 = (bf16[1024,768]{1,0:T(8,128)(2,1)S(1)}, bf16[1024,768]{1,0:T(8,128)(2,1)}, u32[]{:S(2)}, u32[]{:S(2)}) collective-permute-start(bf16[1024,768]{1,0:T(8,128)(2,1)S(1)} %bitcast.138), channel_id=1, source_target_pairs={{0,8},{8,0},{16,24},{24,16},{1,9},{9,1},{17,25},{25,17},{2,10},{10... | collective-permute-start | bytes 4718600 | tf_op jit(solution)/shard_map/ppermute | solution.py:555
  21.4 5.4 %collective-permute-start.1 = (bf16[1024,768]{1,0:T(8,128)(2,1)}, bf16[1024,768]{1,0:T(8,128)(2,1)}, u32[]{:S(2)}, u32[]{:S(2)}) collective-permute-start(bf16[1024,768]{1,0:T(8,128)(2,1)} %bitcast.145), channel_id=1, source_target_pairs={{0,8},{8,0},{16,24},{24,16},{1,9},{9,1},{17,25},{25,17},{2,10},{10... | collective-permute-start | bytes 4718600 | tf_op jit(solution)/shard_map/ppermute | solution.py:557
  58.7 5.8 %collective-permute-start.3 = (bf16[1024,768]{1,0:T(8,128)(2,1)}, bf16[1024,768]{1,0:T(8,128)(2,1)}, u32[]{:S(2)}, u32[]{:S(2)}) collective-permute-start(bf16[1024,768]{1,0:T(8,128)(2,1)} %collective-permute-done.sent), channel_id=1, source_target_pairs={{0,8},{8,0},{16,24},{24,16},{1,9},{9,1},{17,25},{25,17},{2,10},{10... | collective-permute-start | bytes 4718600 | tf_op jit(solution)/shard_map/ppermute | solution.py:636
  137.7 12.1 %copy-start.3 = (bf16[1,1024,768]{2,1,0:T(8,128)(2,1)S(1)}, bf16[1,1024,768]{2,1,0:T(8,128)(2,1)}, u32[]{:S(2)}) copy-start(bf16[1,1024,768]{2,1,0:T(8,128)(2,1)} %param.15) | copy-start | bytes 4718596
  139.3 13.9 %copy-start.21 = (bf16[384,1024]{1,0:T(8,128)(2,1)}, bf16[384,1024]{1,0:T(8,128)(2,1)S(1)}, u32[]{:S(2)}) copy-start(bf16[384,1024]{1,0:T(8,128)(2,1)S(1)} %get-tuple-element.96) | copy-start | bytes 2359300
  139.3 2.5 collective-permute-start.4
  145.9 7.4 %copy-start.23 = (bf16[768,384]{1,0:T(8,128)(2,1)}, bf16[768,384]{1,0:T(8,128)(2,1)S(1)}, u32[]{:S(2)}) copy-start(bf16[768,384]{1,0:T(8,128)(2,1)S(1)} %slice.212) | copy-start | bytes 1769476
  145.9 3.9 collective-permute-start.5
  155.6 3.8 collective-permute-start.6
  159.0 108.5 %copy-start.18 = (bf16[768,768]{1,0:T(8,128)(2,1)}, bf16[768,768]{1,0:T(8,128)(2,1)S(1)}, u32[]{:S(2)}) copy-start(bf16[768,768]{1,0:T(8,128)(2,1)S(1)} %get-tuple-element.178) | copy-start | bytes 3538948
  159.0 15.5 %copy-start.13 = (bf16[2048,768]{1,0:T(8,128)(2,1)S(1)}, bf16[2048,768]{1,0:T(8,128)(2,1)}, u32[]{:S(2)}) copy-start(bf16[2048,768]{1,0:T(8,128)(2,1)} %pad_maximum_fusion) | copy-start | bytes 9437188
  174.5 5.4 %copy-start.35 = (bf16[2048,1536]{1,0:T(8,128)(2,1)}, bf16[2048,1536]{1,0:T(8,128)(2,1)S(1)}, u32[]{:S(2)}) copy-start(bf16[2048,1536]{1,0:T(8,128)(2,1)S(1)} %get-tuple-element.100) | copy-start | bytes 18874372
  189.8 7.2 %copy-start.36 = (bf16[2048,1536]{1,0:T(8,128)(2,1)}, bf16[2048,1536]{1,0:T(8,128)(2,1)S(1)}, u32[]{:S(2)}) copy-start(bf16[2048,1536]{1,0:T(8,128)(2,1)S(1)} %get-tuple-element.211) | copy-start | bytes 18874372
  197.0 3.8 collective-permute-start.8
  197.2 157.7 %reduce-scatter.5.cloned.1.call-start = ((), (), s32[]{:S(2)}) async-start(), calls=%async_computation.7 | async-start | bytes 3317760 | tf_op jit(solution)/shard_map/reduce_scatter | solution.py:675
  197.3 10.9 %copy-start.5 = (f32[1024,768]{1,0:T(8,128)S(1)}, f32[1024,768]{1,0:T(8,128)}, u32[]{:S(2)}) copy-start(f32[1024,768]{1,0:T(8,128)} %copy-done.4) | copy-start | bytes 9437188
  197.3 10.9 %copy-start.10 = (bf16[1,1024,768]{2,1,0:T(8,128)(2,1)S(1)}, bf16[1,1024,768]{2,1,0:T(8,128)(2,1)}, u32[]{:S(2)}) copy-start(bf16[1,1024,768]{2,1,0:T(8,128)(2,1)} %param.29) | copy-start | bytes 4718596
  214.6 11.1 %collective-permute-start.9 = (bf16[384,1024]{1,0:T(8,128)(2,1)S(1)}, bf16[384,1024]{1,0:T(8,128)(2,1)S(1)}, u32[]{:S(2)}, u32[]{:S(2)}) collective-permute-start(bf16[384,1024]{1,0:T(8,128)(2,1)S(1)} %get-tuple-element.183), channel_id=1, source_target_pairs={{0,8},{8,0},{16,24},{24,16},{1,9},{9,1},{17,25},{25,17},{2,10},{10... | collective-permute-start | bytes 2359304 | tf_op jit(solution)/shard_map/ppermute | solution.py:698
  218.0 7.5 %collective-permute-start.10 = (bf16[768,384]{1,0:T(8,128)(2,1)S(1)}, bf16[768,384]{1,0:T(8,128)(2,1)S(1)}, u32[]{:S(2)}, u32[]{:S(2)}) collective-permute-start(bf16[768,384]{1,0:T(8,128)(2,1)S(1)} %constant_dynamic-slice_fusion.1), channel_id=1, source_target_pairs={{0,8},{8,0},{16,24},{24,16},{1,9},{9,1},{17,25},{25,17},{2,10},{10... | collective-permute-start | bytes 1769480 | tf_op jit(solution)/shard_map/ppermute | solution.py:701
  265.2 45.9 %collective-permute-start.11 = (bf16[256,2048]{1,0:T(8,128)(2,1)}, bf16[256,2048]{1,0:T(8,128)(2,1)}, u32[]{:S(2)}, u32[]{:S(2)}) collective-permute-start(bf16[256,2048]{1,0:T(8,128)(2,1)} %get-tuple-element.113), channel_id=1, source_target_pairs={{0,16},{8,24},{1,17},{9,25},{2,18},{10,26},{3,19},{11,27},{4,20},{... | collective-permute-start | bytes 3145736 | tf_op jit(solution)/shard_map/ppermute | solution.py:713
  273.6 117.0 %collective-permute-start.7 = (bf16[1024,768]{1,0:T(8,128)(2,1)}, bf16[1024,768]{1,0:T(8,128)(2,1)}, u32[]{:S(2)}, u32[]{:S(2)}) collective-permute-start(bf16[1024,768]{1,0:T(8,128)(2,1)} %fusion.32), channel_id=1, source_target_pairs={{0,8},{8,0},{16,24},{24,16},{1,9},{9,1},{17,25},{25,17},{2,10},{10... | collective-permute-start | bytes 4718600 | tf_op jit(solution)/shard_map/ppermute | solution.py:664
  311.1 43.8 %collective-permute-start.12 = (bf16[256,2048]{1,0:T(8,128)(2,1)}, bf16[256,2048]{1,0:T(8,128)(2,1)}, u32[]{:S(2)}, u32[]{:S(2)}) collective-permute-start(bf16[256,2048]{1,0:T(8,128)(2,1)} %get-tuple-element.119), channel_id=1, source_target_pairs={{0,16},{8,24},{1,17},{9,25},{2,18},{10,26},{3,19},{11,27},{4,20},{... | collective-permute-start | bytes 3145736 | tf_op jit(solution)/shard_map/ppermute | solution.py:713
  318.2 36.7 %collective-permute-start.13 = (bf16[96,1536]{1,0:T(8,128)(2,1)S(1)}, bf16[96,1536]{1,0:T(8,128)(2,1)S(1)}, u32[]{:S(2)}, u32[]{:S(2)}) collective-permute-start(bf16[96,1536]{1,0:T(8,128)(2,1)S(1)} %copy-done.26), channel_id=1, source_target_pairs={{0,16},{8,24},{16,0},{24,8},{1,17},{9,25},{17,1},{25,9},{2,18},{10... | collective-permute-start | bytes 884744 | tf_op jit(solution)/shard_map/ppermute | solution.py:737
  354.9 24.3 %collective-permute-start.14 = (bf16[256,2048]{1,0:T(8,128)(2,1)}, bf16[256,2048]{1,0:T(8,128)(2,1)}, u32[]{:S(2)}, u32[]{:S(2)}) collective-permute-start(bf16[256,2048]{1,0:T(8,128)(2,1)} %get-tuple-element.123), channel_id=1, source_target_pairs={{0,16},{8,24},{1,17},{9,25},{2,18},{10,26},{3,19},{11,27},{4,20},{... | collective-permute-start | bytes 3145736 | tf_op jit(solution)/shard_map/ppermute | solution.py:713
  364.6 45.1 %all-to-all-start = ((bf16[8,96,768]{2,1,0:T(8,128)(2,1)}), bf16[8,96,768]{2,1,0:T(8,128)(2,1)}, u32[]{:S(2)}, u32[]{:S(2)}) async-start(bf16[8,96,768]{2,1,0:T(8,128)(2,1)} %bitcast.36), calls=%async_computation.2 | async-start | bytes 2359296 | tf_op jit(solution)/shard_map/all_to_all | solution.py:747
  371.0 8.3 %copy-start.15 = (bf16[384,2048]{1,0:T(8,128)(2,1)S(1)}, bf16[384,2048]{1,0:T(8,128)(2,1)}, u32[]{:S(2)}) copy-start(bf16[384,2048]{1,0:T(8,128)(2,1)} %get-tuple-element.130) | copy-start | bytes 4718596
  371.0 19.6 %slice-start = ((s8[6291456]{0:T(1024)(128)(4,1)}), s8[4194304]{0:T(1024)(128)(4,1)S(1)}, s32[]{:S(2)}) async-start(s8[6291456]{0:T(1024)(128)(4,1)} %bitcast.177), calls=%async_computation.8 | async-start | bytes 8388608
  375.8 5.4 %copy-start.14 = (f32[2048,768]{1,0:T(8,128)}, f32[2048,768]{1,0:T(8,128)S(1)}, u32[]{:S(2)}) copy-start(f32[2048,768]{1,0:T(8,128)S(1)} %fusion.23) | copy-start | bytes 18874372
  375.9 5.2 %copy-start.11 = (bf16[2,1,64,2048]{3,2,1,0:T(8,128)(2,1)S(1)}, bf16[2,1,64,2048]{3,2,1,0:T(8,128)(2,1)}, u32[]{:S(2)}) copy-start(bf16[2,1,64,2048]{3,2,1,0:T(8,128)(2,1)} %slice.283) | copy-start | bytes 1572868
  379.3 11.3 %slice-start.1 = ((s8[6291456]{0:T(1024)(128)(4,1)}), s8[2097152]{0:T(1024)(128)(4,1)S(1)}, s32[]{:S(2)}) async-start(s8[6291456]{0:T(1024)(128)(4,1)} %bitcast.177), calls=%async_computation.9 | async-start | bytes 4194304
  381.2 6.6 %copy-start.12 = (bf16[2,3,64,2048]{3,2,1,0:T(8,128)(2,1)}, bf16[2,3,64,2048]{3,2,1,0:T(8,128)(2,1)S(1)}, u32[]{:S(2)}) copy-start(bf16[2,3,64,2048]{3,2,1,0:T(8,128)(2,1)S(1)} %pad_maximum_fusion.11) | copy-start | bytes 4718596
  385.1 5.5 %copy-start.6 = (f32[1024,768]{1,0:T(8,128)S(1)}, f32[1024,768]{1,0:T(8,128)}, u32[]{:S(2)}) copy-start(f32[1024,768]{1,0:T(8,128)} %copy-done.4) | copy-start | bytes 9437188
  385.1 5.5 %copy-start.19 = (bf16[768,768]{1,0:T(8,128)(2,1)S(1)}, bf16[768,768]{1,0:T(8,128)(2,1)}, u32[]{:S(2)}) copy-start(bf16[768,768]{1,0:T(8,128)(2,1)} %copy-done.18) | copy-start | bytes 3538948
  385.1 5.5 %copy-start.20 = (bf16[768,768]{1,0:T(8,128)(2,1)S(1)}, bf16[768,768]{1,0:T(8,128)(2,1)}, u32[]{:S(2)}) copy-start(bf16[768,768]{1,0:T(8,128)(2,1)} %get-tuple-element.179) | copy-start | bytes 3538948
  387.8 29.2 %collective-permute-start.15 = (bf16[1024,768]{1,0:T(8,128)(2,1)}, bf16[1024,768]{1,0:T(8,128)(2,1)}, u32[]{:S(2)}, u32[]{:S(2)}) collective-permute-start(bf16[1024,768]{1,0:T(8,128)(2,1)} %add_convert_fusion.1), channel_id=1, source_target_pairs={{0,8},{8,0},{16,24},{24,16},{1,9},{9,1},{17,25},{25,17},{2,10},{10... | collective-permute-start | bytes 4718600 | tf_op jit(solution)/shard_map/ppermute | solution.py:760
  388.4 11.2 %collective-permute-start.16 = (bf16[96,1920]{1,0:T(8,128)(2,1)S(1)}, bf16[96,1920]{1,0:T(8,128)(2,1)}, u32[]{:S(2)}, u32[]{:S(2)}) collective-permute-start(bf16[96,1920]{1,0:T(8,128)(2,1)S(1)} %copy-done.25), channel_id=1, source_target_pairs={{0,16},{8,24},{16,0},{24,8},{1,17},{9,25},{17,1},{25,9},{2,18},{10... | collective-permute-start | bytes 1105928 | tf_op jit(solution)/shard_map/ppermute | solution.py:767
  400.7 6.0 %copy-start.16 = (bf16[96,1920]{1,0:T(8,128)(2,1)}, bf16[96,1920]{1,0:T(8,128)(2,1)S(1)}, u32[]{:S(2)}) copy-start(bf16[96,1920]{1,0:T(8,128)(2,1)S(1)} %add_convert_fusion.5.mine) | copy-start | bytes 1105924
  400.7 6.0 %collective-permute-start.17 = (bf16[96,1920]{1,0:T(8,128)(2,1)S(1)}, bf16[96,1920]{1,0:T(8,128)(2,1)}, u32[]{:S(2)}, u32[]{:S(2)}) collective-permute-start(bf16[96,1920]{1,0:T(8,128)(2,1)S(1)} %add_convert_fusion.5.mine), channel_id=1, source_target_pairs={{0,8},{8,0},{16,24},{24,16},{1,9},{9,1},{17,25},{25,17},{2,10},{10... | collective-permute-start | bytes 1105928 | tf_op jit(solution)/shard_map/ppermute | solution.py:765
  402.5 4.1 collective-permute-start.18
  409.7 19.0 %all-to-all-start.1 = ((bf16[8,96,384]{2,1,0:T(8,128)(2,1)}), bf16[8,96,384]{2,1,0:T(8,128)(2,1)S(1)}, u32[]{:S(2)}, u32[]{:S(2)}) async-start(bf16[8,96,384]{2,1,0:T(8,128)(2,1)} %bitcast.159), calls=%async_computation.3 | async-start | bytes 1179648 | tf_op jit(solution)/shard_map/all_to_all | solution.py:747
  423.5 27.8 %copy-start.1 = (bf16[96,2304]{1,0:T(8,128)(2,1)S(1)}, bf16[96,2304]{1,0:T(8,128)(2,1)}, u32[]{:S(2)}) copy-start(bf16[96,2304]{1,0:T(8,128)(2,1)} %param.19) | copy-start | bytes 1327108
  (18 other events, 53.3 us)
Sparse Core Ops, SparseCore 0:
  10.8 47.1 all-gather.2
  60.7 84.0 all-gather.4
  197.3 67.2 reduce-scatter.2
  268.0 73.3 reduce-scatter.4

commit v8 on v7

--- a/solution.py
+++ b/solution.py
@@ -102,7 +102,7 @@
 def project(core, mine, other, sent, sent_other, weight, vec, bias, cos_t, sin_t, heads):
     local, width = mine.shape
     span = heads * HD
-    tile = 256
+    tile = 512
     n = local // tile
 
     def place(t, c):

time: 466 us -> 465 us (level)
  transfers between devices with their start and end apart: 25 -> 25, of which waited for: 10 -> 10; matrix products, arithmetic and copies ran while one was open for 24% -> 24% of each run, Pallas kernels for 40% -> 39%
where the time goes in v8:
time: 465 us; the launch traced here: 457 us
  Pallas kernels  195 us (42%)
  matrix products  92.7 us (20%)
  waiting for transfers between devices  47.9 us (10%)
  other arithmetic  37.7 us (8%)
  local copies, waits for them, and re-layouts  37.5 us (8%)
  starting transfers between devices  31.3 us (7%)
  between operations  15 us (3%)
    pallas_call x3, Pallas kernels, attend_back(): pl.pallas_call(functools.partial(attend_back_kernel, group), grid_spec=pl...  107 us
    pallas_call x1, Pallas kernels, attend(): pl.pallas_call(functools.partial(attend_kernel, group), grid_spec=pltpu.P...  51.3 us
    dot_general x4, matrix products, dot(): return jnp.dot(left, right, preferred_element_type=F32)  29 us
    dot_general x4, matrix products, right_transposed(): lax.dot_general(left, right, (((1,), (1,)), ((), ())), preferred_element_...  26.2 us
    ppermute x1, waiting for transfers between devices, on_device(): clean_in = lax.ppermute(tok, 'seq', [(2, 0), (3, 1)])  25.8 us
    pallas_call x1, Pallas kernels, project(): pl.pallas_call(functools.partial(qkv_kernel, heads), grid_spec=pltpu.Pref...  19.2 us
    dot_general x3, matrix products, rows_contract(): lax.dot_general(left, right, (((0,), (0,)), ((), ())), preferred_element_...  16.2 us
    dot_general x3, matrix products, back(): lax.dot_general(own, cols, (((0,), (1,)), ((), ())), preferred_element_ty...  15 us
  transfers between devices with their start and end apart: 25, of which 10 were waited for; matrix products, arithmetic and copies ran while one was open for 24% of the time, Pallas kernels for 39%

profile of v8, /device:TPU:13, one launch (start us, length us, event | category | flops | bytes accessed | tf_op | source)
XLA Modules:
  0.0 457.5 jit_solution(11184465613390568076)
XLA Ops:
  10.7 3.5 reshape.688
  14.2 2.1 constant_dynamic-slice_fusion.5
  27.1 3.8 pad_maximum_fusion
  30.9 25.8 %collective-permute-done.sent = bf16[1024,768]{1,0:T(8,128)(2,1)} collective-permute-done((bf16[1024,768]{1,0:T(8,128)(2,1)S(1)}, bf16[1024,768]{1,0:T(8,128)(2,1)}, u32[]{:S(2)}, u32[]{:S(2)}) %collective-permute-start) | collective-permute-done | bytes 1572896 | tf_op jit(solution)/shard_map/ppermute | solution.py:556
  64.5 19.2 %project.1 = (bf16[384,2048]{1,0:T(8,128)(2,1)}, bf16[384,2048]{1,0:T(8,128)(2,1)}, bf16[384,2048]{1,0:T(8,128)(2,1)}, bf16[384,2048]{1,0:T(8,128)(2,1)}, bf16[3...) custom-call(s32[2]{0:T(128)} %pad_add_fusion.core_ref, bf16[1024,768]{1,0:T(8,128)(2,1)} %bitcast.135, ...), custom_call_target="tpu_custom_call" | custom-call | tf_op jit(solution)/shard_map/project/pallas_call | solution.py:122
  83.7 51.3 %attend.1 = (bf16[384,2048]{1,0:T(8,128)(2,1)}, f32[6,8,2048]{2,1,0:T(8,128)}) custom-call(s32[5,4]{1,0:T(8,128)} %stack.14.bounds, bf16[384,2048]{1,0:T(8,128)(2,1)} %get-tuple-element.88.q, bf16[384,2048]{1,0:T(8,128)(2,1)} %get-tuple-element.89.k, bf16[384,2048]{1,0:T(8,128)(2,1)} %get-tuple-element.90.v, bf16[384,2048]{1,0:T(8,128)(2,1)} %get-tuple-element.91.kc, ...), custom_call_target="tpu_custom_call" | custom-call | flops 25769803776 | bytes 16777216 | tf_op jit(solution)/shard_map/attend/pallas_call | solution.py:240
  136.8 2.4 collective-permute-done.4
  139.2 5.3 %all-gather.5.cloned.1.call-done = bf16[768,3456]{1,0:T(8,128)(2,1)} async-done(((bf16[96,3456]{1,0:T(8,128)(2,1)}), bf16[768,3456]{1,0:T(8,128)(2,1)}) %all-gather.5.cloned.1.call-update) | async-done | bytes 5308432 | tf_op jit(solution)/shard_map/all_gather | solution.py:595
  145.6 2.3 collective-permute-start.5
  149.7 3.5 fusion.72
  156.1 2.8 fusion.69
  159.2 14.7 %add_convert_fusion = (bf16[2048,1536]{1,0:T(8,128)(2,1)}, bf16[2048,1536]{1,0:T(8,128)(2,1)S(1)}) fusion(f32[1536]{0:T(1024)S(1)} %add.354, bf16[768,3456]{1,0:T(8,128)(2,1)} %all-gather.5.cloned.1.call-done, bf16[1024,768]{1,0:T(8,128)(2,1)} %collective-permute-done.6, bf16[1024,768]{1,0:T(8,128)(2,1)} %add_convert_fusion.3), kind=kOutput, calls=%fused_computation.2 | convolution fusion | flops 4891607040 | bytes 18094080 | tf_op jit(solution)/shard_map/dot_general | solution.py:50
  173.9 5.4 %convolution_convert_fusion.1 = bf16[1536,768]{1,0:T(8,128)(2,1)S(1)} fusion(bf16[2048,1536]{1,0:T(8,128)(2,1)S(1)} %get-tuple-element.100, bf16[2048,768]{1,0:T(8,128)(2,1)S(1)} %copy-done.13), kind=kOutput, calls=%fused_computation.19 | convolution fusion | flops 4833017856 | bytes 11796480 | tf_op jit(solution)/shard_map/dot_general | solution.py:42
  181.1 8.0 %convert_reduce_fusion = (f32[1536]{0:T(1024)S(1)}, bf16[2048,1536]{1,0:T(8,128)(2,1)S(1)}) fusion(bf16[2048,1536]{1,0:T(8,128)(2,1)} %get-tuple-element.102, bf16[2048,768]{1,0:T(8,128)(2,1)} %pad_maximum_fusion, bf16[768,768]{1,0:T(8,128)(2,1)} %get-tuple-element.179, bf16[768,768]{1,0:T(8,128)(2,1)S(1)} %get-tuple-element.178), kind=kOutput, calls=%fused_computation | convolution fusion | flops 4852283904 | bytes 18094080 | tf_op jit(solution)/shard_map/dot_general | solution.py:46
  189.2 7.2 %fusion.35 = bf16[1024,768]{1,0:T(8,128)(2,1)} fusion(bf16[768,3456]{1,0:T(8,128)(2,1)} %all-gather.5.cloned.1.call-done, bf16[2048,1536]{1,0:T(8,128)(2,1)S(1)} %get-tuple-element.211), kind=kOutput, calls=%fused_computation.66 | convolution fusion | flops 2416705536 | bytes 7077888 | tf_op jit(solution)/shard_map/dot_general | solution.py:46
  197.0 3.3 collective-permute-done.8
  200.3 7.3 %multiply_reduce_fusion = (f32[768]{0:T(1024)S(1)}, f32[1024]{0:T(1024)S(1)}, f32[1024]{0:T(1024)S(1)}, f32[768]{0:T(1024)S(1)}, f32[1024,768]{1,0:T(8,128)S(1)}) fusion(f32[1024,768]{1,0:T(8,128)} %copy-done.4, f32[1024]{0:T(1024)S(1)} %add_rsqrt_fusion.1, f32[1024]{0:T(1024)S(1)} %broadcast_multiply_fusion.5, f32[768]{0:T(1024)S(1)} %mul.183, ...), kind=kOutput, calls=%fused_computation.34 | convolution fusion | flops 2424566272 | bytes 13394944 | tf_op jit(solution)/shard_map/dot_general | solution.py:46
  209.4 3.6 convolution_convert_fusion.2
  214.4 3.1 convolution_convert_fusion.3
  217.9 7.3 %convolution_convert_fusion = bf16[768,1536]{1,0:T(8,128)(2,1)S(1)} fusion(bf16[2048,1536]{1,0:T(8,128)(2,1)S(1)} %bitcast.180, bf16[1024,768]{1,0:T(8,128)(2,1)} %collective-permute-done.6, bf16[1024,768]{1,0:T(8,128)(2,1)} %add_convert_fusion.3), kind=kOutput, calls=%fused_computation.18 | convolution fusion | flops 4839309312 | bytes 11796480 | tf_op jit(solution)/shard_map/dot_general | solution.py:42
  226.3 1.9 pad_maximum_fusion.3
  229.2 35.7 %attend_back.3 = (bf16[384,2048]{1,0:T(8,128)(2,1)}, bf16[256,2048]{1,0:T(8,128)(2,1)}) custom-call(s32[5,4]{1,0:T(8,128)} %stack.13.bounds, bf16[384,2048]{1,0:T(8,128)(2,1)} %get-tuple-element.88.q, bf16[384,2048]{1,0:T(8,128)(2,1)} %get-tuple-element.89.k, bf16[384,2048]{1,0:T(8,128)(2,1)} %get-tuple-element.90.v, ...), custom_call_target="tpu_custom_call" | custom-call | flops 10737418240 | bytes 8388608 | tf_op jit(solution)/shard_map/attend_back/pallas_call | solution.py:372
  264.9 2.3 collective-permute-start.11
  267.2 6.0 %fusion.32 = bf16[1024,768]{1,0:T(8,128)(2,1)} fusion(bf16[2048,1536]{1,0:T(8,128)(2,1)} %copy-done.35, bf16[768,768]{1,0:T(8,128)(2,1)} %get-tuple-element.179, bf16[768,768]{1,0:T(8,128)(2,1)S(1)} %get-tuple-element.178), kind=kOutput, calls=%fused_computation.65 | convolution fusion | flops 2421424128 | bytes 7077888 | tf_op jit(solution)/shard_map/dot_general | solution.py:50
  275.0 35.6 %attend_back.4 = (bf16[384,2048]{1,0:T(8,128)(2,1)}, bf16[256,2048]{1,0:T(8,128)(2,1)}) custom-call(s32[5,4]{1,0:T(8,128)} %stack.13.bounds, bf16[384,2048]{1,0:T(8,128)(2,1)} %get-tuple-element.88.q, bf16[384,2048]{1,0:T(8,128)(2,1)} %get-tuple-element.89.k, bf16[384,2048]{1,0:T(8,128)(2,1)} %get-tuple-element.90.v, ...), custom_call_target="tpu_custom_call" | custom-call | flops 10737418240 | bytes 8388608 | tf_op jit(solution)/shard_map/attend_back/pallas_call | solution.py:372
  310.6 2.6 collective-permute-start.12
  313.3 2.1 fusion.22
  315.8 1.8 convolution_convert_fusion.6
  317.8 35.5 %attend_back.5 = (bf16[384,2048]{1,0:T(8,128)(2,1)}, bf16[256,2048]{1,0:T(8,128)(2,1)}) custom-call(s32[5,4]{1,0:T(8,128)} %stack.13.bounds, bf16[384,2048]{1,0:T(8,128)(2,1)} %get-tuple-element.88.q, bf16[384,2048]{1,0:T(8,128)(2,1)} %get-tuple-element.89.k, bf16[384,2048]{1,0:T(8,128)(2,1)} %get-tuple-element.90.v, ...), custom_call_target="tpu_custom_call" | custom-call | flops 10737418240 | bytes 8388608 | tf_op jit(solution)/shard_map/attend_back/pallas_call | solution.py:372
  354.4 2.3 collective-permute-start.14
  356.7 2.1 fusion.21
  359.2 1.8 convolution_convert_fusion.5
  362.2 1.9 slice.283
  364.1 6.3 %all-to-all-start = ((bf16[8,96,768]{2,1,0:T(8,128)(2,1)}), bf16[8,96,768]{2,1,0:T(8,128)(2,1)}, u32[]{:S(2)}, u32[]{:S(2)}) async-start(bf16[8,96,768]{2,1,0:T(8,128)(2,1)} %bitcast.36), calls=%async_computation.2 | async-start | bytes 2359296 | tf_op jit(solution)/shard_map/all_to_all | solution.py:747
  370.4 4.8 %fusion.23 = f32[2048,768]{1,0:T(8,128)S(1)} fusion(bf16[384,2048]{1,0:T(8,128)(2,1)} %bitcast.143, bf16[384,2048]{1,0:T(8,128)(2,1)} %bitcast.140, bf16[768,1280]{1,0:T(8,128)(2,1)} %all-gather.3.cloned.1.call-done.w_ref), kind=kOutput, calls=%fused_computation.60 | convolution fusion | flops 2422210560 | bytes 10616832 | tf_op jit(solution)/shard_map/dot_general | solution.py:728
  375.3 3.3 collective-permute-done.14
  380.6 3.8 add_convert_fusion.1
  384.5 2.6 convolution_convert_fusion.4
  387.9 2.2 collective-permute-start.16
  390.1 5.2 %fusion.40 = bf16[1,1024,768]{2,1,0:T(8,128)(2,1)} fusion(f32[1024,768]{1,0:T(8,128)S(1)} %copy-done.6, bf16[1024,768]{1,0:T(8,128)(2,1)} %collective-permute-done.7, f32[768]{0:T(1024)S(1)} %add.365, bf16[2048,1536]{1,0:T(8,128)(2,1)S(1)} %bitcast.178, bf16[768,768]{1,0:T(8,128)(2,1)S(1)} %copy-done.20, bf16[768,768]{1,0:T(8,128)(2,1)S(1)} %copy-done.19), kind=kOutput, calls=%fused_computation.68 | convolution fusion | flops 2424569856 | bytes 11800576 | tf_op jit(solution)/shard_map/dot_general | solution.py:50
  395.7 3.4 collective-permute-done.16
  402.2 2.4 convert_reduce_fusion.1
  406.2 3.1 assemble.1
  409.2 5.6 %all-to-all-start.1 = ((bf16[8,96,384]{2,1,0:T(8,128)(2,1)}), bf16[8,96,384]{2,1,0:T(8,128)(2,1)S(1)}, u32[]{:S(2)}, u32[]{:S(2)}) async-start(bf16[8,96,384]{2,1,0:T(8,128)(2,1)} %bitcast.159), calls=%async_computation.3 | async-start | bytes 1179648 | tf_op jit(solution)/shard_map/all_to_all | solution.py:747
  416.4 6.3 %fusion.9 = (f32[768]{0:T(1024)S(1)}, f32[1024]{0:T(1024)S(1)}, f32[1024]{0:T(1024)S(1)}, f32[768]{0:T(1024)S(1)}, f32[1024,768]{1,0:T(8,128)}) fusion(f32[1024]{0:T(1024)S(1)} %add_rsqrt_fusion, f32[1024]{0:T(1024)S(1)} %broadcast_multiply_fusion.2, bf16[1,1024,768]{2,1,0:T(8,128)(2,1)S(1)} %copy-done.3, f32[768]{0:T(1024)S(1)} %mul.206, ...), kind=kOutput, calls=%fused_computation.24 | convolution fusion | flops 614199808 | bytes 10839040 | tf_op jit(solution)/shard_map/dot_general | solution.py:728
  423.0 4.6 %fusion.8 = f32[1024,768]{1,0:T(8,128)} fusion(f32[1024,768]{1,0:T(8,128)} %copy-done.7, f32[1024,768]{1,0:T(8,128)} %get-tuple-element.209, f32[1024]{0:T(1024)S(1)} %broadcast_multiply_fusion, f32[1024]{0:T(1024)S(1)} %broadcast_multiply_fusion.1, f32[768]{0:T(1024)S(1)} %mul.206, f32[1024]{0:T(1024)S(1)} %add_rsqrt_fusion, ...), kind=kLoop, calls=%fused_computation.23 | loop fusion | flops 7077888 | bytes 11029504 | tf_op jit(solution)/shard_map/add | solution.py:779
  429.6 14.9 %finish.1 = (f32[96,2304]{1,0:T(8,128)}, f32[10,128]{1,0:T(8,128)}) custom-call(bf16[96,1152]{1,0:T(8,128)(2,1)} %pad_maximum_fusion.18.g, f32[8,10,128]{2,1,0:T(8,128)} %copy.95.s), custom_call_target="tpu_custom_call" | custom-call | tf_op jit(solution)/shard_map/finish/pallas_call | solution.py:455
  448.6 2.1 copy.102
  (234 shorter events, 58.0 us)
Async XLA Ops:
  7.2 53.7 %all-gather.3.cloned.1.call-start = ((), (), s32[]{:S(2)}) async-start(), calls=%async_computation.4 | async-start | bytes 2211840 | tf_op jit(solution)/shard_map/all_gather | solution.py:575
  9.9 8.5 %copy-start.30 = (bf16[96,768]{1,0:T(8,128)(2,1)S(1)}, bf16[96,768]{1,0:T(8,128)(2,1)}, u32[]{:S(2)}) copy-start(bf16[96,768]{1,0:T(8,128)(2,1)} %param.21) | copy-start | bytes 442372
  9.9 8.5 %copy-start.28 = (bf16[384,768]{1,0:T(8,128)(2,1)S(1)}, bf16[384,768]{1,0:T(8,128)(2,1)}, u32[]{:S(2)}) copy-start(bf16[384,768]{1,0:T(8,128)(2,1)} %param.27) | copy-start | bytes 1769476
  10.7 133.9 %all-gather.5.cloned.1.call-start = ((), (), s32[]{:S(2)}) async-start(), calls=%async_computation.5 | async-start | bytes 5971968 | tf_op jit(solution)/shard_map/all_gather | solution.py:595
  14.2 5.2 %copy-start.2 = (bf16[1,1024,768]{2,1,0:T(8,128)(2,1)S(1)}, bf16[1,1024,768]{2,1,0:T(8,128)(2,1)}, u32[]{:S(2)}) copy-start(bf16[1,1024,768]{2,1,0:T(8,128)(2,1)} %param.15) | copy-start | bytes 4718596
  14.2 7.5 %copy-start.29 = (s32[1,2048]{1,0:T(1,128)S(1)}, s32[1,2048]{1,0:T(1,128)}, u32[]{:S(2)}) copy-start(s32[1,2048]{1,0:T(1,128)} %param.16) | copy-start | bytes 24580
  19.3 291.3 %reduce-scatter.3.cloned.1.call-start = ((), (), s32[]{:S(2)}) async-start(), calls=%async_computation.6 | async-start | bytes 2654208 | tf_op jit(solution)/shard_map/reduce_scatter | solution.py:675
  19.4 37.3 %collective-permute-start = (bf16[1024,768]{1,0:T(8,128)(2,1)S(1)}, bf16[1024,768]{1,0:T(8,128)(2,1)}, u32[]{:S(2)}, u32[]{:S(2)}) collective-permute-start(bf16[1024,768]{1,0:T(8,128)(2,1)S(1)} %bitcast.137), channel_id=1, source_target_pairs={{16,0},{24,8},{17,1},{25,9},{18,2},{26,10},{19,3},{27,11},{20,4},{... | collective-permute-start | bytes 4718600 | tf_op jit(solution)/shard_map/ppermute | solution.py:556
  20.9 43.6 %collective-permute-start.2 = (bf16[1024,768]{1,0:T(8,128)(2,1)S(1)}, bf16[1024,768]{1,0:T(8,128)(2,1)}, u32[]{:S(2)}, u32[]{:S(2)}) collective-permute-start(bf16[1024,768]{1,0:T(8,128)(2,1)S(1)} %bitcast.138), channel_id=1, source_target_pairs={{0,8},{8,0},{16,24},{24,16},{1,9},{9,1},{17,25},{25,17},{2,10},{10... | collective-permute-start | bytes 4718600 | tf_op jit(solution)/shard_map/ppermute | solution.py:555
  21.7 5.4 %collective-permute-start.1 = (bf16[1024,768]{1,0:T(8,128)(2,1)}, bf16[1024,768]{1,0:T(8,128)(2,1)}, u32[]{:S(2)}, u32[]{:S(2)}) collective-permute-start(bf16[1024,768]{1,0:T(8,128)(2,1)} %bitcast.145), channel_id=1, source_target_pairs={{0,8},{8,0},{16,24},{24,16},{1,9},{9,1},{17,25},{25,17},{2,10},{10... | collective-permute-start | bytes 4718600 | tf_op jit(solution)/shard_map/ppermute | solution.py:557
  58.7 5.8 %collective-permute-start.3 = (bf16[1024,768]{1,0:T(8,128)(2,1)}, bf16[1024,768]{1,0:T(8,128)(2,1)}, u32[]{:S(2)}, u32[]{:S(2)}) collective-permute-start(bf16[1024,768]{1,0:T(8,128)(2,1)} %collective-permute-done.sent), channel_id=1, source_target_pairs={{0,8},{8,0},{16,24},{24,16},{1,9},{9,1},{17,25},{25,17},{2,10},{10... | collective-permute-start | bytes 4718600 | tf_op jit(solution)/shard_map/ppermute | solution.py:636
  135.1 14.6 %copy-start.3 = (bf16[1,1024,768]{2,1,0:T(8,128)(2,1)S(1)}, bf16[1,1024,768]{2,1,0:T(8,128)(2,1)}, u32[]{:S(2)}) copy-start(bf16[1,1024,768]{2,1,0:T(8,128)(2,1)} %param.15) | copy-start | bytes 4718596
  136.7 16.4 %copy-start.21 = (bf16[384,1024]{1,0:T(8,128)(2,1)}, bf16[384,1024]{1,0:T(8,128)(2,1)S(1)}, u32[]{:S(2)}) copy-start(bf16[384,1024]{1,0:T(8,128)(2,1)S(1)} %get-tuple-element.96) | copy-start | bytes 2359300
  136.7 2.5 collective-permute-start.4
  145.6 7.5 %copy-start.23 = (bf16[768,384]{1,0:T(8,128)(2,1)}, bf16[768,384]{1,0:T(8,128)(2,1)S(1)}, u32[]{:S(2)}) copy-start(bf16[768,384]{1,0:T(8,128)(2,1)S(1)} %slice.212) | copy-start | bytes 1769476
  145.6 4.0 collective-permute-start.5
  155.4 3.8 collective-permute-start.6
  158.9 108.3 %copy-start.18 = (bf16[768,768]{1,0:T(8,128)(2,1)}, bf16[768,768]{1,0:T(8,128)(2,1)S(1)}, u32[]{:S(2)}) copy-start(bf16[768,768]{1,0:T(8,128)(2,1)S(1)} %get-tuple-element.178) | copy-start | bytes 3538948
  158.9 15.0 %copy-start.13 = (bf16[2048,768]{1,0:T(8,128)(2,1)S(1)}, bf16[2048,768]{1,0:T(8,128)(2,1)}, u32[]{:S(2)}) copy-start(bf16[2048,768]{1,0:T(8,128)(2,1)} %pad_maximum_fusion) | copy-start | bytes 9437188
  173.9 5.4 %copy-start.35 = (bf16[2048,1536]{1,0:T(8,128)(2,1)}, bf16[2048,1536]{1,0:T(8,128)(2,1)S(1)}, u32[]{:S(2)}) copy-start(bf16[2048,1536]{1,0:T(8,128)(2,1)S(1)} %get-tuple-element.100) | copy-start | bytes 18874372
  189.2 7.2 %copy-start.36 = (bf16[2048,1536]{1,0:T(8,128)(2,1)}, bf16[2048,1536]{1,0:T(8,128)(2,1)S(1)}, u32[]{:S(2)}) copy-start(bf16[2048,1536]{1,0:T(8,128)(2,1)S(1)} %get-tuple-element.211) | copy-start | bytes 18874372
  196.4 3.9 collective-permute-start.8
  196.9 157.5 %reduce-scatter.5.cloned.1.call-start = ((), (), s32[]{:S(2)}) async-start(), calls=%async_computation.7 | async-start | bytes 3317760 | tf_op jit(solution)/shard_map/reduce_scatter | solution.py:675
  197.0 10.7 %copy-start.5 = (f32[1024,768]{1,0:T(8,128)S(1)}, f32[1024,768]{1,0:T(8,128)}, u32[]{:S(2)}) copy-start(f32[1024,768]{1,0:T(8,128)} %copy-done.4) | copy-start | bytes 9437188
  197.0 10.7 %copy-start.10 = (bf16[1,1024,768]{2,1,0:T(8,128)(2,1)S(1)}, bf16[1,1024,768]{2,1,0:T(8,128)(2,1)}, u32[]{:S(2)}) copy-start(bf16[1,1024,768]{2,1,0:T(8,128)(2,1)} %param.29) | copy-start | bytes 4718596
  214.1 11.3 %collective-permute-start.9 = (bf16[384,1024]{1,0:T(8,128)(2,1)S(1)}, bf16[384,1024]{1,0:T(8,128)(2,1)S(1)}, u32[]{:S(2)}, u32[]{:S(2)}) collective-permute-start(bf16[384,1024]{1,0:T(8,128)(2,1)S(1)} %get-tuple-element.183), channel_id=1, source_target_pairs={{0,8},{8,0},{16,24},{24,16},{1,9},{9,1},{17,25},{25,17},{2,10},{10... | collective-permute-start | bytes 2359304 | tf_op jit(solution)/shard_map/ppermute | solution.py:698
  217.6 7.6 %collective-permute-start.10 = (bf16[768,384]{1,0:T(8,128)(2,1)S(1)}, bf16[768,384]{1,0:T(8,128)(2,1)S(1)}, u32[]{:S(2)}, u32[]{:S(2)}) collective-permute-start(bf16[768,384]{1,0:T(8,128)(2,1)S(1)} %constant_dynamic-slice_fusion.1), channel_id=1, source_target_pairs={{0,8},{8,0},{16,24},{24,16},{1,9},{9,1},{17,25},{25,17},{2,10},{10... | collective-permute-start | bytes 1769480 | tf_op jit(solution)/shard_map/ppermute | solution.py:701
  264.9 45.7 %collective-permute-start.11 = (bf16[256,2048]{1,0:T(8,128)(2,1)}, bf16[256,2048]{1,0:T(8,128)(2,1)}, u32[]{:S(2)}, u32[]{:S(2)}) collective-permute-start(bf16[256,2048]{1,0:T(8,128)(2,1)} %get-tuple-element.113), channel_id=1, source_target_pairs={{0,16},{8,24},{1,17},{9,25},{2,18},{10,26},{3,19},{11,27},{4,20},{... | collective-permute-start | bytes 3145736 | tf_op jit(solution)/shard_map/ppermute | solution.py:713
  273.2 116.9 %collective-permute-start.7 = (bf16[1024,768]{1,0:T(8,128)(2,1)}, bf16[1024,768]{1,0:T(8,128)(2,1)}, u32[]{:S(2)}, u32[]{:S(2)}) collective-permute-start(bf16[1024,768]{1,0:T(8,128)(2,1)} %fusion.32), channel_id=1, source_target_pairs={{0,8},{8,0},{16,24},{24,16},{1,9},{9,1},{17,25},{25,17},{2,10},{10... | collective-permute-start | bytes 4718600 | tf_op jit(solution)/shard_map/ppermute | solution.py:664
  310.6 43.8 %collective-permute-start.12 = (bf16[256,2048]{1,0:T(8,128)(2,1)}, bf16[256,2048]{1,0:T(8,128)(2,1)}, u32[]{:S(2)}, u32[]{:S(2)}) collective-permute-start(bf16[256,2048]{1,0:T(8,128)(2,1)} %get-tuple-element.119), channel_id=1, source_target_pairs={{0,16},{8,24},{1,17},{9,25},{2,18},{10,26},{3,19},{11,27},{4,20},{... | collective-permute-start | bytes 3145736 | tf_op jit(solution)/shard_map/ppermute | solution.py:713
  317.7 36.7 %collective-permute-start.13 = (bf16[96,1536]{1,0:T(8,128)(2,1)S(1)}, bf16[96,1536]{1,0:T(8,128)(2,1)S(1)}, u32[]{:S(2)}, u32[]{:S(2)}) collective-permute-start(bf16[96,1536]{1,0:T(8,128)(2,1)S(1)} %copy-done.26), channel_id=1, source_target_pairs={{0,16},{8,24},{16,0},{24,8},{1,17},{9,25},{17,1},{25,9},{2,18},{10... | collective-permute-start | bytes 884744 | tf_op jit(solution)/shard_map/ppermute | solution.py:737
  354.4 24.2 %collective-permute-start.14 = (bf16[256,2048]{1,0:T(8,128)(2,1)}, bf16[256,2048]{1,0:T(8,128)(2,1)}, u32[]{:S(2)}, u32[]{:S(2)}) collective-permute-start(bf16[256,2048]{1,0:T(8,128)(2,1)} %get-tuple-element.123), channel_id=1, source_target_pairs={{0,16},{8,24},{1,17},{9,25},{2,18},{10,26},{3,19},{11,27},{4,20},{... | collective-permute-start | bytes 3145736 | tf_op jit(solution)/shard_map/ppermute | solution.py:713
  364.1 45.1 %all-to-all-start = ((bf16[8,96,768]{2,1,0:T(8,128)(2,1)}), bf16[8,96,768]{2,1,0:T(8,128)(2,1)}, u32[]{:S(2)}, u32[]{:S(2)}) async-start(bf16[8,96,768]{2,1,0:T(8,128)(2,1)} %bitcast.36), calls=%async_computation.2 | async-start | bytes 2359296 | tf_op jit(solution)/shard_map/all_to_all | solution.py:747
  370.4 8.2 %copy-start.15 = (bf16[384,2048]{1,0:T(8,128)(2,1)S(1)}, bf16[384,2048]{1,0:T(8,128)(2,1)}, u32[]{:S(2)}) copy-start(bf16[384,2048]{1,0:T(8,128)(2,1)} %get-tuple-element.130) | copy-start | bytes 4718596
  370.4 19.7 %slice-start = ((s8[6291456]{0:T(1024)(128)(4,1)}), s8[4194304]{0:T(1024)(128)(4,1)S(1)}, s32[]{:S(2)}) async-start(s8[6291456]{0:T(1024)(128)(4,1)} %bitcast.177), calls=%async_computation.8 | async-start | bytes 8388608
  375.3 5.3 %copy-start.14 = (f32[2048,768]{1,0:T(8,128)}, f32[2048,768]{1,0:T(8,128)S(1)}, u32[]{:S(2)}) copy-start(f32[2048,768]{1,0:T(8,128)S(1)} %fusion.23) | copy-start | bytes 18874372
  378.6 11.5 %slice-start.1 = ((s8[6291456]{0:T(1024)(128)(4,1)}), s8[2097152]{0:T(1024)(128)(4,1)S(1)}, s32[]{:S(2)}) async-start(s8[6291456]{0:T(1024)(128)(4,1)} %bitcast.177), calls=%async_computation.9 | async-start | bytes 4194304
  380.6 6.6 %copy-start.12 = (bf16[2,3,64,2048]{3,2,1,0:T(8,128)(2,1)}, bf16[2,3,64,2048]{3,2,1,0:T(8,128)(2,1)S(1)}, u32[]{:S(2)}) copy-start(bf16[2,3,64,2048]{3,2,1,0:T(8,128)(2,1)S(1)} %pad_maximum_fusion.11) | copy-start | bytes 4718596
  384.5 5.6 %copy-start.6 = (f32[1024,768]{1,0:T(8,128)S(1)}, f32[1024,768]{1,0:T(8,128)}, u32[]{:S(2)}) copy-start(f32[1024,768]{1,0:T(8,128)} %copy-done.4) | copy-start | bytes 9437188
  384.5 5.7 %copy-start.19 = (bf16[768,768]{1,0:T(8,128)(2,1)S(1)}, bf16[768,768]{1,0:T(8,128)(2,1)}, u32[]{:S(2)}) copy-start(bf16[768,768]{1,0:T(8,128)(2,1)} %copy-done.18) | copy-start | bytes 3538948
  384.5 5.7 %copy-start.20 = (bf16[768,768]{1,0:T(8,128)(2,1)S(1)}, bf16[768,768]{1,0:T(8,128)(2,1)}, u32[]{:S(2)}) copy-start(bf16[768,768]{1,0:T(8,128)(2,1)} %get-tuple-element.179) | copy-start | bytes 3538948
  387.1 29.2 %collective-permute-start.15 = (bf16[1024,768]{1,0:T(8,128)(2,1)}, bf16[1024,768]{1,0:T(8,128)(2,1)}, u32[]{:S(2)}, u32[]{:S(2)}) collective-permute-start(bf16[1024,768]{1,0:T(8,128)(2,1)} %add_convert_fusion.1), channel_id=1, source_target_pairs={{0,8},{8,0},{16,24},{24,16},{1,9},{9,1},{17,25},{25,17},{2,10},{10... | collective-permute-start | bytes 4718600 | tf_op jit(solution)/shard_map/ppermute | solution.py:760
  387.9 11.2 %collective-permute-start.16 = (bf16[96,1920]{1,0:T(8,128)(2,1)S(1)}, bf16[96,1920]{1,0:T(8,128)(2,1)}, u32[]{:S(2)}, u32[]{:S(2)}) collective-permute-start(bf16[96,1920]{1,0:T(8,128)(2,1)S(1)} %copy-done.25), channel_id=1, source_target_pairs={{0,16},{8,24},{16,0},{24,8},{1,17},{9,25},{17,1},{25,9},{2,18},{10... | collective-permute-start | bytes 1105928 | tf_op jit(solution)/shard_map/ppermute | solution.py:767
  400.2 6.0 %copy-start.16 = (bf16[96,1920]{1,0:T(8,128)(2,1)}, bf16[96,1920]{1,0:T(8,128)(2,1)S(1)}, u32[]{:S(2)}) copy-start(bf16[96,1920]{1,0:T(8,128)(2,1)S(1)} %add_convert_fusion.5.mine) | copy-start | bytes 1105924
  400.2 6.0 %collective-permute-start.17 = (bf16[96,1920]{1,0:T(8,128)(2,1)S(1)}, bf16[96,1920]{1,0:T(8,128)(2,1)}, u32[]{:S(2)}, u32[]{:S(2)}) collective-permute-start(bf16[96,1920]{1,0:T(8,128)(2,1)S(1)} %add_convert_fusion.5.mine), channel_id=1, source_target_pairs={{0,8},{8,0},{16,24},{24,16},{1,9},{9,1},{17,25},{25,17},{2,10},{10... | collective-permute-start | bytes 1105928 | tf_op jit(solution)/shard_map/ppermute | solution.py:765
  402.0 4.1 collective-permute-start.18
  409.2 18.9 %all-to-all-start.1 = ((bf16[8,96,384]{2,1,0:T(8,128)(2,1)}), bf16[8,96,384]{2,1,0:T(8,128)(2,1)S(1)}, u32[]{:S(2)}, u32[]{:S(2)}) async-start(bf16[8,96,384]{2,1,0:T(8,128)(2,1)} %bitcast.159), calls=%async_computation.3 | async-start | bytes 1179648 | tf_op jit(solution)/shard_map/all_to_all | solution.py:747
  423.0 27.8 %copy-start.1 = (bf16[96,2304]{1,0:T(8,128)(2,1)S(1)}, bf16[96,2304]{1,0:T(8,128)(2,1)}, u32[]{:S(2)}) copy-start(bf16[96,2304]{1,0:T(8,128)(2,1)} %param.19) | copy-start | bytes 1327108
  (18 other events, 54.0 us)
Sparse Core Ops, SparseCore 0:
  10.8 47.0 all-gather.2
  60.6 83.8 all-gather.4
  197.0 66.9 reduce-scatter.2
  267.5 73.2 reduce-scatter.4
